TPU v7x, 32 devices: a whole 2x2x4 slice. The times are simulated.
32 devices in a mesh: row: 4 (over z), col: 8 (over y, x, core).
Axes of the slice: x: 2, y: 2, z: 4, core: 2. Of those that a mesh axis runs over, the one named last changes fastest.
Arguments:
- block_input: bfloat16 [8192, 2048], P('row', 'col'), may hold values from -6 to 6
- seq_lengths: int32 [8], replicated, may hold values from 1 to 1024, 6144 in all
- slot_order: int32 [8], replicated, may hold values from 0 to 7, each once
- routes: int32 [8192, 4], P('row'), may hold values from 0 to 7, all different within a row; in each aligned block of 1024 rows (0 to 1023, 1024 to 2047, ...) at most 1024 rows name the same one
- input_gain: bfloat16 [2048], P('col'), may hold values from 0.5 to 1.5
- query_weight: bfloat16 [2048, 2048], P('row', 'col'), may hold values from -0.125 to 0.125
- key_weight: bfloat16 [2048, 2048], P('row', 'col'), may hold values from -0.125 to 0.125
- value_weight: bfloat16 [2048, 2048], P('row', 'col'), may hold values from -0.125 to 0.125
- output_weight: bfloat16 [2048, 2048], P('col', 'row'), may hold values from -2 to 2
- mlp_gain: bfloat16 [2048], P('col'), may hold values from 0.5 to 1.5
- router_weight: bfloat16 [2048, 8], P('row'), may hold values from -0.0625 to 0.0625
- score_shared: bfloat16 [2048], P('row'), may hold values from -0.125 to 0.125
- gate_shared: bfloat16 [2048, 5632], P('row', 'col'), may hold values from -0.125 to 0.125
- up_shared: bfloat16 [2048, 5632], P('row', 'col'), may hold values from -0.125 to 0.125
- down_shared: bfloat16 [5632, 2048], P('col', 'row'), may hold values from -0.21875 to 0.21875
- gate_expert: bfloat16 [8, 2048, 1408], P('col', 'row'), may hold values from -0.125 to 0.125
- up_expert: bfloat16 [8, 2048, 1408], P('col', 'row'), may hold values from -0.125 to 0.125
- down_expert: bfloat16 [8, 1408, 2048], P('col', None, 'row'), may hold values from -1.25 to 1.25
- grad_output: bfloat16 [8192, 2048], P('row', 'col'), may hold values from -6 to 6
Outputs:
- block_output: bfloat16 [8192, 2048], P('row', 'col')
- grad_input: bfloat16 [8192, 2048], P('row', 'col')
- grad_input_gain: float32 [2048], P('col')
- grad_query: float32 [2048, 2048], P('row', 'col')
- grad_key: float32 [2048, 2048], P('row', 'col')
- grad_value: float32 [2048, 2048], P('row', 'col')
- grad_output_weight: float32 [2048, 2048], P('col', 'row')
- grad_mlp_gain: float32 [2048], P('col')
- grad_router: float32 [2048, 8], P('row')
- grad_score_shared: float32 [2048], P('row')
- grad_gate_shared: float32 [2048, 5632], P('row', 'col')
- grad_up_shared: float32 [2048, 5632], P('row', 'col')
- grad_down_shared: float32 [5632, 2048], P('col', 'row')
- grad_gate_expert: float32 [8, 2048, 1408], P('col', 'row')
- grad_up_expert: float32 [8, 2048, 1408], P('col', 'row')
- grad_down_expert: float32 [8, 1408, 2048], P('col', None, 'row')
Inputs may be any that keep to these rules, and one draw needn't show every extreme that they name: `seq_lengths`: they add up to 6144; the longest is exactly 1024. `slot_order`: each slot number appears once. `routes`: each row names 4 different experts; in each aligned block of 1024 consecutive rows (one micro-batch of one row-device's tokens) no expert is named by more than 1024 rows, so any expert may be named by every row of a block, and some block has an expert named by all of its rows.
All inputs are finite; a program needn't handle non-finite values.
Results may differ from a plain program's by a relative error of at most 0.022.
Values may be sent and summed in bfloat16 or wider, within the bound.
A program may use at most 272 MiB of HBM per device.

v0:
```python
import math

import jax
import jax.numpy as jnp
from jax import lax
from jax.sharding import PartitionSpec as P

HEAD_DIM = 128
SEQ_LEN = 1024
MICRO = 2


norm_eps = 1e-06
rope_base = 1000000.0
highest = lax.Precision.HIGHEST


def gated_product(left, right):
    return jnp.dot(left, right, preferred_element_type=jnp.float32)


def product_back(left, right):
    return lax.dot_general(
        left, right, (((1,), (1,)), ((), ())), preferred_element_type=jnp.float32
    )


def gated_product_factor(left, right):
    return lax.dot_general(
        left, right, (((0,), (0,)), ((), ())), preferred_element_type=jnp.float32
    )


def rope_tables(length, width):
    positions = jnp.arange(length).astype(jnp.float32)
    freqs = jnp.power(jnp.float32(rope_base), -jnp.arange(0, width, 2).astype(jnp.float32) / width)
    angles = positions[:, None] * freqs[None, :]
    angles = jnp.concatenate([angles, angles], axis=-1)
    return (jnp.cos(angles)[:, None, :], jnp.sin(angles)[:, None, :])


def rotate(values, cosine, sine):
    half = values.shape[-1] // 2
    turned = jnp.concatenate([-values[..., half:], values[..., :half]], axis=-1)
    return values * cosine + turned * sine


def rotate_back(grads, cosine, sine):
    half = grads.shape[-1] // 2
    moved = grads * sine
    turned = jnp.concatenate([moved[..., half:], -moved[..., :half]], axis=-1)
    return grads * cosine + turned


def visible(start_offset, block, seq, length):
    query_pos = start_offset + jnp.arange(block)[:, None]
    key_pos = jnp.arange(seq)[None, :]
    return (key_pos <= query_pos) & (key_pos < length)


def attend_forward(query, keyset, valueset, lengths, block):
    seq = query.shape[1]
    scale = 1.0 / math.sqrt(query.shape[3])
    starts = jnp.arange(seq // block) * block

    def one_slot(items):
        q_slot, k_slot, v_slot, length = items

        def one_block(start_offset):
            rows = lax.dynamic_slice_in_dim(q_slot, start_offset, block, 0)
            raw = jnp.einsum("qhd,khd->hqk", rows, k_slot, preferred_element_type=jnp.float32)
            scores = jnp.where(visible(start_offset, block, seq, length)[None], raw * scale, -1e30)
            top = jnp.max(scores, axis=-1, keepdims=True)
            expo = jnp.exp(scores - top)
            total = jnp.sum(expo, axis=-1, keepdims=True)
            probs = (expo / total).astype(jnp.bfloat16)
            context = jnp.einsum("hqk,khd->qhd", probs, v_slot, preferred_element_type=jnp.float32)
            return (context, top + jnp.log(total))

        context, spread = lax.map(one_block, starts)
        return (context.reshape(seq, context.shape[2], context.shape[3]), spread)

    return lax.map(one_slot, (query, keyset, valueset, lengths))


def attend_backward(query, keyset, valueset, dcontext, spreads, lengths, block):
    seq = query.shape[1]
    scale = 1.0 / math.sqrt(query.shape[3])
    starts = jnp.arange(seq // block) * block

    def one_slot(items):
        q_slot, k_slot, v_slot, d_slot, s_slot, length = items

        def step(carry, input_tuple):
            dkey, dvalue = carry
            start_offset, spread = input_tuple
            rows = lax.dynamic_slice_in_dim(q_slot, start_offset, block, 0)
            drows = lax.dynamic_slice_in_dim(d_slot, start_offset, block, 0)
            raw = jnp.einsum("qhd,khd->hqk", rows, k_slot, preferred_element_type=jnp.float32)
            scores = jnp.where(visible(start_offset, block, seq, length)[None], raw * scale, -1e30)
            probs = jnp.exp(scores - spread)
            rounded = probs.astype(jnp.bfloat16)
            dvalue = dvalue + jnp.einsum(
                "hqk,qhd->khd", rounded, drows, preferred_element_type=jnp.float32
            )
            dprobs = jnp.einsum("qhd,khd->hqk", drows, v_slot, preferred_element_type=jnp.float32)
            dscore = probs * (dprobs - jnp.sum(dprobs * probs, axis=-1, keepdims=True))
            draw = (dscore * scale).astype(jnp.bfloat16)
            dquery = jnp.einsum("hqk,khd->qhd", draw, k_slot, preferred_element_type=jnp.float32)
            dkey = dkey + jnp.einsum("hqk,qhd->khd", draw, rows, preferred_element_type=jnp.float32)
            return ((dkey, dvalue), dquery)

        zeros = jnp.zeros(k_slot.shape, jnp.float32)
        (dkey, dvalue), dquery = lax.scan(step, (zeros, zeros), (starts, s_slot))
        return (dquery.reshape(k_slot.shape), dkey, dvalue)

    return lax.map(one_slot, (query, keyset, valueset, dcontext, spreads, lengths))


def share_sum(values):
    return lax.psum_scatter(
        values.astype(jnp.bfloat16), "col", scatter_dimension=1, tiled=True
    ).astype(jnp.float32)


def norm_back(grad_share, stream_share, scale, gain_share, full_width):
    weighted = grad_share * gain_share
    inner = lax.psum(jnp.sum(weighted * stream_share, axis=1), "col")
    return scale * weighted - stream_share * (scale * scale * scale) * inner[:, None] / full_width


def reduce_grads(parts):
    return (
        lax.psum_scatter(
            parts[0].astype(jnp.bfloat16), "row", scatter_dimension=0, tiled=True
        ).astype(jnp.float32),
        lax.psum_scatter(
            parts[1].astype(jnp.bfloat16), "row", scatter_dimension=0, tiled=True
        ).astype(jnp.float32),
        lax.psum_scatter(
            parts[2].astype(jnp.bfloat16), "row", scatter_dimension=0, tiled=True
        ).astype(jnp.float32),
        lax.psum_scatter(
            parts[3].astype(jnp.bfloat16), "row", scatter_dimension=1, tiled=True
        ).astype(jnp.float32),
        lax.psum_scatter(
            parts[4].astype(jnp.bfloat16), "row", scatter_dimension=0, tiled=True
        ).astype(jnp.float32),
        lax.psum_scatter(
            parts[5].astype(jnp.bfloat16), "row", scatter_dimension=0, tiled=True
        ).astype(jnp.float32),
        lax.psum_scatter(
            parts[6].astype(jnp.bfloat16), "row", scatter_dimension=0, tiled=True
        ).astype(jnp.float32),
        lax.psum_scatter(
            parts[7].astype(jnp.bfloat16), "row", scatter_dimension=0, tiled=True
        ).astype(jnp.float32),
        lax.psum_scatter(
            parts[8].astype(jnp.bfloat16), "row", scatter_dimension=1, tiled=True
        ).astype(jnp.float32),
        lax.psum_scatter(
            parts[9].astype(jnp.bfloat16), "row", scatter_dimension=1, tiled=True
        ).astype(jnp.float32),
        lax.psum_scatter(
            parts[10].astype(jnp.bfloat16), "row", scatter_dimension=1, tiled=True
        ).astype(jnp.float32),
        lax.psum_scatter(
            parts[11].astype(jnp.bfloat16), "row", scatter_dimension=2, tiled=True
        ).astype(jnp.float32),
    )


def per_device(
    block_input,
    seq_lengths,
    slot_order,
    routes,
    input_gain,
    query_weight,
    key_weight,
    value_weight,
    output_weight,
    mlp_gain,
    router_weight,
    score_shared,
    gate_shared,
    up_shared,
    down_shared,
    gate_expert,
    up_expert,
    down_expert,
    grad_output,
):
    rows_dev = block_input.shape[0]
    mb_rows = rows_dev // MICRO
    slots = mb_rows // SEQ_LEN
    share = block_input.shape[1]
    full_width = share * lax.axis_size("col")
    col_id = lax.axis_index("col")
    row_id = lax.axis_index("row")
    local_experts = gate_expert.shape[0]
    expert_count = router_weight.shape[1]
    capacity = 2 * mb_rows * routes.shape[1] // expert_count
    block = min(512, SEQ_LEN)
    cosine, sine = rope_tables(SEQ_LEN, HEAD_DIM)
    slot_length = seq_lengths[slot_order]
    outputs = []
    input_grads = []
    totals = None
    gain_a_acc = jnp.zeros((share,), jnp.float32)
    gain_b_acc = jnp.zeros((share,), jnp.float32)
    for micro_id in range(MICRO):
        (
            query_full,
            key_full,
            value_full,
            output_full,
            router_full,
            score_full,
            sgate_full,
            sup_full,
            sdown_full,
            egate_full,
            expert_up_complete,
            edown_full,
        ) = (
            lax.all_gather(query_weight, "row", axis=0, tiled=True),
            lax.all_gather(key_weight, "row", axis=0, tiled=True),
            lax.all_gather(value_weight, "row", axis=0, tiled=True),
            lax.all_gather(output_weight, "row", axis=1, tiled=True),
            lax.all_gather(router_weight, "row", axis=0, tiled=True),
            lax.all_gather(score_shared, "row", axis=0, tiled=True),
            lax.all_gather(gate_shared, "row", axis=0, tiled=True),
            lax.all_gather(up_shared, "row", axis=0, tiled=True),
            lax.all_gather(down_shared, "row", axis=1, tiled=True),
            lax.all_gather(gate_expert, "row", axis=1, tiled=True),
            lax.all_gather(up_expert, "row", axis=1, tiled=True),
            lax.all_gather(down_expert, "row", axis=2, tiled=True),
        )
        part_in = lax.slice_in_dim(
            block_input, micro_id * mb_rows, (micro_id + 1) * mb_rows, axis=0
        )
        rows_in, gain_a_b, gain_b_b = (
            lax.all_gather(part_in, "col", axis=1, tiled=True),
            lax.all_gather(input_gain, "col", axis=0, tiled=True),
            lax.all_gather(mlp_gain, "col", axis=0, tiled=True),
        )
        attention_norm_gain = gain_a_b.astype(jnp.float32)
        feedforward_norm_gain = gain_b_b.astype(jnp.float32)
        lengths = lax.dynamic_slice_in_dim(
            slot_length, (row_id * MICRO + micro_id) * slots, slots, 0
        )
        routes_mb = lax.slice_in_dim(routes, micro_id * mb_rows, (micro_id + 1) * mb_rows, axis=0)
        rows_f = rows_in.astype(jnp.float32)
        scale_a = lax.rsqrt(jnp.mean(rows_f * rows_f, axis=-1, keepdims=True) + norm_eps)
        normed_a = (rows_f * scale_a * attention_norm_gain).astype(jnp.bfloat16)
        heads_local = query_full.shape[1] // HEAD_DIM
        shape4 = (slots, SEQ_LEN, heads_local, HEAD_DIM)
        query = rotate(gated_product(normed_a, query_full).reshape(shape4), cosine, sine).astype(
            jnp.bfloat16
        )
        keyset = rotate(gated_product(normed_a, key_full).reshape(shape4), cosine, sine).astype(
            jnp.bfloat16
        )
        valueset = gated_product(normed_a, value_full).reshape(shape4).astype(jnp.bfloat16)
        context, spreads = attend_forward(query, keyset, valueset, lengths, block)
        context_b = context.astype(jnp.bfloat16).reshape(mb_rows, heads_local * HEAD_DIM)
        attn_part = gated_product(context_b, output_full)
        stream = rows_f + lax.psum(attn_part, "col")
        scale_b = lax.rsqrt(jnp.mean(stream * stream, axis=-1, keepdims=True) + norm_eps)
        normed_b = (stream * scale_b * feedforward_norm_gain).astype(jnp.bfloat16)
        logits = gated_product(normed_b, router_full)
        top = jnp.max(logits, axis=-1, keepdims=True)
        expo = jnp.exp(logits - top)
        router_probs = expo / jnp.sum(expo, axis=-1, keepdims=True)
        shared_gate = jax.nn.sigmoid(gated_product(normed_b, score_full))
        sgate_pre = gated_product(normed_b, sgate_full)
        sup_pre = gated_product(normed_b, sup_full)
        shared_hidden = (jax.nn.silu(sgate_pre) * sup_pre).astype(jnp.bfloat16)
        shared_part = gated_product(shared_hidden, sdown_full)
        moe_part = shared_gate[:, None] * shared_part
        local_expert_index = 0
        expert_id = col_id * local_experts + local_expert_index
        expert_membership = jnp.any(routes_mb == expert_id, axis=1)
        index = jnp.nonzero(expert_membership, size=capacity, fill_value=0)[0].astype(jnp.int32)
        valid = jnp.arange(capacity) < jnp.sum(expert_membership.astype(jnp.int32))
        selected_probability = normed_b[index]
        gate_pre = gated_product(selected_probability, egate_full[local_expert_index])
        up_projection_input = gated_product(
            selected_probability, expert_up_complete[local_expert_index]
        )
        hidden_e = (jax.nn.silu(gate_pre) * up_projection_input).astype(jnp.bfloat16)
        result = gated_product(hidden_e, edown_full[local_expert_index])
        column = lax.dynamic_index_in_dim(router_probs, expert_id, 1, False)
        weight_col = jnp.where(valid, column[index], 0.0)
        moe_part = moe_part.at[index].add(weight_col[:, None] * result)
        records = [
            (
                expert_id,
                index,
                valid,
                selected_probability,
                gate_pre,
                up_projection_input,
                hidden_e,
                result,
                weight_col,
            )
        ]
        moe_share = lax.psum_scatter(
            moe_part.astype(jnp.bfloat16), "col", scatter_dimension=1, tiled=True
        ).astype(jnp.float32)
        stream_share = lax.dynamic_slice_in_dim(stream, col_id * share, share, 1)
        outputs.append((stream_share + moe_share).astype(jnp.bfloat16))
        cot_share = lax.slice_in_dim(
            grad_output, micro_id * mb_rows, (micro_id + 1) * mb_rows, axis=0
        )
        cot_rows = lax.all_gather(cot_share, "col", axis=1, tiled=True).astype(jnp.float32)
        dprob = jnp.zeros((mb_rows, expert_count), jnp.float32)
        dnorm_part = jnp.zeros((mb_rows, full_width), jnp.float32)
        local_expert_index = 0
        (
            expert_id,
            index,
            valid,
            selected_probability,
            gate_pre,
            up_projection_input,
            hidden_e,
            result,
            weight_col,
        ) = records[local_expert_index]
        rows_grad = cot_rows[index]
        dprob_e = jnp.where(valid, jnp.sum(rows_grad * result, axis=1), 0.0)
        dprob = dprob.at[index, expert_id].add(dprob_e)
        dresult = (weight_col[:, None] * rows_grad).astype(jnp.bfloat16)
        dhidden = product_back(dresult, edown_full[local_expert_index])
        sigma = jax.nn.sigmoid(gate_pre)
        dgate_b = (dhidden * up_projection_input * sigma * (1.0 + gate_pre * (1.0 - sigma))).astype(
            jnp.bfloat16
        )
        expert_up_cotangent = (dhidden * gate_pre * sigma).astype(jnp.bfloat16)
        edown_grads = [gated_product_factor(hidden_e, dresult)]
        egate_grads = [gated_product_factor(selected_probability, dgate_b)]
        expert_up_gradient = [gated_product_factor(selected_probability, expert_up_cotangent)]
        dpicked = product_back(dgate_b, egate_full[local_expert_index]) + product_back(
            expert_up_cotangent, expert_up_complete[local_expert_index]
        )
        dnorm_part = dnorm_part.at[index].add(dpicked)
        dshared = (shared_gate[:, None] * cot_rows).astype(jnp.bfloat16)
        dshidden = product_back(dshared, sdown_full)
        ssigma = jax.nn.sigmoid(sgate_pre)
        dsgate_b = (dshidden * sup_pre * ssigma * (1.0 + sgate_pre * (1.0 - ssigma))).astype(
            jnp.bfloat16
        )
        dsup_b = (dshidden * sgate_pre * ssigma).astype(jnp.bfloat16)
        grad_sdown = gated_product_factor(shared_hidden, dshared)
        grad_sgate = gated_product_factor(normed_b, dsgate_b)
        grad_sup = gated_product_factor(normed_b, dsup_b)
        dnorm_part = (
            dnorm_part + product_back(dsgate_b, sgate_full) + product_back(dsup_b, sup_full)
        )
        shared_dot = jnp.sum(cot_rows * shared_part, axis=1)
        dprob, shared_dot = (
            lax.psum(dprob.astype(jnp.bfloat16), "col").astype(jnp.float32),
            lax.psum(shared_dot.astype(jnp.bfloat16), "col").astype(jnp.float32),
        )
        dlogits = router_probs * (dprob - jnp.sum(dprob * router_probs, axis=1, keepdims=True))
        dslogit = shared_dot * shared_gate * (1.0 - shared_gate)
        grad_router = jnp.einsum(
            "nd,ne->de", normed_b, dlogits, precision=highest, preferred_element_type=jnp.float32
        )
        grad_score = jnp.einsum(
            "nd,n->d", normed_b, dslogit, precision=highest, preferred_element_type=jnp.float32
        )
        dnorm_b = share_sum(dnorm_part)
        router_rows = lax.dynamic_slice_in_dim(router_full, col_id * share, share, 0)
        score_rows = lax.dynamic_slice_in_dim(score_full, col_id * share, share, 0).astype(
            jnp.float32
        )
        dnorm_b = dnorm_b + jnp.einsum(
            "ne,de->nd", dlogits, router_rows, precision=highest, preferred_element_type=jnp.float32
        )
        dnorm_b = dnorm_b + dslogit[:, None] * score_rows[None, :]
        gain_b_share = lax.dynamic_slice_in_dim(feedforward_norm_gain, col_id * share, share, 0)
        dstream = cot_share.astype(jnp.float32) + norm_back(
            dnorm_b, stream_share, scale_b, gain_b_share, full_width
        )
        gain_b_acc = gain_b_acc + jnp.sum(dnorm_b * stream_share * scale_b, axis=0)
        dattn = lax.all_gather(dstream.astype(jnp.bfloat16), "col", axis=1, tiled=True)
        grad_output_w = gated_product_factor(context_b, dattn)
        dcontext = product_back(dattn, output_full).astype(jnp.bfloat16).reshape(shape4)
        dquery, dkey, dvalue = attend_backward(
            query, keyset, valueset, dcontext, spreads, lengths, block
        )
        flat = (mb_rows, heads_local * HEAD_DIM)
        dquery_b = rotate_back(dquery, cosine, sine).astype(jnp.bfloat16).reshape(flat)
        dkey_b = rotate_back(dkey, cosine, sine).astype(jnp.bfloat16).reshape(flat)
        dvalue_b = dvalue.astype(jnp.bfloat16).reshape(flat)
        grad_q = gated_product_factor(normed_a, dquery_b)
        grad_k = gated_product_factor(normed_a, dkey_b)
        grad_v = gated_product_factor(normed_a, dvalue_b)
        dnorm_a_part = (
            product_back(dquery_b, query_full)
            + product_back(dkey_b, key_full)
            + product_back(dvalue_b, value_full)
        )
        dnorm_a = share_sum(dnorm_a_part)
        rows_share = lax.dynamic_slice_in_dim(rows_f, col_id * share, share, 1)
        gain_a_share = lax.dynamic_slice_in_dim(attention_norm_gain, col_id * share, share, 0)
        dinput = dstream + norm_back(dnorm_a, rows_share, scale_a, gain_a_share, full_width)
        gain_a_acc = gain_a_acc + jnp.sum(dnorm_a * rows_share * scale_a, axis=0)
        input_grads.append(dinput.astype(jnp.bfloat16))
        parts = (
            grad_q,
            grad_k,
            grad_v,
            grad_output_w,
            grad_router,
            grad_score,
            grad_sgate,
            grad_sup,
            grad_sdown,
            jnp.stack(egate_grads),
            jnp.stack(expert_up_gradient),
            jnp.stack(edown_grads),
        )
        reduced = reduce_grads(parts)
        totals = reduced if totals is None else jax.tree.map(jnp.add, totals, reduced)
    grad_gain_a, grad_gain_b = lax.psum((gain_a_acc, gain_b_acc), "row")
    block_output = jnp.concatenate(outputs, axis=0)
    grad_input = jnp.concatenate(input_grads, axis=0)
    return (
        block_output,
        grad_input,
        grad_gain_a,
        totals[0],
        totals[1],
        totals[2],
        totals[3],
        grad_gain_b,
        totals[4],
        totals[5],
        totals[6],
        totals[7],
        totals[8],
        totals[9],
        totals[10],
        totals[11],
    )


def solution(mesh):
    return jax.shard_map(
        per_device,
        mesh=mesh,
        in_specs=(
            P("row", "col"),
            P(),
            P(),
            P("row", None),
            P("col"),
            P("row", "col"),
            P("row", "col"),
            P("row", "col"),
            P("col", "row"),
            P("col"),
            P("row", None),
            P("row"),
            P("row", "col"),
            P("row", "col"),
            P("col", "row"),
            P("col", "row", None),
            P("col", "row", None),
            P("col", None, "row"),
            P("row", "col"),
        ),
        out_specs=(
            P("row", "col"),
            P("row", "col"),
            P("col"),
            P("row", "col"),
            P("row", "col"),
            P("row", "col"),
            P("col", "row"),
            P("col"),
            P("row", None),
            P("row"),
            P("row", "col"),
            P("row", "col"),
            P("col", "row"),
            P("col", "row", None),
            P("col", "row", None),
            P("col", None, "row"),
        ),
        check_vma=False,
    )
```

profile of v0, /device:TPU:0, one launch (start us, length us, event | category | flops | bytes accessed | tf_op | source)
XLA Modules:
  0.0 2860.2 jit_solution(10011600658183676541)
XLA Ops:
  54.4 36.2 %all-gather.42.cloned.1.call-done = bf16[1024,2048]{1,0:T(8,128)(2,1)} async-done(((bf16[1024,256]{1,0:T(8,128)(2,1)}), bf16[1024,2048]{1,0:T(8,128)(2,1)}) %all-gather.42.cloned.1.call-update) | async-done | bytes 4194320 | tf_op jit(solution)/shard_map/all_gather | solution.py:244
  336.2 172.3 %all-reduce.12.cloned.1.call-done = (f32[1024,2048]{1,0:T(8,128)}, f32[1024,2048]{1,0:T(8,128)}) async-done(((f32[1024,2048]{1,0:T(8,128)}, f32[1024,2048]{1,0:T(8,128)}), (f32[1024,2048]{1,0:T(8,128)}, f32[1024,2048]{1,0:T(8,128)})) %all-reduce.12.cloned.1.call-update) | async-done | bytes 16777232 | tf_op jit(solution)/shard_map/psum | solution.py:269
  544.3 72.4 %all-gather.36.cloned.1.call-done = bf16[1,2048,1408]{2,1,0:T(8,128)(2,1)} async-done(((bf16[1,512,1408]{2,1,0:T(8,128)(2,1)}), bf16[1,2048,1408]{2,1,0:T(8,128)(2,1)}) %all-gather.36.cloned.1.call-update) | async-done | bytes 5767184 | tf_op jit(solution)/shard_map/all_gather | solution.py:236
  628.4 95.1 %all-gather.38.cloned.1.call-done = bf16[1,2048,1408]{2,1,0:T(8,128)(2,1)} async-done(((bf16[1,512,1408]{2,1,0:T(8,128)(2,1)}), bf16[1,2048,1408]{2,1,0:T(8,128)(2,1)}) %all-gather.38.cloned.1.call-update) | async-done | bytes 5767184 | tf_op jit(solution)/shard_map/all_gather | solution.py:237
  736.5 93.5 %all-gather.40.cloned.1.call-done = bf16[1,1408,2048]{2,1,0:T(8,128)(2,1)} async-done(((bf16[1,1408,512]{2,1,0:T(8,128)(2,1)}), bf16[1,1408,2048]{2,1,0:T(8,128)(2,1)}) %all-gather.40.cloned.1.call-update) | async-done | bytes 5767184 | tf_op jit(solution)/shard_map/all_gather | solution.py:238
  961.6 46.2 %all-gather.34.cloned.1.call-done = bf16[704,2048]{1,0:T(8,128)(2,1)} async-done(((bf16[704,512]{1,0:T(8,128)(2,1)}), bf16[704,2048]{1,0:T(8,128)(2,1)}) %all-gather.34.cloned.1.call-update) | async-done | bytes 2883600 | tf_op jit(solution)/shard_map/all_gather | solution.py:235
  1038.4 25.2 all-reduce.8
  1123.4 23.5 scatter_custom_fusion.5
  1198.9 23.6 scatter_custom_fusion.4
  1228.7 23.1 scatter_custom_fusion.3
  1306.4 25.1 reduce-scatter.31.cloned.1.call-done
  1331.5 54.7 %reduce-scatter.29.cloned.1.call-done = bf16[1024,256]{1,0:T(8,128)(2,1)} async-done(((bf16[1024,2048]{1,0:T(8,128)(2,1)}), bf16[1024,256]{1,0:T(8,128)(2,1)}) %reduce-scatter.29.cloned.1.call-update) | async-done | bytes 524304 | tf_op jit(solution)/shard_map/reduce_scatter | solution.py:310
  1534.7 61.6 %while.97 = (s32[]{:T(128)}, f32[1024,2,128]{0,2,1:T(8,128)}, f32[1024,2,128]{0,2,1:T(8,128)S(1)}, f32[2,512,2,128]{3,1,2,0:T(8,128)}, s32[2]{0:T(128)S(1)}, /*i...) while((s32[]{:T(128)}, f32[1024,2,128]{0,2,1:T(8,128)}, ...), condition=%wide.region_64.65_spmd.clone, body=%wide.region_62.64_spmd.clone.sunk | while | flops 1358960128 | bytes 56642292 | solution.py:114
  1607.0 59.5 %while.96 = (s32[]{:T(128)}, f32[1024,2,128]{0,2,1:T(8,128)}, f32[1024,2,128]{0,2,1:T(8,128)S(1)}, f32[2,512,2,128]{3,1,2,0:T(8,128)}, s32[2]{0:T(128)S(1)}, /*i...) while((s32[]{:T(128)}, f32[1024,2,128]{0,2,1:T(8,128)}, ...), condition=%wide.region_48.49_spmd.clone, body=%wide.region_46.48_spmd.clone.sunk | while | flops 1358960128 | bytes 54545112 | solution.py:114
  1750.8 48.2 %reduce-scatter.61.cloned.1.call-done = bf16[512,704]{0,1:T(8,128)(2,1)} async-done(((bf16[2048,704]{0,1:T(8,128)(2,1)}), bf16[512,704]{0,1:T(8,128)(2,1)}) %reduce-scatter.61.cloned.1.call-update) | async-done | bytes 720912 | tf_op jit(solution)/shard_map/reduce_scatter | solution.py:152
  1799.0 58.5 %reduce-scatter.63.cloned.1.call-done = bf16[512,704]{0,1:T(8,128)(2,1)} async-done(((bf16[2048,704]{0,1:T(8,128)(2,1)}), bf16[512,704]{0,1:T(8,128)(2,1)}) %reduce-scatter.63.cloned.1.call-update) | async-done | bytes 720912 | tf_op jit(solution)/shard_map/reduce_scatter | solution.py:152
  1861.2 100.7 %reduce-scatter.81.cloned.1.call-done = bf16[1,1408,512]{2,1,0:T(8,128)(2,1)} async-done(((bf16[1,1408,2048]{2,1,0:T(8,128)(2,1)}), bf16[1,1408,512]{2,1,0:T(8,128)(2,1)}) %reduce-scatter.81.cloned.1.call-update) | async-done | bytes 1441808 | tf_op jit(solution)/shard_map/reduce_scatter | solution.py:167
  1961.9 105.2 %reduce-scatter.83.cloned.1.call-done = bf16[1,1408,512]{2,1,0:T(8,128)(2,1)} async-done(((bf16[1,1408,2048]{2,1,0:T(8,128)(2,1)}), bf16[1,1408,512]{2,1,0:T(8,128)(2,1)}) %reduce-scatter.83.cloned.1.call-update) | async-done | bytes 1441808 | tf_op jit(solution)/shard_map/reduce_scatter | solution.py:167
  2070.9 101.4 %reduce-scatter.77.cloned.1.call-done = bf16[1,512,1408]{2,1,0:T(8,128)(2,1)} async-done(((bf16[1,2048,1408]{2,1,0:T(8,128)(2,1)}), bf16[1,512,1408]{2,1,0:T(8,128)(2,1)}) %reduce-scatter.77.cloned.1.call-update) | async-done | bytes 1441808 | tf_op jit(solution)/shard_map/reduce_scatter | solution.py:164
  2172.3 105.1 %reduce-scatter.79.cloned.1.call-done = bf16[1,512,1408]{2,1,0:T(8,128)(2,1)} async-done(((bf16[1,2048,1408]{2,1,0:T(8,128)(2,1)}), bf16[1,512,1408]{2,1,0:T(8,128)(2,1)}) %reduce-scatter.79.cloned.1.call-update) | async-done | bytes 1441808 | tf_op jit(solution)/shard_map/reduce_scatter | solution.py:164
  2281.0 101.6 %reduce-scatter.73.cloned.1.call-done = bf16[1,512,1408]{2,1,0:T(8,128)(2,1)} async-done(((bf16[1,2048,1408]{2,1,0:T(8,128)(2,1)}), bf16[1,512,1408]{2,1,0:T(8,128)(2,1)}) %reduce-scatter.73.cloned.1.call-update) | async-done | bytes 1441808 | tf_op jit(solution)/shard_map/reduce_scatter | solution.py:161
  2382.6 105.2 %reduce-scatter.75.cloned.1.call-done = bf16[1,512,1408]{2,1,0:T(8,128)(2,1)} async-done(((bf16[1,2048,1408]{2,1,0:T(8,128)(2,1)}), bf16[1,512,1408]{2,1,0:T(8,128)(2,1)}) %reduce-scatter.75.cloned.1.call-update) | async-done | bytes 1441808 | tf_op jit(solution)/shard_map/reduce_scatter | solution.py:161
  2491.4 26.3 reduce-scatter.53.cloned.1.call-done
  2517.7 28.0 reduce-scatter.55.cloned.1.call-done
  2547.6 26.3 reduce-scatter.51.cloned.1.call-done
  2573.9 28.0 reduce-scatter.49.cloned.1.call-done
  2603.7 26.4 reduce-scatter.45.cloned.1.call-done
  2630.1 28.1 reduce-scatter.47.cloned.1.call-done
  2660.1 26.4 reduce-scatter.41.cloned.1.call-done
  2686.5 27.9 reduce-scatter.43.cloned.1.call-done
  2716.3 51.9 %reduce-scatter.39.cloned.1.call-done = bf16[1024,256]{1,0:T(8,128)(2,1)} async-done(((bf16[1024,2048]{1,0:T(8,128)(2,1)}), bf16[1024,256]{1,0:T(8,128)(2,1)}) %reduce-scatter.39.cloned.1.call-update) | async-done | bytes 524304 | tf_op jit(solution)/shard_map/reduce_scatter | solution.py:121
  2768.2 54.5 %reduce-scatter.35.cloned.1.call-done = bf16[1024,256]{1,0:T(8,128)(2,1)} async-done(((bf16[1024,2048]{1,0:T(8,128)(2,1)}), bf16[1024,256]{1,0:T(8,128)(2,1)}) %reduce-scatter.35.cloned.1.call-update) | async-done | bytes 524304 | tf_op jit(solution)/shard_map/reduce_scatter | solution.py:121
  (789 shorter events, 1119.9 us)
Async XLA Ops:
  14.7 493.8 %all-reduce.12.cloned.1.call-start = ((), (), s32[]{:S(2)}) async-start(), calls=%async_computation.72 | async-start | bytes 33554432 | tf_op jit(solution)/shard_map/psum | solution.py:269
  237.7 379.1 %all-gather.36.cloned.1.call-start = ((), (), s32[]{:S(2)}) async-start(), calls=%async_computation.36 | async-start | bytes 7208960 | tf_op jit(solution)/shard_map/all_gather | solution.py:236
  238.3 485.2 %all-gather.38.cloned.1.call-start = ((), (), s32[]{:S(2)}) async-start(), calls=%async_computation.37 | async-start | bytes 7208960 | tf_op jit(solution)/shard_map/all_gather | solution.py:237
  239.0 591.0 %all-gather.40.cloned.1.call-start = ((), (), s32[]{:S(2)}) async-start(), calls=%async_computation.38 | async-start | bytes 7208960 | tf_op jit(solution)/shard_map/all_gather | solution.py:238
  239.6 674.6 %all-gather.30.cloned.1.call-start = ((), (), s32[]{:S(2)}) async-start(), calls=%async_computation.33 | async-start | bytes 3604480 | tf_op jit(solution)/shard_map/all_gather | solution.py:233
  240.3 708.2 %all-gather.32.cloned.1.call-start = ((), (), s32[]{:S(2)}) async-start(), calls=%async_computation.34 | async-start | bytes 3604480 | tf_op jit(solution)/shard_map/all_gather | solution.py:234
  240.9 767.0 %all-gather.34.cloned.1.call-start = ((), (), s32[]{:S(2)}) async-start(), calls=%async_computation.35 | async-start | bytes 3604480 | tf_op jit(solution)/shard_map/all_gather | solution.py:235
  241.5 1046.9 %reduce-scatter.37.cloned.1.call-start = ((), (), s32[]{:S(2)}) async-start(), calls=%async_computation.47 | async-start | bytes 4718592 | tf_op jit(solution)/shard_map/reduce_scatter | solution.py:121
  1390.9 352.9 %reduce-scatter.57.cloned.1.call-start = ((), (), s32[]{:S(2)}) async-start(), calls=%async_computation.58 | async-start | bytes 40960 | tf_op jit(solution)/shard_map/reduce_scatter | solution.py:146
  1395.6 348.1 %reduce-scatter.59.cloned.1.call-start = ((), (), s32[]{:S(2)}) async-start(), calls=%async_computation.59 | async-start | bytes 40960 | tf_op jit(solution)/shard_map/reduce_scatter | solution.py:146
  1400.5 344.6 %reduce-scatter.69.cloned.1.call-start = ((), (), s32[]{:S(2)}) async-start(), calls=%async_computation.64 | async-start | bytes 3604480 | tf_op jit(solution)/shard_map/reduce_scatter | solution.py:158
  1407.6 337.5 %reduce-scatter.71.cloned.1.call-start = ((), (), s32[]{:S(2)}) async-start(), calls=%async_computation.65 | async-start | bytes 3604480 | tf_op jit(solution)/shard_map/reduce_scatter | solution.py:158
  1414.7 333.2 %reduce-scatter.65.cloned.1.call-start = ((), (), s32[]{:S(2)}) async-start(), calls=%async_computation.62 | async-start | bytes 3604480 | tf_op jit(solution)/shard_map/reduce_scatter | solution.py:155
  1421.6 326.3 %reduce-scatter.67.cloned.1.call-start = ((), (), s32[]{:S(2)}) async-start(), calls=%async_computation.63 | async-start | bytes 3604480 | tf_op jit(solution)/shard_map/reduce_scatter | solution.py:155
  1428.5 370.6 %reduce-scatter.61.cloned.1.call-start = ((), (), s32[]{:S(2)}) async-start(), calls=%async_computation.60 | async-start | bytes 3604480 | tf_op jit(solution)/shard_map/reduce_scatter | solution.py:152
  1435.6 421.9 %reduce-scatter.63.cloned.1.call-start = ((), (), s32[]{:S(2)}) async-start(), calls=%async_computation.61 | async-start | bytes 3604480 | tf_op jit(solution)/shard_map/reduce_scatter | solution.py:152
  1442.6 519.3 %reduce-scatter.81.cloned.1.call-start = ((), (), s32[]{:S(2)}) async-start(), calls=%async_computation.70 | async-start | bytes 7208960 | tf_op jit(solution)/shard_map/reduce_scatter | solution.py:167
  1454.0 613.1 %reduce-scatter.83.cloned.1.call-start = ((), (), s32[]{:S(2)}) async-start(), calls=%async_computation.71 | async-start | bytes 7208960 | tf_op jit(solution)/shard_map/reduce_scatter | solution.py:167
  1467.9 704.4 %reduce-scatter.77.cloned.1.call-start = ((), (), s32[]{:S(2)}) async-start(), calls=%async_computation.68 | async-start | bytes 7208960 | tf_op jit(solution)/shard_map/reduce_scatter | solution.py:164
  1480.6 796.8 %reduce-scatter.79.cloned.1.call-start = ((), (), s32[]{:S(2)}) async-start(), calls=%async_computation.69 | async-start | bytes 7208960 | tf_op jit(solution)/shard_map/reduce_scatter | solution.py:164
  1493.3 889.3 %reduce-scatter.73.cloned.1.call-start = ((), (), s32[]{:S(2)}) async-start(), calls=%async_computation.66 | async-start | bytes 7208960 | tf_op jit(solution)/shard_map/reduce_scatter | solution.py:161
  1506.0 981.7 %reduce-scatter.75.cloned.1.call-start = ((), (), s32[]{:S(2)}) async-start(), calls=%async_computation.67 | async-start | bytes 7208960 | tf_op jit(solution)/shard_map/reduce_scatter | solution.py:161
  1518.7 999.0 %reduce-scatter.53.cloned.1.call-start = ((), (), s32[]{:S(2)}) async-start(), calls=%async_computation.56 | async-start | bytes 1310720 | tf_op jit(solution)/shard_map/reduce_scatter | solution.py:143
  1524.2 1021.4 %reduce-scatter.55.cloned.1.call-start = ((), (), s32[]{:S(2)}) async-start(), calls=%async_computation.57 | async-start | bytes 1310720 | tf_op jit(solution)/shard_map/reduce_scatter | solution.py:143
  1528.9 1045.0 %reduce-scatter.51.cloned.1.call-start = ((), (), s32[]{:S(2)}) async-start(), calls=%async_computation.55 | async-start | bytes 1310720 | tf_op jit(solution)/shard_map/reduce_scatter | solution.py:140
  1601.8 1000.1 %reduce-scatter.49.cloned.1.call-start = ((), (), s32[]{:S(2)}) async-start(), calls=%async_computation.54 | async-start | bytes 1310720 | tf_op jit(solution)/shard_map/reduce_scatter | solution.py:140
  1672.0 958.1 %reduce-scatter.45.cloned.1.call-start = ((), (), s32[]{:S(2)}) async-start(), calls=%async_computation.52 | async-start | bytes 1310720 | tf_op jit(solution)/shard_map/reduce_scatter | solution.py:137
  1679.2 979.1 %reduce-scatter.47.cloned.1.call-start = ((), (), s32[]{:S(2)}) async-start(), calls=%async_computation.53 | async-start | bytes 1310720 | tf_op jit(solution)/shard_map/reduce_scatter | solution.py:137
  1683.8 1002.7 %reduce-scatter.41.cloned.1.call-start = ((), (), s32[]{:S(2)}) async-start(), calls=%async_computation.50 | async-start | bytes 1310720 | tf_op jit(solution)/shard_map/reduce_scatter | solution.py:134
  1695.7 1018.7 %reduce-scatter.43.cloned.1.call-start = ((), (), s32[]{:S(2)}) async-start(), calls=%async_computation.51 | async-start | bytes 1310720 | tf_op jit(solution)/shard_map/reduce_scatter | solution.py:134
  1700.5 1067.7 %reduce-scatter.39.cloned.1.call-start = ((), (), s32[]{:S(2)}) async-start(), calls=%async_computation.49 | async-start | bytes 4718592 | tf_op jit(solution)/shard_map/reduce_scatter | solution.py:121
  1706.6 1116.1 %reduce-scatter.35.cloned.1.call-start = ((), (), s32[]{:S(2)}) async-start(), calls=%async_computation.45 | async-start | bytes 4718592 | tf_op jit(solution)/shard_map/reduce_scatter | solution.py:121
  (191 other events, 8557.6 us)
Sparse Core Ops, SparseCore 0:
  10.5 40.1 all-gather.19
  53.1 37.4 all-gather.41
  92.2 27.9 all-gather.21
  209.3 36.8 all-gather.43
  248.6 37.4 all-gather.47
  290.2 218.2 all-reduce.11
  510.0 106.6 all-gather.35
  618.4 104.9 all-gather.37
  725.0 104.9 all-gather.39
  831.6 57.3 all-gather.29
  890.6 57.8 all-gather.31
  950.0 57.8 all-gather.33
  1152.9 48.3 reduce-scatter.36
  1228.8 47.6 reduce-scatter.32
  1280.1 51.3 reduce-scatter.30
  1334.8 51.2 reduce-scatter.28
  1390.2 37.4 all-gather.45
  1430.3 37.4 all-gather.49
  1510.7 54.3 reduce-scatter.68
  1567.5 56.0 reduce-scatter.70
  1625.8 56.0 reduce-scatter.64
  1684.2 56.3 reduce-scatter.66
  1742.9 56.0 reduce-scatter.60
  1801.4 56.0 reduce-scatter.62
  1859.8 102.1 reduce-scatter.80
  1964.3 102.7 reduce-scatter.82
  2069.5 102.7 reduce-scatter.76
  2174.6 102.7 reduce-scatter.78
  2279.8 102.7 reduce-scatter.72
  2385.0 102.7 reduce-scatter.74
  2718.1 50.0 reduce-scatter.38
  2771.4 51.2 reduce-scatter.34
  (13 shorter events, 325.7 us)
where the time goes:
time: 2870 us; the launch traced here: 2860 us
  waiting for transfers between devices  1750 us (61%)
  matrix products  554 us (19%)
  other arithmetic  290 us (10%)
  blocking collectives  119 us (4%)
  local copies, waits for them, and re-layouts  105 us (4%)
    reduce_scatter x2, waiting for transfers between devices, reduce_grads(): lax.psum_scatter(parts[9].astype(jnp.bfloat16), 'row', scatter_dimension=...  207 us
    reduce_scatter x2, waiting for transfers between devices, reduce_grads(): lax.psum_scatter(parts[10].astype(jnp.bfloat16), 'row', scatter_dimension...  206 us
    reduce_scatter x2, waiting for transfers between devices, reduce_grads(): lax.psum_scatter(parts[11].astype(jnp.bfloat16), 'row', scatter_dimension...  206 us
    psum x1, waiting for transfers between devices, per_device(): stream = rows_f + lax.psum(attn_part, 'col')  172 us
    dot_general x24, matrix products, gated_product(): return jnp.dot(left, right, preferred_element_type=jnp.float32)  148 us
    dot_general x20, matrix products, gated_product_factor(): lax.dot_general(left, right, (((0,), (0,)), ((), ())), preferred_element_...  140 us
    dot_general x20, matrix products, product_back(): lax.dot_general(left, right, (((1,), (1,)), ((), ())), preferred_element_...  131 us
    reduce_scatter x2, waiting for transfers between devices, reduce_grads(): lax.psum_scatter(parts[6].astype(jnp.bfloat16), 'row', scatter_dimension=...  107 us
  transfers between devices with their start and end apart: 45, of which 31 were waited for; matrix products, arithmetic and copies ran while one was open for 28% of the time, Pallas kernels for 0%

commit v1 on v0

v1 whole, which is shorter than its diff:
```python
import functools
import math

import jax
import jax.numpy as jnp
from jax import lax
from jax.experimental import pallas as pl
from jax.experimental.pallas import tpu as pltpu
from jax.sharding import PartitionSpec as P

HEAD_DIM = 128
SEQ_LEN = 1024
QBLOCK = 256
CHUNK = 512
norm_eps = 1e-06
rope_base = 1000000.0
bf16 = jnp.bfloat16
f32 = jnp.float32


def mm(left, right):
    return jnp.dot(left, right, preferred_element_type=f32)


def mm_nt(left, right):
    return lax.dot_general(left, right, (((1,), (1,)), ((), ())), preferred_element_type=f32)


def mm_tn(left, right):
    return lax.dot_general(left, right, (((0,), (0,)), ((), ())), preferred_element_type=f32)


def rope_tables():
    positions = jnp.arange(SEQ_LEN).astype(f32)
    freqs = jnp.power(f32(rope_base), -jnp.arange(0, HEAD_DIM, 2).astype(f32) / HEAD_DIM)
    angles = positions[:, None] * freqs[None, :]
    cosine, sine = jnp.cos(angles), jnp.sin(angles)
    return (
        jnp.concatenate([cosine, cosine], axis=-1),
        jnp.concatenate([-sine, sine], axis=-1),
    )


def block_scores(rows, keys, start, length, scale):
    raw = mm_nt(rows, keys) * scale
    query_pos = start + lax.broadcasted_iota(jnp.int32, raw.shape, 0)
    key_pos = lax.broadcasted_iota(jnp.int32, raw.shape, 1)
    return jnp.where((key_pos <= query_pos) & (key_pos < length), raw, -1e30)


def attend_forward_kernel(length_ref, raw_ref, cos_ref, sin_ref, qkv_ref, context_ref, lse_ref):
    length = length_ref[pl.program_id(0)]
    scale = 1.0 / math.sqrt(HEAD_DIM)
    hd = HEAD_DIM
    for part in range(2):
        raw = raw_ref[:, part * hd : (part + 1) * hd]
        turned = raw * cos_ref[...] + pltpu.roll(raw, hd // 2, 1) * sin_ref[...]
        qkv_ref[:, part * hd : (part + 1) * hd] = turned.astype(bf16)
    qkv_ref[:, 2 * hd :] = raw_ref[:, 2 * hd :].astype(bf16)
    for at in range(0, SEQ_LEN, QBLOCK):
        seen = at + QBLOCK
        scores = block_scores(
            qkv_ref[at:seen, :hd], qkv_ref[:seen, hd : 2 * hd], at, length, scale
        )
        top = jnp.max(scores, axis=-1, keepdims=True)
        expo = jnp.exp(scores - top)
        total = jnp.sum(expo, axis=-1, keepdims=True)
        probs = (expo / total).astype(bf16)
        context_ref[at:seen, :] = mm(probs, qkv_ref[:seen, 2 * hd :]).astype(bf16)
        lse_ref[at:seen, :] = jnp.broadcast_to(top + jnp.log(total), (QBLOCK, hd))


def attend_forward(raw, lengths, cosine, sine):
    tokens, width = raw.shape
    heads = width // (3 * HEAD_DIM)
    slots = tokens // SEQ_LEN
    wide = pl.BlockSpec((SEQ_LEN, 3 * HEAD_DIM), lambda s, h, _: (s, h))
    one = pl.BlockSpec((SEQ_LEN, HEAD_DIM), lambda s, h, _: (s, h))
    table = pl.BlockSpec((SEQ_LEN, HEAD_DIM), lambda s, h, _: (0, 0))
    pairs = slots * heads * SEQ_LEN * SEQ_LEN
    return pl.pallas_call(
        attend_forward_kernel,
        grid_spec=pltpu.PrefetchScalarGridSpec(
            num_scalar_prefetch=1,
            grid=(slots, heads),
            in_specs=[wide, table, table],
            out_specs=[wide, one, one],
        ),
        out_shape=[
            jax.ShapeDtypeStruct((tokens, width), bf16),
            jax.ShapeDtypeStruct((tokens, heads * HEAD_DIM), bf16),
            jax.ShapeDtypeStruct((tokens, heads * HEAD_DIM), f32),
        ],
        cost_estimate=pl.CostEstimate(
            flops=3 * HEAD_DIM * pairs, bytes_accessed=8 * tokens * width, transcendentals=pairs
        ),
        name="attend_forward",
    )(lengths, raw, cosine, sine)


def attend_backward_kernel(
    length_ref, qkv_ref, dcontext_ref, lse_ref, cos_ref, sin_ref, dqkv_ref, inner_ref, dk_ref, dv_ref
):
    length = length_ref[pl.program_id(0)]
    scale = 1.0 / math.sqrt(HEAD_DIM)
    hd = HEAD_DIM
    dk_ref[...] = jnp.zeros_like(dk_ref)
    dv_ref[...] = jnp.zeros_like(dv_ref)

    def turn_back(grad, rows):
        back = grad * cos_ref[rows, :] - pltpu.roll(grad, hd // 2, 1) * sin_ref[rows, :]
        return back.astype(bf16)

    for at in range(0, SEQ_LEN, QBLOCK):
        seen = at + QBLOCK
        rows = qkv_ref[at:seen, :hd]
        keys = qkv_ref[:seen, hd : 2 * hd]
        drows = dcontext_ref[at:seen, :]
        scores = block_scores(rows, keys, at, length, scale)
        probs = jnp.exp(scores - lse_ref[at:seen, :1])
        dv_ref[:seen, :] += mm_tn(probs.astype(bf16), drows)
        dprobs = mm_nt(drows, qkv_ref[:seen, 2 * hd :])
        dscore = probs * (dprobs - jnp.sum(dprobs * probs, axis=-1, keepdims=True))
        draw = (dscore * scale).astype(bf16)
        dquery = mm(draw, keys)
        dk_ref[:seen, :] += mm_tn(draw, rows)
        dqkv_ref[at:seen, :hd] = turn_back(dquery, slice(at, seen))
        inner_ref[at:seen, :] = jnp.broadcast_to(
            jnp.sum(dquery * rows.astype(f32), axis=-1, keepdims=True), (QBLOCK, hd)
        )
    dkey, dvalue = dk_ref[...], dv_ref[...]
    dqkv_ref[:, hd : 2 * hd] = turn_back(dkey, slice(None))
    dqkv_ref[:, 2 * hd :] = dvalue.astype(bf16)
    inner_ref[...] += jnp.broadcast_to(
        jnp.sum(
            dkey * qkv_ref[:, hd : 2 * hd].astype(f32) + dvalue * qkv_ref[:, 2 * hd :].astype(f32),
            axis=-1,
            keepdims=True,
        ),
        inner_ref.shape,
    )


def attend_backward(qkv, dcontext, lse, lengths, cosine, sine):
    tokens, width = qkv.shape
    heads = width // (3 * HEAD_DIM)
    slots = tokens // SEQ_LEN
    wide = pl.BlockSpec((SEQ_LEN, 3 * HEAD_DIM), lambda s, h, _: (s, h))
    one = pl.BlockSpec((SEQ_LEN, HEAD_DIM), lambda s, h, _: (s, h))
    table = pl.BlockSpec((SEQ_LEN, HEAD_DIM), lambda s, h, _: (0, 0))
    pairs = slots * heads * SEQ_LEN * SEQ_LEN
    return pl.pallas_call(
        attend_backward_kernel,
        grid_spec=pltpu.PrefetchScalarGridSpec(
            num_scalar_prefetch=1,
            grid=(slots, heads),
            in_specs=[wide, one, one, table, table],
            out_specs=[wide, one],
            scratch_shapes=[pltpu.VMEM((SEQ_LEN, HEAD_DIM), f32)] * 2,
        ),
        out_shape=[
            jax.ShapeDtypeStruct((tokens, width), bf16),
            jax.ShapeDtypeStruct((tokens, heads * HEAD_DIM), f32),
        ],
        cost_estimate=pl.CostEstimate(
            flops=8 * HEAD_DIM * pairs, bytes_accessed=8 * tokens * width, transcendentals=pairs
        ),
        name="attend_backward",
    )(lengths, qkv, dcontext, lse, cosine, sine)


def gather_rows(part):
    n = lax.axis_size("row")
    if n > 4:
        return lax.all_gather(part, "row", axis=0, tiled=True)
    z = lax.axis_index("row")
    up, down = [part], [part]
    for step in range(1, n):
        up.append(lax.ppermute(up[-1], "row", [(a, a + 1) for a in range(step - 1, n - 1)]))
        down.append(lax.ppermute(down[-1], "row", [(a, a - 1) for a in range(1, n - step + 1)]))
    whole = jnp.zeros((n,) + part.shape, part.dtype)
    for back in range(n):
        piece = part if back == 0 else up[back] + down[n - back]
        whole = lax.dynamic_update_slice_in_dim(whole, piece[None], lax.rem(z + n - back, n), 0)
    return whole.reshape((n * part.shape[0],) + part.shape[1:])


def reduce_rows(grads):
    n = lax.axis_size("row")
    if n > 4:
        whole = jnp.concatenate([g.astype(bf16) for g in grads], axis=1)
        return lax.psum_scatter(whole, "row", scatter_dimension=0, tiled=True).astype(f32)
    z = lax.axis_index("row")
    size = grads[0].shape[0] // n

    def block(j):
        at = jnp.clip(j, 0, n - 1) * size
        return jnp.concatenate(
            [lax.dynamic_slice_in_dim(g, at, size, 0) for g in grads], axis=1
        ).astype(f32)

    up, down = block(n - 1 + z).astype(bf16), block(z - n + 1).astype(bf16)
    for step in range(1, n):
        up_in = lax.ppermute(up, "row", [(a, a + 1) for a in range(step)])
        down_in = lax.ppermute(down, "row", [(a, a - 1) for a in range(n - step, n)])
        if step < n - 1:
            up = (block(n - 1 - step + z) + up_in.astype(f32)).astype(bf16)
            down = (block(z - n + 1 + step) + down_in.astype(f32)).astype(bf16)
    return block(z) + up_in.astype(f32) + down_in.astype(f32)


def split_three(values):
    high = values.astype(bf16)
    rest = values - high.astype(f32)
    middle = rest.astype(bf16)
    return high, middle, (rest - middle.astype(f32)).astype(bf16)


def cuts_of(width):
    at, cuts = 0, []
    while at < width:
        cuts.append((at, min(at + CHUNK, width)))
        at += CHUNK
    return cuts


def per_device(
    block_input,
    seq_lengths,
    slot_order,
    routes,
    input_gain,
    query_weight,
    key_weight,
    value_weight,
    output_weight,
    mlp_gain,
    router_weight,
    score_shared,
    gate_shared,
    up_shared,
    down_shared,
    gate_expert,
    up_expert,
    down_expert,
    grad_output,
):
    tokens, share = block_input.shape
    cols = lax.axis_size("col")
    col_id = lax.axis_index("col")
    row_id = lax.axis_index("row")
    width = share * cols
    slots = tokens // SEQ_LEN
    local_experts = gate_expert.shape[0]
    experts = router_weight.shape[1]
    head_width = query_weight.shape[1]
    heads = head_width // HEAD_DIM
    rows_block = query_weight.shape[0]
    lengths = lax.dynamic_slice_in_dim(seq_lengths[slot_order], row_id * slots, slots, 0)
    cosine, sine = rope_tables()

    def by_head(weight):
        return weight.reshape(rows_block, heads, 1, HEAD_DIM)

    qkv_pack = jnp.concatenate(
        [by_head(query_weight), by_head(key_weight), by_head(value_weight)], axis=2
    ).reshape(rows_block, 3 * head_width)
    attn_weights = gather_rows(jnp.concatenate([qkv_pack, output_weight.T], axis=1))
    qkv_full = attn_weights[:, : 3 * head_width]
    out_full = attn_weights[:, 3 * head_width :]
    units = []
    chunks = [(None, 0, gate_shared.shape[1])]
    units.append(jnp.concatenate([gate_shared, up_shared, down_shared.T], axis=1))
    for local in range(local_experts):
        for a, b in cuts_of(gate_expert.shape[2]):
            chunks.append((local, a, b))
            units.append(
                jnp.concatenate(
                    [gate_expert[local, :, a:b], up_expert[local, :, a:b], down_expert[local, a:b].T],
                    axis=1,
                )
            )
    gathered = [gather_rows(unit) for unit in units]
    router_pack = jnp.concatenate([router_weight, score_shared[:, None]], axis=1)
    router_full = lax.all_gather(router_pack, "row", axis=0, tiled=True)

    rows_in = lax.all_gather(block_input, "col", axis=1, tiled=True)
    gain_a = lax.all_gather(input_gain, "col", axis=0, tiled=True).astype(f32)
    cot_rows = lax.all_gather(grad_output, "col", axis=1, tiled=True)
    rows_f = rows_in.astype(f32)
    scale_a = lax.rsqrt(jnp.mean(rows_f * rows_f, axis=-1, keepdims=True) + norm_eps)
    normed_a = (rows_f * scale_a * gain_a).astype(bf16)
    qkv, context, lse = attend_forward(mm(normed_a, qkv_full), lengths, cosine, sine)
    attn_part = mm_nt(context, out_full).astype(bf16)
    x_share = block_input.astype(f32)
    stream = x_share + lax.psum_scatter(
        attn_part, "col", scatter_dimension=1, tiled=True
    ).astype(f32)
    gain_b = mlp_gain.astype(f32)
    scaled = lax.all_gather((stream * gain_b).astype(bf16), "col", axis=1, tiled=True)
    squares = lax.psum(jnp.sum(stream * stream, axis=1), "col")
    scale_b = lax.rsqrt(squares / width + norm_eps)[:, None]

    both_logits = scale_b * mm(scaled, router_full)
    logits, slogit = both_logits[:, :experts], both_logits[:, experts]
    top = jnp.max(logits, axis=-1, keepdims=True)
    expo = jnp.exp(logits - top)
    router_probs = expo / jnp.sum(expo, axis=-1, keepdims=True)
    shared_gate = jax.nn.sigmoid(slogit)

    moe_part = None
    dscaled_part = None
    unit_grads = []
    inner = jnp.zeros((tokens,), f32)
    dots = {}
    members, shares = {None: None}, {None: shared_gate}
    for local in range(local_experts):
        expert = col_id * local_experts + local
        members[local] = jnp.any(routes == expert, axis=1)
        column = lax.dynamic_index_in_dim(router_probs, expert, 1, False)
        shares[local] = jnp.where(members[local], column, 0.0)
    for (kind, a, b), full in zip(chunks, gathered):
        size = b - a
        weight = shares[kind][:, None]
        pair = mm(scaled, full[:, : 2 * size])
        dhidden = mm(cot_rows, full[:, 2 * size :])
        gate, up = scale_b * pair[:, :size], scale_b * pair[:, size:]
        sigma = jax.nn.sigmoid(gate)
        silu = gate * sigma
        hidden = silu * up
        weighted = (weight * hidden).astype(bf16)
        dots[kind] = dots.get(kind, 0.0) + jnp.sum(hidden * dhidden, axis=1)
        dhidden = weight * dhidden
        dgate = dhidden * up * sigma * (1.0 + gate * (1.0 - sigma))
        dup = dhidden * silu
        inner = inner + jnp.sum(dgate * gate + dup * up, axis=1)
        dpair = jnp.concatenate([scale_b * dgate, scale_b * dup], axis=1).astype(bf16)
        moe_new = mm_nt(weighted, full[:, 2 * size :])
        dscaled_new = mm_nt(dpair, full[:, : 2 * size])
        moe_part = moe_new if moe_part is None else moe_part + moe_new
        dscaled_part = dscaled_new if dscaled_part is None else dscaled_part + dscaled_new
        unit_grads.append(
            reduce_rows([mm_tn(scaled, dpair).astype(bf16), mm_tn(cot_rows, weighted).astype(bf16)])
        )
    moe_share = lax.psum_scatter(
        moe_part.astype(bf16), "col", scatter_dimension=1, tiled=True
    ).astype(f32)
    block_output = (stream + moe_share).astype(bf16)

    table = jnp.zeros((experts, tokens), f32)
    for local in range(local_experts):
        row = jnp.where(members[local], dots[local], 0.0)[None]
        table = lax.dynamic_update_slice_in_dim(table, row, col_id * local_experts + local, 0)
    table = lax.psum(jnp.concatenate([table, dots[None][None], inner[None]], axis=0), "col")
    dprob, dshared_gate, inner = table[:experts].T, table[experts], table[experts + 1]
    dlogits = router_probs * (dprob - jnp.sum(dprob * router_probs, axis=1, keepdims=True))
    dslogit = dshared_gate * shared_gate * (1.0 - shared_gate)
    dboth = jnp.concatenate([dlogits, dslogit[:, None]], axis=1)
    inner = inner + jnp.sum(dboth * both_logits, axis=1)
    dboth = scale_b * dboth
    parts = split_three(dboth)
    stacked = mm_tn(jnp.concatenate(parts, axis=1), scaled)
    grad_router_part = stacked.reshape(3, experts + 1, width).sum(axis=0)
    grad_router_both = lax.psum_scatter(grad_router_part, "row", scatter_dimension=1, tiled=True)
    router_rows = lax.dynamic_slice_in_dim(router_full, col_id * share, share, 0)
    back = mm_nt(jnp.concatenate(parts, axis=1), jnp.concatenate([router_rows] * 3, axis=1))
    dscaled = back + lax.psum_scatter(
        dscaled_part.astype(bf16), "col", scatter_dimension=1, tiled=True
    ).astype(f32)
    cot_share = grad_output.astype(f32)
    dstream = cot_share + gain_b * dscaled - stream * (scale_b * scale_b * inner[:, None] / width)
    gain_b_grad = jnp.sum(dscaled * stream, axis=0)

    dattn = lax.all_gather(dstream.astype(bf16), "col", axis=1, tiled=True)
    out_grad = reduce_rows([mm_tn(dattn, context).astype(bf16)])
    dcontext = mm(dattn, out_full).astype(bf16)
    dqkv, inner_a = attend_backward(qkv, dcontext, lse, lengths, cosine, sine)
    inner_a = lax.psum(
        jnp.sum(inner_a.reshape(tokens, heads, HEAD_DIM)[:, :, 0], axis=1), "col"
    )[:, None]
    qkv_grad = reduce_rows([mm_tn(normed_a, dqkv).astype(bf16)])
    dnormed_a = lax.psum_scatter(
        mm_nt(dqkv, qkv_full).astype(bf16), "col", scatter_dimension=1, tiled=True
    ).astype(f32)
    gain_a_share = input_gain.astype(f32)
    dinput = dstream + scale_a * gain_a_share * dnormed_a
    dinput = dinput - x_share * (scale_a * scale_a * inner_a / width)
    gain_a_grad = jnp.sum(dnormed_a * x_share * scale_a, axis=0)
    grad_gain_a, grad_gain_b = lax.psum((gain_a_grad, gain_b_grad), "row")

    qkv_grad = qkv_grad.reshape(rows_block, heads, 3, HEAD_DIM)
    grad_query, grad_key, grad_value = (
        qkv_grad[:, :, part].reshape(rows_block, head_width) for part in range(3)
    )
    gates, ups, downs = [], [], []
    for (kind, a, b), grad in zip(chunks, unit_grads):
        size = b - a
        pieces = (grad[:, :size], grad[:, size : 2 * size], grad[:, 2 * size :].T)
        if kind is None:
            grad_gate_shared, grad_up_shared, grad_down_shared = pieces
        else:
            if a == 0:
                for into in (gates, ups, downs):
                    into.append([])
            for into, piece in zip((gates, ups, downs), pieces):
                into[-1].append(piece)
    grad_gate_expert = jnp.stack([jnp.concatenate(one, axis=1) for one in gates])
    grad_up_expert = jnp.stack([jnp.concatenate(one, axis=1) for one in ups])
    grad_down_expert = jnp.stack([jnp.concatenate(one, axis=0) for one in downs])
    return (
        block_output,
        dinput.astype(bf16),
        grad_gain_a,
        grad_query,
        grad_key,
        grad_value,
        out_grad.T,
        grad_gain_b,
        grad_router_both[:experts].T,
        grad_router_both[experts],
        grad_gate_shared,
        grad_up_shared,
        grad_down_shared,
        grad_gate_expert,
        grad_up_expert,
        grad_down_expert,
    )


def solution(mesh):
    return jax.shard_map(
        per_device,
        mesh=mesh,
        in_specs=(
            P("row", "col"),
            P(),
            P(),
            P("row", None),
            P("col"),
            P("row", "col"),
            P("row", "col"),
            P("row", "col"),
            P("col", "row"),
            P("col"),
            P("row", None),
            P("row"),
            P("row", "col"),
            P("row", "col"),
            P("col", "row"),
            P("col", "row", None),
            P("col", "row", None),
            P("col", None, "row"),
            P("row", "col"),
        ),
        out_specs=(
            P("row", "col"),
            P("row", "col"),
            P("col"),
            P("row", "col"),
            P("row", "col"),
            P("row", "col"),
            P("col", "row"),
            P("col"),
            P("row", None),
            P("row"),
            P("row", "col"),
            P("row", "col"),
            P("col", "row"),
            P("col", "row", None),
            P("col", "row", None),
            P("col", None, "row"),
        ),
        check_vma=False,
    )
```

time: 2870 us -> 1520 us (0.53)
  waiting for transfers between devices: 1750 us -> 457 us
  starting transfers between devices: 3.44 us -> 208 us
  matrix products: 554 us -> 368 us
  other arithmetic: 290 us -> 180 us
  Pallas kernels: 0 us -> 40.8 us
    reduce_scatter x28 -> x5, waiting for transfers between devices: 1130 us -> 48.5 us  [the longest x1 48.5 us: per_device(): lax.psum_scatter(attn_part, 'col', scatter_dimension=1, tiled=True)]
    all_gather x16 -> x4, waiting for transfers between devices: 445 us -> 0.01 us  [the longest x1 0.01 us: per_device(): rows_in = lax.all_gather(block_input, 'col', axis=1, tiled=True)]
    ppermute x0 -> x66, waiting for transfers between devices: none -> 407 us  [the longest x15 252 us: gather_rows(): lax.ppermute(down[-1], 'row', [(a, a - 1) for a in range(1, n - step + 1)])]
    ppermute x0 -> x66, starting transfers between devices: none -> 207 us  [the longest x18 120 us: reduce_rows(): up_in = lax.ppermute(up, 'row', [(a, a + 1) for a in range(step)])]
    dot_general x98 -> x33, matrix products: 554 us -> 368 us  [the longest x11 136 us: mm_nt(): lax.dot_general(left, right, (((1,), (1,)), ((), ())), preferred_element_...]
    psum x1, waiting for transfers between devices: 172 us -> 0.01 us  [per_device(): lax.psum(jnp.concatenate([table, dots[None][None], inner[None]], axis=0),...]
    scatter-add x6 -> x0, other arithmetic: 108 us -> none  [the longest x2 47 us: per_device(): dnorm_part = dnorm_part.at[index].add(dpicked)]
    gather x7 -> x1, local copies, waits for them, and re-layouts: 58.3 us -> 0.64 us  [per_device(): seq_lengths[slot_order]]
  transfers between devices with their start and end apart: 45 -> 76, of which waited for: 31 -> 21; matrix products, arithmetic and copies ran while one was open for 28% -> 32% of each run, Pallas kernels for 0% -> 2%
where the time goes in v1:
time: 1520 us; the launch traced here: 1510 us
  waiting for transfers between devices  457 us (30%)
  matrix products  368 us (24%)
  starting transfers between devices  208 us (14%)
  other arithmetic  180 us (12%)
  blocking collectives  129 us (8%)
  local copies, waits for them, and re-layouts  112 us (7%)
  Pallas kernels  40.8 us (3%)
  between operations  16.9 us (1%)
    ppermute x15, waiting for transfers between devices, gather_rows(): lax.ppermute(down[-1], 'row', [(a, a - 1) for a in range(1, n - step + 1)])  252 us
    dot_general x11, matrix products, mm_nt(): lax.dot_general(left, right, (((1,), (1,)), ((), ())), preferred_element_...  136 us
    dot_general x11, matrix products, mm(): return jnp.dot(left, right, preferred_element_type=f32)  135 us
    ppermute x18, waiting for transfers between devices, reduce_rows(): up_in = lax.ppermute(up, 'row', [(a, a + 1) for a in range(step)])  132 us
    ppermute x18, starting transfers between devices, reduce_rows(): up_in = lax.ppermute(up, 'row', [(a, a + 1) for a in range(step)])  120 us
    dot_general x11, matrix products, mm_tn(): lax.dot_general(left, right, (((0,), (0,)), ((), ())), preferred_element_...  96.8 us
    all_gather x1, blocking collectives, per_device(): router_full = lax.all_gather(router_pack, 'row', axis=0, tiled=True)  82.4 us
    reduce_scatter x1, waiting for transfers between devices, per_device(): lax.psum_scatter(attn_part, 'col', scatter_dimension=1, tiled=True)  48.5 us
  transfers between devices with their start and end apart: 76, of which 21 were waited for; matrix products, arithmetic and copies ran while one was open for 32% of the time, Pallas kernels for 2%

profile of v1, /device:TPU:0, one launch (start us, length us, event | category | flops | bytes accessed | tf_op | source)
XLA Modules:
  0.0 1510.6 jit_solution(3837863299106231559)
XLA Ops:
  19.4 20.2 %collective-permute-done.1 = bf16[512,1024]{0,1:T(8,128)(2,1)S(1)} collective-permute-done((bf16[512,1024]{0,1:T(8,128)(2,1)S(1)}, bf16[512,1024]{0,1:T(8,128)(2,1)S(1)}, u32[]{:S(2)}, u32[]{:S(2)}) %collective-permute-start.1) | collective-permute-done | bytes 1048608 | tf_op jit(solution)/shard_map/ppermute | solution.py:180
  43.2 22.8 %collective-permute-done.2 = bf16[512,1024]{0,1:T(8,128)(2,1)} collective-permute-done((bf16[512,1024]{0,1:T(8,128)(2,1)S(1)}, bf16[512,1024]{0,1:T(8,128)(2,1)}, u32[]{:S(2)}, u32[]{:S(2)}) %collective-permute-start.2) | collective-permute-done | bytes 1048608 | tf_op jit(solution)/shard_map/ppermute | solution.py:180
  159.7 48.5 %reduce-scatter.6.cloned.1.call-done = bf16[2048,256]{1,0:T(8,128)(2,1)} async-done(((bf16[2048,2048]{1,0:T(8,128)(2,1)}), bf16[2048,256]{1,0:T(8,128)(2,1)}) %reduce-scatter.6.cloned.1.call-update) | async-done | bytes 1048592 | tf_op jit(solution)/shard_map/reduce_scatter | solution.py:296
  229.7 70.9 %collective-permute-done.13 = bf16[512,1536]{1,0:T(8,128)(2,1)S(1)} collective-permute-done((bf16[512,1536]{1,0:T(8,128)(2,1)S(1)}, bf16[512,1536]{1,0:T(8,128)(2,1)S(1)}, u32[]{:S(2)}, u32[]{:S(2)}) %collective-permute-start.13) | collective-permute-done | bytes 1572896 | tf_op jit(solution)/shard_map/ppermute | solution.py:180
  312.8 13.2 collective-permute-done.26
  340.6 19.1 %collective-permute-done.20 = bf16[512,1536]{1,0:T(8,128)(2,1)} collective-permute-done((bf16[512,1536]{1,0:T(8,128)(2,1)}, bf16[512,1536]{1,0:T(8,128)(2,1)}, u32[]{:S(2)}, u32[]{:S(2)}) %collective-permute-start.20) | collective-permute-done | bytes 1572896 | tf_op jit(solution)/shard_map/ppermute | solution.py:180
  360.5 82.4 %all_gather.21 = bf16[2048,9]{0,1:T(8,128)(2,1)S(1)} all-gather(bf16[512,9]{0,1:T(8,128)(2,1)S(1)} %pad_maximum_fusion.33), channel_id=1, replica_groups=mesh['row'=4,'col'=8] {'row'}, dimensions={0}, use_global_device_ids=true | all-gather | bytes 46080 | tf_op jit(solution)/shard_map/all_gather | solution.py:285
  454.7 29.2 %collective-permute-done.14 = bf16[512,1536]{1,0:T(8,128)(2,1)} collective-permute-done((bf16[512,1536]{1,0:T(8,128)(2,1)S(1)}, bf16[512,1536]{1,0:T(8,128)(2,1)}, u32[]{:S(2)}, u32[]{:S(2)}) %collective-permute-start.14) | collective-permute-done | bytes 1572896 | tf_op jit(solution)/shard_map/ppermute | solution.py:180
  497.7 19.9 %collective-permute-done.21 = bf16[512,1536]{1,0:T(8,128)(2,1)} collective-permute-done((bf16[512,1536]{1,0:T(8,128)(2,1)}, bf16[512,1536]{1,0:T(8,128)(2,1)}, u32[]{:S(2)}, u32[]{:S(2)}) %collective-permute-start.21) | collective-permute-done | bytes 1572896 | tf_op jit(solution)/shard_map/ppermute | solution.py:180
  527.0 24.3 %collective-permute-done.15 = bf16[512,1536]{1,0:T(8,128)(2,1)} collective-permute-done((bf16[512,1536]{1,0:T(8,128)(2,1)}, bf16[512,1536]{1,0:T(8,128)(2,1)}, u32[]{:S(2)}, u32[]{:S(2)}) %collective-permute-start.15) | collective-permute-done | bytes 1572896 | tf_op jit(solution)/shard_map/ppermute | solution.py:180
  562.7 29.2 %collective-permute-done.9 = bf16[512,2112]{0,1:T(8,128)(2,1)S(1)} collective-permute-done((bf16[512,2112]{0,1:T(8,128)(2,1)}, bf16[512,2112]{0,1:T(8,128)(2,1)S(1)}, u32[]{:S(2)}, u32[]{:S(2)}) %collective-permute-start.9) | collective-permute-done | bytes 2162720 | tf_op jit(solution)/shard_map/ppermute | solution.py:180
  673.0 17.7 %fusion.7 = f32[2048,1408]{0,1:T(8,128)} fusion(bf16[2048,2048]{1,0:T(8,128)(2,1)S(1)} %copy-done.2, bf16[2048,2112]{1,0:T(8,128)(2,1)} %bitcast.17), kind=kOutput, calls=%fused_computation.26 | convolution fusion | flops 11811160064 | bytes 25690112 | tf_op jit(solution)/shard_map/dot_general | solution.py:22
  690.7 16.5 %multiply_convert_fusion.1 = (bf16[2048,704]{0,1:T(8,128)(2,1)}, f32[2048,704]{0,1:T(8,128)S(1)}, f32[704,2048]{1,0:T(8,128)}) fusion(f32[2048]{0:T(1024)S(1)} %add_rsqrt_fusion, f32[2048,1408]{0,1:T(8,128)} %fusion.7, f32[2048]{0:T(1024)S(1)} %bitcast.291, bf16[2048,2048]{1,0:T(8,128)(2,1)} %all-gather.10.cloned.1.call-done, bf16[2048,2112]{1,0:T(8,128)(2,1)} %bitcast.17), kind=kOutput, calls=%fused_computation.18 | convolution fusion | flops 5925765120 | bytes 37502976 | tf_op jit(solution)/shard_map/dot_general | solution.py:22
  717.2 13.2 fusion.22
  730.4 13.4 fusion.18
  743.8 17.7 %multiply_convert_fusion.4 = (bf16[2048,512]{0,1:T(8,128)(2,1)S(1)}, f32[2048,512]{0,1:T(8,128)}, bf16[2048,512]{0,1:T(8,128)(2,1)}, bf16[2048,512]{0,1:T(8,128)...) fusion(f32[2048]{0:T(1024)S(1)} %add_rsqrt_fusion, f32[2048,1024]{0,1:T(8,128)} %fusion.18, ...), kind=kOutput, calls=%fused_computation.47 | convolution fusion | flops 4332716032 | bytes 52445184 | tf_op jit(solution)/shard_map/dot_general | solution.py:22
  774.2 15.5 %fusion.20 = f32[2048,2048]{1,0:T(8,128)} fusion(bf16[2048,1536]{1,0:T(8,128)(2,1)} %bitcast.27, bf16[2048,512]{0,1:T(8,128)(2,1)} %get-tuple-element.217, bf16[2048,512]{0,1:T(8,128)(2,1)} %get-tuple-element.218), kind=kOutput, calls=%fused_computation.68 | convolution fusion | flops 8598323200 | bytes 25165824 | tf_op jit(solution)/shard_map/dot_general | solution.py:26
  789.7 14.5 fusion.16
  814.9 26.8 %add_convert_fusion = bf16[2048,2048]{1,0:T(8,128)(2,1)} fusion(f32[2048,2048]{1,0:T(8,128)} %fusion.29, f32[2048,2048]{1,0:T(8,128)} %fusion.16, f32[2048,2048]{1,0:T(8,128)} %fusion.20, bf16[2048,2112]{1,0:T(8,128)(2,1)} %bitcast.17, bf16[2048,704]{0,1:T(8,128)(2,1)S(1)} %copy-done.61, bf16[2048,704]{0,1:T(8,128)(2,1)} %get-tuple-element.104), kind=kOutput, calls=%fused_computation.6 | convolution fusion | flops 11839471616 | bytes 70254592 | tf_op jit(solution)/shard_map/dot_general | solution.py:26
  956.0 15.2 %convolution_convert_fusion = bf16[2048,1408]{0,1:T(8,128)(2,1)S(1)} fusion(bf16[2048,2048]{1,0:T(8,128)(2,1)S(1)} %bitcast.264, bf16[2048,704]{0,1:T(8,128)(2,1)S(1)} %copy-done.62, bf16[2048,704]{0,1:T(8,128)(2,1)} %get-tuple-element.104), kind=kOutput, calls=%fused_computation.8 | convolution fusion | flops 11825577984 | bytes 19922944 | tf_op jit(solution)/shard_map/dot_general | solution.py:30
  1004.8 15.9 %add_convert_fusion.1 = bf16[2048,2048]{1,0:T(8,128)(2,1)} fusion(f32[2048,2048]{1,0:T(8,128)S(1)} %fusion.50, f32[2048,2048]{1,0:T(8,128)} %fusion.35, f32[2048,2048]{1,0:T(8,128)} %fusion.54, bf16[2048,384]{0,1:T(8,128)(2,1)S(1)} %copy-done.6, bf16[2048,1152]{1,0:T(8,128)(2,1)} %bitcast.267), kind=kOutput, calls=%fused_computation.7 | convolution fusion | flops 3238002688 | bytes 61865984 | tf_op jit(solution)/shard_map/dot_general | solution.py:26
  1048.1 34.6 %collective-permute-done.42 = bf16[512,2112]{0,1:T(8,128)(2,1)S(1)} collective-permute-done((bf16[512,2112]{0,1:T(8,128)(2,1)S(1)}, bf16[512,2112]{0,1:T(8,128)(2,1)S(1)}, u32[]{:S(2)}, u32[]{:S(2)}) %collective-permute-start.42) | collective-permute-done | bytes 2162720 | tf_op jit(solution)/shard_map/ppermute | solution.py:204
  1091.2 16.8 %collective-permute-done.61 = bf16[512,1152]{0,1:T(8,128)(2,1)S(1)} collective-permute-done((bf16[512,1152]{0,1:T(8,128)(2,1)S(1)}, bf16[512,1152]{0,1:T(8,128)(2,1)S(1)}, u32[]{:S(2)}, u32[]{:S(2)}) %collective-permute-start.61) | collective-permute-done | bytes 1179680 | tf_op jit(solution)/shard_map/ppermute | solution.py:204
  1123.7 18.0 %collective-permute-done.49 = bf16[512,1536]{0,1:T(8,128)(2,1)S(1)} collective-permute-done((bf16[512,1536]{0,1:T(8,128)(2,1)S(1)}, bf16[512,1536]{0,1:T(8,128)(2,1)S(1)}, u32[]{:S(2)}, u32[]{:S(2)}) %collective-permute-start.49) | collective-permute-done | bytes 1572896 | tf_op jit(solution)/shard_map/ppermute | solution.py:204
  1151.8 23.6 %collective-permute-done.55 = bf16[512,1536]{0,1:T(8,128)(2,1)S(1)} collective-permute-done((bf16[512,1536]{0,1:T(8,128)(2,1)S(1)}, bf16[512,1536]{0,1:T(8,128)(2,1)S(1)}, u32[]{:S(2)}, u32[]{:S(2)}) %collective-permute-start.55) | collective-permute-done | bytes 1572896 | tf_op jit(solution)/shard_map/ppermute | solution.py:204
  1193.6 28.1 %attend_backward.1 = (bf16[2048,768]{1,0:T(8,128)(2,1)}, f32[2048,256]{1,0:T(8,128)}) custom-call(s32[2]{0:T(128)} %dynamic_slice.220.length_ref, bf16[2048,768]{1,0:T(8,128)(2,1)} %get-tuple-element.22.qkv_ref, bf16[2048,256]{1,0:T(8,128)(2,1)} %convolution_convert_fusion.12.dcontext_ref, f32[2048,256]{1,0:T(8,128)} %get-tuple-element.23.lse_ref, ...), custom_call_target="tpu_custom_call" | custom-call | flops 4294967296 | bytes 12582912 | tf_op jit(solution)/shard_map/attend_backward/pallas_call | solution.py:152
  1233.1 14.1 collective-permute-done.62
  1269.7 22.4 %collective-permute-start.44 = (bf16[512,2112]{0,1:T(8,128)(2,1)}, bf16[512,2112]{0,1:T(8,128)(2,1)}, u32[]{:S(2)}, u32[]{:S(2)}) collective-permute-start(bf16[512,2112]{0,1:T(8,128)(2,1)} %add_convert_fusion.4), channel_id=1, source_target_pairs={{0,8},{8,16},{16,24},{1,9},{9,17},{17,25},{2,10},{10,18},{18,26},{... | collective-permute-start | bytes 6488072 | tf_op jit(solution)/shard_map/ppermute | solution.py:204
  1299.6 14.9 collective-permute-done.56
  1387.6 16.9 %collective-permute-start.36 = (bf16[512,256]{1,0:T(8,128)(2,1)S(1)}, bf16[512,256]{1,0:T(8,128)(2,1)S(1)}, u32[]{:S(2)}, u32[]{:S(2)}) collective-permute-start(bf16[512,256]{1,0:T(8,128)(2,1)S(1)} %get-tuple-element.209), channel_id=1, source_target_pairs={{0,8},{1,9},{2,10},{3,11},{4,12},{5,13},{6,14},{7,15}} | collective-permute-start | bytes 786440 | tf_op jit(solution)/shard_map/ppermute | solution.py:204
  1444.6 15.2 %slice_reduce_fusion = f32[2048]{0:T(1024)S(1)} fusion(f32[2048,2,128]{2,1,0:T(2,128)S(1)} %copy-done.11), kind=kLoop, calls=%fused_computation.143 | loop fusion | flops 2048 | bytes 24576 | tf_op jit(solution)/shard_map/reduce_sum | solution.py:379
  1489.6 13.9 all-reduce
  (638 shorter events, 729.1 us)
Async XLA Ops:
  7.2 92.7 %all-gather.6.cloned.1.call-start = ((), (), s32[]{:S(2)}) async-start(), calls=%async_computation.5 | async-start | bytes 9437184 | tf_op jit(solution)/shard_map/all_gather | solution.py:287
  7.9 200.2 %reduce-scatter.6.cloned.1.call-start = ((), (), s32[]{:S(2)}) async-start(), calls=%async_computation.6 | async-start | bytes 9437184 | tf_op jit(solution)/shard_map/reduce_scatter | solution.py:296
  136.3 477.8 %all-gather.10.cloned.1.call-start = ((), (), s32[]{:S(2)}) async-start(), calls=%async_computation.9 | async-start | bytes 9437184 | tf_op jit(solution)/shard_map/all_gather | solution.py:289
  137.0 500.4 %all-gather.8.cloned.1.call-start = ((), (), s32[]{:S(2)}) async-start(), calls=%async_computation.7 | async-start | bytes 9437184 | tf_op jit(solution)/shard_map/all_gather | solution.py:300
  210.9 697.7 %all-reduce.3.cloned.1.call-start = ((), (), s32[]{:S(2)}) async-start(), calls=%async_computation.10 | async-start | bytes 262144 | tf_op jit(solution)/shard_map/psum | solution.py:354
  214.9 88.7 %collective-permute-start.7 = (bf16[512,2112]{0,1:T(8,128)(2,1)}, bf16[512,2112]{0,1:T(8,128)(2,1)}, u32[]{:S(2)}, u32[]{:S(2)}) collective-permute-start(bf16[512,2112]{0,1:T(8,128)(2,1)} %get-tuple-element.172), channel_id=1, source_target_pairs={{8,0},{16,8},{24,16},{9,1},{17,9},{25,17},{10,2},{18,10},{26,18},{... | collective-permute-start | bytes 6488072 | tf_op jit(solution)/shard_map/ppermute | solution.py:180
  216.6 84.1 %collective-permute-start.13 = (bf16[512,1536]{1,0:T(8,128)(2,1)S(1)}, bf16[512,1536]{1,0:T(8,128)(2,1)S(1)}, u32[]{:S(2)}, u32[]{:S(2)}) collective-permute-start(bf16[512,1536]{1,0:T(8,128)(2,1)S(1)} %pad_maximum_fusion.15), channel_id=1, source_target_pairs={{8,0},{16,8},{24,16},{9,1},{17,9},{25,17},{10,2},{18,10},{26,18},{... | collective-permute-start | bytes 4718600 | tf_op jit(solution)/shard_map/ppermute | solution.py:180
  223.2 116.0 %collective-permute-start.6 = (bf16[512,2112]{0,1:T(8,128)(2,1)}, bf16[512,2112]{0,1:T(8,128)(2,1)}, u32[]{:S(2)}, u32[]{:S(2)}) collective-permute-start(bf16[512,2112]{0,1:T(8,128)(2,1)} %get-tuple-element.172), channel_id=1, source_target_pairs={{0,8},{8,16},{16,24},{1,9},{9,17},{17,25},{2,10},{10,18},{18,26},{... | collective-permute-start | bytes 6488072 | tf_op jit(solution)/shard_map/ppermute | solution.py:179
  228.4 97.6 %collective-permute-start.26 = (bf16[512,1152]{1,0:T(8,128)(2,1)}, bf16[512,1152]{1,0:T(8,128)(2,1)}, u32[]{:S(2)}, u32[]{:S(2)}) collective-permute-start(bf16[512,1152]{1,0:T(8,128)(2,1)} %collective-permute-done.25), channel_id=1, source_target_pairs={{8,0},{16,8},{9,1},{17,9},{10,2},{18,10},{11,3},{19,11},{12,4},{20... | collective-permute-start | bytes 3538952 | tf_op jit(solution)/shard_map/ppermute | solution.py:180
  303.6 139.9 %collective-permute-start.22 = (bf16[512,1536]{1,0:T(8,128)(2,1)}, bf16[512,1536]{1,0:T(8,128)(2,1)}, u32[]{:S(2)}, u32[]{:S(2)}) collective-permute-start(bf16[512,1536]{1,0:T(8,128)(2,1)} %collective-permute-done.18), channel_id=1, source_target_pairs={{8,16},{16,24},{9,17},{17,25},{10,18},{18,26},{11,19},{19,27},{12,... | collective-permute-start | bytes 4718600 | tf_op jit(solution)/shard_map/ppermute | solution.py:179
  326.0 119.6 %collective-permute-start.27 = (bf16[512,1152]{1,0:T(8,128)(2,1)}, bf16[512,1152]{1,0:T(8,128)(2,1)}, u32[]{:S(2)}, u32[]{:S(2)}) collective-permute-start(bf16[512,1152]{1,0:T(8,128)(2,1)} %collective-permute-done.26), channel_id=1, source_target_pairs={{8,0},{9,1},{10,2},{11,3},{12,4},{13,5},{14,6},{15,7}} | collective-permute-start | bytes 3538952 | tf_op jit(solution)/shard_map/ppermute | solution.py:180
  332.9 116.5 %collective-permute-start.29 = (bf16[512,1152]{1,0:T(8,128)(2,1)}, bf16[512,1152]{1,0:T(8,128)(2,1)}, u32[]{:S(2)}, u32[]{:S(2)}) collective-permute-start(bf16[512,1152]{1,0:T(8,128)(2,1)} %collective-permute-done.28), channel_id=1, source_target_pairs={{16,24},{17,25},{18,26},{19,27},{20,28},{21,29},{22,30},{23,31}} | collective-permute-start | bytes 3538952 | tf_op jit(solution)/shard_map/ppermute | solution.py:179
  339.2 147.8 %collective-permute-start.8 = (bf16[512,2112]{0,1:T(8,128)(2,1)}, bf16[512,2112]{0,1:T(8,128)(2,1)}, u32[]{:S(2)}, u32[]{:S(2)}) collective-permute-start(bf16[512,2112]{0,1:T(8,128)(2,1)} %collective-permute-done.7), channel_id=1, source_target_pairs={{8,0},{16,8},{9,1},{17,9},{10,2},{18,10},{11,3},{19,11},{12,4},{20... | collective-permute-start | bytes 6488072 | tf_op jit(solution)/shard_map/ppermute | solution.py:180
  359.7 129.2 %collective-permute-start.10 = (bf16[512,2112]{0,1:T(8,128)(2,1)}, bf16[512,2112]{0,1:T(8,128)(2,1)S(1)}, u32[]{:S(2)}, u32[]{:S(2)}) collective-permute-start(bf16[512,2112]{0,1:T(8,128)(2,1)} %collective-permute-done.6), channel_id=1, source_target_pairs={{8,16},{16,24},{9,17},{17,25},{10,18},{18,26},{11,19},{19,27},{12,... | collective-permute-start | bytes 6488072 | tf_op jit(solution)/shard_map/ppermute | solution.py:179
  496.4 95.5 %collective-permute-start.9 = (bf16[512,2112]{0,1:T(8,128)(2,1)}, bf16[512,2112]{0,1:T(8,128)(2,1)S(1)}, u32[]{:S(2)}, u32[]{:S(2)}) collective-permute-start(bf16[512,2112]{0,1:T(8,128)(2,1)} %collective-permute-done.8), channel_id=1, source_target_pairs={{8,0},{9,1},{10,2},{11,3},{12,4},{13,5},{14,6},{15,7}} | collective-permute-start | bytes 6488072 | tf_op jit(solution)/shard_map/ppermute | solution.py:180
  774.1 146.1 %reduce-scatter.10.cloned.1.call-start = ((), (), s32[]{:S(2)}) async-start(), calls=%async_computation.11 | async-start | bytes 9437184 | tf_op jit(solution)/shard_map/reduce_scatter | solution.py:367
  841.8 186.5 %reduce-scatter.14.cloned.1.call-start = ((), (), s32[]{:S(2)}) async-start(), calls=%async_computation.14 | async-start | bytes 163840 | tf_op jit(solution)/shard_map/reduce_scatter | solution.py:364
  872.2 165.0 %collective-permute-start.48 = (bf16[512,1536]{0,1:T(8,128)(2,1)}, bf16[512,1536]{0,1:T(8,128)(2,1)}, u32[]{:S(2)}, u32[]{:S(2)}) collective-permute-start(bf16[512,1536]{0,1:T(8,128)(2,1)} %pad_maximum_fusion.17), channel_id=1, source_target_pairs={{0,8},{1,9},{2,10},{3,11},{4,12},{5,13},{6,14},{7,15}} | collective-permute-start | bytes 4718600 | tf_op jit(solution)/shard_map/ppermute | solution.py:204
  876.5 163.5 %collective-permute-start.51 = (bf16[512,1536]{0,1:T(8,128)(2,1)}, bf16[512,1536]{0,1:T(8,128)(2,1)}, u32[]{:S(2)}, u32[]{:S(2)}) collective-permute-start(bf16[512,1536]{0,1:T(8,128)(2,1)} %pad_maximum_fusion.18), channel_id=1, source_target_pairs={{24,16},{25,17},{26,18},{27,19},{28,20},{29,21},{30,22},{31,23}} | collective-permute-start | bytes 4718600 | tf_op jit(solution)/shard_map/ppermute | solution.py:205
  901.1 142.3 %collective-permute-start.54 = (bf16[512,1536]{0,1:T(8,128)(2,1)}, bf16[512,1536]{0,1:T(8,128)(2,1)}, u32[]{:S(2)}, u32[]{:S(2)}) collective-permute-start(bf16[512,1536]{0,1:T(8,128)(2,1)} %pad_maximum_fusion.19), channel_id=1, source_target_pairs={{0,8},{1,9},{2,10},{3,11},{4,12},{5,13},{6,14},{7,15}} | collective-permute-start | bytes 4718600 | tf_op jit(solution)/shard_map/ppermute | solution.py:204
  918.8 267.6 %all-gather.12.cloned.1.call-start = ((), (), s32[]{:S(2)}) async-start(), calls=%async_computation.12 | async-start | bytes 9437184 | tf_op jit(solution)/shard_map/all_gather | solution.py:374
  924.7 560.6 %reduce-scatter.8.cloned.1.call-start = ((), (), s32[]{:S(2)}) async-start(), calls=%async_computation.8 | async-start | bytes 9437184 | tf_op jit(solution)/shard_map/reduce_scatter | solution.py:345
  937.9 93.1 %collective-permute-start.60 = (bf16[512,1152]{0,1:T(8,128)(2,1)}, bf16[512,1152]{0,1:T(8,128)(2,1)}, u32[]{:S(2)}, u32[]{:S(2)}) collective-permute-start(bf16[512,1152]{0,1:T(8,128)(2,1)} %pad_maximum_fusion.22), channel_id=1, source_target_pairs={{0,8},{1,9},{2,10},{3,11},{4,12},{5,13},{6,14},{7,15}} | collective-permute-start | bytes 3538952 | tf_op jit(solution)/shard_map/ppermute | solution.py:204
  941.6 92.4 %collective-permute-start.63 = (bf16[512,1152]{0,1:T(8,128)(2,1)}, bf16[512,1152]{0,1:T(8,128)(2,1)}, u32[]{:S(2)}, u32[]{:S(2)}) collective-permute-start(bf16[512,1152]{0,1:T(8,128)(2,1)} %pad_maximum_fusion.23), channel_id=1, source_target_pairs={{24,16},{25,17},{26,18},{27,19},{28,20},{29,21},{30,22},{31,23}} | collective-permute-start | bytes 3538952 | tf_op jit(solution)/shard_map/ppermute | solution.py:205
  1020.7 464.6 %reduce-scatter.12.cloned.1.call-start = ((), (), s32[]{:S(2)}) async-start(), calls=%async_computation.13 | async-start | bytes 9437184 | tf_op jit(solution)/shard_map/reduce_scatter | solution.py:382
  1046.1 95.6 %collective-permute-start.49 = (bf16[512,1536]{0,1:T(8,128)(2,1)S(1)}, bf16[512,1536]{0,1:T(8,128)(2,1)S(1)}, u32[]{:S(2)}, u32[]{:S(2)}) collective-permute-start(bf16[512,1536]{0,1:T(8,128)(2,1)S(1)} %add_convert_fusion.13), channel_id=1, source_target_pairs={{0,8},{8,16},{1,9},{9,17},{2,10},{10,18},{3,11},{11,19},{4,12},{12... | collective-permute-start | bytes 4718600 | tf_op jit(solution)/shard_map/ppermute | solution.py:204
  1084.2 91.3 %collective-permute-start.55 = (bf16[512,1536]{0,1:T(8,128)(2,1)S(1)}, bf16[512,1536]{0,1:T(8,128)(2,1)S(1)}, u32[]{:S(2)}, u32[]{:S(2)}) collective-permute-start(bf16[512,1536]{0,1:T(8,128)(2,1)S(1)} %add_convert_fusion.9), channel_id=1, source_target_pairs={{0,8},{8,16},{1,9},{9,17},{2,10},{10,18},{3,11},{11,19},{4,12},{12... | collective-permute-start | bytes 4718600 | tf_op jit(solution)/shard_map/ppermute | solution.py:204
  1110.1 152.6 %collective-permute-start.43 = (bf16[512,2112]{0,1:T(8,128)(2,1)S(1)}, bf16[512,2112]{0,1:T(8,128)(2,1)}, u32[]{:S(2)}, u32[]{:S(2)}) collective-permute-start(bf16[512,2112]{0,1:T(8,128)(2,1)S(1)} %add_convert_fusion.5), channel_id=1, source_target_pairs={{0,8},{8,16},{1,9},{9,17},{2,10},{10,18},{3,11},{11,19},{4,12},{12... | collective-permute-start | bytes 6488072 | tf_op jit(solution)/shard_map/ppermute | solution.py:204
  1141.7 128.0 %collective-permute-start.46 = (bf16[512,2112]{0,1:T(8,128)(2,1)}, bf16[512,2112]{0,1:T(8,128)(2,1)}, u32[]{:S(2)}, u32[]{:S(2)}) collective-permute-start(bf16[512,2112]{0,1:T(8,128)(2,1)} %add_convert_fusion.3), channel_id=1, source_target_pairs={{16,8},{24,16},{17,9},{25,17},{18,10},{26,18},{19,11},{27,19},{20,... | collective-permute-start | bytes 6488072 | tf_op jit(solution)/shard_map/ppermute | solution.py:205
  1145.3 101.8 %collective-permute-start.62 = (bf16[512,1152]{0,1:T(8,128)(2,1)}, bf16[512,1152]{0,1:T(8,128)(2,1)}, u32[]{:S(2)}, u32[]{:S(2)}) collective-permute-start(bf16[512,1152]{0,1:T(8,128)(2,1)} %add_convert_fusion.16), channel_id=1, source_target_pairs={{0,8},{8,16},{16,24},{1,9},{9,17},{17,25},{2,10},{10,18},{18,26},{... | collective-permute-start | bytes 3538952 | tf_op jit(solution)/shard_map/ppermute | solution.py:204
  1178.3 117.6 %collective-permute-start.50 = (bf16[512,1536]{0,1:T(8,128)(2,1)}, bf16[512,1536]{0,1:T(8,128)(2,1)}, u32[]{:S(2)}, u32[]{:S(2)}) collective-permute-start(bf16[512,1536]{0,1:T(8,128)(2,1)} %add_convert_fusion.12), channel_id=1, source_target_pairs={{0,8},{8,16},{16,24},{1,9},{9,17},{17,25},{2,10},{10,18},{18,26},{... | collective-permute-start | bytes 4718600 | tf_op jit(solution)/shard_map/ppermute | solution.py:204
  1269.7 91.2 %collective-permute-start.44 = (bf16[512,2112]{0,1:T(8,128)(2,1)}, bf16[512,2112]{0,1:T(8,128)(2,1)}, u32[]{:S(2)}, u32[]{:S(2)}) collective-permute-start(bf16[512,2112]{0,1:T(8,128)(2,1)} %add_convert_fusion.4), channel_id=1, source_target_pairs={{0,8},{8,16},{16,24},{1,9},{9,17},{17,25},{2,10},{10,18},{18,26},{... | collective-permute-start | bytes 6488072 | tf_op jit(solution)/shard_map/ppermute | solution.py:204
  (195 other events, 5087.2 us)
Sparse Core Ops, SparseCore 0:
  9.9 58.6 all-gather.5
  136.4 71.7 reduce-scatter.5
  210.2 55.9 all-gather.9
  268.6 55.9 all-gather.7
  774.2 50.1 all-reduce.2
  841.9 68.4 reduce-scatter.9
  919.0 16.8 reduce-scatter.13
  938.3 54.0 all-gather.11
  1020.8 68.4 reduce-scatter.7
  1233.2 90.6 reduce-scatter.11

commit v2 on v1

--- a/solution.py
+++ b/solution.py
@@ -11,6 +11,7 @@
 HEAD_DIM = 128
 SEQ_LEN = 1024
 QBLOCK = 256
+TILE = 256
 CHUNK = 512
 norm_eps = 1e-06
 rope_base = 1000000.0
@@ -171,42 +172,239 @@
 
 def gather_rows(part):
     n = lax.axis_size("row")
-    if n > 4:
-        return lax.all_gather(part, "row", axis=0, tiled=True)
+    if n != 4:
+        return (lax.all_gather(part, "row", axis=0, tiled=True),)
+    partner = lax.ppermute(part, "row", [(0, 1), (1, 0), (2, 3), (3, 2)])
+    middle, outward = [(1, 2), (2, 1)], [(1, 0), (2, 3)]
+    near_mid = lax.ppermute(part, "row", middle)
+    far_mid = lax.ppermute(partner, "row", middle)
+    near_out = lax.ppermute(near_mid, "row", outward)
+    far_out = lax.ppermute(far_mid, "row", outward)
+    return part, partner, near_mid, far_mid, near_out, far_out
+
+
+def places(z):
+    pair = z // 2
+    return z, z + 1 - 2 * lax.rem(z, 2), 2 - pair, 3 - 3 * pair
+
+
+def join_rows(pieces):
+    if len(pieces) == 1:
+        return pieces[0]
+    part = pieces[0]
     z = lax.axis_index("row")
-    up, down = [part], [part]
-    for step in range(1, n):
-        up.append(lax.ppermute(up[-1], "row", [(a, a + 1) for a in range(step - 1, n - 1)]))
-        down.append(lax.ppermute(down[-1], "row", [(a, a - 1) for a in range(1, n - step + 1)]))
-    whole = jnp.zeros((n,) + part.shape, part.dtype)
-    for back in range(n):
-        piece = part if back == 0 else up[back] + down[n - back]
-        whole = lax.dynamic_update_slice_in_dim(whole, piece[None], lax.rem(z + n - back, n), 0)
-    return whole.reshape((n * part.shape[0],) + part.shape[1:])
+    whole = jnp.zeros((4,) + part.shape, part.dtype)
+    blocks = (part, pieces[1], pieces[2] + pieces[4], pieces[3] + pieces[5])
+    for at, piece in zip(places(z), blocks):
+        whole = lax.dynamic_update_slice_in_dim(whole, piece[None], at, 0)
+    return whole.reshape((4 * part.shape[0],) + part.shape[1:])
 
 
 def reduce_rows(grads):
     n = lax.axis_size("row")
-    if n > 4:
-        whole = jnp.concatenate([g.astype(bf16) for g in grads], axis=1)
-        return lax.psum_scatter(whole, "row", scatter_dimension=0, tiled=True).astype(f32)
-    z = lax.axis_index("row")
-    size = grads[0].shape[0] // n
-
-    def block(j):
-        at = jnp.clip(j, 0, n - 1) * size
-        return jnp.concatenate(
-            [lax.dynamic_slice_in_dim(g, at, size, 0) for g in grads], axis=1
-        ).astype(f32)
-
-    up, down = block(n - 1 + z).astype(bf16), block(z - n + 1).astype(bf16)
-    for step in range(1, n):
-        up_in = lax.ppermute(up, "row", [(a, a + 1) for a in range(step)])
-        down_in = lax.ppermute(down, "row", [(a, a - 1) for a in range(n - step, n)])
-        if step < n - 1:
-            up = (block(n - 1 - step + z) + up_in.astype(f32)).astype(bf16)
-            down = (block(z - n + 1 + step) + down_in.astype(f32)).astype(bf16)
-    return block(z) + up_in.astype(f32) + down_in.astype(f32)
+    if n != 4:
+        total = lax.psum_scatter(grads, "row", scatter_dimension=0, tiled=True)
+        return total.astype(f32), total
+    own, partner, near, far = places(lax.axis_index("row"))
+    size = grads.shape[0] // n
+    inward, middle = [(0, 1), (3, 2)], [(1, 2), (2, 1)]
+
+    def block(at, *others):
+        piece = lax.dynamic_slice_in_dim(grads, at * size, size, 0)
+        if others:
+            piece = piece.astype(f32)
+            for other in others:
+                piece = piece + other.astype(f32)
+        return piece
+
+    far_in = lax.ppermute(block(far), "row", inward)
+    near_in = lax.ppermute(block(near), "row", inward)
+    far_sum = lax.ppermute(block(far, far_in).astype(bf16), "row", middle)
+    near_sum = lax.ppermute(block(near, near_in).astype(bf16), "row", middle)
+    exchanged = lax.ppermute(
+        block(partner, far_sum).astype(bf16), "row", [(0, 1), (1, 0), (2, 3), (3, 2)]
+    )
+    return block(own, near_sum, exchanged), near_in
+
+
+def after(value, *others):
+    return lax.optimization_barrier((value,) + others)[0]
+
+
+def expert_kernel(size, steps, count, z_ref, *refs):
+    pieces = refs[:count]
+    (x_ref, cot_ref, x_cols, cot_cols, coef_ref) = refs[count : count + 5]
+    (dpair_ref, hidden_ref, sums_ref, grads_ref, whole_ref) = refs[count + 5 : count + 10]
+    weights, dpair, hidden, sems, out_sem = refs[count + 10 :]
+    step = pl.program_id(0)
+    write = pltpu.make_async_copy(weights, whole_ref, out_sem)
+
+    @pl.when(step == 0)
+    def _():
+        if count == 1:
+            copy = pltpu.make_async_copy(pieces[0], weights, sems.at[0])
+            copy.start()
+            copy.wait()
+        else:
+            z = z_ref[0]
+            block = pieces[0].shape[0]
+
+            def copy_of(piece, which):
+                at = pl.multiple_of(places(z)[which] * block, block)
+                return pltpu.make_async_copy(
+                    piece, weights.at[pl.ds(at, block)], sems.at[which]
+                )
+
+            copy_of(pieces[0], 0).start()
+            copy_of(pieces[1], 1).start()
+            in_middle = (z == 1) | (z == 2)
+
+            @pl.when(in_middle)
+            def _():
+                copy_of(pieces[2], 2).start()
+                copy_of(pieces[3], 3).start()
+
+            @pl.when(jnp.logical_not(in_middle))
+            def _():
+                copy_of(pieces[4], 2).start()
+                copy_of(pieces[5], 3).start()
+
+            for which in range(4):
+                copy_of(pieces[which], which).wait()
+        write.start()
+
+    @pl.when(step < steps)
+    def _():
+        at = pl.multiple_of(step * TILE, TILE)
+        rows, cots = x_ref[...], cot_ref[...]
+        scale, weight = coef_ref[:, 0:1], coef_ref[:, 1:2]
+        dots = jnp.zeros((TILE, 1), f32)
+        inner = jnp.zeros((TILE, 1), f32)
+        for a in range(0, size, TILE):
+            b = min(a + TILE, size)
+            gate = scale * mm(rows, weights[:, a:b])
+            up = scale * mm(rows, weights[:, size + a : size + b])
+            dhid = mm(cots, weights[:, 2 * size + a : 2 * size + b])
+            sigma = jax.nn.sigmoid(gate)
+            silu = gate * sigma
+            hid = silu * up
+            dots += jnp.sum(hid * dhid, axis=1, keepdims=True)
+            dhid = weight * dhid
+            dgate = dhid * up * sigma * (1.0 + gate * (1.0 - sigma))
+            dup = dhid * silu
+            inner += jnp.sum(dgate * gate + dup * up, axis=1, keepdims=True)
+            for into, at_col, value in (
+                ((hidden_ref, hidden), a, weight * hid),
+                ((dpair_ref, dpair), a, scale * dgate),
+                ((dpair_ref, dpair), size + a, scale * dup),
+            ):
+                value = value.astype(bf16)
+                into[0][:, at_col : at_col + b - a] = value
+                into[1][pl.ds(at, TILE), at_col : at_col + b - a] = value
+        sums_ref[:, 0:1] = dots
+        sums_ref[:, 1:2] = inner
+
+    @pl.when(step >= steps)
+    def _():
+        for a in range(0, 2 * size, TILE):
+            b = min(a + TILE, 2 * size)
+            grads_ref[:, a:b] = mm_tn(x_cols[...], dpair[:, a:b]).astype(bf16)
+        for a in range(0, size, TILE):
+            b = min(a + TILE, size)
+            grads_ref[:, 2 * size + a : 2 * size + b] = mm_tn(
+                cot_cols[...], hidden[:, a:b]
+            ).astype(bf16)
+
+    @pl.when(step == pl.num_programs(0) - 1)
+    def _():
+        write.wait()
+
+
+def expert_chunk(pieces, scaled, cots, coef):
+    tokens, width = scaled.shape
+    size = pieces[0].shape[1] // 3
+    steps, more = tokens // TILE, width // TILE
+    count = len(pieces)
+    rows = lambda i, _: (jnp.minimum(i, steps - 1), 0)
+    cols = lambda i, _: (0, jnp.maximum(i - steps, 0))
+    down = lambda i, _: (jnp.maximum(i - steps, 0), 0)
+    z = jnp.reshape(lax.axis_index("row"), (1,)).astype(jnp.int32)
+    return pl.pallas_call(
+        functools.partial(expert_kernel, size, steps, count),
+        grid_spec=pltpu.PrefetchScalarGridSpec(
+            num_scalar_prefetch=1,
+            grid=(steps + more,),
+            in_specs=[pl.BlockSpec(memory_space=pl.ANY)] * count
+            + [
+                pl.BlockSpec((TILE, width), rows),
+                pl.BlockSpec((TILE, width), rows),
+                pl.BlockSpec((tokens, TILE), cols),
+                pl.BlockSpec((tokens, TILE), cols),
+                pl.BlockSpec((TILE, 2), rows),
+            ],
+            out_specs=[
+                pl.BlockSpec((TILE, 2 * size), rows),
+                pl.BlockSpec((TILE, size), rows),
+                pl.BlockSpec((TILE, 2), rows),
+                pl.BlockSpec((TILE, 3 * size), down),
+                pl.BlockSpec(memory_space=pl.ANY),
+            ],
+            scratch_shapes=[
+                pltpu.VMEM((width, 3 * size), bf16),
+                pltpu.VMEM((tokens, 2 * size), bf16),
+                pltpu.VMEM((tokens, size), bf16),
+                pltpu.SemaphoreType.DMA((4,)),
+                pltpu.SemaphoreType.DMA,
+            ],
+        ),
+        out_shape=[
+            jax.ShapeDtypeStruct((tokens, 2 * size), bf16),
+            jax.ShapeDtypeStruct((tokens, size), bf16),
+            jax.ShapeDtypeStruct((tokens, 2), f32),
+            jax.ShapeDtypeStruct((width, 3 * size), bf16),
+            jax.ShapeDtypeStruct((width, 3 * size), bf16),
+        ],
+        cost_estimate=pl.CostEstimate(
+            flops=12 * tokens * width * size,
+            bytes_accessed=8 * tokens * width + 24 * width * size,
+            transcendentals=tokens * size,
+        ),
+        name="expert_chunk",
+    )(z, *pieces, scaled, cots, scaled, cots, coef)
+
+
+def joint_kernel(count, *refs):
+    out_ref = refs[-1]
+    for a in range(0, out_ref.shape[1], TILE):
+        total = None
+        for left, weights in zip(refs[:count], refs[count:-1]):
+            part = mm_nt(left[...], weights[a : a + TILE, :])
+            total = part if total is None else total + part
+        out_ref[:, a : a + TILE] = total.astype(bf16)
+
+
+def joint_back(lefts, weights, column):
+    tokens, width = lefts[0].shape[0], weights[0].shape[0]
+    row = lambda i: (i, 0)
+    fixed = lambda i: (0, column)
+    depth = sum(left.shape[1] for left in lefts)
+    return pl.pallas_call(
+        functools.partial(joint_kernel, len(lefts)),
+        grid=(tokens // TILE,),
+        in_specs=[pl.BlockSpec((TILE, left.shape[1]), row) for left in lefts]
+        + [
+            pl.BlockSpec((width, left.shape[1]), fixed, pipeline_mode=pl.Buffered(1))
+            for left in lefts
+        ],
+        out_specs=pl.BlockSpec((TILE, width), row),
+        out_shape=jax.ShapeDtypeStruct((tokens, width), bf16),
+        cost_estimate=pl.CostEstimate(
+            flops=2 * tokens * width * depth,
+            bytes_accessed=2 * (tokens + width) * depth + 2 * tokens * width,
+            transcendentals=0,
+        ),
+        name="joint_back",
+    )(*lefts, *weights)
 
 
 def split_three(values):
@@ -265,31 +463,36 @@
     qkv_pack = jnp.concatenate(
         [by_head(query_weight), by_head(key_weight), by_head(value_weight)], axis=2
     ).reshape(rows_block, 3 * head_width)
-    attn_weights = gather_rows(jnp.concatenate([qkv_pack, output_weight.T], axis=1))
+    router_pack = jnp.concatenate([router_weight, score_shared[:, None]], axis=1)
+    router_pack = jnp.pad(router_pack, ((0, 0), (0, -router_pack.shape[1] % 128)))
+    attn_weights = join_rows(
+        gather_rows(jnp.concatenate([qkv_pack, output_weight.T, router_pack], axis=1))
+    )
     qkv_full = attn_weights[:, : 3 * head_width]
-    out_full = attn_weights[:, 3 * head_width :]
-    units = []
-    chunks = [(None, 0, gate_shared.shape[1])]
-    units.append(jnp.concatenate([gate_shared, up_shared, down_shared.T], axis=1))
-    for local in range(local_experts):
-        for a, b in cuts_of(gate_expert.shape[2]):
-            chunks.append((local, a, b))
-            units.append(
-                jnp.concatenate(
-                    [gate_expert[local, :, a:b], up_expert[local, :, a:b], down_expert[local, a:b].T],
-                    axis=1,
-                )
-            )
-    gathered = [gather_rows(unit) for unit in units]
-    router_pack = jnp.concatenate([router_weight, score_shared[:, None]], axis=1)
-    router_full = lax.all_gather(router_pack, "row", axis=0, tiled=True)
+    out_full = attn_weights[:, 3 * head_width : 4 * head_width]
+    router_full = attn_weights[:, 4 * head_width : 4 * head_width + experts + 1]
+    shared_cuts = [(None, a, b) for a, b in cuts_of(gate_shared.shape[1])]
+    expert_cuts = [
+        (local, a, b) for local in range(local_experts) for a, b in cuts_of(gate_expert.shape[2])
+    ]
+    chunks = shared_cuts[-1:] + expert_cuts[:-1] + shared_cuts[:-1] + expert_cuts[-1:]
+
+    def pack(kind, a, b):
+        if kind is None:
+            parts = [gate_shared[:, a:b], up_shared[:, a:b], down_shared[a:b].T]
+        else:
+            parts = [gate_expert[kind, :, a:b], up_expert[kind, :, a:b], down_expert[kind, a:b].T]
+        fill = -(b - a) % 128
+        return jnp.concatenate([jnp.pad(part, ((0, 0), (0, fill))) for part in parts], axis=1)
+
+    gathered = [gather_rows(pack(*chunk)) for chunk in chunks]
 
     rows_in = lax.all_gather(block_input, "col", axis=1, tiled=True)
-    gain_a = lax.all_gather(input_gain, "col", axis=0, tiled=True).astype(f32)
+    gains = lax.all_gather(jnp.stack([input_gain, mlp_gain]), "col", axis=1, tiled=True).astype(f32)
     cot_rows = lax.all_gather(grad_output, "col", axis=1, tiled=True)
     rows_f = rows_in.astype(f32)
     scale_a = lax.rsqrt(jnp.mean(rows_f * rows_f, axis=-1, keepdims=True) + norm_eps)
-    normed_a = (rows_f * scale_a * gain_a).astype(bf16)
+    normed_a = (rows_f * scale_a * gains[0]).astype(bf16)
     qkv, context, lse = attend_forward(mm(normed_a, qkv_full), lengths, cosine, sine)
     attn_part = mm_nt(context, out_full).astype(bf16)
     x_share = block_input.astype(f32)
@@ -298,8 +501,8 @@
     ).astype(f32)
     gain_b = mlp_gain.astype(f32)
     scaled = lax.all_gather((stream * gain_b).astype(bf16), "col", axis=1, tiled=True)
-    squares = lax.psum(jnp.sum(stream * stream, axis=1), "col")
-    scale_b = lax.rsqrt(squares / width + norm_eps)[:, None]
+    stream_f = scaled.astype(f32) / gains[1]
+    scale_b = lax.rsqrt(jnp.mean(stream_f * stream_f, axis=1, keepdims=True) + norm_eps)
 
     both_logits = scale_b * mm(scaled, router_full)
     logits, slogit = both_logits[:, :experts], both_logits[:, experts]
@@ -308,9 +511,6 @@
     router_probs = expo / jnp.sum(expo, axis=-1, keepdims=True)
     shared_gate = jax.nn.sigmoid(slogit)
 
-    moe_part = None
-    dscaled_part = None
-    unit_grads = []
     inner = jnp.zeros((tokens,), f32)
     dots = {}
     members, shares = {None: None}, {None: shared_gate}
@@ -319,31 +519,23 @@
         members[local] = jnp.any(routes == expert, axis=1)
         column = lax.dynamic_index_in_dim(router_probs, expert, 1, False)
         shares[local] = jnp.where(members[local], column, 0.0)
-    for (kind, a, b), full in zip(chunks, gathered):
-        size = b - a
-        weight = shares[kind][:, None]
-        pair = mm(scaled, full[:, : 2 * size])
-        dhidden = mm(cot_rows, full[:, 2 * size :])
-        gate, up = scale_b * pair[:, :size], scale_b * pair[:, size:]
-        sigma = jax.nn.sigmoid(gate)
-        silu = gate * sigma
-        hidden = silu * up
-        weighted = (weight * hidden).astype(bf16)
-        dots[kind] = dots.get(kind, 0.0) + jnp.sum(hidden * dhidden, axis=1)
-        dhidden = weight * dhidden
-        dgate = dhidden * up * sigma * (1.0 + gate * (1.0 - sigma))
-        dup = dhidden * silu
-        inner = inner + jnp.sum(dgate * gate + dup * up, axis=1)
-        dpair = jnp.concatenate([scale_b * dgate, scale_b * dup], axis=1).astype(bf16)
-        moe_new = mm_nt(weighted, full[:, 2 * size :])
-        dscaled_new = mm_nt(dpair, full[:, : 2 * size])
-        moe_part = moe_new if moe_part is None else moe_part + moe_new
-        dscaled_part = dscaled_new if dscaled_part is None else dscaled_part + dscaled_new
-        unit_grads.append(
-            reduce_rows([mm_tn(scaled, dpair).astype(bf16), mm_tn(cot_rows, weighted).astype(bf16)])
-        )
+    dpairs, hiddens, wholes, unit_grads, arrived = [], [], [], [], []
+    for at, ((kind, a, b), pieces) in enumerate(zip(chunks, gathered)):
+        coef = jnp.concatenate([scale_b, shares[kind][:, None]], axis=1)
+        if at >= 2:
+            coef = after(coef, arrived[at - 2])
+        dpair, hidden, sums, grads, whole = expert_chunk(pieces, scaled, cot_rows, coef)
+        dots[kind] = dots.get(kind, 0.0) + sums[:, 0]
+        inner = inner + sums[:, 1]
+        dpairs.append(dpair)
+        hiddens.append(hidden)
+        wholes.append(whole)
+        reduced, first = reduce_rows(grads)
+        unit_grads.append(reduced)
+        arrived.append(first)
+    dscaled_part = joint_back(dpairs, wholes, 0)
     moe_share = lax.psum_scatter(
-        moe_part.astype(bf16), "col", scatter_dimension=1, tiled=True
+        joint_back(hiddens, wholes, 2), "col", scatter_dimension=1, tiled=True
     ).astype(f32)
     block_output = (stream + moe_share).astype(bf16)
 
@@ -365,20 +557,20 @@
     router_rows = lax.dynamic_slice_in_dim(router_full, col_id * share, share, 0)
     back = mm_nt(jnp.concatenate(parts, axis=1), jnp.concatenate([router_rows] * 3, axis=1))
     dscaled = back + lax.psum_scatter(
-        dscaled_part.astype(bf16), "col", scatter_dimension=1, tiled=True
+        dscaled_part, "col", scatter_dimension=1, tiled=True
     ).astype(f32)
     cot_share = grad_output.astype(f32)
     dstream = cot_share + gain_b * dscaled - stream * (scale_b * scale_b * inner[:, None] / width)
     gain_b_grad = jnp.sum(dscaled * stream, axis=0)
 
     dattn = lax.all_gather(dstream.astype(bf16), "col", axis=1, tiled=True)
-    out_grad = reduce_rows([mm_tn(dattn, context).astype(bf16)])
+    out_grad, _ = reduce_rows(mm_tn(dattn, context).astype(bf16))
     dcontext = mm(dattn, out_full).astype(bf16)
     dqkv, inner_a = attend_backward(qkv, dcontext, lse, lengths, cosine, sine)
     inner_a = lax.psum(
         jnp.sum(inner_a.reshape(tokens, heads, HEAD_DIM)[:, :, 0], axis=1), "col"
     )[:, None]
-    qkv_grad = reduce_rows([mm_tn(normed_a, dqkv).astype(bf16)])
+    qkv_grad, _ = reduce_rows(mm_tn(normed_a, dqkv).astype(bf16))
     dnormed_a = lax.psum_scatter(
         mm_nt(dqkv, qkv_full).astype(bf16), "col", scatter_dimension=1, tiled=True
     ).astype(f32)
@@ -392,21 +584,17 @@
     grad_query, grad_key, grad_value = (
         qkv_grad[:, :, part].reshape(rows_block, head_width) for part in range(3)
     )
-    gates, ups, downs = [], [], []
-    for (kind, a, b), grad in zip(chunks, unit_grads):
-        size = b - a
-        pieces = (grad[:, :size], grad[:, size : 2 * size], grad[:, 2 * size :].T)
-        if kind is None:
-            grad_gate_shared, grad_up_shared, grad_down_shared = pieces
-        else:
-            if a == 0:
-                for into in (gates, ups, downs):
-                    into.append([])
-            for into, piece in zip((gates, ups, downs), pieces):
-                into[-1].append(piece)
-    grad_gate_expert = jnp.stack([jnp.concatenate(one, axis=1) for one in gates])
-    grad_up_expert = jnp.stack([jnp.concatenate(one, axis=1) for one in ups])
-    grad_down_expert = jnp.stack([jnp.concatenate(one, axis=0) for one in downs])
+    def unpack(kind, which):
+        found = []
+        for (of, a, b), grad in zip(chunks, unit_grads):
+            if of == kind:
+                size = grad.shape[1] // 3
+                part = grad[:, which * size : which * size + b - a]
+                found.append((a, part.T if which == 2 else part))
+        found = [part for _, part in sorted(found, key=lambda item: item[0])]
+        return jnp.concatenate(found, axis=0 if which == 2 else 1)
+
+    locals_ = range(local_experts)
     return (
         block_output,
         dinput.astype(bf16),
@@ -418,12 +606,12 @@
         grad_gain_b,
         grad_router_both[:experts].T,
         grad_router_both[experts],
-        grad_gate_shared,
-        grad_up_shared,
-        grad_down_shared,
-        grad_gate_expert,
-        grad_up_expert,
-        grad_down_expert,
+        unpack(None, 0),
+        unpack(None, 1),
+        unpack(None, 2),
+        jnp.stack([unpack(local, 0) for local in locals_]),
+        jnp.stack([unpack(local, 1) for local in locals_]),
+        jnp.stack([unpack(local, 2) for local in locals_]),
     )
 
 

time: 1520 us -> 1440 us (0.947)
  matrix products: 368 us -> 63 us
  Pallas kernels: 40.8 us -> 298 us
  waiting for transfers between devices: 457 us -> 687 us
  blocking collectives: 129 us -> 32.1 us
  starting transfers between devices: 208 us -> 128 us
  other arithmetic: 180 us -> 128 us
  local copies, waits for them, and re-layouts: 112 us -> 85.7 us
    pallas_call x0 -> x7, Pallas kernels: none -> 257 us  [the longest x5 183 us: expert_chunk(): pl.pallas_call(functools.partial(expert_kernel, size, steps, count), grid...]
    dot_general x11 -> x3, matrix products: 135 us -> 20.9 us  [mm(): return jnp.dot(left, right, preferred_element_type=f32)]
    dot_general x11 -> x3, matrix products: 136 us -> 22.5 us  [mm_nt(): lax.dot_general(left, right, (((1,), (1,)), ((), ())), preferred_element_...]
    ppermute x66 -> x65, waiting for transfers between devices: 407 us -> 516 us  [the longest x6 138 us: gather_rows(): far_out = lax.ppermute(far_mid, 'row', outward)]
    all_gather x2 -> x1, blocking collectives: 91.1 us -> 9.09 us  [per_device(): lax.all_gather(jnp.stack([input_gain, mlp_gain]), 'col', axis=1, tiled=True)]
    ppermute x66 -> x65, starting transfers between devices: 207 us -> 127 us  [the longest x7 24.6 us: reduce_rows(): near_in = lax.ppermute(block(near), 'row', inward)]
    dot_general x11 -> x3, matrix products: 96.8 us -> 19.6 us  [mm_tn(): lax.dot_general(left, right, (((0,), (0,)), ((), ())), preferred_element_...]
    reduce_scatter x2, waiting for transfers between devices: 0.02 us -> 60.9 us  [the longest x1 60.9 us: per_device(): lax.psum_scatter(dscaled_part, 'col', scatter_dimension=1, tiled=True)]
  transfers between devices with their start and end apart: 76 -> 75, of which waited for: 21 -> 29; matrix products, arithmetic and copies ran while one was open for 32% -> 16% of each run, Pallas kernels for 2% -> 17%
where the time goes in v2:
time: 1440 us
  waiting for transfers between devices  687 us (48%)
  Pallas kernels  298 us (21%)
  starting transfers between devices  128 us (9%)
  other arithmetic  128 us (9%)
  local copies, waits for them, and re-layouts  85.7 us (6%)
  matrix products  63 us (4%)
  blocking collectives  32.1 us (2%)
  between operations  15.9 us (1%)
    pallas_call x5, Pallas kernels, expert_chunk(): pl.pallas_call(functools.partial(expert_kernel, size, steps, count), grid...  183 us
    ppermute x6, waiting for transfers between devices, gather_rows(): far_out = lax.ppermute(far_mid, 'row', outward)  138 us
    ppermute x7, waiting for transfers between devices, reduce_rows(): far_in = lax.ppermute(block(far), 'row', inward)  98.5 us
    ppermute x7, waiting for transfers between devices, reduce_rows(): lax.ppermute(block(partner, far_sum).astype(bf16), 'row', [(0, 1), (1, 0)...  97.5 us
    ppermute x6, waiting for transfers between devices, gather_rows(): near_out = lax.ppermute(near_mid, 'row', outward)  91.4 us
    pallas_call x2, Pallas kernels, joint_back(): pl.pallas_call(functools.partial(joint_kernel, len(lefts)), grid=(tokens...  73.5 us
    reduce_scatter x1, waiting for transfers between devices, per_device(): lax.psum_scatter(attn_part, 'col', scatter_dimension=1, tiled=True)  71.9 us
    reduce_scatter x1, waiting for transfers between devices, per_device(): lax.psum_scatter(dscaled_part, 'col', scatter_dimension=1, tiled=True)  60.9 us
  transfers between devices with their start and end apart: 75, of which 29 were waited for; matrix products, arithmetic and copies ran while one was open for 16% of the time, Pallas kernels for 17%

profile of v2, /device:TPU:0, one launch (start us, length us, event | category | flops | bytes accessed | tf_op | source)
XLA Modules:
  0.0 1437.1 jit_solution(17282187521956524842)
XLA Ops:
  18.2 22.8 %collective-permute-done = bf16[512,1152]{0,1:T(8,128)(2,1)} collective-permute-done((bf16[512,1152]{0,1:T(8,128)(2,1)}, bf16[512,1152]{0,1:T(8,128)(2,1)}, u32[]{:S(2)}, u32[]{:S(2)}) %collective-permute-start) | collective-permute-done | bytes 1179680 | tf_op jit(solution)/shard_map/ppermute | solution.py:177
  78.5 20.5 %collective-permute-done.4 = bf16[512,1152]{0,1:T(8,128)(2,1)} collective-permute-done((bf16[512,1152]{0,1:T(8,128)(2,1)}, bf16[512,1152]{0,1:T(8,128)(2,1)}, u32[]{:S(2)}, u32[]{:S(2)}) %collective-permute-start.4) | collective-permute-done | bytes 1179680 | tf_op jit(solution)/shard_map/ppermute | solution.py:182
  118.9 12.7 attend_forward.1
  138.9 71.9 %reduce-scatter.6.cloned.1.call-done = bf16[2048,256]{1,0:T(8,128)(2,1)} async-done(((bf16[2048,2048]{1,0:T(8,128)(2,1)}), bf16[2048,256]{1,0:T(8,128)(2,1)}) %reduce-scatter.6.cloned.1.call-update) | async-done | bytes 1048592 | tf_op jit(solution)/shard_map/reduce_scatter | solution.py:499
  236.2 33.2 %all-gather.7.cloned.1.call-done.refs_6_.refs_8_ = bf16[2048,2048]{1,0:T(8,128)(2,1)} async-done(((bf16[2048,256]{1,0:T(8,128)(2,1)}), bf16[2048,2048]{1,0:T(8,128)(2,1)}) %all-gather.7.cloned.1.call-update) | async-done | bytes 8388624 | tf_op jit(solution)/shard_map/all_gather | solution.py:503
  280.3 16.3 %collective-permute-done.27.refs_1_ = bf16[512,1152]{1,0:T(8,128)(2,1)} collective-permute-done((bf16[512,1152]{1,0:T(8,128)(2,1)}, bf16[512,1152]{1,0:T(8,128)(2,1)}, u32[]{:S(2)}, u32[]{:S(2)}) %collective-permute-start.27) | collective-permute-done | bytes 1179680 | tf_op jit(solution)/shard_map/ppermute | solution.py:177
  306.0 45.0 %collective-permute-done.8.refs_4_ = bf16[512,768]{1,0:T(8,128)(2,1)S(1)} collective-permute-done((bf16[512,768]{1,0:T(8,128)(2,1)}, bf16[512,768]{1,0:T(8,128)(2,1)S(1)}, u32[]{:S(2)}, u32[]{:S(2)}) %collective-permute-start.8) | collective-permute-done | bytes 786464 | tf_op jit(solution)/shard_map/ppermute | solution.py:181
  352.3 15.6 %collective-permute-done.9.refs_5_ = bf16[512,768]{1,0:T(8,128)(2,1)} collective-permute-done((bf16[512,768]{1,0:T(8,128)(2,1)S(1)}, bf16[512,768]{1,0:T(8,128)(2,1)}, u32[]{:S(2)}, u32[]{:S(2)}) %collective-permute-start.9) | collective-permute-done | bytes 786464 | tf_op jit(solution)/shard_map/ppermute | solution.py:182
  371.1 27.9 %expert_chunk.5 = (bf16[2048,512]{1,0:T(8,128)(2,1)}, bf16[2048,256]{1,0:T(8,128)(2,1)}, f32[2048,2]{1,0:T(8,128)}, bf16[2048,768]{1,0:T(8,128)(2,1)}, bf16[2048,768]{1,0:T(8,128)(2,1)}) custom-call(s32[1]{0:T(128)} %bitcast.11.z_ref, bf16[512,768]{1,0:T(8,128)(2,1)} %fusion.20.refs_0_, bf16[512,768]{1,0:T(8,128)(2,1)} %collective-permute-done.5.refs_1_, ...), custom_call_target="tpu_custom_call" | custom-call | flops 12884901888 | bytes 46137344 | tf_op jit(solution)/shard_map/expert_chunk/pallas_call | solution.py:332
  410.3 25.0 %collective-permute-done.13.refs_4_ = bf16[512,1536]{1,0:T(8,128)(2,1)} collective-permute-done((bf16[512,1536]{1,0:T(8,128)(2,1)}, bf16[512,1536]{1,0:T(8,128)(2,1)}, u32[]{:S(2)}, u32[]{:S(2)}) %collective-permute-start.13) | collective-permute-done | bytes 1572896 | tf_op jit(solution)/shard_map/ppermute | solution.py:181
  438.3 30.7 %collective-permute-done.14.refs_5_ = bf16[512,1536]{1,0:T(8,128)(2,1)} collective-permute-done((bf16[512,1536]{1,0:T(8,128)(2,1)}, bf16[512,1536]{1,0:T(8,128)(2,1)}, u32[]{:S(2)}, u32[]{:S(2)}) %collective-permute-start.14) | collective-permute-done | bytes 1572896 | tf_op jit(solution)/shard_map/ppermute | solution.py:182
  472.5 39.6 %expert_chunk.6 = (bf16[2048,1024]{1,0:T(8,128)(2,1)}, bf16[2048,512]{1,0:T(8,128)(2,1)}, f32[2048,2]{1,0:T(8,128)}, bf16[2048,1536]{1,0:T(8,128)(2,1)}, bf16[2048,1536]{1,0:T(8,128)(2,1)}) custom-call(s32[1]{0:T(128)} %bitcast.11.z_ref, bf16[512,1536]{1,0:T(8,128)(2,1)} %pad_maximum_fusion.refs_0_, bf16[512,1536]{1,0:T(8,128)(2,1)} %collective-permute-done.10.refs_1_, ...), custom_call_target="tpu_custom_call" | custom-call | flops 25769803776 | bytes 58720256 | tf_op jit(solution)/shard_map/expert_chunk/pallas_call | solution.py:332
  522.1 14.3 collective-permute-done.19.refs_5_
  539.1 39.5 %expert_chunk.7 = (bf16[2048,1024]{1,0:T(8,128)(2,1)}, bf16[2048,512]{1,0:T(8,128)(2,1)}, f32[2048,2]{1,0:T(8,128)}, bf16[2048,1536]{1,0:T(8,128)(2,1)}, bf16[2048,1536]{1,0:T(8,128)(2,1)}) custom-call(s32[1]{0:T(128)} %bitcast.11.z_ref, bf16[512,1536]{1,0:T(8,128)(2,1)} %pad_maximum_fusion.1.refs_0_, bf16[512,1536]{1,0:T(8,128)(2,1)} %collective-permute-done.15.refs_1_, ...), custom_call_target="tpu_custom_call" | custom-call | flops 25769803776 | bytes 58720256 | tf_op jit(solution)/shard_map/expert_chunk/pallas_call | solution.py:332
  595.4 56.9 %collective-permute-done.25.refs_5_ = bf16[512,1536]{1,0:T(8,128)(2,1)} collective-permute-done((bf16[512,1536]{1,0:T(8,128)(2,1)}, bf16[512,1536]{1,0:T(8,128)(2,1)}, u32[]{:S(2)}, u32[]{:S(2)}) %collective-permute-start.25) | collective-permute-done | bytes 1572896 | tf_op jit(solution)/shard_map/ppermute | solution.py:182
  652.4 39.5 %expert_chunk.8 = (bf16[2048,1024]{1,0:T(8,128)(2,1)}, bf16[2048,512]{1,0:T(8,128)(2,1)}, f32[2048,2]{1,0:T(8,128)}, bf16[2048,1536]{1,0:T(8,128)(2,1)}, bf16[2048,1536]{1,0:T(8,128)(2,1)}) custom-call(s32[1]{0:T(128)} %bitcast.11.z_ref, bf16[512,1536]{1,0:T(8,128)(2,1)} %pad_maximum_fusion.2.refs_0_, bf16[512,1536]{1,0:T(8,128)(2,1)} %collective-permute-done.21.refs_1_, ...), custom_call_target="tpu_custom_call" | custom-call | flops 25769803776 | bytes 58720256 | tf_op jit(solution)/shard_map/expert_chunk/pallas_call | solution.py:332
  694.4 36.9 %expert_chunk.9 = (bf16[2048,768]{1,0:T(8,128)(2,1)}, bf16[2048,384]{1,0:T(8,128)(2,1)}, f32[2048,2]{1,0:T(8,128)}, bf16[2048,1152]{1,0:T(8,128)(2,1)}, bf16[2048,1152]{1,0:T(8,128)(2,1)}) custom-call(s32[1]{0:T(128)} %bitcast.11.z_ref, bf16[512,1152]{1,0:T(8,128)(2,1)} %pad_maximum_fusion.7.refs_0_, bf16[512,1152]{1,0:T(8,128)(2,1)} %collective-permute-done.27.refs_1_, ...), custom_call_target="tpu_custom_call" | custom-call | flops 19327352832 | bytes 52428800 | tf_op jit(solution)/shard_map/expert_chunk/pallas_call | solution.py:332
  737.3 47.0 %joint_back.3 = bf16[2048,2048]{1,0:T(8,128)(2,1)} custom-call(bf16[2048,512]{1,0:T(8,128)(2,1)} %get-tuple-element.71.refs_0_, bf16[2048,1024]{1,0:T(8,128)(2,1)} %get-tuple-element.72.refs_1_, bf16[2048,1024]{1,0:T(8,128)(2,1)} %get-tuple-element.73.refs_2_, bf16[2048,1024]{1,0:T(8,128)(2,1)} %get-tuple-element.74.refs_3_, ...), custom_call_target="tpu_custom_call" | custom-call | flops 36507222016 | bytes 44040192 | tf_op jit(solution)/shard_map/joint_back/pallas_call | solution.py:391
  803.1 60.9 %reduce-scatter.10.cloned.1.call-done = bf16[2048,256]{1,0:T(8,128)(2,1)} async-done(((bf16[2048,2048]{1,0:T(8,128)(2,1)}), bf16[2048,256]{1,0:T(8,128)(2,1)}) %reduce-scatter.10.cloned.1.call-update) | async-done | bytes 1048592 | tf_op jit(solution)/shard_map/reduce_scatter | solution.py:559
  867.9 26.6 %joint_back.2 = bf16[2048,2048]{1,0:T(8,128)(2,1)} custom-call(bf16[2048,256]{1,0:T(8,128)(2,1)} %get-tuple-element.50.refs_0_, bf16[2048,512]{1,0:T(8,128)(2,1)} %get-tuple-element.51.refs_1_, bf16[2048,512]{1,0:T(8,128)(2,1)} %get-tuple-element.54.refs_2_, bf16[2048,512]{1,0:T(8,128)(2,1)} %get-tuple-element.57.refs_3_, ...), custom_call_target="tpu_custom_call" | custom-call | flops 18253611008 | bytes 26214400 | tf_op jit(solution)/shard_map/joint_back/pallas_call | solution.py:391
  902.8 13.4 collective-permute-done.49
  926.6 23.3 %collective-permute-done.53 = bf16[512,1536]{1,0:T(8,128)(2,1)} collective-permute-done((bf16[512,1536]{1,0:T(8,128)(2,1)}, bf16[512,1536]{1,0:T(8,128)(2,1)}, u32[]{:S(2)}, u32[]{:S(2)}) %collective-permute-start.53) | collective-permute-done | bytes 1572896 | tf_op jit(solution)/shard_map/ppermute | solution.py:220
  964.4 19.2 %collective-permute-done.57 = bf16[512,1536]{1,0:T(8,128)(2,1)S(1)} collective-permute-done((bf16[512,1536]{1,0:T(8,128)(2,1)}, bf16[512,1536]{1,0:T(8,128)(2,1)S(1)}, u32[]{:S(2)}, u32[]{:S(2)}) %collective-permute-start.57) | collective-permute-done | bytes 1572896 | tf_op jit(solution)/shard_map/ppermute | solution.py:220
  1007.9 26.3 %collective-permute-done.43 = bf16[512,1536]{1,0:T(8,128)(2,1)} collective-permute-done((bf16[512,1536]{1,0:T(8,128)(2,1)}, bf16[512,1536]{1,0:T(8,128)(2,1)}, u32[]{:S(2)}, u32[]{:S(2)}) %collective-permute-start.43) | collective-permute-done | bytes 1572896 | tf_op jit(solution)/shard_map/ppermute | solution.py:221
  1042.2 25.7 %collective-permute-done.45 = bf16[512,1536]{1,0:T(8,128)(2,1)} collective-permute-done((bf16[512,1536]{1,0:T(8,128)(2,1)}, bf16[512,1536]{1,0:T(8,128)(2,1)}, u32[]{:S(2)}, u32[]{:S(2)}) %collective-permute-start.45) | collective-permute-done | bytes 1572896 | tf_op jit(solution)/shard_map/ppermute | solution.py:220
  1096.3 20.9 %collective-permute-done.60 = bf16[512,1152]{1,0:T(8,128)(2,1)S(1)} collective-permute-done((bf16[512,1152]{1,0:T(8,128)(2,1)S(1)}, bf16[512,1152]{1,0:T(8,128)(2,1)S(1)}, u32[]{:S(2)}, u32[]{:S(2)}) %collective-permute-start.60) | collective-permute-done | bytes 1179680 | tf_op jit(solution)/shard_map/ppermute | solution.py:221
  1127.2 28.0 %attend_backward.1 = (bf16[2048,768]{1,0:T(8,128)(2,1)}, f32[2048,256]{1,0:T(8,128)}) custom-call(s32[2]{0:T(128)} %dynamic_slice.108.length_ref, bf16[2048,768]{1,0:T(8,128)(2,1)} %get-tuple-element.76.qkv_ref, bf16[2048,256]{1,0:T(8,128)(2,1)} %convolution_convert_fusion.4.dcontext_ref, f32[2048,256]{1,0:T(8,128)} %get-tuple-element.77.lse_ref, ...), custom_call_target="tpu_custom_call" | custom-call | flops 4294967296 | bytes 12582912 | tf_op jit(solution)/shard_map/attend_backward/pallas_call | solution.py:153
  1182.3 24.1 %collective-permute-done.55 = bf16[512,1536]{1,0:T(8,128)(2,1)S(1)} collective-permute-done((bf16[512,1536]{1,0:T(8,128)(2,1)}, bf16[512,1536]{1,0:T(8,128)(2,1)S(1)}, u32[]{:S(2)}, u32[]{:S(2)}) %collective-permute-start.55) | collective-permute-done | bytes 1572896 | tf_op jit(solution)/shard_map/ppermute | solution.py:224
  1212.9 27.2 %collective-permute-done.59 = bf16[512,1536]{1,0:T(8,128)(2,1)S(1)} collective-permute-done((bf16[512,1536]{1,0:T(8,128)(2,1)S(1)}, bf16[512,1536]{1,0:T(8,128)(2,1)S(1)}, u32[]{:S(2)}, u32[]{:S(2)}) %collective-permute-start.59) | collective-permute-done | bytes 1572896 | tf_op jit(solution)/shard_map/ppermute | solution.py:224
  1244.4 21.0 %collective-permute-done.64 = bf16[512,1152]{1,0:T(8,128)(2,1)S(1)} collective-permute-done((bf16[512,1152]{1,0:T(8,128)(2,1)S(1)}, bf16[512,1152]{1,0:T(8,128)(2,1)S(1)}, u32[]{:S(2)}, u32[]{:S(2)}) %collective-permute-start.64) | collective-permute-done | bytes 1179680 | tf_op jit(solution)/shard_map/ppermute | solution.py:224
  1279.0 18.3 %collective-permute-done.47 = bf16[512,1536]{1,0:T(8,128)(2,1)} collective-permute-done((bf16[512,1536]{1,0:T(8,128)(2,1)}, bf16[512,1536]{1,0:T(8,128)(2,1)}, u32[]{:S(2)}, u32[]{:S(2)}) %collective-permute-start.47) | collective-permute-done | bytes 1572896 | tf_op jit(solution)/shard_map/ppermute | solution.py:224
  1374.3 15.2 %slice_reduce_fusion = f32[2048]{0:T(1024)S(1)} fusion(f32[2048,2,128]{2,1,0:T(2,128)S(1)} %copy-done.8), kind=kLoop, calls=%fused_computation.46 | loop fusion | flops 2048 | bytes 24576 | tf_op jit(solution)/shard_map/reduce_sum | solution.py:571
  (463 shorter events, 475.8 us)
Async XLA Ops:
  7.2 95.4 %all-gather.5.cloned.1.call-start = ((), (), s32[]{:S(2)}) async-start(), calls=%async_computation.5 | async-start | bytes 9437184 | tf_op jit(solution)/shard_map/all_gather | solution.py:490
  8.0 202.8 %reduce-scatter.6.cloned.1.call-start = ((), (), s32[]{:S(2)}) async-start(), calls=%async_computation.6 | async-start | bytes 9437184 | tf_op jit(solution)/shard_map/reduce_scatter | solution.py:499
  138.8 130.6 %all-gather.7.cloned.1.call-start = ((), (), s32[]{:S(2)}) async-start(), calls=%async_computation.7 | async-start | bytes 9437184 | tf_op jit(solution)/shard_map/all_gather | solution.py:503
  213.3 157.8 %all-gather.9.cloned.1.call-start = ((), (), s32[]{:S(2)}) async-start(), calls=%async_computation.8 | async-start | bytes 9437184 | tf_op jit(solution)/shard_map/all_gather | solution.py:492
  213.9 576.0 %all-reduce.7.cloned.1.call-start = ((), (), s32[]{:S(2)}) async-start(), calls=%async_computation.10 | async-start | bytes 262144 | tf_op jit(solution)/shard_map/psum | solution.py:546
  218.0 80.1 %collective-permute-start.10 = (bf16[512,1536]{1,0:T(8,128)(2,1)}, bf16[512,1536]{1,0:T(8,128)(2,1)}, u32[]{:S(2)}, u32[]{:S(2)}) collective-permute-start(bf16[512,1536]{1,0:T(8,128)(2,1)} %pad_maximum_fusion.refs_0_), channel_id=1, source_target_pairs={{0,8},{8,0},{16,24},{24,16},{1,9},{9,1},{17,25},{25,17},{2,10},{10... | collective-permute-start | bytes 4718600 | tf_op jit(solution)/shard_map/ppermute | solution.py:177
  219.5 83.2 %collective-permute-start.11 = (bf16[512,1536]{1,0:T(8,128)(2,1)}, bf16[512,1536]{1,0:T(8,128)(2,1)}, u32[]{:S(2)}, u32[]{:S(2)}) collective-permute-start(bf16[512,1536]{1,0:T(8,128)(2,1)} %pad_maximum_fusion.refs_0_), channel_id=1, source_target_pairs={{8,16},{16,8},{9,17},{17,9},{10,18},{18,10},{11,19},{19,11},{12,20... | collective-permute-start | bytes 4718600 | tf_op jit(solution)/shard_map/ppermute | solution.py:179
  302.7 98.7 %collective-permute-start.16 = (bf16[512,1536]{1,0:T(8,128)(2,1)}, bf16[512,1536]{1,0:T(8,128)(2,1)}, u32[]{:S(2)}, u32[]{:S(2)}) collective-permute-start(bf16[512,1536]{1,0:T(8,128)(2,1)} %pad_maximum_fusion.1.refs_0_), channel_id=1, source_target_pairs={{8,16},{16,8},{9,17},{17,9},{10,18},{18,10},{11,19},{19,11},{12,20... | collective-permute-start | bytes 4718600 | tf_op jit(solution)/shard_map/ppermute | solution.py:179
  351.0 84.3 %collective-permute-start.13 = (bf16[512,1536]{1,0:T(8,128)(2,1)}, bf16[512,1536]{1,0:T(8,128)(2,1)}, u32[]{:S(2)}, u32[]{:S(2)}) collective-permute-start(bf16[512,1536]{1,0:T(8,128)(2,1)} %collective-permute-done.11.refs_2_), channel_id=1, source_target_pairs={{8,0},{16,24},{9,1},{17,25},{10,2},{18,26},{11,3},{19,27},{12,4},{... | collective-permute-start | bytes 4718600 | tf_op jit(solution)/shard_map/ppermute | solution.py:181
  369.8 99.2 %collective-permute-start.14 = (bf16[512,1536]{1,0:T(8,128)(2,1)}, bf16[512,1536]{1,0:T(8,128)(2,1)}, u32[]{:S(2)}, u32[]{:S(2)}) collective-permute-start(bf16[512,1536]{1,0:T(8,128)(2,1)} %collective-permute-done.12.refs_3_), channel_id=1, source_target_pairs={{8,0},{16,24},{9,1},{17,25},{10,2},{18,26},{11,3},{19,27},{12,4},{... | collective-permute-start | bytes 4718600 | tf_op jit(solution)/shard_map/ppermute | solution.py:182
  408.5 108.4 %collective-permute-start.22 = (bf16[512,1536]{1,0:T(8,128)(2,1)S(1)}, bf16[512,1536]{1,0:T(8,128)(2,1)}, u32[]{:S(2)}, u32[]{:S(2)}) collective-permute-start(bf16[512,1536]{1,0:T(8,128)(2,1)S(1)} %copy-done.32), channel_id=1, source_target_pairs={{8,16},{16,8},{9,17},{17,9},{10,18},{18,10},{11,19},{19,11},{12,20... | collective-permute-start | bytes 4718600 | tf_op jit(solution)/shard_map/ppermute | solution.py:179
  435.3 82.9 %collective-permute-start.29 = (bf16[512,1152]{1,0:T(8,128)(2,1)}, bf16[512,1152]{1,0:T(8,128)(2,1)}, u32[]{:S(2)}, u32[]{:S(2)}) collective-permute-start(bf16[512,1152]{1,0:T(8,128)(2,1)} %collective-permute-done.27.refs_1_), channel_id=1, source_target_pairs={{8,16},{16,8},{9,17},{17,9},{10,18},{18,10},{11,19},{19,11},{12,20... | collective-permute-start | bytes 3538952 | tf_op jit(solution)/shard_map/ppermute | solution.py:180
  437.0 82.5 %collective-permute-start.18 = (bf16[512,1536]{1,0:T(8,128)(2,1)}, bf16[512,1536]{1,0:T(8,128)(2,1)}, u32[]{:S(2)}, u32[]{:S(2)}) collective-permute-start(bf16[512,1536]{1,0:T(8,128)(2,1)} %collective-permute-done.16.refs_2_), channel_id=1, source_target_pairs={{8,0},{16,24},{9,1},{17,25},{10,2},{18,26},{11,3},{19,27},{12,4},{... | collective-permute-start | bytes 4718600 | tf_op jit(solution)/shard_map/ppermute | solution.py:181
  516.9 177.5 %collective-permute-start.30 = (bf16[512,1152]{1,0:T(8,128)(2,1)}, bf16[512,1152]{1,0:T(8,128)(2,1)}, u32[]{:S(2)}, u32[]{:S(2)}) collective-permute-start(bf16[512,1152]{1,0:T(8,128)(2,1)} %copy-done.63), channel_id=1, source_target_pairs={{8,0},{16,24},{9,1},{17,25},{10,2},{18,26},{11,3},{19,27},{12,4},{... | collective-permute-start | bytes 3538952 | tf_op jit(solution)/shard_map/ppermute | solution.py:181
  518.2 77.2 %collective-permute-start.24 = (bf16[512,1536]{1,0:T(8,128)(2,1)}, bf16[512,1536]{1,0:T(8,128)(2,1)}, u32[]{:S(2)}, u32[]{:S(2)}) collective-permute-start(bf16[512,1536]{1,0:T(8,128)(2,1)} %collective-permute-done.22.refs_2_), channel_id=1, source_target_pairs={{8,0},{16,24},{9,1},{17,25},{10,2},{18,26},{11,3},{19,27},{12,4},{... | collective-permute-start | bytes 4718600 | tf_op jit(solution)/shard_map/ppermute | solution.py:181
  519.5 174.9 %collective-permute-start.31 = (bf16[512,1152]{1,0:T(8,128)(2,1)}, bf16[512,1152]{1,0:T(8,128)(2,1)}, u32[]{:S(2)}, u32[]{:S(2)}) collective-permute-start(bf16[512,1152]{1,0:T(8,128)(2,1)} %collective-permute-done.29.refs_3_), channel_id=1, source_target_pairs={{8,0},{16,24},{9,1},{17,25},{10,2},{18,26},{11,3},{19,27},{12,4},{... | collective-permute-start | bytes 3538952 | tf_op jit(solution)/shard_map/ppermute | solution.py:182
  520.8 131.5 %collective-permute-start.25 = (bf16[512,1536]{1,0:T(8,128)(2,1)}, bf16[512,1536]{1,0:T(8,128)(2,1)}, u32[]{:S(2)}, u32[]{:S(2)}) collective-permute-start(bf16[512,1536]{1,0:T(8,128)(2,1)} %collective-permute-done.23.refs_3_), channel_id=1, source_target_pairs={{8,0},{16,24},{9,1},{17,25},{10,2},{18,26},{11,3},{19,27},{12,4},{... | collective-permute-start | bytes 4718600 | tf_op jit(solution)/shard_map/ppermute | solution.py:182
  581.9 110.0 %collective-permute-start.32 = (bf16[512,1536]{1,0:T(8,128)(2,1)S(1)}, bf16[512,1536]{1,0:T(8,128)(2,1)S(1)}, u32[]{:S(2)}, u32[]{:S(2)}) collective-permute-start(bf16[512,1536]{1,0:T(8,128)(2,1)S(1)} %get-tuple-element.173), channel_id=1, source_target_pairs={{0,8},{24,16},{1,9},{25,17},{2,10},{26,18},{3,11},{27,19},{4,12},{... | collective-permute-start | bytes 4718600 | tf_op jit(solution)/shard_map/ppermute | solution.py:221
  736.8 127.1 %reduce-scatter.10.cloned.1.call-start = ((), (), s32[]{:S(2)}) async-start(), calls=%async_computation.11 | async-start | bytes 9437184 | tf_op jit(solution)/shard_map/reduce_scatter | solution.py:559
  784.3 221.0 %reduce-scatter.14.cloned.1.call-start = ((), (), s32[]{:S(2)}) async-start(), calls=%async_computation.14 | async-start | bytes 163840 | tf_op jit(solution)/shard_map/reduce_scatter | solution.py:556
  801.4 318.8 %all-gather.11.cloned.1.call-start = ((), (), s32[]{:S(2)}) async-start(), calls=%async_computation.12 | async-start | bytes 9437184 | tf_op jit(solution)/shard_map/all_gather | solution.py:566
  867.9 546.9 %reduce-scatter.8.cloned.1.call-start = ((), (), s32[]{:S(2)}) async-start(), calls=%async_computation.9 | async-start | bytes 9437184 | tf_op jit(solution)/shard_map/reduce_scatter | solution.py:537
  894.5 520.2 %reduce-scatter.12.cloned.1.call-start = ((), (), s32[]{:S(2)}) async-start(), calls=%async_computation.13 | async-start | bytes 9437184 | tf_op jit(solution)/shard_map/reduce_scatter | solution.py:574
  901.3 82.3 %collective-permute-start.57 = (bf16[512,1536]{1,0:T(8,128)(2,1)}, bf16[512,1536]{1,0:T(8,128)(2,1)S(1)}, u32[]{:S(2)}, u32[]{:S(2)}) collective-permute-start(bf16[512,1536]{1,0:T(8,128)(2,1)} %get-tuple-element.172), channel_id=1, source_target_pairs={{0,8},{24,16},{1,9},{25,17},{2,10},{26,18},{3,11},{27,19},{4,12},{... | collective-permute-start | bytes 4718600 | tf_op jit(solution)/shard_map/ppermute | solution.py:220
  924.6 256.6 %collective-permute-start.52 = (bf16[512,1536]{1,0:T(8,128)(2,1)}, bf16[512,1536]{1,0:T(8,128)(2,1)}, u32[]{:S(2)}, u32[]{:S(2)}) collective-permute-start(bf16[512,1536]{1,0:T(8,128)(2,1)} %add_convert_fusion.5), channel_id=1, source_target_pairs={{8,16},{16,8},{9,17},{17,9},{10,18},{18,10},{11,19},{19,11},{12,20... | collective-permute-start | bytes 4718600 | tf_op jit(solution)/shard_map/ppermute | solution.py:223
  953.0 122.8 %collective-permute-start.54 = (bf16[512,1536]{1,0:T(8,128)(2,1)}, bf16[512,1536]{1,0:T(8,128)(2,1)}, u32[]{:S(2)}, u32[]{:S(2)}) collective-permute-start(bf16[512,1536]{1,0:T(8,128)(2,1)} %add_convert_fusion.4), channel_id=1, source_target_pairs={{8,16},{16,8},{9,17},{17,9},{10,18},{18,10},{11,19},{19,11},{12,20... | collective-permute-start | bytes 4718600 | tf_op jit(solution)/shard_map/ppermute | solution.py:222
  991.1 76.8 %collective-permute-start.45 = (bf16[512,1536]{1,0:T(8,128)(2,1)}, bf16[512,1536]{1,0:T(8,128)(2,1)}, u32[]{:S(2)}, u32[]{:S(2)}) collective-permute-start(bf16[512,1536]{1,0:T(8,128)(2,1)} %get-tuple-element.175), channel_id=1, source_target_pairs={{0,8},{24,16},{1,9},{25,17},{2,10},{26,18},{3,11},{27,19},{4,12},{... | collective-permute-start | bytes 4718600 | tf_op jit(solution)/shard_map/ppermute | solution.py:220
  1000.4 166.3 %collective-permute-start.58 = (bf16[512,1536]{1,0:T(8,128)(2,1)}, bf16[512,1536]{1,0:T(8,128)(2,1)}, u32[]{:S(2)}, u32[]{:S(2)}) collective-permute-start(bf16[512,1536]{1,0:T(8,128)(2,1)} %add_convert_fusion.1), channel_id=1, source_target_pairs={{8,16},{16,8},{9,17},{17,9},{10,18},{18,10},{11,19},{19,11},{12,20... | collective-permute-start | bytes 4718600 | tf_op jit(solution)/shard_map/ppermute | solution.py:222
  1075.8 136.9 %collective-permute-start.56 = (bf16[512,1536]{1,0:T(8,128)(2,1)}, bf16[512,1536]{1,0:T(8,128)(2,1)}, u32[]{:S(2)}, u32[]{:S(2)}) collective-permute-start(bf16[512,1536]{1,0:T(8,128)(2,1)} %add_convert_fusion.2), channel_id=1, source_target_pairs={{8,16},{16,8},{9,17},{17,9},{10,18},{18,10},{11,19},{19,11},{12,20... | collective-permute-start | bytes 4718600 | tf_op jit(solution)/shard_map/ppermute | solution.py:223
  1093.2 82.0 %collective-permute-start.46 = (bf16[512,1536]{1,0:T(8,128)(2,1)}, bf16[512,1536]{1,0:T(8,128)(2,1)}, u32[]{:S(2)}, u32[]{:S(2)}) collective-permute-start(bf16[512,1536]{1,0:T(8,128)(2,1)} %add_convert_fusion.7), channel_id=1, source_target_pairs={{8,16},{16,8},{9,17},{17,9},{10,18},{18,10},{11,19},{19,11},{12,20... | collective-permute-start | bytes 4718600 | tf_op jit(solution)/shard_map/ppermute | solution.py:222
  1175.2 103.8 %collective-permute-start.44 = (bf16[512,1536]{1,0:T(8,128)(2,1)}, bf16[512,1536]{1,0:T(8,128)(2,1)}, u32[]{:S(2)}, u32[]{:S(2)}) collective-permute-start(bf16[512,1536]{1,0:T(8,128)(2,1)} %add_convert_fusion.8), channel_id=1, source_target_pairs={{8,16},{16,8},{9,17},{17,9},{10,18},{18,10},{11,19},{19,11},{12,20... | collective-permute-start | bytes 4718600 | tf_op jit(solution)/shard_map/ppermute | solution.py:223
  1212.7 84.6 %collective-permute-start.47 = (bf16[512,1536]{1,0:T(8,128)(2,1)}, bf16[512,1536]{1,0:T(8,128)(2,1)}, u32[]{:S(2)}, u32[]{:S(2)}) collective-permute-start(bf16[512,1536]{1,0:T(8,128)(2,1)} %add_convert_fusion.6), channel_id=1, source_target_pairs={{0,8},{8,0},{16,24},{24,16},{1,9},{9,1},{17,25},{25,17},{2,10},{10... | collective-permute-start | bytes 4718600 | tf_op jit(solution)/shard_map/ppermute | solution.py:224
  (127 other events, 3769.1 us)
Sparse Core Ops, SparseCore 0:
  9.9 58.6 all-gather.4
  139.0 71.7 reduce-scatter.5
  213.4 55.9 all-gather.6
  271.3 55.9 all-gather.8
  737.0 52.9 all-reduce.6
  793.3 70.6 reduce-scatter.9
  866.8 19.1 reduce-scatter.13
  888.5 54.0 all-gather.10
  946.1 71.2 reduce-scatter.7
  1166.8 72.0 reduce-scatter.11

commit v3 on v2

--- a/solution.py
+++ b/solution.py
@@ -105,6 +105,10 @@
     length = length_ref[pl.program_id(0)]
     scale = 1.0 / math.sqrt(HEAD_DIM)
     hd = HEAD_DIM
+    @pl.when(pl.program_id(1) == 0)
+    def _():
+        inner_ref[...] = jnp.zeros_like(inner_ref)
+
     dk_ref[...] = jnp.zeros_like(dk_ref)
     dv_ref[...] = jnp.zeros_like(dv_ref)
 
@@ -126,19 +130,14 @@
         dquery = mm(draw, keys)
         dk_ref[:seen, :] += mm_tn(draw, rows)
         dqkv_ref[at:seen, :hd] = turn_back(dquery, slice(at, seen))
-        inner_ref[at:seen, :] = jnp.broadcast_to(
-            jnp.sum(dquery * rows.astype(f32), axis=-1, keepdims=True), (QBLOCK, hd)
-        )
+        inner_ref[at:seen, :] += jnp.sum(dquery * rows.astype(f32), axis=-1, keepdims=True)
     dkey, dvalue = dk_ref[...], dv_ref[...]
     dqkv_ref[:, hd : 2 * hd] = turn_back(dkey, slice(None))
     dqkv_ref[:, 2 * hd :] = dvalue.astype(bf16)
-    inner_ref[...] += jnp.broadcast_to(
-        jnp.sum(
-            dkey * qkv_ref[:, hd : 2 * hd].astype(f32) + dvalue * qkv_ref[:, 2 * hd :].astype(f32),
-            axis=-1,
-            keepdims=True,
-        ),
-        inner_ref.shape,
+    inner_ref[...] += jnp.sum(
+        dkey * qkv_ref[:, hd : 2 * hd].astype(f32) + dvalue * qkv_ref[:, 2 * hd :].astype(f32),
+        axis=-1,
+        keepdims=True,
     )
 
 
@@ -156,12 +155,12 @@
             num_scalar_prefetch=1,
             grid=(slots, heads),
             in_specs=[wide, one, one, table, table],
-            out_specs=[wide, one],
+            out_specs=[wide, pl.BlockSpec((SEQ_LEN, 1), lambda s, h, _: (s, 0))],
             scratch_shapes=[pltpu.VMEM((SEQ_LEN, HEAD_DIM), f32)] * 2,
         ),
         out_shape=[
             jax.ShapeDtypeStruct((tokens, width), bf16),
-            jax.ShapeDtypeStruct((tokens, heads * HEAD_DIM), f32),
+            jax.ShapeDtypeStruct((tokens, 1), f32),
         ],
         cost_estimate=pl.CostEstimate(
             flops=8 * HEAD_DIM * pairs, bytes_accessed=8 * tokens * width, transcendentals=pairs
@@ -173,14 +172,15 @@
 def gather_rows(part):
     n = lax.axis_size("row")
     if n != 4:
-        return (lax.all_gather(part, "row", axis=0, tiled=True),)
+        return (lax.all_gather(part, "row", axis=0, tiled=True),), ((), (), ())
     partner = lax.ppermute(part, "row", [(0, 1), (1, 0), (2, 3), (3, 2)])
     middle, outward = [(1, 2), (2, 1)], [(1, 0), (2, 3)]
     near_mid = lax.ppermute(part, "row", middle)
     far_mid = lax.ppermute(partner, "row", middle)
     near_out = lax.ppermute(near_mid, "row", outward)
     far_out = lax.ppermute(far_mid, "row", outward)
-    return part, partner, near_mid, far_mid, near_out, far_out
+    hops = ((partner, near_mid), (far_mid, near_out), (far_out,))
+    return (part, partner, near_mid, far_mid, near_out, far_out), hops
 
 
 def places(z):
@@ -204,7 +204,7 @@
     n = lax.axis_size("row")
     if n != 4:
         total = lax.psum_scatter(grads, "row", scatter_dimension=0, tiled=True)
-        return total.astype(f32), total
+        return total.astype(f32), ((), (), ())
     own, partner, near, far = places(lax.axis_index("row"))
     size = grads.shape[0] // n
     inward, middle = [(0, 1), (3, 2)], [(1, 2), (2, 1)]
@@ -224,11 +224,13 @@
     exchanged = lax.ppermute(
         block(partner, far_sum).astype(bf16), "row", [(0, 1), (1, 0), (2, 3), (3, 2)]
     )
-    return block(own, near_sum, exchanged), near_in
-
-
-def after(value, *others):
-    return lax.optimization_barrier((value,) + others)[0]
+    hops = ((far_in, near_in), (far_sum, near_sum), (exchanged,))
+    return block(own, near_sum, exchanged), hops
+
+
+def after(value, *groups):
+    others = tuple(item for group in groups for item in group)
+    return lax.optimization_barrier((value,) + others)[0] if others else value
 
 
 def expert_kernel(size, steps, count, z_ref, *refs):
@@ -466,7 +468,7 @@
     router_pack = jnp.concatenate([router_weight, score_shared[:, None]], axis=1)
     router_pack = jnp.pad(router_pack, ((0, 0), (0, -router_pack.shape[1] % 128)))
     attn_weights = join_rows(
-        gather_rows(jnp.concatenate([qkv_pack, output_weight.T, router_pack], axis=1))
+        gather_rows(jnp.concatenate([qkv_pack, output_weight.T, router_pack], axis=1))[0]
     )
     qkv_full = attn_weights[:, : 3 * head_width]
     out_full = attn_weights[:, 3 * head_width : 4 * head_width]
@@ -485,20 +487,25 @@
         fill = -(b - a) % 128
         return jnp.concatenate([jnp.pad(part, ((0, 0), (0, fill))) for part in parts], axis=1)
 
-    gathered = [gather_rows(pack(*chunk)) for chunk in chunks]
+    gathered, came = zip(*[gather_rows(pack(*chunk)) for chunk in chunks])
+
+    def hop(arrivals, at, which):
+        return arrivals[at][which] if 0 <= at < len(arrivals) else ()
 
     rows_in = lax.all_gather(block_input, "col", axis=1, tiled=True)
     gains = lax.all_gather(jnp.stack([input_gain, mlp_gain]), "col", axis=1, tiled=True).astype(f32)
     cot_rows = lax.all_gather(grad_output, "col", axis=1, tiled=True)
     rows_f = rows_in.astype(f32)
     scale_a = lax.rsqrt(jnp.mean(rows_f * rows_f, axis=-1, keepdims=True) + norm_eps)
-    normed_a = (rows_f * scale_a * gains[0]).astype(bf16)
+    normed_a = after((rows_f * scale_a * gains[0]).astype(bf16), hop(came, 0, 0))
     qkv, context, lse = attend_forward(mm(normed_a, qkv_full), lengths, cosine, sine)
-    attn_part = mm_nt(context, out_full).astype(bf16)
+    attn_part = after(mm_nt(context, out_full).astype(bf16), (cot_rows,))
     x_share = block_input.astype(f32)
-    stream = x_share + lax.psum_scatter(
-        attn_part, "col", scatter_dimension=1, tiled=True
-    ).astype(f32)
+    attn_sum = lax.psum_scatter(attn_part, "col", scatter_dimension=1, tiled=True)
+    attn_sum = after(
+        attn_sum, hop(came, 0, 1), hop(came, 0, 2), hop(came, 1, 0), hop(came, 1, 1)
+    )
+    stream = x_share + attn_sum.astype(f32)
     gain_b = mlp_gain.astype(f32)
     scaled = lax.all_gather((stream * gain_b).astype(bf16), "col", axis=1, tiled=True)
     stream_f = scaled.astype(f32) / gains[1]
@@ -519,20 +526,32 @@
         members[local] = jnp.any(routes == expert, axis=1)
         column = lax.dynamic_index_in_dim(router_probs, expert, 1, False)
         shares[local] = jnp.where(members[local], column, 0.0)
-    dpairs, hiddens, wholes, unit_grads, arrived = [], [], [], [], []
+    dpairs, hiddens, wholes, unit_grads, went = [], [], [], [], []
     for at, ((kind, a, b), pieces) in enumerate(zip(chunks, gathered)):
         coef = jnp.concatenate([scale_b, shares[kind][:, None]], axis=1)
-        if at >= 2:
-            coef = after(coef, arrived[at - 2])
+        if at == 0:
+            coef = after(coef, hop(came, 1, 2), hop(came, 2, 0))
+        elif at == 1:
+            coef = after(coef, hop(came, 2, 1))
+        else:
+            coef = after(
+                coef,
+                hop(came, at + 1, 0),
+                hop(went, at - 2, 0),
+                hop(went, at - 3, 1),
+                hop(went, at - 4, 2),
+            )
         dpair, hidden, sums, grads, whole = expert_chunk(pieces, scaled, cot_rows, coef)
         dots[kind] = dots.get(kind, 0.0) + sums[:, 0]
         inner = inner + sums[:, 1]
         dpairs.append(dpair)
         hiddens.append(hidden)
         wholes.append(whole)
-        reduced, first = reduce_rows(grads)
+        reduced, arrivals = reduce_rows(grads)
         unit_grads.append(reduced)
-        arrived.append(first)
+        went.append(arrivals)
+    last = len(chunks) - 1
+    dpairs[-1] = after(dpairs[-1], hop(went, last - 1, 0), hop(went, last - 2, 1))
     dscaled_part = joint_back(dpairs, wholes, 0)
     moe_share = lax.psum_scatter(
         joint_back(hiddens, wholes, 2), "col", scatter_dimension=1, tiled=True
@@ -556,24 +575,29 @@
     grad_router_both = lax.psum_scatter(grad_router_part, "row", scatter_dimension=1, tiled=True)
     router_rows = lax.dynamic_slice_in_dim(router_full, col_id * share, share, 0)
     back = mm_nt(jnp.concatenate(parts, axis=1), jnp.concatenate([router_rows] * 3, axis=1))
-    dscaled = back + lax.psum_scatter(
-        dscaled_part, "col", scatter_dimension=1, tiled=True
-    ).astype(f32)
+    dscaled_sum = after(
+        lax.psum_scatter(dscaled_part, "col", scatter_dimension=1, tiled=True),
+        hop(went, last - 3, 2),
+        hop(went, last - 2, 2),
+        hop(went, last - 1, 1),
+        hop(went, last, 0),
+    )
+    dscaled = back + dscaled_sum.astype(f32)
     cot_share = grad_output.astype(f32)
     dstream = cot_share + gain_b * dscaled - stream * (scale_b * scale_b * inner[:, None] / width)
     gain_b_grad = jnp.sum(dscaled * stream, axis=0)
 
     dattn = lax.all_gather(dstream.astype(bf16), "col", axis=1, tiled=True)
+    dattn = after(dattn, hop(went, last - 1, 2), hop(went, last, 1))
     out_grad, _ = reduce_rows(mm_tn(dattn, context).astype(bf16))
     dcontext = mm(dattn, out_full).astype(bf16)
     dqkv, inner_a = attend_backward(qkv, dcontext, lse, lengths, cosine, sine)
-    inner_a = lax.psum(
-        jnp.sum(inner_a.reshape(tokens, heads, HEAD_DIM)[:, :, 0], axis=1), "col"
-    )[:, None]
+    inner_a = lax.psum(inner_a[:, 0], "col")[:, None]
     qkv_grad, _ = reduce_rows(mm_tn(normed_a, dqkv).astype(bf16))
-    dnormed_a = lax.psum_scatter(
+    dnormed_sum = lax.psum_scatter(
         mm_nt(dqkv, qkv_full).astype(bf16), "col", scatter_dimension=1, tiled=True
-    ).astype(f32)
+    )
+    dnormed_a = after(dnormed_sum, (inner_a,), hop(went, last, 2)).astype(f32)
     gain_a_share = input_gain.astype(f32)
     dinput = dstream + scale_a * gain_a_share * dnormed_a
     dinput = dinput - x_share * (scale_a * scale_a * inner_a / width)

time: 1440 us -> 1210 us (0.84)
  waiting for transfers between devices: 687 us -> 443 us
    reduce_scatter x1, waiting for transfers between devices: 71.9 us -> 0.01 us  [per_device(): lax.psum_scatter(attn_part, 'col', scatter_dimension=1, tiled=True)]
    reduce_scatter x1, waiting for transfers between devices: 60.9 us -> 0.02 us  [per_device(): lax.psum_scatter(dscaled_part, 'col', scatter_dimension=1, tiled=True)]
    ppermute x7, waiting for transfers between devices: 97.5 us -> 38.2 us  [reduce_rows(): lax.ppermute(block(partner, far_sum).astype(bf16), 'row', [(0, 1), (1, 0)...]
    ppermute x7, waiting for transfers between devices: 98.5 us -> 61.8 us  [reduce_rows(): far_in = lax.ppermute(block(far), 'row', inward)]
    ppermute x6, waiting for transfers between devices: 39.1 us -> 75.7 us  [gather_rows(): partner = lax.ppermute(part, 'row', [(0, 1), (1, 0), (2, 3), (3, 2)])]
    ppermute x6, waiting for transfers between devices: 138 us -> 108 us  [gather_rows(): far_out = lax.ppermute(far_mid, 'row', outward)]
    all_gather x1, waiting for transfers between devices: 33.2 us -> 11.4 us  [per_device(): lax.all_gather((stream * gain_b).astype(bf16), 'col', axis=1, tiled=True)]
    all_gather x1, waiting for transfers between devices: 0.01 us -> 21.7 us  [per_device(): dattn = lax.all_gather(dstream.astype(bf16), 'col', axis=1, tiled=True)]
  transfers between devices with their start and end apart: 75 -> 75, of which waited for: 29 -> 21; matrix products, arithmetic and copies ran while one was open for 16% -> 21% of each run, Pallas kernels for 17% -> 25%
where the time goes in v3:
time: 1210 us; the launch traced here: 1200 us
  waiting for transfers between devices  443 us (37%)
  Pallas kernels  298 us (25%)
  starting transfers between devices  138 us (11%)
  other arithmetic  130 us (11%)
  local copies, waits for them, and re-layouts  77.1 us (6%)
  matrix products  62 us (5%)
  blocking collectives  33.1 us (3%)
  between operations  16.2 us (1%)
    pallas_call x5, Pallas kernels, expert_chunk(): pl.pallas_call(functools.partial(expert_kernel, size, steps, count), grid...  184 us
    ppermute x6, waiting for transfers between devices, gather_rows(): far_out = lax.ppermute(far_mid, 'row', outward)  108 us
    ppermute x6, waiting for transfers between devices, gather_rows(): partner = lax.ppermute(part, 'row', [(0, 1), (1, 0), (2, 3), (3, 2)])  75.7 us
    pallas_call x2, Pallas kernels, joint_back(): pl.pallas_call(functools.partial(joint_kernel, len(lefts)), grid=(tokens...  73.4 us
    ppermute x6, waiting for transfers between devices, gather_rows(): near_out = lax.ppermute(near_mid, 'row', outward)  70.5 us
    ppermute x7, waiting for transfers between devices, reduce_rows(): far_in = lax.ppermute(block(far), 'row', inward)  61.8 us
    ppermute x7, waiting for transfers between devices, reduce_rows(): near_in = lax.ppermute(block(near), 'row', inward)  53.9 us
    ppermute x7, waiting for transfers between devices, reduce_rows(): lax.ppermute(block(partner, far_sum).astype(bf16), 'row', [(0, 1), (1, 0)...  38.2 us
  transfers between devices with their start and end apart: 75, of which 21 were waited for; matrix products, arithmetic and copies ran while one was open for 21% of the time, Pallas kernels for 25%

profile of v3, /device:TPU:0, one launch (start us, length us, event | category | flops | bytes accessed | tf_op | source)
XLA Modules:
  0.0 1198.0 jit_solution(6674822240847767322)
XLA Ops:
  24.8 15.9 %collective-permute-done.2 = bf16[512,1152]{0,1:T(8,128)(2,1)} collective-permute-done((bf16[512,1152]{0,1:T(8,128)(2,1)}, bf16[512,1152]{0,1:T(8,128)(2,1)}, u32[]{:S(2)}, u32[]{:S(2)}) %collective-permute-start.2) | collective-permute-done | bytes 1179680 | tf_op jit(solution)/shard_map/ppermute | solution.py:176
  63.4 18.7 %collective-permute-done.4 = bf16[512,1152]{0,1:T(8,128)(2,1)} collective-permute-done((bf16[512,1152]{0,1:T(8,128)(2,1)}, bf16[512,1152]{0,1:T(8,128)(2,1)}, u32[]{:S(2)}, u32[]{:S(2)}) %collective-permute-start.4) | collective-permute-done | bytes 1179680 | tf_op jit(solution)/shard_map/ppermute | solution.py:180
  85.7 27.6 %collective-permute-done.6 = bf16[512,1152]{0,1:T(8,128)(2,1)} collective-permute-done((bf16[512,1152]{0,1:T(8,128)(2,1)S(1)}, bf16[512,1152]{0,1:T(8,128)(2,1)}, u32[]{:S(2)}, u32[]{:S(2)}) %collective-permute-start.6) | collective-permute-done | bytes 1179680 | tf_op jit(solution)/shard_map/ppermute | solution.py:181
  131.5 11.6 fusion.4.raw_ref
  143.1 12.9 %attend_forward.1 = (bf16[2048,768]{1,0:T(8,128)(2,1)}, bf16[2048,256]{1,0:T(8,128)(2,1)}, f32[2048,256]{1,0:T(8,128)}) custom-call(s32[2]{0:T(128)} %dynamic_slice.108.length_ref, f32[2048,768]{1,0:T(8,128)} %fusion.4.raw_ref, f32[1024,128]{1,0:T(8,128)} %get-tuple-element.242.cos_ref, f32[1024,128]{1,0:T(8,128)} %get-tuple-element.243.sin_ref), custom_call_target="tpu_custom_call" | custom-call | flops 1610612736 | bytes 12582912 | tf_op jit(solution)/shard_map/attend_forward/pallas_call | solution.py:82
  171.3 31.0 %collective-permute-done.10.refs_1_ = bf16[512,1536]{1,0:T(8,128)(2,1)S(1)} collective-permute-done((bf16[512,1536]{1,0:T(8,128)(2,1)S(1)}, bf16[512,1536]{1,0:T(8,128)(2,1)S(1)}, u32[]{:S(2)}, u32[]{:S(2)}) %collective-permute-start.10) | collective-permute-done | bytes 1572896 | tf_op jit(solution)/shard_map/ppermute | solution.py:176
  206.7 51.8 %collective-permute-done.8.refs_4_ = bf16[512,768]{1,0:T(8,128)(2,1)S(1)} collective-permute-done((bf16[512,768]{1,0:T(8,128)(2,1)}, bf16[512,768]{1,0:T(8,128)(2,1)S(1)}, u32[]{:S(2)}, u32[]{:S(2)}) %collective-permute-start.8) | collective-permute-done | bytes 786464 | tf_op jit(solution)/shard_map/ppermute | solution.py:180
  258.5 11.2 collective-permute-done.9.refs_5_
  286.6 28.8 %collective-permute-done.15.refs_1_ = bf16[512,1536]{1,0:T(8,128)(2,1)} collective-permute-done((bf16[512,1536]{1,0:T(8,128)(2,1)}, bf16[512,1536]{1,0:T(8,128)(2,1)}, u32[]{:S(2)}, u32[]{:S(2)}) %collective-permute-start.15) | collective-permute-done | bytes 1572896 | tf_op jit(solution)/shard_map/ppermute | solution.py:176
  318.5 11.4 all-gather.9.cloned.1.call-done.refs_6_.refs_8_
  340.4 69.4 %collective-permute-done.14.refs_5_ = bf16[512,1536]{1,0:T(8,128)(2,1)S(1)} collective-permute-done((bf16[512,1536]{1,0:T(8,128)(2,1)}, bf16[512,1536]{1,0:T(8,128)(2,1)S(1)}, u32[]{:S(2)}, u32[]{:S(2)}) %collective-permute-start.14) | collective-permute-done | bytes 1572896 | tf_op jit(solution)/shard_map/ppermute | solution.py:181
  411.3 28.3 %expert_chunk.5 = (bf16[2048,512]{1,0:T(8,128)(2,1)}, bf16[2048,256]{1,0:T(8,128)(2,1)}, f32[2048,2]{1,0:T(8,128)}, bf16[2048,768]{1,0:T(8,128)(2,1)}, bf16[2048,768]{1,0:T(8,128)(2,1)}) custom-call(s32[1]{0:T(128)} %bitcast.16.z_ref, bf16[512,768]{1,0:T(8,128)(2,1)} %fusion.18.refs_0_, bf16[512,768]{1,0:T(8,128)(2,1)} %collective-permute-done.refs_1_, ...), custom_call_target="tpu_custom_call" | custom-call | flops 12884901888 | bytes 46137344 | tf_op jit(solution)/shard_map/expert_chunk/pallas_call | solution.py:334
  450.6 10.2 collective-permute-done.23
  465.0 12.6 %collective-permute-done.22 = bf16[512,768]{1,0:T(8,128)(2,1)S(1)} collective-permute-done((bf16[512,768]{1,0:T(8,128)(2,1)S(1)}, bf16[512,768]{1,0:T(8,128)(2,1)S(1)}, u32[]{:S(2)}, u32[]{:S(2)}) %collective-permute-start.22) | collective-permute-done | bytes 786464 | tf_op jit(solution)/shard_map/ppermute | solution.py:220
  479.2 39.5 %expert_chunk.6 = (bf16[2048,1024]{1,0:T(8,128)(2,1)}, bf16[2048,512]{1,0:T(8,128)(2,1)}, f32[2048,2]{1,0:T(8,128)}, bf16[2048,1536]{1,0:T(8,128)(2,1)}, bf16[2048,1536]{1,0:T(8,128)(2,1)}) custom-call(s32[1]{0:T(128)} %bitcast.16.z_ref, bf16[512,1536]{1,0:T(8,128)(2,1)} %copy-done.21, bf16[512,1536]{1,0:T(8,128)(2,1)} %copy-done.52, ...), custom_call_target="tpu_custom_call" | custom-call | flops 25769803776 | bytes 58720256 | tf_op jit(solution)/shard_map/expert_chunk/pallas_call | solution.py:334
  540.0 39.7 %expert_chunk.7 = (bf16[2048,1024]{1,0:T(8,128)(2,1)}, bf16[2048,512]{1,0:T(8,128)(2,1)}, f32[2048,2]{1,0:T(8,128)}, bf16[2048,1536]{1,0:T(8,128)(2,1)}, bf16[2048,1536]{1,0:T(8,128)(2,1)}) custom-call(s32[1]{0:T(128)} %bitcast.16.z_ref, bf16[512,1536]{1,0:T(8,128)(2,1)} %pad_maximum_fusion.1.refs_0_, bf16[512,1536]{1,0:T(8,128)(2,1)} %collective-permute-done.15.refs_1_, ...), custom_call_target="tpu_custom_call" | custom-call | flops 25769803776 | bytes 58720256 | tf_op jit(solution)/shard_map/expert_chunk/pallas_call | solution.py:334
  588.1 14.4 %collective-permute-done.29 = bf16[512,1536]{1,0:T(8,128)(2,1)} collective-permute-done((bf16[512,1536]{1,0:T(8,128)(2,1)S(1)}, bf16[512,1536]{1,0:T(8,128)(2,1)}, u32[]{:S(2)}, u32[]{:S(2)}) %collective-permute-start.29) | collective-permute-done | bytes 1572896 | tf_op jit(solution)/shard_map/ppermute | solution.py:220
  619.3 39.5 %expert_chunk.8 = (bf16[2048,1024]{1,0:T(8,128)(2,1)}, bf16[2048,512]{1,0:T(8,128)(2,1)}, f32[2048,2]{1,0:T(8,128)}, bf16[2048,1536]{1,0:T(8,128)(2,1)}, bf16[2048,1536]{1,0:T(8,128)(2,1)}) custom-call(s32[1]{0:T(128)} %bitcast.16.z_ref, bf16[512,1536]{1,0:T(8,128)(2,1)} %pad_maximum_fusion.2.refs_0_, bf16[512,1536]{1,0:T(8,128)(2,1)} %collective-permute-done.20.refs_1_, ...), custom_call_target="tpu_custom_call" | custom-call | flops 25769803776 | bytes 58720256 | tf_op jit(solution)/shard_map/expert_chunk/pallas_call | solution.py:334
  676.5 26.0 %collective-permute-done.40 = bf16[512,768]{1,0:T(8,128)(2,1)S(1)} collective-permute-done((bf16[512,768]{1,0:T(8,128)(2,1)S(1)}, bf16[512,768]{1,0:T(8,128)(2,1)S(1)}, u32[]{:S(2)}, u32[]{:S(2)}) %collective-permute-start.40) | collective-permute-done | bytes 786464 | tf_op jit(solution)/shard_map/ppermute | solution.py:224
  712.6 36.6 %expert_chunk.9 = (bf16[2048,768]{1,0:T(8,128)(2,1)}, bf16[2048,384]{1,0:T(8,128)(2,1)}, f32[2048,2]{1,0:T(8,128)}, bf16[2048,1152]{1,0:T(8,128)(2,1)}, bf16[2048,1152]{1,0:T(8,128)(2,1)}) custom-call(s32[1]{0:T(128)} %bitcast.16.z_ref, bf16[512,1152]{1,0:T(8,128)(2,1)} %pad_maximum_fusion.7.refs_0_, bf16[512,1152]{1,0:T(8,128)(2,1)} %collective-permute-done.27.refs_1_, ...), custom_call_target="tpu_custom_call" | custom-call | flops 19327352832 | bytes 52428800 | tf_op jit(solution)/shard_map/expert_chunk/pallas_call | solution.py:334
  756.7 46.8 %joint_back.3 = bf16[2048,2048]{1,0:T(8,128)(2,1)} custom-call(bf16[2048,512]{1,0:T(8,128)(2,1)} %get-tuple-element.85.refs_0_, bf16[2048,1024]{1,0:T(8,128)(2,1)} %get-tuple-element.86.refs_1_, bf16[2048,1024]{1,0:T(8,128)(2,1)} %get-tuple-element.87.refs_2_, bf16[2048,1024]{1,0:T(8,128)(2,1)} %get-tuple-element.88.refs_3_, ...), custom_call_target="tpu_custom_call" | custom-call | flops 36507222016 | bytes 44040192 | tf_op jit(solution)/shard_map/joint_back/pallas_call | solution.py:393
  829.8 34.6 %collective-permute-done.50 = bf16[512,1152]{1,0:T(8,128)(2,1)} collective-permute-done((bf16[512,1152]{1,0:T(8,128)(2,1)}, bf16[512,1152]{1,0:T(8,128)(2,1)}, u32[]{:S(2)}, u32[]{:S(2)}) %collective-permute-start.50) | collective-permute-done | bytes 1179680 | tf_op jit(solution)/shard_map/ppermute | solution.py:221
  873.6 20.3 %collective-permute-done.49 = bf16[512,1152]{1,0:T(8,128)(2,1)} collective-permute-done((bf16[512,1152]{1,0:T(8,128)(2,1)}, bf16[512,1152]{1,0:T(8,128)(2,1)}, u32[]{:S(2)}, u32[]{:S(2)}) %collective-permute-start.49) | collective-permute-done | bytes 1179680 | tf_op jit(solution)/shard_map/ppermute | solution.py:220
  923.0 10.4 collective-permute-done.51
  933.4 21.7 %all-gather.11.cloned.1.call-done = bf16[2048,2048]{1,0:T(8,128)(2,1)} async-done(((bf16[2048,256]{1,0:T(8,128)(2,1)}), bf16[2048,2048]{1,0:T(8,128)(2,1)}) %all-gather.11.cloned.1.call-update) | async-done | bytes 8388624 | tf_op jit(solution)/shard_map/all_gather | solution.py:590
  962.1 28.2 %attend_backward.1 = (bf16[2048,768]{1,0:T(8,128)(2,1)}, f32[2048,1]{1,0:T(8,128)}) custom-call(s32[2]{0:T(128)} %dynamic_slice.108.length_ref, bf16[2048,768]{1,0:T(8,128)(2,1)} %get-tuple-element.94.qkv_ref, bf16[2048,256]{1,0:T(8,128)(2,1)} %convolution_convert_fusion.4.dcontext_ref, f32[2048,256]{1,0:T(8,128)} %get-tuple-element.96.lse_ref, ...), custom_call_target="tpu_custom_call" | custom-call | flops 4294967296 | bytes 12582912 | tf_op jit(solution)/shard_map/attend_backward/pallas_call | solution.py:152
  990.2 11.3 convolution_convert_fusion
  1001.8 26.6 %joint_back.2 = bf16[2048,2048]{1,0:T(8,128)(2,1)} custom-call(bf16[2048,256]{1,0:T(8,128)(2,1)} %get-tuple-element.63.refs_0_, bf16[2048,512]{1,0:T(8,128)(2,1)} %get-tuple-element.65.refs_1_, bf16[2048,512]{1,0:T(8,128)(2,1)} %get-tuple-element.68.refs_2_, bf16[2048,512]{1,0:T(8,128)(2,1)} %get-tuple-element.71.refs_3_, ...), custom_call_target="tpu_custom_call" | custom-call | flops 18253611008 | bytes 26214400 | tf_op jit(solution)/shard_map/joint_back/pallas_call | solution.py:393
  1074.1 9.5 convolution_convert_fusion.2
  1096.6 14.5 %collective-permute-done.62 = bf16[512,256]{1,0:T(8,128)(2,1)S(1)} collective-permute-done((bf16[512,256]{1,0:T(8,128)(2,1)S(1)}, bf16[512,256]{1,0:T(8,128)(2,1)S(1)}, u32[]{:S(2)}, u32[]{:S(2)}) %collective-permute-start.62) | collective-permute-done | bytes 262176 | tf_op jit(solution)/shard_map/ppermute | solution.py:220
  1149.4 12.1 %psum.29 = f32[2048]{0:T(1024)S(1)} all-reduce(f32[2048]{0:T(1024)S(1)} %reduce.3), channel_id=1, replica_groups=mesh['row'=4,'col'=8] {'col'}, use_global_device_ids=true, to_apply=%region_12.13 | all-reduce | flops 2048 | bytes 16384 | tf_op jit(solution)/shard_map/psum | solution.py:595
  1179.2 11.5 all-reduce.4
  (437 shorter events, 397.1 us)
Async XLA Ops:
  7.2 109.3 %all-gather.5.cloned.1.call-start = ((), (), s32[]{:S(2)}) async-start(), calls=%async_computation.5 | async-start | bytes 9437184 | tf_op jit(solution)/shard_map/all_gather | solution.py:495
  8.0 155.3 %all-gather.7.cloned.1.call-start = ((), (), s32[]{:S(2)}) async-start(), calls=%async_computation.6 | async-start | bytes 9437184 | tf_op jit(solution)/shard_map/all_gather | solution.py:497
  8.7 262.9 %reduce-scatter.6.cloned.1.call-start = ((), (), s32[]{:S(2)}) async-start(), calls=%async_computation.7 | async-start | bytes 9437184 | tf_op jit(solution)/shard_map/reduce_scatter | solution.py:504
  16.8 114.7 %collective-permute-start.1 = (bf16[512,768]{1,0:T(8,128)(2,1)}, bf16[512,768]{1,0:T(8,128)(2,1)}, u32[]{:S(2)}, u32[]{:S(2)}) collective-permute-start(bf16[512,768]{1,0:T(8,128)(2,1)} %fusion.18.refs_0_), channel_id=1, source_target_pairs={{8,16},{16,8},{9,17},{17,9},{10,18},{18,10},{11,19},{19,11},{12,20... | collective-permute-start | bytes 2359304 | tf_op jit(solution)/shard_map/ppermute | solution.py:178
  18.3 113.2 %collective-permute-start = (bf16[512,768]{1,0:T(8,128)(2,1)}, bf16[512,768]{1,0:T(8,128)(2,1)}, u32[]{:S(2)}, u32[]{:S(2)}) collective-permute-start(bf16[512,768]{1,0:T(8,128)(2,1)} %fusion.18.refs_0_), channel_id=1, source_target_pairs={{0,8},{8,0},{16,24},{24,16},{1,9},{9,1},{17,25},{25,17},{2,10},{10... | collective-permute-start | bytes 2359304 | tf_op jit(solution)/shard_map/ppermute | solution.py:176
  163.3 166.6 %all-gather.9.cloned.1.call-start = ((), (), s32[]{:S(2)}) async-start(), calls=%async_computation.8 | async-start | bytes 9437184 | tf_op jit(solution)/shard_map/all_gather | solution.py:510
  170.0 99.7 %collective-permute-start.13 = (bf16[512,1536]{1,0:T(8,128)(2,1)S(1)}, bf16[512,1536]{1,0:T(8,128)(2,1)S(1)}, u32[]{:S(2)}, u32[]{:S(2)}) collective-permute-start(bf16[512,1536]{1,0:T(8,128)(2,1)S(1)} %collective-permute-done.11.refs_2_), channel_id=1, source_target_pairs={{8,0},{16,24},{9,1},{17,25},{10,2},{18,26},{11,3},{19,27},{12,4},{... | collective-permute-start | bytes 4718600 | tf_op jit(solution)/shard_map/ppermute | solution.py:180
  202.3 69.4 %collective-permute-start.12 = (bf16[512,1536]{1,0:T(8,128)(2,1)S(1)}, bf16[512,1536]{1,0:T(8,128)(2,1)}, u32[]{:S(2)}, u32[]{:S(2)}) collective-permute-start(bf16[512,1536]{1,0:T(8,128)(2,1)S(1)} %collective-permute-done.10.refs_1_), channel_id=1, source_target_pairs={{8,16},{16,8},{9,17},{17,9},{10,18},{18,10},{11,19},{19,11},{12,20... | collective-permute-start | bytes 4718600 | tf_op jit(solution)/shard_map/ppermute | solution.py:179
  274.2 595.8 %all-reduce.7.cloned.1.call-start = ((), (), s32[]{:S(2)}) async-start(), calls=%async_computation.10 | async-start | bytes 262144 | tf_op jit(solution)/shard_map/psum | solution.py:565
  281.0 182.8 %collective-permute-start.21 = (bf16[512,1536]{1,0:T(8,128)(2,1)}, bf16[512,1536]{1,0:T(8,128)(2,1)}, u32[]{:S(2)}, u32[]{:S(2)}) collective-permute-start(bf16[512,1536]{1,0:T(8,128)(2,1)} %pad_maximum_fusion.2.refs_0_), channel_id=1, source_target_pairs={{8,16},{16,8},{9,17},{17,9},{10,18},{18,10},{11,19},{19,11},{12,20... | collective-permute-start | bytes 4718600 | tf_op jit(solution)/shard_map/ppermute | solution.py:178
  282.8 167.7 %collective-permute-start.20 = (bf16[512,1536]{1,0:T(8,128)(2,1)}, bf16[512,1536]{1,0:T(8,128)(2,1)}, u32[]{:S(2)}, u32[]{:S(2)}) collective-permute-start(bf16[512,1536]{1,0:T(8,128)(2,1)} %pad_maximum_fusion.2.refs_0_), channel_id=1, source_target_pairs={{0,8},{8,0},{16,24},{24,16},{1,9},{9,1},{17,25},{25,17},{2,10},{10... | collective-permute-start | bytes 4718600 | tf_op jit(solution)/shard_map/ppermute | solution.py:176
  285.3 157.8 %collective-permute-start.18 = (bf16[512,1536]{1,0:T(8,128)(2,1)}, bf16[512,1536]{1,0:T(8,128)(2,1)}, u32[]{:S(2)}, u32[]{:S(2)}) collective-permute-start(bf16[512,1536]{1,0:T(8,128)(2,1)} %collective-permute-done.16.refs_2_), channel_id=1, source_target_pairs={{8,0},{16,24},{9,1},{17,25},{10,2},{18,26},{11,3},{19,27},{12,4},{... | collective-permute-start | bytes 4718600 | tf_op jit(solution)/shard_map/ppermute | solution.py:180
  315.4 131.4 %collective-permute-start.17 = (bf16[512,1536]{1,0:T(8,128)(2,1)}, bf16[512,1536]{1,0:T(8,128)(2,1)}, u32[]{:S(2)}, u32[]{:S(2)}) collective-permute-start(bf16[512,1536]{1,0:T(8,128)(2,1)} %collective-permute-done.15.refs_1_), channel_id=1, source_target_pairs={{8,16},{16,8},{9,17},{17,9},{10,18},{18,10},{11,19},{19,11},{12,20... | collective-permute-start | bytes 4718600 | tf_op jit(solution)/shard_map/ppermute | solution.py:179
  317.2 92.6 %collective-permute-start.14 = (bf16[512,1536]{1,0:T(8,128)(2,1)}, bf16[512,1536]{1,0:T(8,128)(2,1)S(1)}, u32[]{:S(2)}, u32[]{:S(2)}) collective-permute-start(bf16[512,1536]{1,0:T(8,128)(2,1)} %collective-permute-done.12.refs_3_), channel_id=1, source_target_pairs={{8,0},{16,24},{9,1},{17,25},{10,2},{18,26},{11,3},{19,27},{12,4},{... | collective-permute-start | bytes 4718600 | tf_op jit(solution)/shard_map/ppermute | solution.py:181
  446.8 77.8 %collective-permute-start.28 = (bf16[512,1152]{1,0:T(8,128)(2,1)}, bf16[512,1152]{1,0:T(8,128)(2,1)}, u32[]{:S(2)}, u32[]{:S(2)}) collective-permute-start(bf16[512,1152]{1,0:T(8,128)(2,1)} %pad_maximum_fusion.7.refs_0_), channel_id=1, source_target_pairs={{8,16},{16,8},{9,17},{17,9},{10,18},{18,10},{11,19},{19,11},{12,20... | collective-permute-start | bytes 3538952 | tf_op jit(solution)/shard_map/ppermute | solution.py:178
  450.5 76.7 %collective-permute-start.27 = (bf16[512,1152]{1,0:T(8,128)(2,1)}, bf16[512,1152]{1,0:T(8,128)(2,1)}, u32[]{:S(2)}, u32[]{:S(2)}) collective-permute-start(bf16[512,1152]{1,0:T(8,128)(2,1)} %pad_maximum_fusion.7.refs_0_), channel_id=1, source_target_pairs={{0,8},{8,0},{16,24},{24,16},{1,9},{9,1},{17,25},{25,17},{2,10},{10... | collective-permute-start | bytes 3538952 | tf_op jit(solution)/shard_map/ppermute | solution.py:176
  463.7 72.3 %collective-permute-start.19 = (bf16[512,1536]{1,0:T(8,128)(2,1)}, bf16[512,1536]{1,0:T(8,128)(2,1)}, u32[]{:S(2)}, u32[]{:S(2)}) collective-permute-start(bf16[512,1536]{1,0:T(8,128)(2,1)} %collective-permute-done.17.refs_3_), channel_id=1, source_target_pairs={{8,0},{16,24},{9,1},{17,25},{10,2},{18,26},{11,3},{19,27},{12,4},{... | collective-permute-start | bytes 4718600 | tf_op jit(solution)/shard_map/ppermute | solution.py:181
  524.6 91.0 %collective-permute-start.25 = (bf16[512,1536]{1,0:T(8,128)(2,1)}, bf16[512,1536]{1,0:T(8,128)(2,1)}, u32[]{:S(2)}, u32[]{:S(2)}) collective-permute-start(bf16[512,1536]{1,0:T(8,128)(2,1)} %collective-permute-done.21.refs_2_), channel_id=1, source_target_pairs={{8,0},{16,24},{9,1},{17,25},{10,2},{18,26},{11,3},{19,27},{12,4},{... | collective-permute-start | bytes 4718600 | tf_op jit(solution)/shard_map/ppermute | solution.py:180
  525.9 91.5 %collective-permute-start.26 = (bf16[512,1536]{1,0:T(8,128)(2,1)}, bf16[512,1536]{1,0:T(8,128)(2,1)}, u32[]{:S(2)}, u32[]{:S(2)}) collective-permute-start(bf16[512,1536]{1,0:T(8,128)(2,1)} %collective-permute-done.24.refs_3_), channel_id=1, source_target_pairs={{8,0},{16,24},{9,1},{17,25},{10,2},{18,26},{11,3},{19,27},{12,4},{... | collective-permute-start | bytes 4718600 | tf_op jit(solution)/shard_map/ppermute | solution.py:181
  536.0 66.5 %collective-permute-start.29 = (bf16[512,1536]{1,0:T(8,128)(2,1)S(1)}, bf16[512,1536]{1,0:T(8,128)(2,1)}, u32[]{:S(2)}, u32[]{:S(2)}) collective-permute-start(bf16[512,1536]{1,0:T(8,128)(2,1)S(1)} %get-tuple-element.193), channel_id=1, source_target_pairs={{0,8},{24,16},{1,9},{25,17},{2,10},{26,18},{3,11},{27,19},{4,12},{... | collective-permute-start | bytes 4718600 | tf_op jit(solution)/shard_map/ppermute | solution.py:220
  583.5 78.9 %collective-permute-start.33 = (bf16[512,1152]{1,0:T(8,128)(2,1)}, bf16[512,1152]{1,0:T(8,128)(2,1)}, u32[]{:S(2)}, u32[]{:S(2)}) collective-permute-start(bf16[512,1152]{1,0:T(8,128)(2,1)} %collective-permute-done.27.refs_1_), channel_id=1, source_target_pairs={{8,16},{16,8},{9,17},{17,9},{10,18},{18,10},{11,19},{19,11},{12,20... | collective-permute-start | bytes 3538952 | tf_op jit(solution)/shard_map/ppermute | solution.py:179
  585.2 78.5 %collective-permute-start.37 = (bf16[512,1536]{1,0:T(8,128)(2,1)}, bf16[512,1536]{1,0:T(8,128)(2,1)}, u32[]{:S(2)}, u32[]{:S(2)}) collective-permute-start(bf16[512,1536]{1,0:T(8,128)(2,1)} %get-tuple-element.190), channel_id=1, source_target_pairs={{0,8},{24,16},{1,9},{25,17},{2,10},{26,18},{3,11},{27,19},{4,12},{... | collective-permute-start | bytes 4718600 | tf_op jit(solution)/shard_map/ppermute | solution.py:221
  615.6 89.5 %collective-permute-start.39 = (bf16[512,1536]{1,0:T(8,128)(2,1)}, bf16[512,1536]{1,0:T(8,128)(2,1)}, u32[]{:S(2)}, u32[]{:S(2)}) collective-permute-start(bf16[512,1536]{1,0:T(8,128)(2,1)} %add_convert_fusion.7), channel_id=1, source_target_pairs={{8,16},{16,8},{9,17},{17,9},{10,18},{18,10},{11,19},{19,11},{12,20... | collective-permute-start | bytes 4718600 | tf_op jit(solution)/shard_map/ppermute | solution.py:223
  617.5 90.1 %collective-permute-start.38 = (bf16[512,1536]{1,0:T(8,128)(2,1)}, bf16[512,1536]{1,0:T(8,128)(2,1)}, u32[]{:S(2)}, u32[]{:S(2)}) collective-permute-start(bf16[512,1536]{1,0:T(8,128)(2,1)} %add_convert_fusion.8), channel_id=1, source_target_pairs={{8,16},{16,8},{9,17},{17,9},{10,18},{18,10},{11,19},{19,11},{12,20... | collective-permute-start | bytes 4718600 | tf_op jit(solution)/shard_map/ppermute | solution.py:222
  756.6 137.4 %reduce-scatter.10.cloned.1.call-start = ((), (), s32[]{:S(2)}) async-start(), calls=%async_computation.11 | async-start | bytes 9437184 | tf_op jit(solution)/shard_map/reduce_scatter | solution.py:579
  803.5 151.6 %all-gather.11.cloned.1.call-start = ((), (), s32[]{:S(2)}) async-start(), calls=%async_computation.12 | async-start | bytes 9437184 | tf_op jit(solution)/shard_map/all_gather | solution.py:590
  808.2 85.7 %collective-permute-start.45 = (bf16[512,1536]{1,0:T(8,128)(2,1)}, bf16[512,1536]{1,0:T(8,128)(2,1)}, u32[]{:S(2)}, u32[]{:S(2)}) collective-permute-start(bf16[512,1536]{1,0:T(8,128)(2,1)} %add_convert_fusion.4), channel_id=1, source_target_pairs={{0,8},{8,0},{16,24},{24,16},{1,9},{9,1},{17,25},{25,17},{2,10},{10... | collective-permute-start | bytes 4718600 | tf_op jit(solution)/shard_map/ppermute | solution.py:224
  817.9 76.1 %collective-permute-start.48 = (bf16[512,1536]{1,0:T(8,128)(2,1)}, bf16[512,1536]{1,0:T(8,128)(2,1)}, u32[]{:S(2)}, u32[]{:S(2)}) collective-permute-start(bf16[512,1536]{1,0:T(8,128)(2,1)} %add_convert_fusion.1), channel_id=1, source_target_pairs={{8,16},{16,8},{9,17},{17,9},{10,18},{18,10},{11,19},{19,11},{12,20... | collective-permute-start | bytes 4718600 | tf_op jit(solution)/shard_map/ppermute | solution.py:223
  823.1 70.8 %collective-permute-start.47 = (bf16[512,1536]{1,0:T(8,128)(2,1)}, bf16[512,1536]{1,0:T(8,128)(2,1)}, u32[]{:S(2)}, u32[]{:S(2)}) collective-permute-start(bf16[512,1536]{1,0:T(8,128)(2,1)} %add_convert_fusion.2), channel_id=1, source_target_pairs={{8,16},{16,8},{9,17},{17,9},{10,18},{18,10},{11,19},{19,11},{12,20... | collective-permute-start | bytes 4718600 | tf_op jit(solution)/shard_map/ppermute | solution.py:222
  897.8 134.3 %reduce-scatter.14.cloned.1.call-start = ((), (), s32[]{:S(2)}) async-start(), calls=%async_computation.14 | async-start | bytes 163840 | tf_op jit(solution)/shard_map/reduce_scatter | solution.py:575
  922.9 251.9 %reduce-scatter.12.cloned.1.call-start = ((), (), s32[]{:S(2)}) async-start(), calls=%async_computation.13 | async-start | bytes 9437184 | tf_op jit(solution)/shard_map/reduce_scatter | solution.py:597
  1001.6 173.2 %reduce-scatter.8.cloned.1.call-start = ((), (), s32[]{:S(2)}) async-start(), calls=%async_computation.9 | async-start | bytes 9437184 | tf_op jit(solution)/shard_map/reduce_scatter | solution.py:556
  (115 other events, 3265.4 us)
Sparse Core Ops, SparseCore 0:
  10.0 58.6 all-gather.4
  70.5 55.9 all-gather.6
  163.5 71.2 reduce-scatter.5
  274.4 55.4 all-gather.8
  756.7 53.0 all-reduce.6
  813.1 70.6 reduce-scatter.9
  897.9 57.1 all-gather.10
  958.0 19.1 reduce-scatter.13
  1001.7 71.2 reduce-scatter.11
  1076.7 71.2 reduce-scatter.7

commit v4 on v3

--- a/solution.py
+++ b/solution.py
@@ -375,38 +375,39 @@
     )(z, *pieces, scaled, cots, scaled, cots, coef)
 
 
-def joint_kernel(count, *refs):
+def joint_kernel(count, based, *refs):
     out_ref = refs[-1]
     for a in range(0, out_ref.shape[1], TILE):
-        total = None
-        for left, weights in zip(refs[:count], refs[count:-1]):
+        total = refs[2 * count][:, a : a + TILE] if based else None
+        for left, weights in zip(refs[:count], refs[count : 2 * count]):
             part = mm_nt(left[...], weights[a : a + TILE, :])
             total = part if total is None else total + part
-        out_ref[:, a : a + TILE] = total.astype(bf16)
-
-
-def joint_back(lefts, weights, column):
+        out_ref[:, a : a + TILE] = total.astype(out_ref.dtype)
+
+
+def joint_back(lefts, weights, column, kind, *base):
     tokens, width = lefts[0].shape[0], weights[0].shape[0]
     row = lambda i: (i, 0)
     fixed = lambda i: (0, column)
     depth = sum(left.shape[1] for left in lefts)
     return pl.pallas_call(
-        functools.partial(joint_kernel, len(lefts)),
+        functools.partial(joint_kernel, len(lefts), len(base) > 0),
         grid=(tokens // TILE,),
         in_specs=[pl.BlockSpec((TILE, left.shape[1]), row) for left in lefts]
         + [
             pl.BlockSpec((width, left.shape[1]), fixed, pipeline_mode=pl.Buffered(1))
             for left in lefts
-        ],
+        ]
+        + [pl.BlockSpec((TILE, width), row)] * len(base),
         out_specs=pl.BlockSpec((TILE, width), row),
-        out_shape=jax.ShapeDtypeStruct((tokens, width), bf16),
+        out_shape=jax.ShapeDtypeStruct((tokens, width), kind),
         cost_estimate=pl.CostEstimate(
             flops=2 * tokens * width * depth,
-            bytes_accessed=2 * (tokens + width) * depth + 2 * tokens * width,
+            bytes_accessed=2 * (tokens + width) * depth + 4 * tokens * width,
             transcendentals=0,
         ),
         name="joint_back",
-    )(*lefts, *weights)
+    )(*lefts, *weights, *base)
 
 
 def split_three(values):
@@ -467,12 +468,11 @@
     ).reshape(rows_block, 3 * head_width)
     router_pack = jnp.concatenate([router_weight, score_shared[:, None]], axis=1)
     router_pack = jnp.pad(router_pack, ((0, 0), (0, -router_pack.shape[1] % 128)))
-    attn_weights = join_rows(
-        gather_rows(jnp.concatenate([qkv_pack, output_weight.T, router_pack], axis=1))[0]
-    )
-    qkv_full = attn_weights[:, : 3 * head_width]
-    out_full = attn_weights[:, 3 * head_width : 4 * head_width]
-    router_full = attn_weights[:, 4 * head_width : 4 * head_width + experts + 1]
+    qkv_full = join_rows(gather_rows(qkv_pack)[0])
+    out_pack = jnp.concatenate([output_weight.T, router_pack], axis=1)
+    out_weights = join_rows(gather_rows(out_pack)[0])
+    out_full = out_weights[:, :head_width]
+    router_full = out_weights[:, head_width : head_width + experts + 1]
     shared_cuts = [(None, a, b) for a, b in cuts_of(gate_shared.shape[1])]
     expert_cuts = [
         (local, a, b) for local in range(local_experts) for a, b in cuts_of(gate_expert.shape[2])
@@ -497,14 +497,12 @@
     cot_rows = lax.all_gather(grad_output, "col", axis=1, tiled=True)
     rows_f = rows_in.astype(f32)
     scale_a = lax.rsqrt(jnp.mean(rows_f * rows_f, axis=-1, keepdims=True) + norm_eps)
-    normed_a = after((rows_f * scale_a * gains[0]).astype(bf16), hop(came, 0, 0))
+    normed_a = (rows_f * scale_a * gains[0]).astype(bf16)
     qkv, context, lse = attend_forward(mm(normed_a, qkv_full), lengths, cosine, sine)
-    attn_part = after(mm_nt(context, out_full).astype(bf16), (cot_rows,))
+    attn_part = after(mm_nt(context, out_full).astype(bf16), (cot_rows,), hop(came, 0, 0))
     x_share = block_input.astype(f32)
     attn_sum = lax.psum_scatter(attn_part, "col", scatter_dimension=1, tiled=True)
-    attn_sum = after(
-        attn_sum, hop(came, 0, 1), hop(came, 0, 2), hop(came, 1, 0), hop(came, 1, 1)
-    )
+    attn_sum = after(attn_sum, hop(came, 0, 1), hop(came, 0, 2), hop(came, 1, 0))
     stream = x_share + attn_sum.astype(f32)
     gain_b = mlp_gain.astype(f32)
     scaled = lax.all_gather((stream * gain_b).astype(bf16), "col", axis=1, tiled=True)
@@ -527,12 +525,13 @@
         column = lax.dynamic_index_in_dim(router_probs, expert, 1, False)
         shares[local] = jnp.where(members[local], column, 0.0)
     dpairs, hiddens, wholes, unit_grads, went = [], [], [], [], []
+    last = len(chunks) - 1
     for at, ((kind, a, b), pieces) in enumerate(zip(chunks, gathered)):
         coef = jnp.concatenate([scale_b, shares[kind][:, None]], axis=1)
         if at == 0:
-            coef = after(coef, hop(came, 1, 2), hop(came, 2, 0))
+            coef = after(coef, hop(came, 1, 1), hop(came, 1, 2))
         elif at == 1:
-            coef = after(coef, hop(came, 2, 1))
+            coef = after(coef, hop(came, 2, 0))
         else:
             coef = after(
                 coef,
@@ -541,6 +540,10 @@
                 hop(went, at - 3, 1),
                 hop(went, at - 4, 2),
             )
+        if at == last:
+            dscaled_early = joint_back(dpairs, wholes, 0, f32)
+            moe_early = joint_back(hiddens, wholes, 2, f32)
+            coef = after(coef, (dscaled_early, moe_early))
         dpair, hidden, sums, grads, whole = expert_chunk(pieces, scaled, cot_rows, coef)
         dots[kind] = dots.get(kind, 0.0) + sums[:, 0]
         inner = inner + sums[:, 1]
@@ -550,20 +553,13 @@
         reduced, arrivals = reduce_rows(grads)
         unit_grads.append(reduced)
         went.append(arrivals)
-    last = len(chunks) - 1
-    dpairs[-1] = after(dpairs[-1], hop(went, last - 1, 0), hop(went, last - 2, 1))
-    dscaled_part = joint_back(dpairs, wholes, 0)
-    moe_share = lax.psum_scatter(
-        joint_back(hiddens, wholes, 2), "col", scatter_dimension=1, tiled=True
-    ).astype(f32)
-    block_output = (stream + moe_share).astype(bf16)
-
-    table = jnp.zeros((experts, tokens), f32)
-    for local in range(local_experts):
-        row = jnp.where(members[local], dots[local], 0.0)[None]
-        table = lax.dynamic_update_slice_in_dim(table, row, col_id * local_experts + local, 0)
-    table = lax.psum(jnp.concatenate([table, dots[None][None], inner[None]], axis=0), "col")
-    dprob, dshared_gate, inner = table[:experts].T, table[experts], table[experts + 1]
+    dscaled_part = joint_back([dpair], [whole], 0, bf16, dscaled_early)
+    moe_part = joint_back([hidden], [whole], 2, bf16, moe_early)
+
+    named = [jnp.where(members[local], dots[local], 0.0) for local in range(local_experts)]
+    table = lax.all_gather(jnp.stack(named + [dots[None], inner]), "col", axis=0)
+    dprob = table[:, :local_experts].reshape(experts, tokens).T
+    dshared_gate, inner = jnp.sum(table[:, local_experts], axis=0), jnp.sum(table[:, local_experts + 1], axis=0)
     dlogits = router_probs * (dprob - jnp.sum(dprob * router_probs, axis=1, keepdims=True))
     dslogit = dshared_gate * shared_gate * (1.0 - shared_gate)
     dboth = jnp.concatenate([dlogits, dslogit[:, None]], axis=1)
@@ -577,8 +573,10 @@
     back = mm_nt(jnp.concatenate(parts, axis=1), jnp.concatenate([router_rows] * 3, axis=1))
     dscaled_sum = after(
         lax.psum_scatter(dscaled_part, "col", scatter_dimension=1, tiled=True),
+        (moe_part,),
+        hop(went, last - 1, 0),
+        hop(went, last - 2, 1),
         hop(went, last - 3, 2),
-        hop(went, last - 2, 2),
         hop(went, last - 1, 1),
         hop(went, last, 0),
     )
@@ -588,7 +586,11 @@
     gain_b_grad = jnp.sum(dscaled * stream, axis=0)
 
     dattn = lax.all_gather(dstream.astype(bf16), "col", axis=1, tiled=True)
-    dattn = after(dattn, hop(went, last - 1, 2), hop(went, last, 1))
+    dattn = after(dattn, hop(went, last - 2, 2), hop(went, last - 1, 2), hop(went, last, 1))
+    moe_share = lax.psum_scatter(
+        after(moe_part, (dattn,)), "col", scatter_dimension=1, tiled=True
+    ).astype(f32)
+    block_output = (stream + moe_share).astype(bf16)
     out_grad, _ = reduce_rows(mm_tn(dattn, context).astype(bf16))
     dcontext = mm(dattn, out_full).astype(bf16)
     dqkv, inner_a = attend_backward(qkv, dcontext, lse, lengths, cosine, sine)

time: 1210 us -> 1250 us (1.033)
  starting transfers between devices: 138 us -> 160 us
  waiting for transfers between devices: 443 us -> 461 us
  Pallas kernels: 298 us -> 315 us
  other arithmetic: 130 us -> 115 us
    ppermute x6 -> x7, waiting for transfers between devices: 75.7 us -> 18.7 us  [gather_rows(): partner = lax.ppermute(part, 'row', [(0, 1), (1, 0), (2, 3), (3, 2)])]
    ppermute x6 -> x7, waiting for transfers between devices: 70.5 us -> 109 us  [gather_rows(): near_out = lax.ppermute(near_mid, 'row', outward)]
    ppermute x6 -> x7, starting transfers between devices: 11.5 us -> 39.5 us  [gather_rows(): partner = lax.ppermute(part, 'row', [(0, 1), (1, 0), (2, 3), (3, 2)])]
    all_gather x1, waiting for transfers between devices: 11.4 us -> 38.1 us  [per_device(): lax.all_gather((stream * gain_b).astype(bf16), 'col', axis=1, tiled=True)]
    all_gather x1, waiting for transfers between devices: 21.7 us -> 0.01 us  [per_device(): dattn = lax.all_gather(dstream.astype(bf16), 'col', axis=1, tiled=True)]
    pallas_call x2 -> x4, Pallas kernels: 73.4 us -> 91.5 us  [joint_back(): pl.pallas_call(functools.partial(joint_kernel, len(lefts), len(base) > 0)...]
    ppermute x6 -> x7, waiting for transfers between devices: 108 us -> 124 us  [gather_rows(): far_out = lax.ppermute(far_mid, 'row', outward)]
    unnamed x147 -> x174, local copies, waits for them, and re-layouts: 22.3 us -> 25.2 us
  transfers between devices with their start and end apart: 75 -> 79, of which waited for: 21 -> 28; matrix products, arithmetic and copies ran while one was open for 21% -> 19% of each run, Pallas kernels for 25% -> 21%
where the time goes in v4:
time: 1250 us; the launch traced here: 1240 us
  waiting for transfers between devices  461 us (37%)
  Pallas kernels  315 us (25%)
  starting transfers between devices  160 us (13%)
  other arithmetic  115 us (9%)
  local copies, waits for them, and re-layouts  75.1 us (6%)
  matrix products  57.3 us (5%)
  blocking collectives  42.6 us (3%)
  between operations  16.2 us (1%)
    pallas_call x5, Pallas kernels, expert_chunk(): pl.pallas_call(functools.partial(expert_kernel, size, steps, count), grid...  183 us
    ppermute x7, waiting for transfers between devices, gather_rows(): far_out = lax.ppermute(far_mid, 'row', outward)  124 us
    ppermute x7, waiting for transfers between devices, gather_rows(): near_out = lax.ppermute(near_mid, 'row', outward)  109 us
    pallas_call x4, Pallas kernels, joint_back(): pl.pallas_call(functools.partial(joint_kernel, len(lefts), len(base) > 0)...  91.5 us
    ppermute x7, waiting for transfers between devices, reduce_rows(): far_in = lax.ppermute(block(far), 'row', inward)  67 us
    ppermute x7, waiting for transfers between devices, reduce_rows(): near_in = lax.ppermute(block(near), 'row', inward)  53.8 us
    ppermute x7, waiting for transfers between devices, reduce_rows(): lax.ppermute(block(partner, far_sum).astype(bf16), 'row', [(0, 1), (1, 0)...  46.6 us
    ppermute x7, starting transfers between devices, gather_rows(): partner = lax.ppermute(part, 'row', [(0, 1), (1, 0), (2, 3), (3, 2)])  39.5 us
  transfers between devices with their start and end apart: 79, of which 28 were waited for; matrix products, arithmetic and copies ran while one was open for 19% of the time, Pallas kernels for 21%

profile of v4, /device:TPU:0, one launch (start us, length us, event | category | flops | bytes accessed | tf_op | source)
XLA Modules:
  0.0 1242.5 jit_solution(6729462481580143044)
XLA Ops:
  56.2 20.2 %collective-permute-start.10 = (bf16[512,768]{1,0:T(8,128)(2,1)}, bf16[512,768]{1,0:T(8,128)(2,1)}, u32[]{:S(2)}, u32[]{:S(2)}) collective-permute-start(bf16[512,768]{1,0:T(8,128)(2,1)} %fusion.18.refs_0_), channel_id=1, source_target_pairs={{0,8},{8,0},{16,24},{24,16},{1,9},{9,1},{17,25},{25,17},{2,10},{10... | collective-permute-start | bytes 2359304 | tf_op jit(solution)/shard_map/ppermute | solution.py:176
  81.8 16.8 %collective-permute-done.2 = bf16[512,768]{0,1:T(8,128)(2,1)} collective-permute-done((bf16[512,768]{0,1:T(8,128)(2,1)}, bf16[512,768]{0,1:T(8,128)(2,1)}, u32[]{:S(2)}, u32[]{:S(2)}) %collective-permute-start.2) | collective-permute-done | bytes 786464 | tf_op jit(solution)/shard_map/ppermute | solution.py:180
  101.4 28.0 %collective-permute-done.4 = bf16[512,768]{0,1:T(8,128)(2,1)} collective-permute-done((bf16[512,768]{0,1:T(8,128)(2,1)}, bf16[512,768]{0,1:T(8,128)(2,1)}, u32[]{:S(2)}, u32[]{:S(2)}) %collective-permute-start.4) | collective-permute-done | bytes 786464 | tf_op jit(solution)/shard_map/ppermute | solution.py:181
  148.3 12.7 %attend_forward.1 = (bf16[2048,768]{1,0:T(8,128)(2,1)}, bf16[2048,256]{1,0:T(8,128)(2,1)}, f32[2048,256]{1,0:T(8,128)}) custom-call(s32[2]{0:T(128)} %dynamic_slice.108.length_ref, f32[2048,768]{1,0:T(8,128)} %fusion.4.raw_ref, f32[1024,128]{1,0:T(8,128)} %get-tuple-element.227.cos_ref, f32[1024,128]{1,0:T(8,128)} %get-tuple-element.228.sin_ref), custom_call_target="tpu_custom_call" | custom-call | flops 1610612736 | bytes 12582912 | tf_op jit(solution)/shard_map/attend_forward/pallas_call | solution.py:82
  179.7 46.2 %collective-permute-done.13.refs_4_ = bf16[512,768]{1,0:T(8,128)(2,1)S(1)} collective-permute-done((bf16[512,768]{1,0:T(8,128)(2,1)}, bf16[512,768]{1,0:T(8,128)(2,1)S(1)}, u32[]{:S(2)}, u32[]{:S(2)}) %collective-permute-start.13) | collective-permute-done | bytes 786464 | tf_op jit(solution)/shard_map/ppermute | solution.py:180
  228.5 13.2 %collective-permute-done.14.refs_5_ = bf16[512,768]{1,0:T(8,128)(2,1)} collective-permute-done((bf16[512,768]{1,0:T(8,128)(2,1)S(1)}, bf16[512,768]{1,0:T(8,128)(2,1)}, u32[]{:S(2)}, u32[]{:S(2)}) %collective-permute-start.14) | collective-permute-done | bytes 786464 | tf_op jit(solution)/shard_map/ppermute | solution.py:181
  261.6 38.1 %all-gather.11.cloned.1.call-done.refs_6_.refs_8_ = bf16[2048,2048]{1,0:T(8,128)(2,1)} async-done(((bf16[2048,256]{1,0:T(8,128)(2,1)}), bf16[2048,2048]{1,0:T(8,128)(2,1)}) %all-gather.11.cloned.1.call-update) | async-done | bytes 8388624 | tf_op jit(solution)/shard_map/all_gather | solution.py:508
  308.5 17.0 %collective-permute-done.22.refs_1_ = bf16[512,1536]{1,0:T(8,128)(2,1)} collective-permute-done((bf16[512,1536]{1,0:T(8,128)(2,1)}, bf16[512,1536]{1,0:T(8,128)(2,1)}, u32[]{:S(2)}, u32[]{:S(2)}) %collective-permute-start.22) | collective-permute-done | bytes 1572896 | tf_op jit(solution)/shard_map/ppermute | solution.py:176
  327.4 31.7 %collective-permute-done.30.refs_4_ = bf16[512,1536]{1,0:T(8,128)(2,1)S(1)} collective-permute-done((bf16[512,1536]{1,0:T(8,128)(2,1)}, bf16[512,1536]{1,0:T(8,128)(2,1)S(1)}, u32[]{:S(2)}, u32[]{:S(2)}) %collective-permute-start.30) | collective-permute-done | bytes 1572896 | tf_op jit(solution)/shard_map/ppermute | solution.py:180
  360.9 29.9 %collective-permute-done.31.refs_5_ = bf16[512,1536]{1,0:T(8,128)(2,1)} collective-permute-done((bf16[512,1536]{1,0:T(8,128)(2,1)}, bf16[512,1536]{1,0:T(8,128)(2,1)}, u32[]{:S(2)}, u32[]{:S(2)}) %collective-permute-start.31) | collective-permute-done | bytes 1572896 | tf_op jit(solution)/shard_map/ppermute | solution.py:181
  392.2 27.9 %expert_chunk.5 = (bf16[2048,512]{1,0:T(8,128)(2,1)}, bf16[2048,256]{1,0:T(8,128)(2,1)}, f32[2048,2]{1,0:T(8,128)}, bf16[2048,768]{1,0:T(8,128)(2,1)}, bf16[2048,768]{1,0:T(8,128)(2,1)}) custom-call(s32[1]{0:T(128)} %bitcast.21.z_ref, bf16[512,768]{1,0:T(8,128)(2,1)} %fusion.18.refs_0_, bf16[512,768]{1,0:T(8,128)(2,1)} %collective-permute-done.10.refs_1_, ...), custom_call_target="tpu_custom_call" | custom-call | flops 12884901888 | bytes 46137344 | tf_op jit(solution)/shard_map/expert_chunk/pallas_call | solution.py:334
  461.5 39.5 %expert_chunk.7 = (bf16[2048,1024]{1,0:T(8,128)(2,1)}, bf16[2048,512]{1,0:T(8,128)(2,1)}, f32[2048,2]{1,0:T(8,128)}, bf16[2048,1536]{1,0:T(8,128)(2,1)}, bf16[2048,1536]{1,0:T(8,128)(2,1)}) custom-call(s32[1]{0:T(128)} %bitcast.21.z_ref, bf16[512,1536]{1,0:T(8,128)(2,1)} %copy-done.29, bf16[512,1536]{1,0:T(8,128)(2,1)} %copy-done.63, ...), custom_call_target="tpu_custom_call" | custom-call | flops 25769803776 | bytes 58720256 | tf_op jit(solution)/shard_map/expert_chunk/pallas_call | solution.py:334
  521.0 27.1 %collective-permute-done.26.refs_5_ = bf16[512,1536]{1,0:T(8,128)(2,1)} collective-permute-done((bf16[512,1536]{1,0:T(8,128)(2,1)}, bf16[512,1536]{1,0:T(8,128)(2,1)}, u32[]{:S(2)}, u32[]{:S(2)}) %collective-permute-start.26) | collective-permute-done | bytes 1572896 | tf_op jit(solution)/shard_map/ppermute | solution.py:181
  552.3 39.5 %expert_chunk.6 = (bf16[2048,1024]{1,0:T(8,128)(2,1)}, bf16[2048,512]{1,0:T(8,128)(2,1)}, f32[2048,2]{1,0:T(8,128)}, bf16[2048,1536]{1,0:T(8,128)(2,1)}, bf16[2048,1536]{1,0:T(8,128)(2,1)}) custom-call(s32[1]{0:T(128)} %bitcast.21.z_ref, bf16[512,1536]{1,0:T(8,128)(2,1)} %pad_maximum_fusion.1.refs_0_, bf16[512,1536]{1,0:T(8,128)(2,1)} %collective-permute-done.22.refs_1_, ...), custom_call_target="tpu_custom_call" | custom-call | flops 25769803776 | bytes 58720256 | tf_op jit(solution)/shard_map/expert_chunk/pallas_call | solution.py:334
  617.5 39.5 %expert_chunk.8 = (bf16[2048,1024]{1,0:T(8,128)(2,1)}, bf16[2048,512]{1,0:T(8,128)(2,1)}, f32[2048,2]{1,0:T(8,128)}, bf16[2048,1536]{1,0:T(8,128)(2,1)}, bf16[2048,1536]{1,0:T(8,128)(2,1)}) custom-call(s32[1]{0:T(128)} %bitcast.21.z_ref, bf16[512,1536]{1,0:T(8,128)(2,1)} %pad_maximum_fusion.2.refs_0_, bf16[512,1536]{1,0:T(8,128)(2,1)} %collective-permute-done.27.refs_1_, ...), custom_call_target="tpu_custom_call" | custom-call | flops 25769803776 | bytes 58720256 | tf_op jit(solution)/shard_map/expert_chunk/pallas_call | solution.py:334
  662.3 39.4 %joint_back.4.refs_2_ = f32[2048,2048]{1,0:T(8,128)} custom-call(bf16[2048,512]{1,0:T(8,128)(2,1)} %get-tuple-element.68.refs_0_, bf16[2048,1024]{1,0:T(8,128)(2,1)} %get-tuple-element.69.refs_1_, bf16[2048,1024]{1,0:T(8,128)(2,1)} %get-tuple-element.70.refs_2_, bf16[2048,1024]{1,0:T(8,128)(2,1)} %get-tuple-element.72.refs_3_, ...), custom_call_target="tpu_custom_call" | custom-call | flops 30064771072 | bytes 46137344 | tf_op jit(solution)/shard_map/joint_back/pallas_call | solution.py:393
  704.7 22.0 %joint_back.5.refs_2_ = f32[2048,2048]{1,0:T(8,128)} custom-call(bf16[2048,256]{1,0:T(8,128)(2,1)} %get-tuple-element.77.refs_0_, bf16[2048,512]{1,0:T(8,128)(2,1)} %get-tuple-element.78.refs_1_, bf16[2048,512]{1,0:T(8,128)(2,1)} %get-tuple-element.79.refs_2_, bf16[2048,512]{1,0:T(8,128)(2,1)} %get-tuple-element.80.refs_3_, ...), custom_call_target="tpu_custom_call" | custom-call | flops 15032385536 | bytes 31457280 | tf_op jit(solution)/shard_map/joint_back/pallas_call | solution.py:393
  732.8 17.9 %collective-permute-done.21.refs_5_ = bf16[512,1152]{1,0:T(8,128)(2,1)} collective-permute-done((bf16[512,1152]{1,0:T(8,128)(2,1)}, bf16[512,1152]{1,0:T(8,128)(2,1)}, u32[]{:S(2)}, u32[]{:S(2)}) %collective-permute-start.21) | collective-permute-done | bytes 1179680 | tf_op jit(solution)/shard_map/ppermute | solution.py:181
  750.7 36.2 %expert_chunk.9 = (bf16[2048,768]{1,0:T(8,128)(2,1)}, bf16[2048,384]{1,0:T(8,128)(2,1)}, f32[2048,2]{1,0:T(8,128)}, bf16[2048,1152]{1,0:T(8,128)(2,1)}, bf16[2048,1152]{1,0:T(8,128)(2,1)}) custom-call(s32[1]{0:T(128)} %bitcast.21.z_ref, bf16[512,1152]{1,0:T(8,128)(2,1)} %pad_maximum_fusion.6.refs_0_, bf16[512,1152]{1,0:T(8,128)(2,1)} %collective-permute-done.17.refs_1_, ...), custom_call_target="tpu_custom_call" | custom-call | flops 19327352832 | bytes 52428800 | tf_op jit(solution)/shard_map/expert_chunk/pallas_call | solution.py:334
  786.9 15.7 %joint_back.7 = bf16[2048,2048]{1,0:T(8,128)(2,1)} custom-call(bf16[2048,768]{1,0:T(8,128)(2,1)} %get-tuple-element.89.refs_0_, bf16[2048,1152]{1,0:T(8,128)(2,1)} %get-tuple-element.83.refs_1_, f32[2048,2048]{1,0:T(8,128)} %joint_back.4.refs_2_), custom_call_target="tpu_custom_call" | custom-call | flops 6442450944 | bytes 23068672 | tf_op jit(solution)/shard_map/joint_back/pallas_call | solution.py:393
  822.4 19.8 %collective-permute-done.47 = bf16[512,1536]{1,0:T(8,128)(2,1)S(1)} collective-permute-done((bf16[512,1536]{1,0:T(8,128)(2,1)S(1)}, bf16[512,1536]{1,0:T(8,128)(2,1)S(1)}, u32[]{:S(2)}, u32[]{:S(2)}) %collective-permute-start.47) | collective-permute-done | bytes 1572896 | tf_op jit(solution)/shard_map/ppermute | solution.py:221
  848.1 27.9 %collective-permute-done.46 = bf16[512,1536]{1,0:T(8,128)(2,1)S(1)} collective-permute-done((bf16[512,1536]{1,0:T(8,128)(2,1)S(1)}, bf16[512,1536]{1,0:T(8,128)(2,1)S(1)}, u32[]{:S(2)}, u32[]{:S(2)}) %collective-permute-start.46) | collective-permute-done | bytes 1572896 | tf_op jit(solution)/shard_map/ppermute | solution.py:220
  900.8 14.4 %joint_back.6 = bf16[2048,2048]{1,0:T(8,128)(2,1)} custom-call(bf16[2048,384]{1,0:T(8,128)(2,1)} %get-tuple-element.82.refs_0_, bf16[2048,1152]{1,0:T(8,128)(2,1)} %get-tuple-element.83.refs_1_, f32[2048,2048]{1,0:T(8,128)} %joint_back.5.refs_2_), custom_call_target="tpu_custom_call" | custom-call | flops 3221225472 | bytes 19922944 | tf_op jit(solution)/shard_map/joint_back/pallas_call | solution.py:393
  915.2 15.1 %collective-permute-done.54 = bf16[512,1152]{1,0:T(8,128)(2,1)} collective-permute-done((bf16[512,1152]{1,0:T(8,128)(2,1)}, bf16[512,1152]{1,0:T(8,128)(2,1)}, u32[]{:S(2)}, u32[]{:S(2)}) %collective-permute-start.54) | collective-permute-done | bytes 1179680 | tf_op jit(solution)/shard_map/ppermute | solution.py:221
  930.3 21.8 %collective-permute-done.53 = bf16[512,1152]{1,0:T(8,128)(2,1)} collective-permute-done((bf16[512,1152]{1,0:T(8,128)(2,1)}, bf16[512,1152]{1,0:T(8,128)(2,1)}, u32[]{:S(2)}, u32[]{:S(2)}) %collective-permute-start.53) | collective-permute-done | bytes 1179680 | tf_op jit(solution)/shard_map/ppermute | solution.py:220
  981.8 15.9 %collective-permute-done.55 = bf16[512,1536]{1,0:T(8,128)(2,1)} collective-permute-done((bf16[512,1536]{1,0:T(8,128)(2,1)}, bf16[512,1536]{1,0:T(8,128)(2,1)}, u32[]{:S(2)}, u32[]{:S(2)}) %collective-permute-start.55) | collective-permute-done | bytes 1572896 | tf_op jit(solution)/shard_map/ppermute | solution.py:224
  997.7 30.7 %collective-permute-done.56 = bf16[512,1536]{1,0:T(8,128)(2,1)} collective-permute-done((bf16[512,1536]{1,0:T(8,128)(2,1)}, bf16[512,1536]{1,0:T(8,128)(2,1)}, u32[]{:S(2)}, u32[]{:S(2)}) %collective-permute-start.56) | collective-permute-done | bytes 1572896 | tf_op jit(solution)/shard_map/ppermute | solution.py:224
  1035.5 28.2 %attend_backward.1 = (bf16[2048,768]{1,0:T(8,128)(2,1)}, f32[2048,1]{1,0:T(8,128)}) custom-call(s32[2]{0:T(128)} %dynamic_slice.108.length_ref, bf16[2048,768]{1,0:T(8,128)(2,1)} %get-tuple-element.95.qkv_ref, bf16[2048,256]{1,0:T(8,128)(2,1)} %convolution_convert_fusion.4.dcontext_ref, f32[2048,256]{1,0:T(8,128)} %get-tuple-element.96.lse_ref, ...), custom_call_target="tpu_custom_call" | custom-call | flops 4294967296 | bytes 12582912 | tf_op jit(solution)/shard_map/attend_backward/pallas_call | solution.py:152
  1063.6 11.4 convolution_convert_fusion
  1142.3 14.7 %collective-permute-done.67 = bf16[512,256]{1,0:T(8,128)(2,1)S(1)} collective-permute-done((bf16[512,256]{1,0:T(8,128)(2,1)S(1)}, bf16[512,256]{1,0:T(8,128)(2,1)S(1)}, u32[]{:S(2)}, u32[]{:S(2)}) %collective-permute-start.67) | collective-permute-done | bytes 262176 | tf_op jit(solution)/shard_map/ppermute | solution.py:220
  1191.5 12.2 psum.21
  1223.3 12.2 all-reduce.4
  (479 shorter events, 443.5 us)
Async XLA Ops:
  7.3 124.8 %all-gather.7.cloned.1.call-start = ((), (), s32[]{:S(2)}) async-start(), calls=%async_computation.5 | async-start | bytes 9437184 | tf_op jit(solution)/shard_map/all_gather | solution.py:495
  8.0 160.0 %all-gather.9.cloned.1.call-start = ((), (), s32[]{:S(2)}) async-start(), calls=%async_computation.6 | async-start | bytes 9437184 | tf_op jit(solution)/shard_map/all_gather | solution.py:497
  8.7 232.9 %reduce-scatter.6.cloned.1.call-start = ((), (), s32[]{:S(2)}) async-start(), calls=%async_computation.7 | async-start | bytes 9437184 | tf_op jit(solution)/shard_map/reduce_scatter | solution.py:504
  22.1 145.9 %collective-permute-start.11 = (bf16[512,768]{1,0:T(8,128)(2,1)}, bf16[512,768]{1,0:T(8,128)(2,1)}, u32[]{:S(2)}, u32[]{:S(2)}) collective-permute-start(bf16[512,768]{1,0:T(8,128)(2,1)} %fusion.18.refs_0_), channel_id=1, source_target_pairs={{8,16},{16,8},{9,17},{17,9},{10,18},{18,10},{11,19},{19,11},{12,20... | collective-permute-start | bytes 2359304 | tf_op jit(solution)/shard_map/ppermute | solution.py:178
  56.2 111.8 %collective-permute-start.10 = (bf16[512,768]{1,0:T(8,128)(2,1)}, bf16[512,768]{1,0:T(8,128)(2,1)}, u32[]{:S(2)}, u32[]{:S(2)}) collective-permute-start(bf16[512,768]{1,0:T(8,128)(2,1)} %fusion.18.refs_0_), channel_id=1, source_target_pairs={{0,8},{8,0},{16,24},{24,16},{1,9},{9,1},{17,25},{25,17},{2,10},{10... | collective-permute-start | bytes 2359304 | tf_op jit(solution)/shard_map/ppermute | solution.py:176
  168.0 131.6 %all-gather.11.cloned.1.call-start = ((), (), s32[]{:S(2)}) async-start(), calls=%async_computation.8 | async-start | bytes 9437184 | tf_op jit(solution)/shard_map/all_gather | solution.py:508
  244.2 707.9 %reduce-scatter.8.cloned.1.call-start = ((), (), s32[]{:S(2)}) async-start(), calls=%async_computation.9 | async-start | bytes 9437184 | tf_op jit(solution)/shard_map/reduce_scatter | solution.py:575
  252.3 201.2 %collective-permute-start.28 = (bf16[512,1536]{1,0:T(8,128)(2,1)}, bf16[512,1536]{1,0:T(8,128)(2,1)}, u32[]{:S(2)}, u32[]{:S(2)}) collective-permute-start(bf16[512,1536]{1,0:T(8,128)(2,1)} %pad_maximum_fusion.2.refs_0_), channel_id=1, source_target_pairs={{8,16},{16,8},{9,17},{17,9},{10,18},{18,10},{11,19},{19,11},{12,20... | collective-permute-start | bytes 4718600 | tf_op jit(solution)/shard_map/ppermute | solution.py:178
  254.2 200.6 %collective-permute-start.27 = (bf16[512,1536]{1,0:T(8,128)(2,1)}, bf16[512,1536]{1,0:T(8,128)(2,1)}, u32[]{:S(2)}, u32[]{:S(2)}) collective-permute-start(bf16[512,1536]{1,0:T(8,128)(2,1)} %pad_maximum_fusion.2.refs_0_), channel_id=1, source_target_pairs={{0,8},{8,0},{16,24},{24,16},{1,9},{9,1},{17,25},{25,17},{2,10},{10... | collective-permute-start | bytes 4718600 | tf_op jit(solution)/shard_map/ppermute | solution.py:176
  258.9 100.2 %collective-permute-start.30 = (bf16[512,1536]{1,0:T(8,128)(2,1)}, bf16[512,1536]{1,0:T(8,128)(2,1)S(1)}, u32[]{:S(2)}, u32[]{:S(2)}) collective-permute-start(bf16[512,1536]{1,0:T(8,128)(2,1)} %copy-done.62), channel_id=1, source_target_pairs={{8,0},{16,24},{9,1},{17,25},{10,2},{18,26},{11,3},{19,27},{12,4},{... | collective-permute-start | bytes 4718600 | tf_op jit(solution)/shard_map/ppermute | solution.py:180
  260.3 130.6 %collective-permute-start.31 = (bf16[512,1536]{1,0:T(8,128)(2,1)}, bf16[512,1536]{1,0:T(8,128)(2,1)}, u32[]{:S(2)}, u32[]{:S(2)}) collective-permute-start(bf16[512,1536]{1,0:T(8,128)(2,1)} %collective-permute-done.29.refs_3_), channel_id=1, source_target_pairs={{8,0},{16,24},{9,1},{17,25},{10,2},{18,26},{11,3},{19,27},{12,4},{... | collective-permute-start | bytes 4718600 | tf_op jit(solution)/shard_map/ppermute | solution.py:181
  325.5 101.0 %collective-permute-start.23 = (bf16[512,1536]{1,0:T(8,128)(2,1)}, bf16[512,1536]{1,0:T(8,128)(2,1)}, u32[]{:S(2)}, u32[]{:S(2)}) collective-permute-start(bf16[512,1536]{1,0:T(8,128)(2,1)} %pad_maximum_fusion.1.refs_0_), channel_id=1, source_target_pairs={{8,16},{16,8},{9,17},{17,9},{10,18},{18,10},{11,19},{19,11},{12,20... | collective-permute-start | bytes 4718600 | tf_op jit(solution)/shard_map/ppermute | solution.py:178
  359.1 97.6 %collective-permute-start.24 = (bf16[512,1536]{1,0:T(8,128)(2,1)}, bf16[512,1536]{1,0:T(8,128)(2,1)}, u32[]{:S(2)}, u32[]{:S(2)}) collective-permute-start(bf16[512,1536]{1,0:T(8,128)(2,1)} %collective-permute-done.22.refs_1_), channel_id=1, source_target_pairs={{8,16},{16,8},{9,17},{17,9},{10,18},{18,10},{11,19},{19,11},{12,20... | collective-permute-start | bytes 4718600 | tf_op jit(solution)/shard_map/ppermute | solution.py:179
  456.7 91.4 %collective-permute-start.26 = (bf16[512,1536]{1,0:T(8,128)(2,1)}, bf16[512,1536]{1,0:T(8,128)(2,1)}, u32[]{:S(2)}, u32[]{:S(2)}) collective-permute-start(bf16[512,1536]{1,0:T(8,128)(2,1)} %collective-permute-done.24.refs_3_), channel_id=1, source_target_pairs={{8,0},{16,24},{9,1},{17,25},{10,2},{18,26},{11,3},{19,27},{12,4},{... | collective-permute-start | bytes 4718600 | tf_op jit(solution)/shard_map/ppermute | solution.py:181
  460.6 90.2 %collective-permute-start.45 = (bf16[512,768]{1,0:T(8,128)(2,1)S(1)}, bf16[512,768]{1,0:T(8,128)(2,1)S(1)}, u32[]{:S(2)}, u32[]{:S(2)}) collective-permute-start(bf16[512,768]{1,0:T(8,128)(2,1)S(1)} %add_convert_fusion.16), channel_id=1, source_target_pairs={{8,16},{16,8},{9,17},{17,9},{10,18},{18,10},{11,19},{19,11},{12,20... | collective-permute-start | bytes 2359304 | tf_op jit(solution)/shard_map/ppermute | solution.py:223
  507.2 102.0 %collective-permute-start.43 = (bf16[512,1536]{1,0:T(8,128)(2,1)}, bf16[512,1536]{1,0:T(8,128)(2,1)}, u32[]{:S(2)}, u32[]{:S(2)}) collective-permute-start(bf16[512,1536]{1,0:T(8,128)(2,1)} %collective-permute-done.28.refs_2_), channel_id=1, source_target_pairs={{8,0},{16,24},{9,1},{17,25},{10,2},{18,26},{11,3},{19,27},{12,4},{... | collective-permute-start | bytes 4718600 | tf_op jit(solution)/shard_map/ppermute | solution.py:180
  508.5 107.0 %collective-permute-start.44 = (bf16[512,1536]{1,0:T(8,128)(2,1)}, bf16[512,1536]{1,0:T(8,128)(2,1)}, u32[]{:S(2)}, u32[]{:S(2)}) collective-permute-start(bf16[512,1536]{1,0:T(8,128)(2,1)} %collective-permute-done.42.refs_3_), channel_id=1, source_target_pairs={{8,0},{16,24},{9,1},{17,25},{10,2},{18,26},{11,3},{19,27},{12,4},{... | collective-permute-start | bytes 4718600 | tf_op jit(solution)/shard_map/ppermute | solution.py:181
  514.4 81.2 %collective-permute-start.38 = (bf16[512,1536]{1,0:T(8,128)(2,1)}, bf16[512,1536]{1,0:T(8,128)(2,1)}, u32[]{:S(2)}, u32[]{:S(2)}) collective-permute-start(bf16[512,1536]{1,0:T(8,128)(2,1)} %get-tuple-element.176), channel_id=1, source_target_pairs={{0,8},{24,16},{1,9},{25,17},{2,10},{26,18},{3,11},{27,19},{4,12},{... | collective-permute-start | bytes 4718600 | tf_op jit(solution)/shard_map/ppermute | solution.py:221
  595.6 107.4 %collective-permute-start.35 = (bf16[512,1536]{1,0:T(8,128)(2,1)S(1)}, bf16[512,1536]{1,0:T(8,128)(2,1)}, u32[]{:S(2)}, u32[]{:S(2)}) collective-permute-start(bf16[512,1536]{1,0:T(8,128)(2,1)S(1)} %get-tuple-element.178), channel_id=1, source_target_pairs={{0,8},{24,16},{1,9},{25,17},{2,10},{26,18},{3,11},{27,19},{4,12},{... | collective-permute-start | bytes 4718600 | tf_op jit(solution)/shard_map/ppermute | solution.py:221
  599.6 127.2 %collective-permute-start.34 = (bf16[512,1536]{1,0:T(8,128)(2,1)S(1)}, bf16[512,1536]{1,0:T(8,128)(2,1)}, u32[]{:S(2)}, u32[]{:S(2)}) collective-permute-start(bf16[512,1536]{1,0:T(8,128)(2,1)S(1)} %get-tuple-element.179), channel_id=1, source_target_pairs={{0,8},{24,16},{1,9},{25,17},{2,10},{26,18},{3,11},{27,19},{4,12},{... | collective-permute-start | bytes 4718600 | tf_op jit(solution)/shard_map/ppermute | solution.py:220
  609.2 92.5 %collective-permute-start.41 = (bf16[512,768]{1,0:T(8,128)(2,1)}, bf16[512,768]{1,0:T(8,128)(2,1)}, u32[]{:S(2)}, u32[]{:S(2)}) collective-permute-start(bf16[512,768]{1,0:T(8,128)(2,1)} %add_convert_fusion.17), channel_id=1, source_target_pairs={{0,8},{8,0},{16,24},{24,16},{1,9},{9,1},{17,25},{25,17},{2,10},{10... | collective-permute-start | bytes 2359304 | tf_op jit(solution)/shard_map/ppermute | solution.py:224
  615.5 111.2 %collective-permute-start.39 = (bf16[512,1536]{1,0:T(8,128)(2,1)}, bf16[512,1536]{1,0:T(8,128)(2,1)}, u32[]{:S(2)}, u32[]{:S(2)}) collective-permute-start(bf16[512,1536]{1,0:T(8,128)(2,1)} %add_convert_fusion.7), channel_id=1, source_target_pairs={{8,16},{16,8},{9,17},{17,9},{10,18},{18,10},{11,19},{19,11},{12,20... | collective-permute-start | bytes 4718600 | tf_op jit(solution)/shard_map/ppermute | solution.py:223
  802.6 225.8 %all-gather.13.cloned.1.call-start = ((), (), s32[]{:S(2)}) async-start(), calls=%async_computation.10 | async-start | bytes 9437184 | tf_op jit(solution)/shard_map/all_gather | solution.py:588
  807.5 68.4 %collective-permute-start.46 = (bf16[512,1536]{1,0:T(8,128)(2,1)S(1)}, bf16[512,1536]{1,0:T(8,128)(2,1)S(1)}, u32[]{:S(2)}, u32[]{:S(2)}) collective-permute-start(bf16[512,1536]{1,0:T(8,128)(2,1)S(1)} %get-tuple-element.175), channel_id=1, source_target_pairs={{0,8},{24,16},{1,9},{25,17},{2,10},{26,18},{3,11},{27,19},{4,12},{... | collective-permute-start | bytes 4718600 | tf_op jit(solution)/shard_map/ppermute | solution.py:220
  810.9 79.6 %collective-permute-start.49 = (bf16[512,1536]{1,0:T(8,128)(2,1)S(1)}, bf16[512,1536]{1,0:T(8,128)(2,1)S(1)}, u32[]{:S(2)}, u32[]{:S(2)}) collective-permute-start(bf16[512,1536]{1,0:T(8,128)(2,1)S(1)} %add_convert_fusion.5), channel_id=1, source_target_pairs={{8,16},{16,8},{9,17},{17,9},{10,18},{18,10},{11,19},{19,11},{12,20... | collective-permute-start | bytes 4718600 | tf_op jit(solution)/shard_map/ppermute | solution.py:223
  813.9 84.4 %collective-permute-start.48 = (bf16[512,1536]{1,0:T(8,128)(2,1)S(1)}, bf16[512,1536]{1,0:T(8,128)(2,1)S(1)}, u32[]{:S(2)}, u32[]{:S(2)}) collective-permute-start(bf16[512,1536]{1,0:T(8,128)(2,1)S(1)} %add_convert_fusion.6), channel_id=1, source_target_pairs={{8,16},{16,8},{9,17},{17,9},{10,18},{18,10},{11,19},{19,11},{12,20... | collective-permute-start | bytes 4718600 | tf_op jit(solution)/shard_map/ppermute | solution.py:222
  818.8 133.3 %collective-permute-start.50 = (bf16[512,1536]{1,0:T(8,128)(2,1)}, bf16[512,1536]{1,0:T(8,128)(2,1)}, u32[]{:S(2)}, u32[]{:S(2)}) collective-permute-start(bf16[512,1536]{1,0:T(8,128)(2,1)} %add_convert_fusion.4), channel_id=1, source_target_pairs={{0,8},{8,0},{16,24},{24,16},{1,9},{9,1},{17,25},{25,17},{2,10},{10... | collective-permute-start | bytes 4718600 | tf_op jit(solution)/shard_map/ppermute | solution.py:224
  843.8 108.3 %collective-permute-start.52 = (bf16[512,1536]{1,0:T(8,128)(2,1)}, bf16[512,1536]{1,0:T(8,128)(2,1)}, u32[]{:S(2)}, u32[]{:S(2)}) collective-permute-start(bf16[512,1536]{1,0:T(8,128)(2,1)} %add_convert_fusion.2), channel_id=1, source_target_pairs={{8,16},{16,8},{9,17},{17,9},{10,18},{18,10},{11,19},{19,11},{12,20... | collective-permute-start | bytes 4718600 | tf_op jit(solution)/shard_map/ppermute | solution.py:223
  877.5 74.6 %collective-permute-start.51 = (bf16[512,1536]{1,0:T(8,128)(2,1)}, bf16[512,1536]{1,0:T(8,128)(2,1)}, u32[]{:S(2)}, u32[]{:S(2)}) collective-permute-start(bf16[512,1536]{1,0:T(8,128)(2,1)} %add_convert_fusion.3), channel_id=1, source_target_pairs={{8,16},{16,8},{9,17},{17,9},{10,18},{18,10},{11,19},{19,11},{12,20... | collective-permute-start | bytes 4718600 | tf_op jit(solution)/shard_map/ppermute | solution.py:222
  956.0 122.9 %reduce-scatter.14.cloned.1.call-start = ((), (), s32[]{:S(2)}) async-start(), calls=%async_computation.13 | async-start | bytes 163840 | tf_op jit(solution)/shard_map/reduce_scatter | solution.py:571
  981.7 235.4 %reduce-scatter.12.cloned.1.call-start = ((), (), s32[]{:S(2)}) async-start(), calls=%async_computation.12 | async-start | bytes 9437184 | tf_op jit(solution)/shard_map/reduce_scatter | solution.py:599
  1075.1 143.9 %reduce-scatter.10.cloned.1.call-start = ((), (), s32[]{:S(2)}) async-start(), calls=%async_computation.11 | async-start | bytes 9437184 | tf_op jit(solution)/shard_map/reduce_scatter | solution.py:590
  (132 other events, 3375.9 us)
Sparse Core Ops, SparseCore 0:
  10.0 58.6 all-gather.6
  70.6 55.9 all-gather.8
  168.1 71.2 reduce-scatter.5
  244.3 55.2 all-gather.10
  802.7 70.8 reduce-scatter.7
  956.1 56.9 all-gather.12
  1015.9 19.2 reduce-scatter.13
  1075.2 68.7 reduce-scatter.11
  1147.5 71.4 reduce-scatter.9

commit v5 on v4

--- a/solution.py
+++ b/solution.py
@@ -12,7 +12,6 @@
 SEQ_LEN = 1024
 QBLOCK = 256
 TILE = 256
-CHUNK = 512
 norm_eps = 1e-06
 rope_base = 1000000.0
 bf16 = jnp.bfloat16
@@ -188,6 +187,102 @@
     return z, z + 1 - 2 * lax.rem(z, 2), 2 - pair, 3 - 3 * pair
 
 
+def gather_kernel(count, *refs):
+    packs, wholes, (send_sems, recv_sems) = refs[:count], refs[count : 2 * count], refs[2 * count :]
+    z = lax.axis_index("row")
+    own, partner, near, far = places(z)
+    across = 3 - z
+    in_middle = (z == 1) | (z == 2)
+    barrier = pltpu.get_barrier_semaphore()
+
+    def copy_of(kind, at, source, block, target):
+        return pltpu.make_async_remote_copy(
+            src_ref=source,
+            dst_ref=wholes[at].at[block],
+            send_sem=send_sems.at[kind, at],
+            recv_sem=recv_sems.at[kind, at],
+            device_id={"row": target},
+            device_id_type=pl.DeviceIdType.MESH,
+        )
+
+    def swap(at):
+        return copy_of(0, at, packs[at], own, partner)
+
+    def swap_middle(at):
+        return copy_of(1, at, packs[at], own, across)
+
+    def second_middle(at):
+        return copy_of(2, at, wholes[at].at[partner], partner, across)
+
+    def hand_near(at):
+        return copy_of(3, at, wholes[at].at[near], near, partner)
+
+    def hand_far(at):
+        return copy_of(4, at, wholes[at].at[far], far, partner)
+
+    pl.semaphore_signal(barrier, inc=1, device_id={"row": partner}, device_id_type=pl.DeviceIdType.MESH)
+
+    @pl.when(in_middle)
+    def _():
+        pl.semaphore_signal(
+            barrier, inc=1, device_id={"row": across}, device_id_type=pl.DeviceIdType.MESH
+        )
+        pl.semaphore_wait(barrier, 2)
+        for at in range(count):
+            swap_middle(at).start()
+            swap(at).start()
+        for at in range(count):
+            swap_middle(at).wait_recv()
+            hand_near(at).start()
+            swap(at).wait_recv()
+            second_middle(at).start()
+        for at in range(count):
+            second_middle(at).wait_recv()
+            hand_far(at).start()
+        for at in range(count):
+            for copy in (swap, swap_middle, second_middle, hand_near, hand_far):
+                copy(at).wait_send()
+
+    @pl.when(jnp.logical_not(in_middle))
+    def _():
+        pl.semaphore_wait(barrier, 1)
+        for at in range(count):
+            swap(at).start()
+        for at in range(count):
+            swap(at).wait()
+            hand_near(at).wait_recv()
+            hand_far(at).wait_recv()
+
+
+def gather_now(packs, number):
+    if lax.axis_size("row") != 4:
+        return [lax.all_gather(pack, "row", axis=0, tiled=True) for pack in packs]
+    count = len(packs)
+    sent = sum(pack.size for pack in packs) * 2
+    anywhere = pl.BlockSpec(memory_space=pl.ANY)
+    wholes = pl.pallas_call(
+        functools.partial(gather_kernel, count),
+        in_specs=[anywhere] * count,
+        out_specs=[anywhere] * count,
+        out_shape=[jax.ShapeDtypeStruct((4,) + pack.shape, pack.dtype) for pack in packs],
+        scratch_shapes=[pltpu.SemaphoreType.DMA((5, count)), pltpu.SemaphoreType.DMA((5, count))],
+        compiler_params=pltpu.CompilerParams(collective_id=number, has_side_effects=True),
+        cost_estimate=pl.CostEstimate(
+            flops=6 * 9000 * sent, bytes_accessed=6 * sent, transcendentals=0
+        ),
+        name="gather_rows",
+    )(*packs)
+    return [whole.reshape((4 * whole.shape[1],) + whole.shape[2:]) for whole in wholes]
+
+
+def put_own(whole, part):
+    if lax.axis_size("row") != 4:
+        return whole
+    return lax.dynamic_update_slice_in_dim(
+        whole, part, lax.axis_index("row") * part.shape[0], 0
+    )
+
+
 def join_rows(pieces):
     if len(pieces) == 1:
         return pieces[0]
@@ -247,6 +342,18 @@
             copy = pltpu.make_async_copy(pieces[0], weights, sems.at[0])
             copy.start()
             copy.wait()
+        elif count == 2:
+            block = pieces[0].shape[0]
+
+            def block_copy(back):
+                at = pl.multiple_of(lax.rem(z_ref[0] + back, 4) * block, block)
+                source = pieces[1].at[pl.ds(at, block)] if back else pieces[0]
+                return pltpu.make_async_copy(source, weights.at[pl.ds(at, block)], sems.at[back])
+
+            for back in range(4):
+                block_copy(back).start()
+            for back in range(4):
+                block_copy(back).wait()
         else:
             z = z_ref[0]
             block = pieces[0].shape[0]
@@ -417,12 +524,13 @@
     return high, middle, (rest - middle.astype(f32)).astype(bf16)
 
 
-def cuts_of(width):
-    at, cuts = 0, []
-    while at < width:
-        cuts.append((at, min(at + CHUNK, width)))
-        at += CHUNK
-    return cuts
+def cuts_of(width, sizes):
+    cuts, at = [], 0
+    for size in sizes:
+        if at + size < width:
+            cuts.append((at, at + size))
+            at += size
+    return cuts + [(at, width)]
 
 
 def per_device(
@@ -468,16 +576,18 @@
     ).reshape(rows_block, 3 * head_width)
     router_pack = jnp.concatenate([router_weight, score_shared[:, None]], axis=1)
     router_pack = jnp.pad(router_pack, ((0, 0), (0, -router_pack.shape[1] % 128)))
-    qkv_full = join_rows(gather_rows(qkv_pack)[0])
     out_pack = jnp.concatenate([output_weight.T, router_pack], axis=1)
-    out_weights = join_rows(gather_rows(out_pack)[0])
+    qkv_whole, out_whole = gather_now([qkv_pack, out_pack], 0)
+    qkv_full, out_weights = put_own(qkv_whole, qkv_pack), put_own(out_whole, out_pack)
     out_full = out_weights[:, :head_width]
     router_full = out_weights[:, head_width : head_width + experts + 1]
-    shared_cuts = [(None, a, b) for a, b in cuts_of(gate_shared.shape[1])]
+    shared_cuts = [(None, a, b) for a, b in cuts_of(gate_shared.shape[1], (512,))]
     expert_cuts = [
-        (local, a, b) for local in range(local_experts) for a, b in cuts_of(gate_expert.shape[2])
+        (local, a, b)
+        for local in range(local_experts)
+        for a, b in cuts_of(gate_expert.shape[2], (384, 256, 384))
     ]
-    chunks = shared_cuts[-1:] + expert_cuts[:-1] + shared_cuts[:-1] + expert_cuts[-1:]
+    chunks = shared_cuts[-1:] + expert_cuts[:2] + shared_cuts[:-1] + expert_cuts[2:]
 
     def pack(kind, a, b):
         if kind is None:
@@ -487,10 +597,16 @@
         fill = -(b - a) % 128
         return jnp.concatenate([jnp.pad(part, ((0, 0), (0, fill))) for part in parts], axis=1)
 
-    gathered, came = zip(*[gather_rows(pack(*chunk)) for chunk in chunks])
+    packs = [pack(*chunk) for chunk in chunks]
+    chained = lax.axis_size("row") == 4
+    gathered, came = {}, {}
+    early = 3 if chained else len(chunks)
+    for at in range(early):
+        if not (chained and at in (1, 2)):
+            gathered[at], came[at] = gather_rows(packs[at])
 
     def hop(arrivals, at, which):
-        return arrivals[at][which] if 0 <= at < len(arrivals) else ()
+        return arrivals[at][which] if 0 <= at < len(chunks) and at in arrivals else ()
 
     rows_in = lax.all_gather(block_input, "col", axis=1, tiled=True)
     gains = lax.all_gather(jnp.stack([input_gain, mlp_gain]), "col", axis=1, tiled=True).astype(f32)
@@ -498,14 +614,27 @@
     rows_f = rows_in.astype(f32)
     scale_a = lax.rsqrt(jnp.mean(rows_f * rows_f, axis=-1, keepdims=True) + norm_eps)
     normed_a = (rows_f * scale_a * gains[0]).astype(bf16)
-    qkv, context, lse = attend_forward(mm(normed_a, qkv_full), lengths, cosine, sine)
-    attn_part = after(mm_nt(context, out_full).astype(bf16), (cot_rows,), hop(came, 0, 0))
+    raw = after(mm(normed_a, qkv_full), hop(came, 0, 0))
+    qkv, context, lse = attend_forward(raw, lengths, cosine, sine)
+    attn_part = after(mm_nt(context, out_full).astype(bf16), (cot_rows,), hop(came, 0, 1))
     x_share = block_input.astype(f32)
     attn_sum = lax.psum_scatter(attn_part, "col", scatter_dimension=1, tiled=True)
-    attn_sum = after(attn_sum, hop(came, 0, 1), hop(came, 0, 2), hop(came, 1, 0))
+    wait_for = ()
+    if chained:
+        wait_for = gather_now([after(packs[1], (attn_part,))], 1)
+        gathered[1] = (packs[1], wait_for[0])
+    attn_sum = after(attn_sum, wait_for, hop(came, 0, 2))
     stream = x_share + attn_sum.astype(f32)
     gain_b = mlp_gain.astype(f32)
-    scaled = lax.all_gather((stream * gain_b).astype(bf16), "col", axis=1, tiled=True)
+    scaled_share = (stream * gain_b).astype(bf16)
+    scaled = lax.all_gather(scaled_share, "col", axis=1, tiled=True)
+    wait_for = ()
+    if chained:
+        wait_for = gather_now([after(packs[2], (scaled_share,))], 2)
+        gathered[2] = (packs[2], wait_for[0])
+    for at in range(early, len(chunks)):
+        gathered[at], came[at] = gather_rows(after(packs[at], wait_for))
+    scaled = after(scaled, wait_for)
     stream_f = scaled.astype(f32) / gains[1]
     scale_b = lax.rsqrt(jnp.mean(stream_f * stream_f, axis=1, keepdims=True) + norm_eps)
 
@@ -524,26 +653,27 @@
         members[local] = jnp.any(routes == expert, axis=1)
         column = lax.dynamic_index_in_dim(router_probs, expert, 1, False)
         shares[local] = jnp.where(members[local], column, 0.0)
-    dpairs, hiddens, wholes, unit_grads, went = [], [], [], [], []
+    dpairs, hiddens, wholes, unit_grads, went = [], [], [], [], {}
     last = len(chunks) - 1
-    for at, ((kind, a, b), pieces) in enumerate(zip(chunks, gathered)):
+    for at, (kind, a, b) in enumerate(chunks):
+        pieces = gathered[at]
         coef = jnp.concatenate([scale_b, shares[kind][:, None]], axis=1)
-        if at == 0:
-            coef = after(coef, hop(came, 1, 1), hop(came, 1, 2))
-        elif at == 1:
-            coef = after(coef, hop(came, 2, 0))
-        else:
+        if at == 1:
+            coef = after(coef, hop(came, 3, 0))
+        elif at == 2:
+            coef = after(coef, hop(came, 3, 1), hop(came, 4, 0), hop(went, 0, 0))
+        elif at > 2:
             coef = after(
                 coef,
                 hop(came, at + 1, 0),
+                hop(came, at + 1, 1),
                 hop(went, at - 2, 0),
                 hop(went, at - 3, 1),
                 hop(went, at - 4, 2),
             )
         if at == last:
             dscaled_early = joint_back(dpairs, wholes, 0, f32)
-            moe_early = joint_back(hiddens, wholes, 2, f32)
-            coef = after(coef, (dscaled_early, moe_early))
+            coef = after(coef, (dscaled_early,))
         dpair, hidden, sums, grads, whole = expert_chunk(pieces, scaled, cot_rows, coef)
         dots[kind] = dots.get(kind, 0.0) + sums[:, 0]
         inner = inner + sums[:, 1]
@@ -552,9 +682,9 @@
         wholes.append(whole)
         reduced, arrivals = reduce_rows(grads)
         unit_grads.append(reduced)
-        went.append(arrivals)
+        went[at] = arrivals
     dscaled_part = joint_back([dpair], [whole], 0, bf16, dscaled_early)
-    moe_part = joint_back([hidden], [whole], 2, bf16, moe_early)
+    moe_part = joint_back(hiddens, wholes, 2, bf16)
 
     named = [jnp.where(members[local], dots[local], 0.0) for local in range(local_experts)]
     table = lax.all_gather(jnp.stack(named + [dots[None], inner]), "col", axis=0)
@@ -585,10 +715,11 @@
     dstream = cot_share + gain_b * dscaled - stream * (scale_b * scale_b * inner[:, None] / width)
     gain_b_grad = jnp.sum(dscaled * stream, axis=0)
 
-    dattn = lax.all_gather(dstream.astype(bf16), "col", axis=1, tiled=True)
+    dstream_low = dstream.astype(bf16)
+    dattn = lax.all_gather(dstream_low, "col", axis=1, tiled=True)
     dattn = after(dattn, hop(went, last - 2, 2), hop(went, last - 1, 2), hop(went, last, 1))
     moe_share = lax.psum_scatter(
-        after(moe_part, (dattn,)), "col", scatter_dimension=1, tiled=True
+        after(moe_part, (dstream_low,)), "col", scatter_dimension=1, tiled=True
     ).astype(f32)
     block_output = (stream + moe_share).astype(bf16)
     out_grad, _ = reduce_rows(mm_tn(dattn, context).astype(bf16))
@@ -596,9 +727,8 @@
     dqkv, inner_a = attend_backward(qkv, dcontext, lse, lengths, cosine, sine)
     inner_a = lax.psum(inner_a[:, 0], "col")[:, None]
     qkv_grad, _ = reduce_rows(mm_tn(normed_a, dqkv).astype(bf16))
-    dnormed_sum = lax.psum_scatter(
-        mm_nt(dqkv, qkv_full).astype(bf16), "col", scatter_dimension=1, tiled=True
-    )
+    dnormed_part = after(mm_nt(dqkv, qkv_full).astype(bf16), (moe_share,))
+    dnormed_sum = lax.psum_scatter(dnormed_part, "col", scatter_dimension=1, tiled=True)
     dnormed_a = after(dnormed_sum, (inner_a,), hop(went, last, 2)).astype(f32)
     gain_a_share = input_gain.astype(f32)
     dinput = dstream + scale_a * gain_a_share * dnormed_a

time: 1250 us -> 1220 us (0.976)
  waiting for transfers between devices: 461 us -> 168 us
  Pallas kernels: 315 us -> 571 us
    pallas_call x0 -> x3, Pallas kernels: none -> 241 us  [gather_now(): pl.pallas_call(functools.partial(gather_kernel, count), in_specs=[anywher...]
    ppermute x7 -> x4, waiting for transfers between devices: 124 us -> 0.01 us  [gather_rows(): far_out = lax.ppermute(far_mid, 'row', outward)]
    ppermute x7 -> x4, waiting for transfers between devices: 109 us -> 8.67 us  [gather_rows(): near_out = lax.ppermute(near_mid, 'row', outward)]
    all_gather x2, waiting for transfers between devices: 38.1 us -> 1.1 us  [the longest x1 1.1 us: per_device(): dattn = lax.all_gather(dstream_low, 'col', axis=1, tiled=True)]
    ppermute x7 -> x8, starting transfers between devices: 24.9 us -> 56.6 us  [reduce_rows(): near_in = lax.ppermute(block(near), 'row', inward)]
    ppermute x7 -> x4, starting transfers between devices: 39.5 us -> 8.14 us  [gather_rows(): partner = lax.ppermute(part, 'row', [(0, 1), (1, 0), (2, 3), (3, 2)])]
    ppermute x7 -> x8, waiting for transfers between devices: 53.8 us -> 31.8 us  [reduce_rows(): near_in = lax.ppermute(block(near), 'row', inward)]
    pallas_call x5 -> x6, Pallas kernels: 183 us -> 204 us  [expert_chunk(): pl.pallas_call(functools.partial(expert_kernel, size, steps, count), grid...]
  transfers between devices with their start and end apart: 79 -> 69, of which waited for: 28 -> 15; matrix products, arithmetic and copies ran while one was open for 19% -> 19% of each run, Pallas kernels for 21% -> 43%
where the time goes in v5:
time: 1220 us; the launch traced here: 1210 us
  Pallas kernels  571 us (47%)
  waiting for transfers between devices  168 us (14%)
  starting transfers between devices  158 us (13%)
  other arithmetic  110 us (9%)
  local copies, waits for them, and re-layouts  84.3 us (7%)
  matrix products  57 us (5%)
  blocking collectives  42.8 us (4%)
  between operations  15.9 us (1%)
    pallas_call x3, Pallas kernels, gather_now(): pl.pallas_call(functools.partial(gather_kernel, count), in_specs=[anywher...  241 us
    pallas_call x6, Pallas kernels, expert_chunk(): pl.pallas_call(functools.partial(expert_kernel, size, steps, count), grid...  204 us
    pallas_call x3, Pallas kernels, joint_back(): pl.pallas_call(functools.partial(joint_kernel, len(lefts), len(base) > 0)...  84.3 us
    ppermute x8, starting transfers between devices, reduce_rows(): near_in = lax.ppermute(block(near), 'row', inward)  56.6 us
    ppermute x8, waiting for transfers between devices, reduce_rows(): far_in = lax.ppermute(block(far), 'row', inward)  52.8 us
    ppermute x8, waiting for transfers between devices, reduce_rows(): lax.ppermute(block(partner, far_sum).astype(bf16), 'row', [(0, 1), (1, 0)...  47 us
    unnamed x193, local copies, waits for them, and re-layouts  32 us
    ppermute x8, waiting for transfers between devices, reduce_rows(): near_in = lax.ppermute(block(near), 'row', inward)  31.8 us
  transfers between devices with their start and end apart: 69, of which 15 were waited for; matrix products, arithmetic and copies ran while one was open for 19% of the time, Pallas kernels for 43%

profile of v5, /device:TPU:0, one launch (start us, length us, event | category | flops | bytes accessed | tf_op | source)
XLA Modules:
  0.0 1206.0 jit_solution(2233653041534243805)
XLA Ops:
  18.9 90.5 %gather_rows.3 = (bf16[4,512,768]{2,1,0:T(8,128)(2,1)}, bf16[4,512,384]{2,1,0:T(8,128)(2,1)}) custom-call(bf16[512,768]{1,0:T(8,128)(2,1)} %copy.96.refs_0_, bf16[512,384]{1,0:T(8,128)(2,1)} %copy-done.36), custom_call_target="tpu_custom_call" | custom-call | flops 63700992000 | bytes 7077888 | tf_op jit(solution)/shard_map/gather_rows/pallas_call | solution.py:263
  112.4 8.9 all_gather.22
  136.4 10.5 fusion.4.raw_ref
  146.9 12.7 %attend_forward.1 = (bf16[2048,768]{1,0:T(8,128)(2,1)}, bf16[2048,256]{1,0:T(8,128)(2,1)}, f32[2048,256]{1,0:T(8,128)}) custom-call(s32[2]{0:T(128)} %dynamic_slice.122.length_ref, f32[2048,768]{1,0:T(8,128)} %fusion.4.raw_ref, f32[1024,128]{1,0:T(8,128)} %pad_maximum_fusion.9.cos_ref, f32[1024,128]{1,0:T(8,128)} %pad_maximum_fusion.10.sin_ref), custom_call_target="tpu_custom_call" | custom-call | flops 1610612736 | bytes 12582912 | tf_op jit(solution)/shard_map/attend_forward/pallas_call | solution.py:81
  175.5 97.9 %gather_rows.4 = bf16[4,512,1152]{2,1,0:T(8,128)(2,1)} custom-call(bf16[512,1152]{1,0:T(8,128)(2,1)} %pad_maximum_fusion.4.refs_0_), custom_call_target="tpu_custom_call" | custom-call | flops 63700992000 | bytes 7077888 | tf_op jit(solution)/shard_map/gather_rows/pallas_call | solution.py:263
  287.2 53.0 %gather_rows.5 = bf16[4,512,768]{2,1,0:T(8,128)(2,1)} custom-call(bf16[512,768]{1,0:T(8,128)(2,1)} %pad_maximum_fusion.8.refs_0_), custom_call_target="tpu_custom_call" | custom-call | flops 42467328000 | bytes 4718592 | tf_op jit(solution)/shard_map/gather_rows/pallas_call | solution.py:263
  355.5 24.2 %collective-permute-done.5.refs_1_ = bf16[512,1536]{1,0:T(8,128)(2,1)} collective-permute-done((bf16[512,1536]{1,0:T(8,128)(2,1)}, bf16[512,1536]{1,0:T(8,128)(2,1)}, u32[]{:S(2)}, u32[]{:S(2)}) %collective-permute-start.5) | collective-permute-done | bytes 1572896 | tf_op jit(solution)/shard_map/ppermute | solution.py:175
  394.2 27.9 %expert_chunk.6 = (bf16[2048,512]{1,0:T(8,128)(2,1)}, bf16[2048,256]{1,0:T(8,128)(2,1)}, f32[2048,2]{1,0:T(8,128)}, bf16[2048,768]{1,0:T(8,128)(2,1)}, bf16[2048,768]{1,0:T(8,128)(2,1)}) custom-call(s32[1]{0:T(128)} %bitcast.14.z_ref, bf16[512,768]{1,0:T(8,128)(2,1)} %copy-done.45, bf16[512,768]{1,0:T(8,128)(2,1)} %collective-permute-done.refs_1_, ...), custom_call_target="tpu_custom_call" | custom-call | flops 12884901888 | bytes 46137344 | tf_op jit(solution)/shard_map/expert_chunk/pallas_call | solution.py:441
  432.5 36.2 %expert_chunk.7 = (bf16[2048,768]{1,0:T(8,128)(2,1)}, bf16[2048,384]{1,0:T(8,128)(2,1)}, f32[2048,2]{1,0:T(8,128)}, bf16[2048,1152]{1,0:T(8,128)(2,1)}, bf16[2048,1152]{1,0:T(8,128)(2,1)}) custom-call(s32[1]{0:T(128)} %bitcast.14.z_ref, bf16[512,1152]{1,0:T(8,128)(2,1)} %pad_maximum_fusion.4.refs_0_, bf16[2048,1152]{1,0:T(8,128)(2,1)} %bitcast.126, ...), custom_call_target="tpu_custom_call" | custom-call | flops 19327352832 | bytes 52428800 | tf_op jit(solution)/shard_map/expert_chunk/pallas_call | solution.py:441
  484.2 27.9 %expert_chunk.8 = (bf16[2048,512]{1,0:T(8,128)(2,1)}, bf16[2048,256]{1,0:T(8,128)(2,1)}, f32[2048,2]{1,0:T(8,128)}, bf16[2048,768]{1,0:T(8,128)(2,1)}, bf16[2048,768]{1,0:T(8,128)(2,1)}) custom-call(s32[1]{0:T(128)} %bitcast.14.z_ref, bf16[512,768]{1,0:T(8,128)(2,1)} %pad_maximum_fusion.8.refs_0_, bf16[2048,768]{1,0:T(8,128)(2,1)} %bitcast.127, ...), custom_call_target="tpu_custom_call" | custom-call | flops 12884901888 | bytes 46137344 | tf_op jit(solution)/shard_map/expert_chunk/pallas_call | solution.py:441
  524.9 15.9 %collective-permute-done.16 = bf16[512,1152]{1,0:T(8,128)(2,1)} collective-permute-done((bf16[512,1152]{1,0:T(8,128)(2,1)S(1)}, bf16[512,1152]{1,0:T(8,128)(2,1)}, u32[]{:S(2)}, u32[]{:S(2)}) %collective-permute-start.16) | collective-permute-done | bytes 1179680 | tf_op jit(solution)/shard_map/ppermute | solution.py:315
  546.9 8.7 collective-permute-done.15.refs_4_
  560.7 28.3 %collective-permute-start.26 = (bf16[512,768]{1,0:T(8,128)(2,1)S(1)}, bf16[512,768]{1,0:T(8,128)(2,1)S(1)}, u32[]{:S(2)}, u32[]{:S(2)}) collective-permute-start(bf16[512,768]{1,0:T(8,128)(2,1)S(1)} %get-tuple-element.201), channel_id=1, source_target_pairs={{0,8},{24,16},{1,9},{25,17},{2,10},{26,18},{3,11},{27,19},{4,12},{... | collective-permute-start | bytes 2359304 | tf_op jit(solution)/shard_map/ppermute | solution.py:316
  592.1 39.5 %expert_chunk.9 = (bf16[2048,1024]{1,0:T(8,128)(2,1)}, bf16[2048,512]{1,0:T(8,128)(2,1)}, f32[2048,2]{1,0:T(8,128)}, bf16[2048,1536]{1,0:T(8,128)(2,1)}, bf16[2048,1536]{1,0:T(8,128)(2,1)}) custom-call(s32[1]{0:T(128)} %bitcast.14.z_ref, bf16[512,1536]{1,0:T(8,128)(2,1)} %pad_maximum_fusion.refs_0_, bf16[512,1536]{1,0:T(8,128)(2,1)} %collective-permute-done.5.refs_1_, ...), custom_call_target="tpu_custom_call" | custom-call | flops 25769803776 | bytes 58720256 | tf_op jit(solution)/shard_map/expert_chunk/pallas_call | solution.py:441
  656.2 8.5 collective-permute-done.29
  676.4 36.2 %expert_chunk.10 = (bf16[2048,768]{1,0:T(8,128)(2,1)}, bf16[2048,384]{1,0:T(8,128)(2,1)}, f32[2048,2]{1,0:T(8,128)}, bf16[2048,1152]{1,0:T(8,128)(2,1)}, bf16[2048,1152]{1,0:T(8,128)(2,1)}) custom-call(s32[1]{0:T(128)} %bitcast.14.z_ref, bf16[512,1152]{1,0:T(8,128)(2,1)} %pad_maximum_fusion.5.refs_0_, bf16[512,1152]{1,0:T(8,128)(2,1)} %collective-permute-done.9.refs_1_, ...), custom_call_target="tpu_custom_call" | custom-call | flops 19327352832 | bytes 52428800 | tf_op jit(solution)/shard_map/expert_chunk/pallas_call | solution.py:441
  712.8 39.6 %joint_back.3.refs_2_ = f32[2048,2048]{1,0:T(8,128)} custom-call(bf16[2048,512]{1,0:T(8,128)(2,1)} %get-tuple-element.99.refs_0_, bf16[2048,768]{1,0:T(8,128)(2,1)} %get-tuple-element.100.refs_1_, bf16[2048,512]{1,0:T(8,128)(2,1)} %get-tuple-element.101.refs_2_, bf16[2048,1024]{1,0:T(8,128)(2,1)} %get-tuple-element.102.refs_3_, ...), custom_call_target="tpu_custom_call" | custom-call | flops 30064771072 | bytes 46137344 | tf_op jit(solution)/shard_map/joint_back/pallas_call | solution.py:500
  753.8 36.2 %expert_chunk.11 = (bf16[2048,768]{1,0:T(8,128)(2,1)}, bf16[2048,384]{1,0:T(8,128)(2,1)}, f32[2048,2]{1,0:T(8,128)}, bf16[2048,1152]{1,0:T(8,128)(2,1)}, bf16[2048,1152]{1,0:T(8,128)(2,1)}) custom-call(s32[1]{0:T(128)} %bitcast.14.z_ref, bf16[512,1152]{1,0:T(8,128)(2,1)} %pad_maximum_fusion.6.refs_0_, bf16[512,1152]{1,0:T(8,128)(2,1)} %collective-permute-done.21.refs_1_, ...), custom_call_target="tpu_custom_call" | custom-call | flops 19327352832 | bytes 52428800 | tf_op jit(solution)/shard_map/expert_chunk/pallas_call | solution.py:441
  790.0 15.7 %joint_back.5 = bf16[2048,2048]{1,0:T(8,128)(2,1)} custom-call(bf16[2048,768]{1,0:T(8,128)(2,1)} %get-tuple-element.118.refs_0_, bf16[2048,1152]{1,0:T(8,128)(2,1)} %get-tuple-element.111.refs_11_.refs_1_, f32[2048,2048]{1,0:T(8,128)} %joint_back.3.refs_2_), custom_call_target="tpu_custom_call" | custom-call | flops 6442450944 | bytes 23068672 | tf_op jit(solution)/shard_map/joint_back/pallas_call | solution.py:500
  829.1 10.3 all-gather.1
  848.8 17.6 %collective-permute-done.36 = bf16[512,1152]{1,0:T(8,128)(2,1)S(1)} collective-permute-done((bf16[512,1152]{1,0:T(8,128)(2,1)S(1)}, bf16[512,1152]{1,0:T(8,128)(2,1)S(1)}, u32[]{:S(2)}, u32[]{:S(2)}) %collective-permute-start.36) | collective-permute-done | bytes 1179680 | tf_op jit(solution)/shard_map/ppermute | solution.py:315
  874.9 16.8 %collective-permute-done.44 = bf16[512,1152]{1,0:T(8,128)(2,1)S(1)} collective-permute-done((bf16[512,1152]{1,0:T(8,128)(2,1)S(1)}, bf16[512,1152]{1,0:T(8,128)(2,1)S(1)}, u32[]{:S(2)}, u32[]{:S(2)}) %collective-permute-start.44) | collective-permute-done | bytes 1179680 | tf_op jit(solution)/shard_map/ppermute | solution.py:316
  893.4 29.0 %joint_back.4 = bf16[2048,2048]{1,0:T(8,128)(2,1)} custom-call(bf16[2048,256]{1,0:T(8,128)(2,1)} %get-tuple-element.82.refs_0_, bf16[2048,384]{1,0:T(8,128)(2,1)} %get-tuple-element.85.refs_1_, bf16[2048,256]{1,0:T(8,128)(2,1)} %get-tuple-element.89.refs_2_, bf16[2048,512]{1,0:T(8,128)(2,1)} %get-tuple-element.92.refs_3_, ...), custom_call_target="tpu_custom_call" | custom-call | flops 18253611008 | bytes 34603008 | tf_op jit(solution)/shard_map/joint_back/pallas_call | solution.py:500
  952.1 31.3 %collective-permute-done.46 = bf16[512,1152]{1,0:T(8,128)(2,1)} collective-permute-done((bf16[512,1152]{1,0:T(8,128)(2,1)}, bf16[512,1152]{1,0:T(8,128)(2,1)}, u32[]{:S(2)}, u32[]{:S(2)}) %collective-permute-start.46) | collective-permute-done | bytes 1179680 | tf_op jit(solution)/shard_map/ppermute | solution.py:319
  991.5 28.2 %attend_backward.1 = (bf16[2048,768]{1,0:T(8,128)(2,1)}, f32[2048,1]{1,0:T(8,128)}) custom-call(s32[2]{0:T(128)} %dynamic_slice.122.length_ref, bf16[2048,768]{1,0:T(8,128)(2,1)} %get-tuple-element.123.qkv_ref, bf16[2048,256]{1,0:T(8,128)(2,1)} %convolution_convert_fusion.4.dcontext_ref, f32[2048,256]{1,0:T(8,128)} %get-tuple-element.125.lse_ref, ...), custom_call_target="tpu_custom_call" | custom-call | flops 4294967296 | bytes 12582912 | tf_op jit(solution)/shard_map/attend_backward/pallas_call | solution.py:151
  1019.7 11.3 convolution_convert_fusion
  1068.9 7.2 collective-permute-done.49
  1081.9 10.4 convolution_convert_fusion.2
  1104.8 14.7 %collective-permute-done.57 = bf16[512,256]{1,0:T(8,128)(2,1)S(1)} collective-permute-done((bf16[512,256]{1,0:T(8,128)(2,1)S(1)}, bf16[512,256]{1,0:T(8,128)(2,1)S(1)}, u32[]{:S(2)}, u32[]{:S(2)}) %collective-permute-start.57) | collective-permute-done | bytes 262176 | tf_op jit(solution)/shard_map/ppermute | solution.py:315
  1127.4 7.5 collective-permute-start.59
  1157.9 12.5 %psum.21 = f32[2048]{0:T(1024)S(1)} all-reduce(f32[2048]{0:T(1024)S(1)} %reduce.5), channel_id=1, replica_groups=mesh['row'=4,'col'=8] {'col'}, use_global_device_ids=true, to_apply=%region_13.14 | all-reduce | flops 2048 | bytes 16384 | tf_op jit(solution)/shard_map/psum | solution.py:728
  1188.1 11.2 all-reduce.4
  (477 shorter events, 363.7 us)
Async XLA Ops:
  7.2 122.7 %all-gather.7.cloned.1.call-start = ((), (), s32[]{:S(2)}) async-start(), calls=%async_computation.5 | async-start | bytes 9437184 | tf_op jit(solution)/shard_map/all_gather | solution.py:611
  8.0 158.4 %all-gather.9.cloned.1.call-start = ((), (), s32[]{:S(2)}) async-start(), calls=%async_computation.6 | async-start | bytes 9437184 | tf_op jit(solution)/shard_map/all_gather | solution.py:613
  8.8 264.6 %reduce-scatter.6.cloned.1.call-start = ((), (), s32[]{:S(2)}) async-start(), calls=%async_computation.7 | async-start | bytes 9437184 | tf_op jit(solution)/shard_map/reduce_scatter | solution.py:621
  9.4 117.1 %collective-permute-start.1 = (bf16[512,768]{1,0:T(8,128)(2,1)S(1)}, bf16[512,768]{1,0:T(8,128)(2,1)}, u32[]{:S(2)}, u32[]{:S(2)}) collective-permute-start(bf16[512,768]{1,0:T(8,128)(2,1)S(1)} %fusion.18.refs_0_), channel_id=1, source_target_pairs={{8,16},{16,8},{9,17},{17,9},{10,18},{18,10},{11,19},{19,11},{12,20... | collective-permute-start | bytes 2359304 | tf_op jit(solution)/shard_map/ppermute | solution.py:177
  11.0 116.8 %collective-permute-start = (bf16[512,768]{1,0:T(8,128)(2,1)S(1)}, bf16[512,768]{1,0:T(8,128)(2,1)}, u32[]{:S(2)}, u32[]{:S(2)}) collective-permute-start(bf16[512,768]{1,0:T(8,128)(2,1)S(1)} %fusion.18.refs_0_), channel_id=1, source_target_pairs={{0,8},{8,0},{16,24},{24,16},{1,9},{9,1},{17,25},{25,17},{2,10},{10... | collective-permute-start | bytes 2359304 | tf_op jit(solution)/shard_map/ppermute | solution.py:175
  167.3 214.3 %all-gather.11.cloned.1.call-start = ((), (), s32[]{:S(2)}) async-start(), calls=%async_computation.8 | async-start | bytes 9437184 | tf_op jit(solution)/shard_map/all_gather | solution.py:630
  174.0 99.3 %collective-permute-start.4 = (bf16[512,768]{1,0:T(8,128)(2,1)}, bf16[512,768]{1,0:T(8,128)(2,1)}, u32[]{:S(2)}, u32[]{:S(2)}) collective-permute-start(bf16[512,768]{1,0:T(8,128)(2,1)} %collective-permute-done.2.refs_3_), channel_id=1, source_target_pairs={{8,0},{16,24},{9,1},{17,25},{10,2},{18,26},{11,3},{19,27},{12,4},{... | collective-permute-start | bytes 2359304 | tf_op jit(solution)/shard_map/ppermute | solution.py:180
  276.0 646.5 %reduce-scatter.8.cloned.1.call-start = ((), (), s32[]{:S(2)}) async-start(), calls=%async_computation.9 | async-start | bytes 9437184 | tf_op jit(solution)/shard_map/reduce_scatter | solution.py:705
  349.8 80.6 %collective-permute-start.10 = (bf16[512,1152]{1,0:T(8,128)(2,1)}, bf16[512,1152]{1,0:T(8,128)(2,1)}, u32[]{:S(2)}, u32[]{:S(2)}) collective-permute-start(bf16[512,1152]{1,0:T(8,128)(2,1)} %pad_maximum_fusion.5.refs_0_), channel_id=1, source_target_pairs={{8,16},{16,8},{9,17},{17,9},{10,18},{18,10},{11,19},{19,11},{12,20... | collective-permute-start | bytes 3538952 | tf_op jit(solution)/shard_map/ppermute | solution.py:177
  351.6 119.0 %collective-permute-start.9 = (bf16[512,1152]{1,0:T(8,128)(2,1)}, bf16[512,1152]{1,0:T(8,128)(2,1)}, u32[]{:S(2)}, u32[]{:S(2)}) collective-permute-start(bf16[512,1152]{1,0:T(8,128)(2,1)} %pad_maximum_fusion.5.refs_0_), channel_id=1, source_target_pairs={{0,8},{8,0},{16,24},{24,16},{1,9},{9,1},{17,25},{25,17},{2,10},{10... | collective-permute-start | bytes 3538952 | tf_op jit(solution)/shard_map/ppermute | solution.py:175
  354.2 118.0 %collective-permute-start.8 = (bf16[512,1536]{1,0:T(8,128)(2,1)}, bf16[512,1536]{1,0:T(8,128)(2,1)}, u32[]{:S(2)}, u32[]{:S(2)}) collective-permute-start(bf16[512,1536]{1,0:T(8,128)(2,1)} %collective-permute-done.6.refs_2_), channel_id=1, source_target_pairs={{8,0},{16,24},{9,1},{17,25},{10,2},{18,26},{11,3},{19,27},{12,4},{... | collective-permute-start | bytes 4718600 | tf_op jit(solution)/shard_map/ppermute | solution.py:179
  379.8 92.5 %collective-permute-start.7 = (bf16[512,1536]{1,0:T(8,128)(2,1)}, bf16[512,1536]{1,0:T(8,128)(2,1)}, u32[]{:S(2)}, u32[]{:S(2)}) collective-permute-start(bf16[512,1536]{1,0:T(8,128)(2,1)} %collective-permute-done.5.refs_1_), channel_id=1, source_target_pairs={{8,16},{16,8},{9,17},{17,9},{10,18},{18,10},{11,19},{19,11},{12,20... | collective-permute-start | bytes 4718600 | tf_op jit(solution)/shard_map/ppermute | solution.py:178
  472.3 118.1 %collective-permute-start.13 = (bf16[512,1536]{1,0:T(8,128)(2,1)}, bf16[512,1536]{1,0:T(8,128)(2,1)}, u32[]{:S(2)}, u32[]{:S(2)}) collective-permute-start(bf16[512,1536]{1,0:T(8,128)(2,1)} %collective-permute-done.7.refs_3_), channel_id=1, source_target_pairs={{8,0},{16,24},{9,1},{17,25},{10,2},{18,26},{11,3},{19,27},{12,4},{... | collective-permute-start | bytes 4718600 | tf_op jit(solution)/shard_map/ppermute | solution.py:180
  480.3 60.5 %collective-permute-start.16 = (bf16[512,1152]{1,0:T(8,128)(2,1)S(1)}, bf16[512,1152]{1,0:T(8,128)(2,1)}, u32[]{:S(2)}, u32[]{:S(2)}) collective-permute-start(bf16[512,1152]{1,0:T(8,128)(2,1)S(1)} %get-tuple-element.195), channel_id=1, source_target_pairs={{0,8},{24,16},{1,9},{25,17},{2,10},{26,18},{3,11},{27,19},{4,12},{... | collective-permute-start | bytes 3538952 | tf_op jit(solution)/shard_map/ppermute | solution.py:315
  555.5 97.6 %collective-permute-start.24 = (bf16[512,1152]{1,0:T(8,128)(2,1)}, bf16[512,1152]{1,0:T(8,128)(2,1)}, u32[]{:S(2)}, u32[]{:S(2)}) collective-permute-start(bf16[512,1152]{1,0:T(8,128)(2,1)} %collective-permute-done.22.refs_2_), channel_id=1, source_target_pairs={{8,0},{16,24},{9,1},{17,25},{10,2},{18,26},{11,3},{19,27},{12,4},{... | collective-permute-start | bytes 3538952 | tf_op jit(solution)/shard_map/ppermute | solution.py:179
  556.8 78.8 %collective-permute-start.23 = (bf16[512,1152]{1,0:T(8,128)(2,1)}, bf16[512,1152]{1,0:T(8,128)(2,1)}, u32[]{:S(2)}, u32[]{:S(2)}) collective-permute-start(bf16[512,1152]{1,0:T(8,128)(2,1)} %collective-permute-done.21.refs_1_), channel_id=1, source_target_pairs={{8,16},{16,8},{9,17},{17,9},{10,18},{18,10},{11,19},{19,11},{12,20... | collective-permute-start | bytes 3538952 | tf_op jit(solution)/shard_map/ppermute | solution.py:178
  558.5 115.1 %collective-permute-start.20 = (bf16[512,1152]{1,0:T(8,128)(2,1)}, bf16[512,1152]{1,0:T(8,128)(2,1)}, u32[]{:S(2)}, u32[]{:S(2)}) collective-permute-start(bf16[512,1152]{1,0:T(8,128)(2,1)} %collective-permute-done.14.refs_3_), channel_id=1, source_target_pairs={{8,0},{16,24},{9,1},{17,25},{10,2},{18,26},{11,3},{19,27},{12,4},{... | collective-permute-start | bytes 3538952 | tf_op jit(solution)/shard_map/ppermute | solution.py:180
  560.7 70.9 %collective-permute-start.26 = (bf16[512,768]{1,0:T(8,128)(2,1)S(1)}, bf16[512,768]{1,0:T(8,128)(2,1)S(1)}, u32[]{:S(2)}, u32[]{:S(2)}) collective-permute-start(bf16[512,768]{1,0:T(8,128)(2,1)S(1)} %get-tuple-element.201), channel_id=1, source_target_pairs={{0,8},{24,16},{1,9},{25,17},{2,10},{26,18},{3,11},{27,19},{4,12},{... | collective-permute-start | bytes 2359304 | tf_op jit(solution)/shard_map/ppermute | solution.py:316
  590.4 58.5 %collective-permute-start.27 = (bf16[512,1152]{1,0:T(8,128)(2,1)}, bf16[512,1152]{1,0:T(8,128)(2,1)}, u32[]{:S(2)}, u32[]{:S(2)}) collective-permute-start(bf16[512,1152]{1,0:T(8,128)(2,1)} %add_convert_fusion.11), channel_id=1, source_target_pairs={{8,16},{16,8},{9,17},{17,9},{10,18},{18,10},{11,19},{19,11},{12,20... | collective-permute-start | bytes 3538952 | tf_op jit(solution)/shard_map/ppermute | solution.py:317
  648.9 104.9 %collective-permute-start.30 = (bf16[512,1152]{1,0:T(8,128)(2,1)}, bf16[512,1152]{1,0:T(8,128)(2,1)}, u32[]{:S(2)}, u32[]{:S(2)}) collective-permute-start(bf16[512,1152]{1,0:T(8,128)(2,1)} %collective-permute-done.23.refs_3_), channel_id=1, source_target_pairs={{8,0},{16,24},{9,1},{17,25},{10,2},{18,26},{11,3},{19,27},{12,4},{... | collective-permute-start | bytes 3538952 | tf_op jit(solution)/shard_map/ppermute | solution.py:180
  653.1 59.6 %collective-permute-start.34 = (bf16[512,768]{1,0:T(8,128)(2,1)}, bf16[512,768]{1,0:T(8,128)(2,1)}, u32[]{:S(2)}, u32[]{:S(2)}) collective-permute-start(bf16[512,768]{1,0:T(8,128)(2,1)} %add_convert_fusion.17), channel_id=1, source_target_pairs={{8,16},{16,8},{9,17},{17,9},{10,18},{18,10},{11,19},{19,11},{12,20... | collective-permute-start | bytes 2359304 | tf_op jit(solution)/shard_map/ppermute | solution.py:318
  654.6 97.7 %collective-permute-start.33 = (bf16[512,768]{1,0:T(8,128)(2,1)}, bf16[512,768]{1,0:T(8,128)(2,1)}, u32[]{:S(2)}, u32[]{:S(2)}) collective-permute-start(bf16[512,768]{1,0:T(8,128)(2,1)} %add_convert_fusion.18), channel_id=1, source_target_pairs={{8,16},{16,8},{9,17},{17,9},{10,18},{18,10},{11,19},{19,11},{12,20... | collective-permute-start | bytes 2359304 | tf_op jit(solution)/shard_map/ppermute | solution.py:317
  665.6 86.8 %collective-permute-start.32 = (bf16[512,1536]{1,0:T(8,128)(2,1)S(1)}, bf16[512,1536]{1,0:T(8,128)(2,1)}, u32[]{:S(2)}, u32[]{:S(2)}) collective-permute-start(bf16[512,1536]{1,0:T(8,128)(2,1)S(1)} %get-tuple-element.188), channel_id=1, source_target_pairs={{0,8},{24,16},{1,9},{25,17},{2,10},{26,18},{3,11},{27,19},{4,12},{... | collective-permute-start | bytes 4718600 | tf_op jit(solution)/shard_map/ppermute | solution.py:316
  673.6 78.8 %collective-permute-start.31 = (bf16[512,1536]{1,0:T(8,128)(2,1)S(1)}, bf16[512,1536]{1,0:T(8,128)(2,1)}, u32[]{:S(2)}, u32[]{:S(2)}) collective-permute-start(bf16[512,1536]{1,0:T(8,128)(2,1)S(1)} %get-tuple-element.189), channel_id=1, source_target_pairs={{0,8},{24,16},{1,9},{25,17},{2,10},{26,18},{3,11},{27,19},{4,12},{... | collective-permute-start | bytes 4718600 | tf_op jit(solution)/shard_map/ppermute | solution.py:315
  805.7 178.8 %all-gather.13.cloned.1.call-start = ((), (), s32[]{:S(2)}) async-start(), calls=%async_computation.11 | async-start | bytes 9437184 | tf_op jit(solution)/shard_map/all_gather | solution.py:719
  808.2 64.9 %collective-permute-start.40 = (bf16[512,768]{1,0:T(8,128)(2,1)S(1)}, bf16[512,768]{1,0:T(8,128)(2,1)S(1)}, u32[]{:S(2)}, u32[]{:S(2)}) collective-permute-start(bf16[512,768]{1,0:T(8,128)(2,1)S(1)} %add_convert_fusion.16), channel_id=1, source_target_pairs={{0,8},{8,0},{16,24},{24,16},{1,9},{9,1},{17,25},{25,17},{2,10},{10... | collective-permute-start | bytes 2359304 | tf_op jit(solution)/shard_map/ppermute | solution.py:319
  819.2 103.3 %collective-permute-start.39 = (bf16[512,1536]{1,0:T(8,128)(2,1)}, bf16[512,1536]{1,0:T(8,128)(2,1)}, u32[]{:S(2)}, u32[]{:S(2)}) collective-permute-start(bf16[512,1536]{1,0:T(8,128)(2,1)} %add_convert_fusion.1), channel_id=1, source_target_pairs={{8,16},{16,8},{9,17},{17,9},{10,18},{18,10},{11,19},{19,11},{12,20... | collective-permute-start | bytes 4718600 | tf_op jit(solution)/shard_map/ppermute | solution.py:318
  824.5 97.9 %collective-permute-start.38 = (bf16[512,1536]{1,0:T(8,128)(2,1)}, bf16[512,1536]{1,0:T(8,128)(2,1)}, u32[]{:S(2)}, u32[]{:S(2)}) collective-permute-start(bf16[512,1536]{1,0:T(8,128)(2,1)} %add_convert_fusion.2), channel_id=1, source_target_pairs={{8,16},{16,8},{9,17},{17,9},{10,18},{18,10},{11,19},{19,11},{12,20... | collective-permute-start | bytes 4718600 | tf_op jit(solution)/shard_map/ppermute | solution.py:317
  866.4 56.0 %collective-permute-start.43 = (bf16[512,1152]{1,0:T(8,128)(2,1)}, bf16[512,1152]{1,0:T(8,128)(2,1)}, u32[]{:S(2)}, u32[]{:S(2)}) collective-permute-start(bf16[512,1152]{1,0:T(8,128)(2,1)} %get-tuple-element.191), channel_id=1, source_target_pairs={{0,8},{24,16},{1,9},{25,17},{2,10},{26,18},{3,11},{27,19},{4,12},{... | collective-permute-start | bytes 3538952 | tf_op jit(solution)/shard_map/ppermute | solution.py:315
  926.3 115.3 %reduce-scatter.14.cloned.1.call-start = ((), (), s32[]{:S(2)}) async-start(), calls=%async_computation.13 | async-start | bytes 163840 | tf_op jit(solution)/shard_map/reduce_scatter | solution.py:701
  952.1 231.6 %reduce-scatter.12.cloned.1.call-start = ((), (), s32[]{:S(2)}) async-start(), calls=%async_computation.12 | async-start | bytes 9437184 | tf_op jit(solution)/shard_map/reduce_scatter | solution.py:731
  1031.0 152.6 %reduce-scatter.10.cloned.1.call-start = ((), (), s32[]{:S(2)}) async-start(), calls=%async_computation.10 | async-start | bytes 9437184 | tf_op jit(solution)/shard_map/reduce_scatter | solution.py:721
  (130 other events, 2857.1 us)
Sparse Core Ops, SparseCore 0:
  9.9 58.6 all-gather.6
  70.5 55.9 all-gather.8
  166.6 72.4 reduce-scatter.5
  276.1 54.3 all-gather.10
  805.9 71.5 reduce-scatter.7
  926.4 58.0 all-gather.12
  986.8 19.2 reduce-scatter.13
  1031.1 71.2 reduce-scatter.11
  1105.9 71.5 reduce-scatter.9

commit v6 on v5

--- a/solution.py
+++ b/solution.py
@@ -168,18 +168,38 @@
     )(lengths, qkv, dcontext, lse, cosine, sine)
 
 
-def gather_rows(part):
-    n = lax.axis_size("row")
-    if n != 4:
-        return (lax.all_gather(part, "row", axis=0, tiled=True),), ((), (), ())
-    partner = lax.ppermute(part, "row", [(0, 1), (1, 0), (2, 3), (3, 2)])
-    middle, outward = [(1, 2), (2, 1)], [(1, 0), (2, 3)]
-    near_mid = lax.ppermute(part, "row", middle)
-    far_mid = lax.ppermute(partner, "row", middle)
-    near_out = lax.ppermute(near_mid, "row", outward)
-    far_out = lax.ppermute(far_mid, "row", outward)
-    hops = ((partner, near_mid), (far_mid, near_out), (far_out,))
-    return (part, partner, near_mid, far_mid, near_out, far_out), hops
+PAIRS = [(0, 1), (1, 0), (2, 3), (3, 2)]
+MIDDLE = [(1, 2), (2, 1)]
+OUTWARD = [(1, 0), (2, 3)]
+INWARD = [(0, 1), (3, 2)]
+
+
+class Gathered:
+    def __init__(self, part, *groups):
+        self.part = part
+        if lax.axis_size("row") != 4:
+            self.pieces = (lax.all_gather(part, "row", axis=0, tiled=True),)
+            return
+        part = after(part, *groups)
+        self.partner = lax.ppermute(part, "row", PAIRS)
+        self.near_mid = lax.ppermute(part, "row", MIDDLE)
+        self.pieces = None
+
+    def second(self, *groups):
+        if self.pieces is None:
+            self.near_out = lax.ppermute(after(self.near_mid, *groups), "row", OUTWARD)
+            self.far_mid = lax.ppermute(after(self.partner, *groups), "row", MIDDLE)
+            return (self.partner, self.near_mid)
+        return ()
+
+    def third(self, *groups):
+        if self.pieces is None:
+            self.far_out = lax.ppermute(after(self.far_mid, *groups), "row", OUTWARD)
+            self.pieces = (
+                self.part, self.partner, self.near_mid, self.far_mid, self.near_out, self.far_out
+            )
+            return (self.far_mid, self.near_out)
+        return ()
 
 
 def places(z):
@@ -187,71 +207,311 @@
     return z, z + 1 - 2 * lax.rem(z, 2), 2 - pair, 3 - 3 * pair
 
 
-def gather_kernel(count, *refs):
-    packs, wholes, (send_sems, recv_sems) = refs[:count], refs[count : 2 * count], refs[2 * count :]
-    z = lax.axis_index("row")
-    own, partner, near, far = places(z)
-    across = 3 - z
-    in_middle = (z == 1) | (z == 2)
-    barrier = pltpu.get_barrier_semaphore()
-
-    def copy_of(kind, at, source, block, target):
+class RowGather:
+    def __init__(self, packs, wholes, sems):
+        self.packs, self.wholes, (self.send_sems, self.recv_sems) = packs, wholes, sems
+        self.z = lax.axis_index("row")
+        self.own, self.partner, self.near, self.far = places(self.z)
+        self.across = 3 - self.z
+        self.in_middle = (self.z == 1) | (self.z == 2)
+        self.outside = jnp.logical_not(self.in_middle)
+
+    def copy_of(self, kind, at, source, block, target):
         return pltpu.make_async_remote_copy(
             src_ref=source,
-            dst_ref=wholes[at].at[block],
-            send_sem=send_sems.at[kind, at],
-            recv_sem=recv_sems.at[kind, at],
+            dst_ref=self.wholes[at].at[block],
+            send_sem=self.send_sems.at[kind, at],
+            recv_sem=self.recv_sems.at[kind, at],
             device_id={"row": target},
             device_id_type=pl.DeviceIdType.MESH,
         )
 
-    def swap(at):
-        return copy_of(0, at, packs[at], own, partner)
-
-    def swap_middle(at):
-        return copy_of(1, at, packs[at], own, across)
-
-    def second_middle(at):
-        return copy_of(2, at, wholes[at].at[partner], partner, across)
-
-    def hand_near(at):
-        return copy_of(3, at, wholes[at].at[near], near, partner)
-
-    def hand_far(at):
-        return copy_of(4, at, wholes[at].at[far], far, partner)
-
-    pl.semaphore_signal(barrier, inc=1, device_id={"row": partner}, device_id_type=pl.DeviceIdType.MESH)
-
-    @pl.when(in_middle)
-    def _():
-        pl.semaphore_signal(
-            barrier, inc=1, device_id={"row": across}, device_id_type=pl.DeviceIdType.MESH
+    def swap(self, at):
+        return self.copy_of(0, at, self.packs[at], self.own, self.partner)
+
+    def swap_middle(self, at):
+        return self.copy_of(1, at, self.packs[at], self.own, self.across)
+
+    def second_middle(self, at):
+        return self.copy_of(2, at, self.wholes[at].at[self.partner], self.partner, self.across)
+
+    def hand_near(self, at):
+        return self.copy_of(3, at, self.wholes[at].at[self.near], self.near, self.partner)
+
+    def hand_far(self, at):
+        return self.copy_of(4, at, self.wholes[at].at[self.far], self.far, self.partner)
+
+    def greet(self, barrier):
+        signal_to(barrier, {"row": self.partner})
+
+        @pl.when(self.in_middle)
+        def _():
+            signal_to(barrier, {"row": self.across})
+            pl.semaphore_wait(barrier, 2)
+
+        @pl.when(self.outside)
+        def _():
+            pl.semaphore_wait(barrier, 1)
+
+    def begin(self):
+        for at in range(len(self.packs)):
+            @pl.when(self.in_middle)
+            def _():
+                self.swap_middle(at).start()
+
+            self.swap(at).start()
+
+    def hand_on(self, at):
+        @pl.when(self.in_middle)
+        def _():
+            self.swap_middle(at).wait_recv()
+            self.hand_near(at).start()
+            self.swap(at).wait_recv()
+            self.second_middle(at).start()
+
+    def hand_last(self, at):
+        @pl.when(self.in_middle)
+        def _():
+            self.second_middle(at).wait_recv()
+            self.hand_far(at).start()
+
+    def finish(self):
+        for at in range(len(self.packs)):
+            @pl.when(self.in_middle)
+            def _():
+                for copy in (
+                    self.swap,
+                    self.swap_middle,
+                    self.second_middle,
+                    self.hand_near,
+                    self.hand_far,
+                ):
+                    copy(at).wait_send()
+
+            @pl.when(self.outside)
+            def _():
+                self.swap(at).wait()
+                self.hand_near(at).wait_recv()
+                self.hand_far(at).wait_recv()
+
+
+def signal_to(barrier, device):
+    pl.semaphore_signal(barrier, inc=1, device_id=device, device_id_type=pl.DeviceIdType.MESH)
+
+
+def gather_kernel(count, *refs):
+    rows = RowGather(refs[:count], refs[count : 2 * count], refs[2 * count :])
+    rows.greet(pltpu.get_barrier_semaphore())
+    rows.begin()
+    for at in range(count):
+        rows.hand_on(at)
+    for at in range(count):
+        rows.hand_last(at)
+    rows.finish()
+
+
+PIECES = 4
+
+
+def plane_kernel(pointwise, given, made, gather, count, *refs):
+    p_ref, inputs = refs[0], refs[1 : 1 + given]
+    at = 1 + given
+    packs = refs[at : at + count]
+    at += count
+    results = refs[at : at + made]
+    at += made
+    whole_refs = refs[at : at + gather + count]
+    at += gather + count
+    mine, from_core, from_first, summed, from_second, shared, send_sems, recv_sems, local_sems = refs[
+        at : at + 9
+    ]
+    out_ref = whole_refs[0] if gather else None
+    me = lax.axis_index("col")
+    core, x, y = lax.rem(me, 2), lax.rem(me // 2, 2), me // 4
+    core_mate, x_mate, y_mate = me + 1 - 2 * core, me + 2 - 4 * x, me + 4 - 8 * y
+    diagonal = x_mate + 4 - 8 * y
+    size = mine.shape[3]
+    share = mine.shape[4]
+    barrier = pltpu.get_barrier_semaphore()
+    for mate in (core_mate, x_mate, y_mate):
+        signal_to(barrier, {"col": mate})
+    rows = None
+    if count:
+        rows = RowGather(packs, whole_refs[gather:], refs[at + 9 : at + 11])
+        signal_to(barrier, {"row": rows.partner})
+
+        @pl.when(rows.in_middle)
+        def _():
+            signal_to(barrier, {"row": rows.across})
+            pl.semaphore_wait(barrier, 5)
+
+        @pl.when(rows.outside)
+        def _():
+            pl.semaphore_wait(barrier, 4)
+
+        rows.begin()
+    else:
+        pl.semaphore_wait(barrier, 3)
+
+    def remote(kind, i, source, target, mate):
+        return pltpu.make_async_remote_copy(
+            src_ref=source,
+            dst_ref=target,
+            send_sem=send_sems.at[kind, i],
+            recv_sem=recv_sems.at[kind, i],
+            device_id={"col": mate},
+            device_id_type=pl.DeviceIdType.MESH,
         )
-        pl.semaphore_wait(barrier, 2)
+
+    def x_first(i):
+        return i < PIECES // 2
+
+    def span(i):
+        return pl.ds(i * size, size)
+
+    def core_copy(i):
+        return remote(0, i, p_ref.at[:, :, 1 - core, span(i), :], from_core.at[i], core_mate)
+
+    def load(i):
+        return pltpu.make_async_copy(
+            p_ref.at[:, :, core, span(i), :], mine.at[i], local_sems.at[0, i]
+        )
+
+    def first_copy(i):
+        if x_first(i):
+            return remote(1, i, mine.at[i, :, 1 - x], from_first.at[i], x_mate)
+        return remote(1, i, mine.at[i, 1 - y], from_first.at[i], y_mate)
+
+    def second_copy(i):
+        if x_first(i):
+            return remote(2, i, summed.at[i, 1 - y], from_second.at[i], y_mate)
+        return remote(2, i, summed.at[i, 1 - x], from_second.at[i], x_mate)
+
+    def columns(i, device):
+        return out_ref.at[span(i), pl.ds(pl.multiple_of(device * share, share), share)]
+
+    def spread(kind, i, mate):
+        return remote(kind, i, shared.at[i], columns(i, me), mate)
+
+    def keep(i):
+        return pltpu.make_async_copy(shared.at[i], columns(i, me), local_sems.at[1, i])
+
+    def pass_on(kind, i, device, mate):
+        return remote(kind, i, columns(i, device), columns(i, device), mate)
+
+    def forward(i):
+        if x_first(i):
+            return pass_on(6, i, y_mate, x_mate)
+        return pass_on(6, i, x_mate, y_mate)
+
+    order = [0, 2, 1, 3]
+    for i in order:
+        core_copy(i).start()
+        load(i).start()
+    for i in order:
+        load(i).wait()
+        core_copy(i).wait_recv()
+        for a in range(2):
+            for b in range(2):
+                mine[i, a, b] = (mine[i, a, b].astype(f32) + from_core[i, a, b].astype(f32)).astype(bf16)
+        first_copy(i).start()
+    for i in order:
+        first_copy(i).wait_recv()
+        for a in range(2):
+            kept = mine[i, a, x] if x_first(i) else mine[i, y, a]
+            summed[i, a] = (kept.astype(f32) + from_first[i, a].astype(f32)).astype(bf16)
+        second_copy(i).start()
+    if count:
         for at in range(count):
-            swap_middle(at).start()
-            swap(at).start()
-        for at in range(count):
-            swap_middle(at).wait_recv()
-            hand_near(at).start()
-            swap(at).wait_recv()
-            second_middle(at).start()
-        for at in range(count):
-            second_middle(at).wait_recv()
-            hand_far(at).start()
-        for at in range(count):
-            for copy in (swap, swap_middle, second_middle, hand_near, hand_far):
-                copy(at).wait_send()
-
-    @pl.when(jnp.logical_not(in_middle))
-    def _():
-        pl.semaphore_wait(barrier, 1)
-        for at in range(count):
-            swap(at).start()
-        for at in range(count):
-            swap(at).wait()
-            hand_near(at).wait_recv()
-            hand_far(at).wait_recv()
+            rows.hand_on(at)
+    for i in order:
+        second_copy(i).wait_recv()
+        total = summed[i, y if x_first(i) else x].astype(f32) + from_second[i].astype(f32)
+        span_rows = slice(i * size, (i + 1) * size)
+        values = pointwise(
+            total, *[ref[span_rows, :] if ref.shape[0] > 8 else ref[...] for ref in inputs]
+        )
+        if gather:
+            shared[i] = values[0].astype(bf16)
+            values = values[1:]
+        for ref, value in zip(results, values):
+            ref[span_rows, :] = value
+        if gather:
+            spread(4, i, x_mate).start()
+            spread(5, i, y_mate).start()
+            spread(3, i, core_mate).start()
+            keep(i).start()
+    if count:
+        rows.hand_last(0)
+    if gather:
+        for i in order:
+            spread(5 if x_first(i) else 4, i, y_mate).wait_recv()
+            forward(i).start()
+            pass_on(7, i, y_mate if x_first(i) else x_mate, core_mate).start()
+        for i in order:
+            spread(4 if x_first(i) else 5, i, x_mate).wait_recv()
+            pass_on(8, i, x_mate if x_first(i) else y_mate, core_mate).start()
+    if count:
+        for at in range(1, count):
+            rows.hand_last(at)
+    if gather:
+        for i in order:
+            forward(i).wait_recv()
+            pass_on(9, i, diagonal, core_mate).start()
+    for i in order:
+        core_copy(i).wait_send()
+        first_copy(i).wait_send()
+        second_copy(i).wait_send()
+        if gather:
+            keep(i).wait()
+            spread(3, i, core_mate).wait()
+            spread(4, i, x_mate).wait_send()
+            spread(5, i, y_mate).wait_send()
+            forward(i).wait_send()
+            for kind, device in (
+                (7, y_mate if x_first(i) else x_mate),
+                (8, x_mate if x_first(i) else y_mate),
+                (9, diagonal),
+            ):
+                pass_on(kind, i, device, core_mate).wait()
+    if count:
+        rows.finish()
+
+
+def plane_step(partial, pointwise, inputs, made, gather, number, packs=()):
+    tokens, share = partial.shape[3:]
+    size = tokens // PIECES
+    count = len(packs)
+    anywhere = pl.BlockSpec(memory_space=pl.ANY)
+    vmem = pl.BlockSpec(memory_space=pltpu.VMEM)
+    whole_shapes = [jax.ShapeDtypeStruct((tokens, 8 * share), bf16)] * gather + [
+        jax.ShapeDtypeStruct((4,) + pack.shape, bf16) for pack in packs
+    ]
+    outs = pl.pallas_call(
+        functools.partial(plane_kernel, pointwise, len(inputs), made, gather, count),
+        in_specs=[anywhere] + [vmem] * len(inputs) + [anywhere] * count,
+        out_specs=[vmem] * made + [anywhere] * (gather + count),
+        out_shape=[jax.ShapeDtypeStruct((tokens, share), f32)] * made + whole_shapes,
+        scratch_shapes=[
+            pltpu.VMEM((PIECES, 2, 2, size, share), bf16),
+            pltpu.VMEM((PIECES, 2, 2, size, share), bf16),
+            pltpu.VMEM((PIECES, 2, size, share), bf16),
+            pltpu.VMEM((PIECES, 2, size, share), bf16),
+            pltpu.VMEM((PIECES, size, share), bf16),
+            pltpu.VMEM((PIECES, size, share), bf16),
+            pltpu.SemaphoreType.DMA((10, PIECES)),
+            pltpu.SemaphoreType.DMA((10, PIECES)),
+            pltpu.SemaphoreType.DMA((2, PIECES)),
+        ]
+        + [pltpu.SemaphoreType.DMA((5, count))] * (2 if count else 0),
+        compiler_params=pltpu.CompilerParams(collective_id=number, has_side_effects=True),
+        cost_estimate=pl.CostEstimate(
+            flops=60 * 10**9, bytes_accessed=32 * tokens * share, transcendentals=0
+        ),
+        name="plane_step",
+    )(partial, *inputs, *packs)
+    wholes = [whole.reshape((4 * whole.shape[1],) + whole.shape[2:]) for whole in outs[made + gather :]]
+    return outs[:made], outs[made : made + gather], wholes
 
 
 def gather_now(packs, number):
@@ -283,44 +543,47 @@
     )
 
 
-def join_rows(pieces):
-    if len(pieces) == 1:
-        return pieces[0]
-    part = pieces[0]
-    z = lax.axis_index("row")
-    whole = jnp.zeros((4,) + part.shape, part.dtype)
-    blocks = (part, pieces[1], pieces[2] + pieces[4], pieces[3] + pieces[5])
-    for at, piece in zip(places(z), blocks):
-        whole = lax.dynamic_update_slice_in_dim(whole, piece[None], at, 0)
-    return whole.reshape((4 * part.shape[0],) + part.shape[1:])
-
-
-def reduce_rows(grads):
-    n = lax.axis_size("row")
-    if n != 4:
-        total = lax.psum_scatter(grads, "row", scatter_dimension=0, tiled=True)
-        return total.astype(f32), ((), (), ())
-    own, partner, near, far = places(lax.axis_index("row"))
-    size = grads.shape[0] // n
-    inward, middle = [(0, 1), (3, 2)], [(1, 2), (2, 1)]
-
-    def block(at, *others):
-        piece = lax.dynamic_slice_in_dim(grads, at * size, size, 0)
+class Reduced:
+    def __init__(self, grads):
+        n = lax.axis_size("row")
+        self.chained = n == 4
+        self.total = None
+        if not self.chained:
+            self.total = lax.psum_scatter(grads, "row", scatter_dimension=0, tiled=True).astype(f32)
+            return
+        self.grads, self.size = grads, grads.shape[0] // n
+        self.own, self.partner, self.near, self.far = places(lax.axis_index("row"))
+        self.far_in = lax.ppermute(self.block(self.far), "row", INWARD)
+        self.near_in = lax.ppermute(self.block(self.near), "row", INWARD)
+
+    def block(self, at, *others):
+        piece = lax.dynamic_slice_in_dim(self.grads, at * self.size, self.size, 0)
         if others:
             piece = piece.astype(f32)
             for other in others:
                 piece = piece + other.astype(f32)
         return piece
 
-    far_in = lax.ppermute(block(far), "row", inward)
-    near_in = lax.ppermute(block(near), "row", inward)
-    far_sum = lax.ppermute(block(far, far_in).astype(bf16), "row", middle)
-    near_sum = lax.ppermute(block(near, near_in).astype(bf16), "row", middle)
-    exchanged = lax.ppermute(
-        block(partner, far_sum).astype(bf16), "row", [(0, 1), (1, 0), (2, 3), (3, 2)]
-    )
-    hops = ((far_in, near_in), (far_sum, near_sum), (exchanged,))
-    return block(own, near_sum, exchanged), hops
+    def second(self, *groups):
+        if not self.chained:
+            return ()
+        far = self.block(self.far, after(self.far_in, *groups)).astype(bf16)
+        near = self.block(self.near, after(self.near_in, *groups)).astype(bf16)
+        self.far_sum = lax.ppermute(far, "row", MIDDLE)
+        self.near_sum = lax.ppermute(near, "row", MIDDLE)
+        return (far, near)
+
+    def third(self, *groups):
+        if not self.chained:
+            return ()
+        piece = self.block(self.partner, after(self.far_sum, *groups)).astype(bf16)
+        self.exchanged = lax.ppermute(piece, "row", PAIRS)
+        return (piece,)
+
+    def result(self, *groups):
+        if self.total is None:
+            self.total = self.block(self.own, after(self.near_sum, *groups), self.exchanged)
+        return self.total
 
 
 def after(value, *groups):
@@ -482,23 +745,27 @@
     )(z, *pieces, scaled, cots, scaled, cots, coef)
 
 
-def joint_kernel(count, based, *refs):
+def joint_kernel(count, based, planar, *refs):
     out_ref = refs[-1]
-    for a in range(0, out_ref.shape[1], TILE):
+    for a in range(0, refs[count].shape[0], TILE):
         total = refs[2 * count][:, a : a + TILE] if based else None
         for left, weights in zip(refs[:count], refs[count : 2 * count]):
             part = mm_nt(left[...], weights[a : a + TILE, :])
             total = part if total is None else total + part
-        out_ref[:, a : a + TILE] = total.astype(out_ref.dtype)
-
-
-def joint_back(lefts, weights, column, kind, *base):
+        if planar:
+            at = a // TILE
+            out_ref[at // 4, at // 2 % 2, at % 2] = total.astype(out_ref.dtype)
+        else:
+            out_ref[:, a : a + TILE] = total.astype(out_ref.dtype)
+
+
+def joint_back(lefts, weights, column, kind, *base, planar=False):
     tokens, width = lefts[0].shape[0], weights[0].shape[0]
     row = lambda i: (i, 0)
     fixed = lambda i: (0, column)
     depth = sum(left.shape[1] for left in lefts)
     return pl.pallas_call(
-        functools.partial(joint_kernel, len(lefts), len(base) > 0),
+        functools.partial(joint_kernel, len(lefts), len(base) > 0, planar),
         grid=(tokens // TILE,),
         in_specs=[pl.BlockSpec((TILE, left.shape[1]), row) for left in lefts]
         + [
@@ -506,8 +773,10 @@
             for left in lefts
         ]
         + [pl.BlockSpec((TILE, width), row)] * len(base),
-        out_specs=pl.BlockSpec((TILE, width), row),
-        out_shape=jax.ShapeDtypeStruct((tokens, width), kind),
+        out_specs=pl.BlockSpec((2, 2, 2, TILE, TILE), lambda i: (0, 0, 0, i, 0))
+        if planar
+        else pl.BlockSpec((TILE, width), row),
+        out_shape=jax.ShapeDtypeStruct((2, 2, 2, tokens, TILE) if planar else (tokens, width), kind),
         cost_estimate=pl.CostEstimate(
             flops=2 * tokens * width * depth,
             bytes_accessed=2 * (tokens + width) * depth + 4 * tokens * width,
@@ -531,6 +800,17 @@
             cuts.append((at, at + size))
             at += size
     return cuts + [(at, width)]
+
+
+def stream_step(total, rows, gain):
+    stream = rows.astype(f32) + total
+    return stream * gain, stream
+
+
+def dstream_step(total, back, cots, stream, damp, gain):
+    dscaled = back + total
+    dstream = cots.astype(f32) + gain * dscaled - stream * damp
+    return dstream, dstream, dscaled
 
 
 def per_device(
@@ -585,7 +865,7 @@
     expert_cuts = [
         (local, a, b)
         for local in range(local_experts)
-        for a, b in cuts_of(gate_expert.shape[2], (384, 256, 384))
+        for a, b in cuts_of(gate_expert.shape[2], (256, 256, 512))
     ]
     chunks = shared_cuts[-1:] + expert_cuts[:2] + shared_cuts[:-1] + expert_cuts[2:]
 
@@ -599,14 +879,9 @@
 
     packs = [pack(*chunk) for chunk in chunks]
     chained = lax.axis_size("row") == 4
-    gathered, came = {}, {}
-    early = 3 if chained else len(chunks)
-    for at in range(early):
-        if not (chained and at in (1, 2)):
-            gathered[at], came[at] = gather_rows(packs[at])
-
-    def hop(arrivals, at, which):
-        return arrivals[at][which] if 0 <= at < len(chunks) and at in arrivals else ()
+    planar = chained and cols == 8 and share == TILE
+    gathered = {}
+    gathered[0] = Gathered(packs[0])
 
     rows_in = lax.all_gather(block_input, "col", axis=1, tiled=True)
     gains = lax.all_gather(jnp.stack([input_gain, mlp_gain]), "col", axis=1, tiled=True).astype(f32)
@@ -614,27 +889,32 @@
     rows_f = rows_in.astype(f32)
     scale_a = lax.rsqrt(jnp.mean(rows_f * rows_f, axis=-1, keepdims=True) + norm_eps)
     normed_a = (rows_f * scale_a * gains[0]).astype(bf16)
-    raw = after(mm(normed_a, qkv_full), hop(came, 0, 0))
+    raw = mm(normed_a, qkv_full)
+    raw = after(raw, gathered[0].second())
     qkv, context, lse = attend_forward(raw, lengths, cosine, sine)
-    attn_part = after(mm_nt(context, out_full).astype(bf16), (cot_rows,), hop(came, 0, 1))
+    context = after(context, gathered[0].third())
     x_share = block_input.astype(f32)
-    attn_sum = lax.psum_scatter(attn_part, "col", scatter_dimension=1, tiled=True)
-    wait_for = ()
-    if chained:
-        wait_for = gather_now([after(packs[1], (attn_part,))], 1)
-        gathered[1] = (packs[1], wait_for[0])
-    attn_sum = after(attn_sum, wait_for, hop(came, 0, 2))
-    stream = x_share + attn_sum.astype(f32)
     gain_b = mlp_gain.astype(f32)
-    scaled_share = (stream * gain_b).astype(bf16)
-    scaled = lax.all_gather(scaled_share, "col", axis=1, tiled=True)
-    wait_for = ()
-    if chained:
-        wait_for = gather_now([after(packs[2], (scaled_share,))], 2)
-        gathered[2] = (packs[2], wait_for[0])
-    for at in range(early, len(chunks)):
-        gathered[at], came[at] = gather_rows(after(packs[at], wait_for))
-    scaled = after(scaled, wait_for)
+    if planar:
+        attn_part = joint_back([context], [out_weights], 0, bf16, planar=True)
+        attn_part = after(attn_part, (cot_rows,))
+        (stream,), (scaled,), wholes_now = plane_step(
+            attn_part, stream_step, [block_input, gain_b[None]], 1, 1, 1, packs[1:3]
+        )
+        for at in (1, 2):
+            gathered[at] = (packs[at], wholes_now[at - 1])
+    else:
+        attn_part = mm_nt(context, out_full).astype(bf16)
+        attn_sum = lax.psum_scatter(attn_part, "col", scatter_dimension=1, tiled=True)
+        scaled_share, stream = stream_step(attn_sum.astype(f32), block_input, gain_b[None])
+        scaled = lax.all_gather(scaled_share.astype(bf16), "col", axis=1, tiled=True)
+    for at in range(1, len(chunks)):
+        if at not in gathered and (at <= 3 or not chained):
+            gathered[at] = Gathered(packs[at], (scaled,))
+
+    def pieces_of(at):
+        return gathered[at] if isinstance(gathered[at], tuple) else gathered[at].pieces
+
     stream_f = scaled.astype(f32) / gains[1]
     scale_b = lax.rsqrt(jnp.mean(stream_f * stream_f, axis=1, keepdims=True) + norm_eps)
 
@@ -653,37 +933,50 @@
         members[local] = jnp.any(routes == expert, axis=1)
         column = lax.dynamic_index_in_dim(router_probs, expert, 1, False)
         shares[local] = jnp.where(members[local], column, 0.0)
-    dpairs, hiddens, wholes, unit_grads, went = [], [], [], [], {}
+    dpairs, hiddens, wholes, reduced = [], [], [], []
     last = len(chunks) - 1
+    waits = ()
     for at, (kind, a, b) in enumerate(chunks):
-        pieces = gathered[at]
-        coef = jnp.concatenate([scale_b, shares[kind][:, None]], axis=1)
-        if at == 1:
-            coef = after(coef, hop(came, 3, 0))
-        elif at == 2:
-            coef = after(coef, hop(came, 3, 1), hop(came, 4, 0), hop(went, 0, 0))
-        elif at > 2:
-            coef = after(
-                coef,
-                hop(came, at + 1, 0),
-                hop(came, at + 1, 1),
-                hop(went, at - 2, 0),
-                hop(went, at - 3, 1),
-                hop(went, at - 4, 2),
-            )
-        if at == last:
-            dscaled_early = joint_back(dpairs, wholes, 0, f32)
-            coef = after(coef, (dscaled_early,))
-        dpair, hidden, sums, grads, whole = expert_chunk(pieces, scaled, cot_rows, coef)
+        coef = after(jnp.concatenate([scale_b, shares[kind][:, None]], axis=1), waits)
+        dpair, hidden, sums, grads, whole = expert_chunk(pieces_of(at), scaled, cot_rows, coef)
         dots[kind] = dots.get(kind, 0.0) + sums[:, 0]
         inner = inner + sums[:, 1]
         dpairs.append(dpair)
         hiddens.append(hidden)
         wholes.append(whole)
-        reduced, arrivals = reduce_rows(grads)
-        unit_grads.append(reduced)
-        went[at] = arrivals
-    dscaled_part = joint_back([dpair], [whole], 0, bf16, dscaled_early)
+        now = (sums,)
+        waits = ()
+        if planar:
+            if at == 0:
+                waits += gathered[3].second(now)
+            elif at == 1:
+                waits += gathered[3].third(now)
+                gathered[4] = Gathered(packs[4], now)
+            elif at == 3:
+                waits += gathered[4].second(now)
+                gathered[5] = Gathered(packs[5], now)
+                dscaled_early = joint_back(dpairs, wholes, 0, f32)
+                early = (dscaled_early,)
+                waits += early
+                waits += gathered[4].third(early)
+                waits += gathered[5].second(early)
+            elif at == 4:
+                waits += gathered[5].third(now)
+        elif at == last - 1:
+            dscaled_early = joint_back(dpairs, wholes, 0, f32)
+        if at >= 1:
+            waits += reduced[at - 1].second(now)
+        if at >= 2:
+            waits += reduced[at - 2].third(now)
+        reduced.append(Reduced(grads))
+        if at >= 3:
+            waits += (reduced[at - 3].result(now),) if chained else ()
+    if planar:
+        late_pairs, late_wholes = dpairs[4:], wholes[4:]
+    else:
+        late_pairs, late_wholes = dpairs[last:], wholes[last:]
+    late_pairs[-1] = after(late_pairs[-1], waits)
+    dscaled_part = joint_back(late_pairs, late_wholes, 0, bf16, dscaled_early, planar=planar)
     moe_part = joint_back(hiddens, wholes, 2, bf16)
 
     named = [jnp.where(members[local], dots[local], 0.0) for local in range(local_experts)]
@@ -700,36 +993,38 @@
     grad_router_part = stacked.reshape(3, experts + 1, width).sum(axis=0)
     grad_router_both = lax.psum_scatter(grad_router_part, "row", scatter_dimension=1, tiled=True)
     router_rows = lax.dynamic_slice_in_dim(router_full, col_id * share, share, 0)
-    back = mm_nt(jnp.concatenate(parts, axis=1), jnp.concatenate([router_rows] * 3, axis=1))
-    dscaled_sum = after(
-        lax.psum_scatter(dscaled_part, "col", scatter_dimension=1, tiled=True),
-        (moe_part,),
-        hop(went, last - 1, 0),
-        hop(went, last - 2, 1),
-        hop(went, last - 3, 2),
-        hop(went, last - 1, 1),
-        hop(went, last, 0),
-    )
-    dscaled = back + dscaled_sum.astype(f32)
-    cot_share = grad_output.astype(f32)
-    dstream = cot_share + gain_b * dscaled - stream * (scale_b * scale_b * inner[:, None] / width)
+    back_term = mm_nt(jnp.concatenate(parts, axis=1), jnp.concatenate([router_rows] * 3, axis=1))
+    damp = scale_b * scale_b * inner[:, None] / width
+    step_inputs = [back_term, grad_output, stream, damp, gain_b[None]]
+    if planar:
+        (dstream, dscaled), (dattn,), _ = plane_step(dscaled_part, dstream_step, step_inputs, 2, 1, 2)
+    else:
+        dscaled_sum = lax.psum_scatter(dscaled_part, "col", scatter_dimension=1, tiled=True)
+        dstream_low, dstream, dscaled = dstream_step(dscaled_sum.astype(f32), *step_inputs)
+        dattn = lax.all_gather(dstream_low.astype(bf16), "col", axis=1, tiled=True)
     gain_b_grad = jnp.sum(dscaled * stream, axis=0)
 
-    dstream_low = dstream.astype(bf16)
-    dattn = lax.all_gather(dstream_low, "col", axis=1, tiled=True)
-    dattn = after(dattn, hop(went, last - 2, 2), hop(went, last - 1, 2), hop(went, last, 1))
     moe_share = lax.psum_scatter(
-        after(moe_part, (dstream_low,)), "col", scatter_dimension=1, tiled=True
+        after(moe_part, (dattn,)), "col", scatter_dimension=1, tiled=True
     ).astype(f32)
     block_output = (stream + moe_share).astype(bf16)
-    out_grad, _ = reduce_rows(mm_tn(dattn, context).astype(bf16))
-    dcontext = mm(dattn, out_full).astype(bf16)
+    now = (dattn,)
+    waits = reduced[last].second(now) + reduced[last - 1].third(now)
+    out_reduced = Reduced(mm_tn(dattn, context).astype(bf16))
+    dcontext = after(mm(dattn, out_full).astype(bf16), waits)
     dqkv, inner_a = attend_backward(qkv, dcontext, lse, lengths, cosine, sine)
+    now = (inner_a,)
+    waits = reduced[last].third(now) + out_reduced.second(now)
+    dnormed_part = after(mm_nt(dqkv, qkv_full).astype(bf16), waits)
+    dnormed_sum = lax.psum_scatter(dnormed_part, "col", scatter_dimension=1, tiled=True)
+    qkv_reduced = Reduced(mm_tn(normed_a, dqkv).astype(bf16))
+    out_reduced.third()
+    qkv_reduced.second()
+    qkv_reduced.third()
     inner_a = lax.psum(inner_a[:, 0], "col")[:, None]
-    qkv_grad, _ = reduce_rows(mm_tn(normed_a, dqkv).astype(bf16))
-    dnormed_part = after(mm_nt(dqkv, qkv_full).astype(bf16), (moe_share,))
-    dnormed_sum = lax.psum_scatter(dnormed_part, "col", scatter_dimension=1, tiled=True)
-    dnormed_a = after(dnormed_sum, (inner_a,), hop(went, last, 2)).astype(f32)
+    qkv_grad, out_grad = qkv_reduced.result(), out_reduced.result()
+    unit_grads = [one.result() for one in reduced]
+    dnormed_a = after(dnormed_sum, (inner_a,)).astype(f32)
     gain_a_share = input_gain.astype(f32)
     dinput = dstream + scale_a * gain_a_share * dnormed_a
     dinput = dinput - x_share * (scale_a * scale_a * inner_a / width)

time: 1220 us -> 1320 us (1.082)
  starting transfers between devices: 158 us -> 213 us
  Pallas kernels: 571 us -> 617 us
  local copies, waits for them, and re-layouts: 84.3 us -> 63.5 us
  waiting for transfers between devices: 168 us -> 188 us
    pallas_call x3 -> x6, Pallas kernels: 84.3 us -> 295 us  [the longest x2 208 us: plane_step(): pl.pallas_call(functools.partial(plane_kernel, pointwise, len(inputs), ma...]
    pallas_call x3 -> x1, Pallas kernels: 241 us -> 81.7 us  [gather_now(): pl.pallas_call(functools.partial(gather_kernel, count), in_specs=[anywher...]
    ppermute x60, starting transfers between devices: 157 us -> 212 us  [the longest x8 92.2 us: third(): self.exchanged = lax.ppermute(piece, 'row', PAIRS)]
    ppermute x60, waiting for transfers between devices: 165 us -> 187 us  [the longest x8 86.5 us: third(): self.exchanged = lax.ppermute(piece, 'row', PAIRS)]
    unnamed x193 -> x175, local copies, waits for them, and re-layouts: 32 us -> 21 us
    convert_element_type x26 -> x24, other arithmetic: 49.4 us -> 52.7 us  [the longest x8 20.3 us: third(): piece = self.block(self.partner, after(self.far_sum, *groups)).astype(bf16)]
  transfers between devices with their start and end apart: 69 -> 65, of which waited for: 15 -> 11; matrix products, arithmetic and copies ran while one was open for 19% -> 17% of each run, Pallas kernels for 43% -> 47%
where the time goes in v6:
time: 1320 us; the launch traced here: 1310 us
  Pallas kernels  617 us (47%)
  starting transfers between devices  213 us (16%)
  waiting for transfers between devices  188 us (14%)
  other arithmetic  118 us (9%)
  local copies, waits for them, and re-layouts  63.5 us (5%)
  matrix products  54.9 us (4%)
  blocking collectives  43.6 us (3%)
  between operations  15.8 us (1%)
    pallas_call x2, Pallas kernels, plane_step(): pl.pallas_call(functools.partial(plane_kernel, pointwise, len(inputs), ma...  208 us
    pallas_call x6, Pallas kernels, expert_chunk(): pl.pallas_call(functools.partial(expert_kernel, size, steps, count), grid...  199 us
    ppermute x8, starting transfers between devices, third(): self.exchanged = lax.ppermute(piece, 'row', PAIRS)  92.2 us
    pallas_call x4, Pallas kernels, joint_back(): pl.pallas_call(functools.partial(joint_kernel, len(lefts), len(base) > 0,...  87.4 us
    ppermute x8, waiting for transfers between devices, third(): self.exchanged = lax.ppermute(piece, 'row', PAIRS)  86.5 us
    pallas_call x1, Pallas kernels, gather_now(): pl.pallas_call(functools.partial(gather_kernel, count), in_specs=[anywher...  81.7 us
    ppermute x8, starting transfers between devices, __init__(): self.near_in = lax.ppermute(self.block(self.near), 'row', INWARD)  46.7 us
    ppermute x8, waiting for transfers between devices, __init__(): self.far_in = lax.ppermute(self.block(self.far), 'row', INWARD)  44.4 us
  transfers between devices with their start and end apart: 65, of which 11 were waited for; matrix products, arithmetic and copies ran while one was open for 17% of the time, Pallas kernels for 47%

profile of v6, /device:TPU:0, one launch (start us, length us, event | category | flops | bytes accessed | tf_op | source)
XLA Modules:
  0.0 1313.2 jit_solution(15295778183776441555)
XLA Ops:
  25.4 81.7 %gather_rows.1 = (bf16[4,512,768]{2,1,0:T(8,128)(2,1)}, bf16[4,512,384]{2,1,0:T(8,128)(2,1)}) custom-call(bf16[512,768]{1,0:T(8,128)(2,1)} %copy.137.refs_0_, bf16[512,384]{1,0:T(8,128)(2,1)} %fusion.19.refs_1_), custom_call_target="tpu_custom_call" | custom-call | flops 63700992000 | bytes 7077888 | tf_op jit(solution)/shard_map/gather_rows/pallas_call | solution.py:523
  111.1 9.1 all_gather.16
  141.9 10.5 fusion.4.raw_ref
  152.4 12.7 attend_forward.1
  165.1 8.7 joint_back.4.refs_0_
  173.8 125.5 %plane_step.2 = (f32[2048,256]{1,0:T(8,128)}, bf16[2048,2048]{1,0:T(8,128)(2,1)}, bf16[4,512,768]{2,1,0:T(8,128)(2,1)}, bf16[4,512,768]{2,1,0:T(8,128)(2,1)}) custom-call(bf16[2,2,2,2048,256]{4,3,2,1,0:T(8,128)(2,1)} %joint_back.4.refs_0_, bf16[2048,256]{1,0:T(8,128)(2,1)} %refs_1_.1, f32[1,256]{1,0:T(1,128)} %reshape_convert_fusion.refs_2_.refs_5_, ...), custom_call_target="tpu_custom_call" | custom-call | flops 60000002048 | bytes 16777216 | tf_op jit(solution)/shard_map/plane_step/pallas_call | solution.py:490
  312.9 27.9 %expert_chunk.6 = (bf16[2048,512]{1,0:T(8,128)(2,1)}, bf16[2048,256]{1,0:T(8,128)(2,1)}, f32[2048,2]{1,0:T(8,128)}, bf16[2048,768]{1,0:T(8,128)(2,1)}, bf16[2048,768]{1,0:T(8,128)(2,1)}) custom-call(s32[1]{0:T(128)} %bitcast.17.z_ref, bf16[512,768]{1,0:T(8,128)(2,1)} %fusion.17.refs_0_, bf16[512,768]{1,0:T(8,128)(2,1)} %collective-permute-done.refs_1_, ...), custom_call_target="tpu_custom_call" | custom-call | flops 12884901888 | bytes 46137344 | tf_op jit(solution)/shard_map/expert_chunk/pallas_call | solution.py:704
  355.5 27.9 %expert_chunk.7 = (bf16[2048,512]{1,0:T(8,128)(2,1)}, bf16[2048,256]{1,0:T(8,128)(2,1)}, f32[2048,2]{1,0:T(8,128)}, bf16[2048,768]{1,0:T(8,128)(2,1)}, bf16[2048,768]{1,0:T(8,128)(2,1)}) custom-call(s32[1]{0:T(128)} %bitcast.17.z_ref, bf16[512,768]{1,0:T(8,128)(2,1)} %get-tuple-element.330.refs_3_.refs_0_, bf16[2048,768]{1,0:T(8,128)(2,1)} %bitcast.125, ...), custom_call_target="tpu_custom_call" | custom-call | flops 12884901888 | bytes 46137344 | tf_op jit(solution)/shard_map/expert_chunk/pallas_call | solution.py:704
  387.8 9.9 collective-permute-start.13
  406.6 27.9 %expert_chunk.8 = (bf16[2048,512]{1,0:T(8,128)(2,1)}, bf16[2048,256]{1,0:T(8,128)(2,1)}, f32[2048,2]{1,0:T(8,128)}, bf16[2048,768]{1,0:T(8,128)(2,1)}, bf16[2048,768]{1,0:T(8,128)(2,1)}) custom-call(s32[1]{0:T(128)} %bitcast.17.z_ref, bf16[512,768]{1,0:T(8,128)(2,1)} %get-tuple-element.331.refs_4_.refs_0_, bf16[2048,768]{1,0:T(8,128)(2,1)} %bitcast.124, ...), custom_call_target="tpu_custom_call" | custom-call | flops 12884901888 | bytes 46137344 | tf_op jit(solution)/shard_map/expert_chunk/pallas_call | solution.py:704
  455.8 39.5 %expert_chunk.9 = (bf16[2048,1024]{1,0:T(8,128)(2,1)}, bf16[2048,512]{1,0:T(8,128)(2,1)}, f32[2048,2]{1,0:T(8,128)}, bf16[2048,1536]{1,0:T(8,128)(2,1)}, bf16[2048,1536]{1,0:T(8,128)(2,1)}) custom-call(s32[1]{0:T(128)} %bitcast.17.z_ref, bf16[512,1536]{1,0:T(8,128)(2,1)} %pad_maximum_fusion.refs_0_, bf16[512,1536]{1,0:T(8,128)(2,1)} %collective-permute-done.5.refs_1_, ...), custom_call_target="tpu_custom_call" | custom-call | flops 25769803776 | bytes 58720256 | tf_op jit(solution)/shard_map/expert_chunk/pallas_call | solution.py:704
  498.6 29.4 %joint_back.5.refs_4_ = f32[2048,2048]{1,0:T(8,128)} custom-call(bf16[2048,512]{1,0:T(8,128)(2,1)} %get-tuple-element.142.refs_0_, bf16[2048,512]{1,0:T(8,128)(2,1)} %get-tuple-element.143.refs_1_, bf16[2048,512]{1,0:T(8,128)(2,1)} %get-tuple-element.144.refs_2_, bf16[2048,1024]{1,0:T(8,128)(2,1)} %get-tuple-element.145.refs_3_, ...), custom_call_target="tpu_custom_call" | custom-call | flops 21474836480 | bytes 37748736 | tf_op jit(solution)/shard_map/joint_back/pallas_call | solution.py:767
  544.4 73.6 %collective-permute-done.26 = bf16[512,768]{1,0:T(8,128)(2,1)S(1)} collective-permute-done((bf16[512,768]{1,0:T(8,128)(2,1)S(1)}, bf16[512,768]{1,0:T(8,128)(2,1)S(1)}, u32[]{:S(2)}, u32[]{:S(2)}) %collective-permute-start.26) | collective-permute-done | bytes 786464 | tf_op jit(solution)/shard_map/ppermute | solution.py:580
  624.2 13.7 %collective-permute-done.20.refs_1_ = bf16[512,1152]{1,0:T(8,128)(2,1)S(1)} collective-permute-done((bf16[512,1152]{1,0:T(8,128)(2,1)}, bf16[512,1152]{1,0:T(8,128)(2,1)S(1)}, u32[]{:S(2)}, u32[]{:S(2)}) %collective-permute-start.20) | collective-permute-done | bytes 1179680 | tf_op jit(solution)/shard_map/ppermute | solution.py:184
  646.3 39.5 %expert_chunk.10 = (bf16[2048,1024]{1,0:T(8,128)(2,1)}, bf16[2048,512]{1,0:T(8,128)(2,1)}, f32[2048,2]{1,0:T(8,128)}, bf16[2048,1536]{1,0:T(8,128)(2,1)}, bf16[2048,1536]{1,0:T(8,128)(2,1)}) custom-call(s32[1]{0:T(128)} %bitcast.17.z_ref, bf16[512,1536]{1,0:T(8,128)(2,1)} %pad_maximum_fusion.1.refs_0_, bf16[512,1536]{1,0:T(8,128)(2,1)} %collective-permute-done.15.refs_1_, ...), custom_call_target="tpu_custom_call" | custom-call | flops 25769803776 | bytes 58720256 | tf_op jit(solution)/shard_map/expert_chunk/pallas_call | solution.py:704
  685.8 19.1 %collective-permute-done.30 = bf16[512,1536]{1,0:T(8,128)(2,1)} collective-permute-done((bf16[512,1536]{1,0:T(8,128)(2,1)S(1)}, bf16[512,1536]{1,0:T(8,128)(2,1)}, u32[]{:S(2)}, u32[]{:S(2)}) %collective-permute-start.30) | collective-permute-done | bytes 1572896 | tf_op jit(solution)/shard_map/ppermute | solution.py:556
  733.7 17.8 %collective-permute-done.28.refs_4_ = bf16[512,1152]{1,0:T(8,128)(2,1)} collective-permute-done((bf16[512,1152]{1,0:T(8,128)(2,1)}, bf16[512,1152]{1,0:T(8,128)(2,1)}, u32[]{:S(2)}, u32[]{:S(2)}) %collective-permute-start.28) | collective-permute-done | bytes 1179680 | tf_op jit(solution)/shard_map/ppermute | solution.py:190
  758.7 16.3 %collective-permute-done.29.refs_5_ = bf16[512,1152]{1,0:T(8,128)(2,1)} collective-permute-done((bf16[512,1152]{1,0:T(8,128)(2,1)}, bf16[512,1152]{1,0:T(8,128)(2,1)}, u32[]{:S(2)}, u32[]{:S(2)}) %collective-permute-start.29) | collective-permute-done | bytes 1179680 | tf_op jit(solution)/shard_map/ppermute | solution.py:197
  778.0 36.2 %expert_chunk.11 = (bf16[2048,768]{1,0:T(8,128)(2,1)}, bf16[2048,384]{1,0:T(8,128)(2,1)}, f32[2048,2]{1,0:T(8,128)}, bf16[2048,1152]{1,0:T(8,128)(2,1)}, bf16[2048,1152]{1,0:T(8,128)(2,1)}) custom-call(s32[1]{0:T(128)} %bitcast.17.z_ref, bf16[512,1152]{1,0:T(8,128)(2,1)} %pad_maximum_fusion.5.refs_0_, bf16[512,1152]{1,0:T(8,128)(2,1)} %copy-done.69, ...), custom_call_target="tpu_custom_call" | custom-call | flops 19327352832 | bytes 52428800 | tf_op jit(solution)/shard_map/expert_chunk/pallas_call | solution.py:704
  821.0 10.8 all-gather.1
  838.4 26.7 %joint_back.6 = bf16[2048,2048]{1,0:T(8,128)(2,1)} custom-call(bf16[2048,256]{1,0:T(8,128)(2,1)} %get-tuple-element.115.refs_0_, bf16[2048,256]{1,0:T(8,128)(2,1)} %get-tuple-element.119.refs_1_, bf16[2048,256]{1,0:T(8,128)(2,1)} %get-tuple-element.129.refs_2_, bf16[2048,512]{1,0:T(8,128)(2,1)} %get-tuple-element.137.refs_3_, ...), custom_call_target="tpu_custom_call" | custom-call | flops 18253611008 | bytes 34603008 | tf_op jit(solution)/shard_map/joint_back/pallas_call | solution.py:767
  882.5 22.5 %joint_back.7.refs_0_ = bf16[2,2,2,2048,256]{4,3,2,1,0:T(8,128)(2,1)} custom-call(bf16[2048,1024]{1,0:T(8,128)(2,1)} %get-tuple-element.172.refs_0_, bf16[2048,768]{1,0:T(8,128)(2,1)} %get-tuple-element.180.refs_1_, bf16[2048,1536]{1,0:T(8,128)(2,1)} %get-tuple-element.170.refs_10_.refs_2_, bf16[2048,1152]{1,0:T(8,128)(2,1)} %get-tuple-element.171.refs_11_.refs_3_, ...), custom_call_target="tpu_custom_call" | custom-call | flops 15032385536 | bytes 31457280 | tf_op jit(solution)/shard_map/joint_back/pallas_call | solution.py:767
  905.0 82.1 %plane_step.3 = (f32[2048,256]{1,0:T(8,128)}, f32[2048,256]{1,0:T(8,128)}, bf16[2048,2048]{1,0:T(8,128)(2,1)}) custom-call(bf16[2,2,2,2048,256]{4,3,2,1,0:T(8,128)(2,1)} %joint_back.7.refs_0_, f32[2048,256]{1,0:T(8,128)} %fusion.29.refs_1_, bf16[2048,256]{1,0:T(8,128)(2,1)} %refs_2_.1, f32[2048,256]{1,0:T(8,128)} %get-tuple-element.113.refs_3_, ...), custom_call_target="tpu_custom_call" | custom-call | flops 60000002048 | bytes 16777216 | tf_op jit(solution)/shard_map/plane_step/pallas_call | solution.py:490
  1016.8 25.3 %collective-permute-done.40 = bf16[512,1152]{1,0:T(8,128)(2,1)S(1)} collective-permute-done((bf16[512,1152]{1,0:T(8,128)(2,1)S(1)}, bf16[512,1152]{1,0:T(8,128)(2,1)S(1)}, u32[]{:S(2)}, u32[]{:S(2)}) %collective-permute-start.40) | collective-permute-done | bytes 1179680 | tf_op jit(solution)/shard_map/ppermute | solution.py:556
  1048.3 28.2 %attend_backward.1 = (bf16[2048,768]{1,0:T(8,128)(2,1)}, f32[2048,1]{1,0:T(8,128)}) custom-call(s32[2]{0:T(128)} %dynamic_slice.122.length_ref, bf16[2048,768]{1,0:T(8,128)(2,1)} %get-tuple-element.184.qkv_ref, bf16[2048,256]{1,0:T(8,128)(2,1)} %convolution_convert_fusion.3.dcontext_ref, f32[2048,256]{1,0:T(8,128)} %get-tuple-element.190.lse_ref, ...), custom_call_target="tpu_custom_call" | custom-call | flops 4294967296 | bytes 12582912 | tf_op jit(solution)/shard_map/attend_backward/pallas_call | solution.py:151
  1078.4 11.4 convolution_convert_fusion
  1110.4 10.9 convolution_convert_fusion.1
  1122.8 17.4 %collective-permute-start.46 = (bf16[512,768]{0,1:T(8,128)(2,1)}, bf16[512,768]{0,1:T(8,128)(2,1)}, u32[]{:S(2)}, u32[]{:S(2)}) collective-permute-start(bf16[512,768]{0,1:T(8,128)(2,1)} %get-tuple-element.281), channel_id=1, source_target_pairs={{0,8},{24,16},{1,9},{25,17},{2,10},{26,18},{3,11},{27,19},{4,12},{... | collective-permute-start | bytes 2359304 | tf_op jit(solution)/shard_map/ppermute | solution.py:557
  1153.1 16.8 %collective-permute-start.53 = (bf16[512,256]{1,0:T(8,128)(2,1)}, bf16[512,256]{1,0:T(8,128)(2,1)}, u32[]{:S(2)}, u32[]{:S(2)}) collective-permute-start(bf16[512,256]{1,0:T(8,128)(2,1)} %add_convert_fusion.22), channel_id=1, source_target_pairs={{0,8},{8,0},{16,24},{24,16},{1,9},{9,1},{17,25},{25,17},{2,10},{10... | collective-permute-start | bytes 786440 | tf_op jit(solution)/shard_map/ppermute | solution.py:580
  1179.3 12.2 psum.21
  1212.6 53.1 %collective-permute-start.50 = (bf16[512,768]{0,1:T(8,128)(2,1)}, bf16[512,768]{0,1:T(8,128)(2,1)}, u32[]{:S(2)}, u32[]{:S(2)}) collective-permute-start(bf16[512,768]{0,1:T(8,128)(2,1)} %add_convert_fusion.10), channel_id=1, source_target_pairs={{0,8},{8,0},{16,24},{24,16},{1,9},{9,1},{17,25},{25,17},{2,10},{10... | collective-permute-start | bytes 2359304 | tf_op jit(solution)/shard_map/ppermute | solution.py:580
  1294.7 11.5 all-reduce.4
  (451 shorter events, 341.4 us)
Async XLA Ops:
  7.2 128.8 %all-gather.5.cloned.1.call-start = ((), (), s32[]{:S(2)}) async-start(), calls=%async_computation.3 | async-start | bytes 9437184 | tf_op jit(solution)/shard_map/all_gather | solution.py:886
  8.0 165.9 %all-gather.7.cloned.1.call-start = ((), (), s32[]{:S(2)}) async-start(), calls=%async_computation.4 | async-start | bytes 9437184 | tf_op jit(solution)/shard_map/all_gather | solution.py:888
  8.7 1090.8 %reduce-scatter.8.cloned.1.call-start = ((), (), s32[]{:S(2)}) async-start(), calls=%async_computation.7 | async-start | bytes 163840 | tf_op jit(solution)/shard_map/reduce_scatter | solution.py:994
  10.2 119.6 %collective-permute-start = (bf16[512,768]{1,0:T(8,128)(2,1)}, bf16[512,768]{1,0:T(8,128)(2,1)}, u32[]{:S(2)}, u32[]{:S(2)}) collective-permute-start(bf16[512,768]{1,0:T(8,128)(2,1)} %fusion.17.refs_0_), channel_id=1, source_target_pairs={{0,8},{8,0},{16,24},{24,16},{1,9},{9,1},{17,25},{25,17},{2,10},{10... | collective-permute-start | bytes 2359304 | tf_op jit(solution)/shard_map/ppermute | solution.py:184
  13.2 120.0 %collective-permute-start.1 = (bf16[512,768]{1,0:T(8,128)(2,1)}, bf16[512,768]{1,0:T(8,128)(2,1)}, u32[]{:S(2)}, u32[]{:S(2)}) collective-permute-start(bf16[512,768]{1,0:T(8,128)(2,1)} %fusion.17.refs_0_), channel_id=1, source_target_pairs={{8,16},{16,8},{9,17},{17,9},{10,18},{18,10},{11,19},{19,11},{12,20... | collective-permute-start | bytes 2359304 | tf_op jit(solution)/shard_map/ppermute | solution.py:185
  134.5 178.3 %collective-permute-start.4 = (bf16[512,768]{1,0:T(8,128)(2,1)}, bf16[512,768]{1,0:T(8,128)(2,1)}, u32[]{:S(2)}, u32[]{:S(2)}) collective-permute-start(bf16[512,768]{1,0:T(8,128)(2,1)} %collective-permute-done.2.refs_3_), channel_id=1, source_target_pairs={{8,0},{16,24},{9,1},{17,25},{10,2},{18,26},{11,3},{19,27},{12,4},{... | collective-permute-start | bytes 2359304 | tf_op jit(solution)/shard_map/ppermute | solution.py:197
  402.2 127.1 %collective-permute-start.25 = (bf16[512,768]{1,0:T(8,128)(2,1)}, bf16[512,768]{1,0:T(8,128)(2,1)}, u32[]{:S(2)}, u32[]{:S(2)}) collective-permute-start(bf16[512,768]{1,0:T(8,128)(2,1)} %add_convert_fusion.20), channel_id=1, source_target_pairs={{8,16},{16,8},{9,17},{17,9},{10,18},{18,10},{11,19},{19,11},{12,20... | collective-permute-start | bytes 2359304 | tf_op jit(solution)/shard_map/ppermute | solution.py:573
  443.0 89.9 %collective-permute-start.24 = (bf16[512,768]{1,0:T(8,128)(2,1)}, bf16[512,768]{1,0:T(8,128)(2,1)}, u32[]{:S(2)}, u32[]{:S(2)}) collective-permute-start(bf16[512,768]{1,0:T(8,128)(2,1)} %add_convert_fusion.19), channel_id=1, source_target_pairs={{8,16},{16,8},{9,17},{17,9},{10,18},{18,10},{11,19},{19,11},{12,20... | collective-permute-start | bytes 2359304 | tf_op jit(solution)/shard_map/ppermute | solution.py:572
  451.7 86.1 %collective-permute-start.23 = (bf16[512,768]{1,0:T(8,128)(2,1)}, bf16[512,768]{1,0:T(8,128)(2,1)S(1)}, u32[]{:S(2)}, u32[]{:S(2)}) collective-permute-start(bf16[512,768]{1,0:T(8,128)(2,1)} %get-tuple-element.283), channel_id=1, source_target_pairs={{0,8},{24,16},{1,9},{25,17},{2,10},{26,18},{3,11},{27,19},{4,12},{... | collective-permute-start | bytes 2359304 | tf_op jit(solution)/shard_map/ppermute | solution.py:557
  528.0 112.6 %collective-permute-start.18 = (bf16[512,1536]{1,0:T(8,128)(2,1)}, bf16[512,1536]{1,0:T(8,128)(2,1)}, u32[]{:S(2)}, u32[]{:S(2)}) collective-permute-start(bf16[512,1536]{1,0:T(8,128)(2,1)} %collective-permute-done.16.refs_2_), channel_id=1, source_target_pairs={{8,0},{16,24},{9,1},{17,25},{10,2},{18,26},{11,3},{19,27},{12,4},{... | collective-permute-start | bytes 4718600 | tf_op jit(solution)/shard_map/ppermute | solution.py:190
  529.3 115.1 %collective-permute-start.19 = (bf16[512,1536]{1,0:T(8,128)(2,1)}, bf16[512,1536]{1,0:T(8,128)(2,1)}, u32[]{:S(2)}, u32[]{:S(2)}) collective-permute-start(bf16[512,1536]{1,0:T(8,128)(2,1)} %collective-permute-done.17.refs_3_), channel_id=1, source_target_pairs={{8,0},{16,24},{9,1},{17,25},{10,2},{18,26},{11,3},{19,27},{12,4},{... | collective-permute-start | bytes 4718600 | tf_op jit(solution)/shard_map/ppermute | solution.py:197
  532.9 85.1 %collective-permute-start.26 = (bf16[512,768]{1,0:T(8,128)(2,1)S(1)}, bf16[512,768]{1,0:T(8,128)(2,1)S(1)}, u32[]{:S(2)}, u32[]{:S(2)}) collective-permute-start(bf16[512,768]{1,0:T(8,128)(2,1)S(1)} %copy-done.47), channel_id=1, source_target_pairs={{0,8},{8,0},{16,24},{24,16},{1,9},{9,1},{17,25},{25,17},{2,10},{10... | collective-permute-start | bytes 2359304 | tf_op jit(solution)/shard_map/ppermute | solution.py:580
  537.8 100.0 %collective-permute-start.20 = (bf16[512,1152]{1,0:T(8,128)(2,1)}, bf16[512,1152]{1,0:T(8,128)(2,1)S(1)}, u32[]{:S(2)}, u32[]{:S(2)}) collective-permute-start(bf16[512,1152]{1,0:T(8,128)(2,1)} %pad_maximum_fusion.5.refs_0_), channel_id=1, source_target_pairs={{0,8},{8,0},{16,24},{24,16},{1,9},{9,1},{17,25},{25,17},{2,10},{10... | collective-permute-start | bytes 3538952 | tf_op jit(solution)/shard_map/ppermute | solution.py:184
  537.9 84.7 %collective-permute-start.21 = (bf16[512,1152]{1,0:T(8,128)(2,1)}, bf16[512,1152]{1,0:T(8,128)(2,1)S(1)}, u32[]{:S(2)}, u32[]{:S(2)}) collective-permute-start(bf16[512,1152]{1,0:T(8,128)(2,1)} %pad_maximum_fusion.5.refs_0_), channel_id=1, source_target_pairs={{8,16},{16,8},{9,17},{17,9},{10,18},{18,10},{11,19},{19,11},{12,20... | collective-permute-start | bytes 3538952 | tf_op jit(solution)/shard_map/ppermute | solution.py:185
  618.0 89.5 %collective-permute-start.33 = (bf16[512,768]{1,0:T(8,128)(2,1)}, bf16[512,768]{1,0:T(8,128)(2,1)}, u32[]{:S(2)}, u32[]{:S(2)}) collective-permute-start(bf16[512,768]{1,0:T(8,128)(2,1)} %add_convert_fusion.18), channel_id=1, source_target_pairs={{8,16},{16,8},{9,17},{17,9},{10,18},{18,10},{11,19},{19,11},{12,20... | collective-permute-start | bytes 2359304 | tf_op jit(solution)/shard_map/ppermute | solution.py:573
  622.6 89.3 %collective-permute-start.32 = (bf16[512,768]{1,0:T(8,128)(2,1)}, bf16[512,768]{1,0:T(8,128)(2,1)}, u32[]{:S(2)}, u32[]{:S(2)}) collective-permute-start(bf16[512,768]{1,0:T(8,128)(2,1)} %add_convert_fusion.16), channel_id=1, source_target_pairs={{8,16},{16,8},{9,17},{17,9},{10,18},{18,10},{11,19},{19,11},{12,20... | collective-permute-start | bytes 2359304 | tf_op jit(solution)/shard_map/ppermute | solution.py:572
  637.9 75.5 %collective-permute-start.31 = (bf16[512,1536]{1,0:T(8,128)(2,1)S(1)}, bf16[512,1536]{1,0:T(8,128)(2,1)}, u32[]{:S(2)}, u32[]{:S(2)}) collective-permute-start(bf16[512,1536]{1,0:T(8,128)(2,1)S(1)} %get-tuple-element.271), channel_id=1, source_target_pairs={{0,8},{24,16},{1,9},{25,17},{2,10},{26,18},{3,11},{27,19},{4,12},{... | collective-permute-start | bytes 4718600 | tf_op jit(solution)/shard_map/ppermute | solution.py:557
  711.9 154.6 %collective-permute-start.38 = (bf16[512,768]{1,0:T(8,128)(2,1)}, bf16[512,768]{1,0:T(8,128)(2,1)}, u32[]{:S(2)}, u32[]{:S(2)}) collective-permute-start(bf16[512,768]{1,0:T(8,128)(2,1)} %add_convert_fusion.15), channel_id=1, source_target_pairs={{8,16},{16,8},{9,17},{17,9},{10,18},{18,10},{11,19},{19,11},{12,20... | collective-permute-start | bytes 2359304 | tf_op jit(solution)/shard_map/ppermute | solution.py:573
  717.1 153.5 %collective-permute-start.39 = (bf16[512,768]{1,0:T(8,128)(2,1)}, bf16[512,768]{1,0:T(8,128)(2,1)}, u32[]{:S(2)}, u32[]{:S(2)}) collective-permute-start(bf16[512,768]{1,0:T(8,128)(2,1)} %add_convert_fusion.13), channel_id=1, source_target_pairs={{0,8},{8,0},{16,24},{24,16},{1,9},{9,1},{17,25},{25,17},{2,10},{10... | collective-permute-start | bytes 2359304 | tf_op jit(solution)/shard_map/ppermute | solution.py:580
  726.1 146.4 %collective-permute-start.37 = (bf16[512,1536]{1,0:T(8,128)(2,1)}, bf16[512,1536]{1,0:T(8,128)(2,1)}, u32[]{:S(2)}, u32[]{:S(2)}) collective-permute-start(bf16[512,1536]{1,0:T(8,128)(2,1)} %add_convert_fusion.5), channel_id=1, source_target_pairs={{8,16},{16,8},{9,17},{17,9},{10,18},{18,10},{11,19},{19,11},{12,20... | collective-permute-start | bytes 4718600 | tf_op jit(solution)/shard_map/ppermute | solution.py:572
  756.1 116.4 %collective-permute-start.36 = (bf16[512,1536]{1,0:T(8,128)(2,1)}, bf16[512,1536]{1,0:T(8,128)(2,1)}, u32[]{:S(2)}, u32[]{:S(2)}) collective-permute-start(bf16[512,1536]{1,0:T(8,128)(2,1)} %get-tuple-element.269), channel_id=1, source_target_pairs={{0,8},{24,16},{1,9},{25,17},{2,10},{26,18},{3,11},{27,19},{4,12},{... | collective-permute-start | bytes 4718600 | tf_op jit(solution)/shard_map/ppermute | solution.py:557
  775.0 104.3 %collective-permute-start.35 = (bf16[512,1536]{1,0:T(8,128)(2,1)S(1)}, bf16[512,1536]{1,0:T(8,128)(2,1)}, u32[]{:S(2)}, u32[]{:S(2)}) collective-permute-start(bf16[512,1536]{1,0:T(8,128)(2,1)S(1)} %get-tuple-element.270), channel_id=1, source_target_pairs={{0,8},{24,16},{1,9},{25,17},{2,10},{26,18},{3,11},{27,19},{4,12},{... | collective-permute-start | bytes 4718600 | tf_op jit(solution)/shard_map/ppermute | solution.py:556
  837.8 449.9 %reduce-scatter.4.cloned.1.call-start = ((), (), s32[]{:S(2)}) async-start(), calls=%async_computation.5 | async-start | bytes 9437184 | tf_op jit(solution)/shard_map/reduce_scatter | solution.py:1007
  987.1 304.6 %reduce-scatter.6.cloned.1.call-start = ((), (), s32[]{:S(2)}) async-start(), calls=%async_computation.6 | async-start | bytes 9437184 | tf_op jit(solution)/shard_map/reduce_scatter | solution.py:1019
  1005.5 71.1 %collective-permute-start.44 = (bf16[512,256]{1,0:T(8,128)(2,1)S(1)}, bf16[512,256]{1,0:T(8,128)(2,1)S(1)}, u32[]{:S(2)}, u32[]{:S(2)}) collective-permute-start(bf16[512,256]{1,0:T(8,128)(2,1)S(1)} %get-tuple-element.315), channel_id=1, source_target_pairs={{0,8},{24,16},{1,9},{25,17},{2,10},{26,18},{3,11},{27,19},{4,12},{... | collective-permute-start | bytes 786440 | tf_op jit(solution)/shard_map/ppermute | solution.py:556
  1006.8 69.8 %collective-permute-start.45 = (bf16[512,256]{1,0:T(8,128)(2,1)S(1)}, bf16[512,256]{1,0:T(8,128)(2,1)}, u32[]{:S(2)}, u32[]{:S(2)}) collective-permute-start(bf16[512,256]{1,0:T(8,128)(2,1)S(1)} %get-tuple-element.314), channel_id=1, source_target_pairs={{0,8},{24,16},{1,9},{25,17},{2,10},{26,18},{3,11},{27,19},{4,12},{... | collective-permute-start | bytes 786440 | tf_op jit(solution)/shard_map/ppermute | solution.py:557
  1107.1 95.8 %collective-permute-start.58 = (bf16[512,1152]{1,0:T(8,128)(2,1)}, bf16[512,1152]{1,0:T(8,128)(2,1)}, u32[]{:S(2)}, u32[]{:S(2)}) collective-permute-start(bf16[512,1152]{1,0:T(8,128)(2,1)} %add_convert_fusion.7), channel_id=1, source_target_pairs={{8,16},{16,8},{9,17},{17,9},{10,18},{18,10},{11,19},{19,11},{12,20... | collective-permute-start | bytes 3538952 | tf_op jit(solution)/shard_map/ppermute | solution.py:573
  1122.8 72.6 %collective-permute-start.46 = (bf16[512,768]{0,1:T(8,128)(2,1)}, bf16[512,768]{0,1:T(8,128)(2,1)}, u32[]{:S(2)}, u32[]{:S(2)}) collective-permute-start(bf16[512,768]{0,1:T(8,128)(2,1)} %get-tuple-element.281), channel_id=1, source_target_pairs={{0,8},{24,16},{1,9},{25,17},{2,10},{26,18},{3,11},{27,19},{4,12},{... | collective-permute-start | bytes 2359304 | tf_op jit(solution)/shard_map/ppermute | solution.py:557
  1191.5 74.2 %collective-permute-start.56 = (bf16[512,1536]{1,0:T(8,128)(2,1)}, bf16[512,1536]{1,0:T(8,128)(2,1)}, u32[]{:S(2)}, u32[]{:S(2)}) collective-permute-start(bf16[512,1536]{1,0:T(8,128)(2,1)} %add_convert_fusion.2), channel_id=1, source_target_pairs={{8,16},{16,8},{9,17},{17,9},{10,18},{18,10},{11,19},{19,11},{12,20... | collective-permute-start | bytes 4718600 | tf_op jit(solution)/shard_map/ppermute | solution.py:573
  1195.4 70.3 %collective-permute-start.57 = (bf16[512,1536]{1,0:T(8,128)(2,1)S(1)}, bf16[512,1536]{1,0:T(8,128)(2,1)S(1)}, u32[]{:S(2)}, u32[]{:S(2)}) collective-permute-start(bf16[512,1536]{1,0:T(8,128)(2,1)S(1)} %copy-done.33), channel_id=1, source_target_pairs={{0,8},{8,0},{16,24},{24,16},{1,9},{9,1},{17,25},{25,17},{2,10},{10... | collective-permute-start | bytes 4718600 | tf_op jit(solution)/shard_map/ppermute | solution.py:580
  1199.7 78.0 %collective-permute-start.47 = (bf16[512,768]{0,1:T(8,128)(2,1)}, bf16[512,768]{0,1:T(8,128)(2,1)}, u32[]{:S(2)}, u32[]{:S(2)}) collective-permute-start(bf16[512,768]{0,1:T(8,128)(2,1)} %add_convert_fusion.12), channel_id=1, source_target_pairs={{8,16},{16,8},{9,17},{17,9},{10,18},{18,10},{11,19},{19,11},{12,20... | collective-permute-start | bytes 2359304 | tf_op jit(solution)/shard_map/ppermute | solution.py:573
  1212.6 70.1 %collective-permute-start.50 = (bf16[512,768]{0,1:T(8,128)(2,1)}, bf16[512,768]{0,1:T(8,128)(2,1)}, u32[]{:S(2)}, u32[]{:S(2)}) collective-permute-start(bf16[512,768]{0,1:T(8,128)(2,1)} %add_convert_fusion.10), channel_id=1, source_target_pairs={{0,8},{8,0},{16,24},{24,16},{1,9},{9,1},{17,25},{25,17},{2,10},{10... | collective-permute-start | bytes 2359304 | tf_op jit(solution)/shard_map/ppermute | solution.py:580
  (119 other events, 2759.0 us)
Sparse Core Ops, SparseCore 0:
  9.9 58.6 all-gather.4
  70.5 55.9 all-gather.6
  838.0 16.4 reduce-scatter.7
  987.2 68.5 reduce-scatter.3
  1092.8 72.0 reduce-scatter.5

commit v7 on v6

--- a/solution.py
+++ b/solution.py
@@ -935,49 +935,56 @@
         shares[local] = jnp.where(members[local], column, 0.0)
     dpairs, hiddens, wholes, reduced = [], [], [], []
     last = len(chunks) - 1
-    waits = ()
+    came, went = {}, {}
+
+    def gather_all(at, *groups):
+        gathered[at] = Gathered(packs[at], *groups)
+        came[at] = (gathered[at].second(), gathered[at].third())
+
+    def hop(arrivals, at, which):
+        return arrivals[at][which] if at in arrivals else ()
+
+    if planar:
+        came[3] = (gathered[3].second(), gathered[3].third())
     for at, (kind, a, b) in enumerate(chunks):
-        coef = after(jnp.concatenate([scale_b, shares[kind][:, None]], axis=1), waits)
+        coef = jnp.concatenate([scale_b, shares[kind][:, None]], axis=1)
+        if planar:
+            if at == 1:
+                coef = after(coef, hop(came, 3, 0))
+                gather_all(4, (sums,))
+            if at == 2:
+                coef = after(coef, hop(came, 3, 1), hop(went, 0, 0))
+                gather_all(5, (sums,))
+            if at == 3:
+                coef = after(coef, hop(came, 4, 0), hop(went, 1, 0), hop(went, 0, 1))
+            if at == 4:
+                dscaled_early = joint_back(dpairs, wholes, 0, f32)
+                coef = after(
+                    coef, (dscaled_early,), hop(came, 5, 0), hop(went, 2, 0), hop(went, 1, 1), hop(went, 0, 2)
+                )
+            if at == 5:
+                moe_early = joint_back(hiddens, wholes, 2, f32)
+                coef = after(coef, (moe_early,), hop(went, 3, 0), hop(went, 2, 1), hop(went, 1, 2))
+        elif at == last:
+            dscaled_early = joint_back(dpairs, wholes, 0, f32)
+            moe_early = joint_back(hiddens, wholes, 2, f32)
         dpair, hidden, sums, grads, whole = expert_chunk(pieces_of(at), scaled, cot_rows, coef)
         dots[kind] = dots.get(kind, 0.0) + sums[:, 0]
         inner = inner + sums[:, 1]
         dpairs.append(dpair)
         hiddens.append(hidden)
         wholes.append(whole)
-        now = (sums,)
-        waits = ()
-        if planar:
-            if at == 0:
-                waits += gathered[3].second(now)
-            elif at == 1:
-                waits += gathered[3].third(now)
-                gathered[4] = Gathered(packs[4], now)
-            elif at == 3:
-                waits += gathered[4].second(now)
-                gathered[5] = Gathered(packs[5], now)
-                dscaled_early = joint_back(dpairs, wholes, 0, f32)
-                early = (dscaled_early,)
-                waits += early
-                waits += gathered[4].third(early)
-                waits += gathered[5].second(early)
-            elif at == 4:
-                waits += gathered[5].third(now)
-        elif at == last - 1:
-            dscaled_early = joint_back(dpairs, wholes, 0, f32)
-        if at >= 1:
-            waits += reduced[at - 1].second(now)
-        if at >= 2:
-            waits += reduced[at - 2].third(now)
-        reduced.append(Reduced(grads))
-        if at >= 3:
-            waits += (reduced[at - 3].result(now),) if chained else ()
+        one = Reduced(grads)
+        reduced.append(one)
+        if chained:
+            went[at] = ((one.far_in, one.near_in), one.second(), one.third())
+            went[at] = (went[at][0], (one.far_sum, one.near_sum), (one.exchanged,))
+    first_late = 4 if planar else last
+    late_pairs, late_wholes = dpairs[first_late:], wholes[first_late:]
     if planar:
-        late_pairs, late_wholes = dpairs[4:], wholes[4:]
-    else:
-        late_pairs, late_wholes = dpairs[last:], wholes[last:]
-    late_pairs[-1] = after(late_pairs[-1], waits)
+        late_pairs[-1] = after(late_pairs[-1], hop(went, 4, 0), hop(went, 3, 1), hop(went, 2, 2))
     dscaled_part = joint_back(late_pairs, late_wholes, 0, bf16, dscaled_early, planar=planar)
-    moe_part = joint_back(hiddens, wholes, 2, bf16)
+    moe_part = joint_back(hiddens[last:], wholes[last:], 2, bf16, moe_early)
 
     named = [jnp.where(members[local], dots[local], 0.0) for local in range(local_experts)]
     table = lax.all_gather(jnp.stack(named + [dots[None], inner]), "col", axis=0)
@@ -1008,13 +1015,12 @@
         after(moe_part, (dattn,)), "col", scatter_dimension=1, tiled=True
     ).astype(f32)
     block_output = (stream + moe_share).astype(bf16)
-    now = (dattn,)
-    waits = reduced[last].second(now) + reduced[last - 1].third(now)
+    waits = hop(went, 4, 1) + hop(went, 3, 2) + hop(went, 5, 0)
     out_reduced = Reduced(mm_tn(dattn, context).astype(bf16))
     dcontext = after(mm(dattn, out_full).astype(bf16), waits)
     dqkv, inner_a = attend_backward(qkv, dcontext, lse, lengths, cosine, sine)
-    now = (inner_a,)
-    waits = reduced[last].third(now) + out_reduced.second(now)
+    waits = hop(went, 5, 1) + hop(went, 4, 2)
+    out_reduced.second()
     dnormed_part = after(mm_nt(dqkv, qkv_full).astype(bf16), waits)
     dnormed_sum = lax.psum_scatter(dnormed_part, "col", scatter_dimension=1, tiled=True)
     qkv_reduced = Reduced(mm_tn(normed_a, dqkv).astype(bf16))

time: 1320 us -> 1260 us (0.955)
  starting transfers between devices: 213 us -> 167 us
  waiting for transfers between devices: 188 us -> 148 us
  Pallas kernels: 617 us -> 632 us
  local copies, waits for them, and re-layouts: 63.5 us -> 77.9 us
    ppermute x8, waiting for transfers between devices: 86.5 us -> 28.2 us  [third(): self.exchanged = lax.ppermute(piece, 'row', PAIRS)]
    ppermute x8, starting transfers between devices: 92.2 us -> 46 us  [third(): self.exchanged = lax.ppermute(piece, 'row', PAIRS)]
    ppermute x8, waiting for transfers between devices: 8.04 us -> 53.9 us  [__init__(): self.near_in = lax.ppermute(self.block(self.near), 'row', INWARD)]
    ppermute x8, starting transfers between devices: 19.4 us -> 44.1 us  [__init__(): self.far_in = lax.ppermute(self.block(self.far), 'row', INWARD)]
    ppermute x8, starting transfers between devices: 46.7 us -> 24.4 us  [__init__(): self.near_in = lax.ppermute(self.block(self.near), 'row', INWARD)]
    ppermute x4, waiting for transfers between devices: 13.7 us -> 0.01 us  [__init__(): self.partner = lax.ppermute(part, 'row', PAIRS)]
    pallas_call x4 -> x5, Pallas kernels: 87.4 us -> 97.2 us  [joint_back(): pl.pallas_call(functools.partial(joint_kernel, len(lefts), len(base) > 0,...]
  transfers between devices with their start and end apart: 65 -> 65, of which waited for: 11 -> 14; matrix products, arithmetic and copies ran while one was open for 17% -> 18% of each run, Pallas kernels for 47% -> 51%
where the time goes in v7:
time: 1260 us; the launch traced here: 1250 us
  Pallas kernels  632 us (50%)
  starting transfers between devices  167 us (13%)
  waiting for transfers between devices  148 us (12%)
  other arithmetic  114 us (9%)
  local copies, waits for them, and re-layouts  77.9 us (6%)
  matrix products  49.6 us (4%)
  blocking collectives  44.3 us (4%)
  between operations  15.6 us (1%)
    pallas_call x2, Pallas kernels, plane_step(): pl.pallas_call(functools.partial(plane_kernel, pointwise, len(inputs), ma...  207 us
    pallas_call x6, Pallas kernels, expert_chunk(): pl.pallas_call(functools.partial(expert_kernel, size, steps, count), grid...  199 us
    pallas_call x5, Pallas kernels, joint_back(): pl.pallas_call(functools.partial(joint_kernel, len(lefts), len(base) > 0,...  97.2 us
    pallas_call x1, Pallas kernels, gather_now(): pl.pallas_call(functools.partial(gather_kernel, count), in_specs=[anywher...  87.6 us
    ppermute x8, waiting for transfers between devices, __init__(): self.near_in = lax.ppermute(self.block(self.near), 'row', INWARD)  53.9 us
    ppermute x8, starting transfers between devices, third(): self.exchanged = lax.ppermute(piece, 'row', PAIRS)  46 us
    ppermute x8, starting transfers between devices, __init__(): self.far_in = lax.ppermute(self.block(self.far), 'row', INWARD)  44.1 us
    ppermute x8, waiting for transfers between devices, __init__(): self.far_in = lax.ppermute(self.block(self.far), 'row', INWARD)  40.7 us
  transfers between devices with their start and end apart: 65, of which 14 were waited for; matrix products, arithmetic and copies ran while one was open for 18% of the time, Pallas kernels for 51%

profile of v7, /device:TPU:0, one launch (start us, length us, event | category | flops | bytes accessed | tf_op | source)
XLA Modules:
  0.0 1248.0 jit_solution(14305002734832256020)
XLA Ops:
  18.6 87.6 %gather_rows.1 = (bf16[4,512,768]{2,1,0:T(8,128)(2,1)}, bf16[4,512,384]{2,1,0:T(8,128)(2,1)}) custom-call(bf16[512,768]{1,0:T(8,128)(2,1)} %copy.137.refs_0_, bf16[512,384]{1,0:T(8,128)(2,1)} %fusion.19.refs_1_), custom_call_target="tpu_custom_call" | custom-call | flops 63700992000 | bytes 7077888 | tf_op jit(solution)/shard_map/gather_rows/pallas_call | solution.py:523
  115.9 9.0 all_gather.16
  141.8 10.5 fusion.4.raw_ref
  152.3 12.7 %attend_forward.1 = (bf16[2048,768]{1,0:T(8,128)(2,1)}, bf16[2048,256]{1,0:T(8,128)(2,1)}, f32[2048,256]{1,0:T(8,128)}) custom-call(s32[2]{0:T(128)} %dynamic_slice.122.length_ref, f32[2048,768]{1,0:T(8,128)} %fusion.4.raw_ref, f32[1024,128]{1,0:T(8,128)} %pad_maximum_fusion.9.cos_ref, f32[1024,128]{1,0:T(8,128)} %pad_maximum_fusion.10.sin_ref), custom_call_target="tpu_custom_call" | custom-call | flops 1610612736 | bytes 12582912 | tf_op jit(solution)/shard_map/attend_forward/pallas_call | solution.py:81
  165.0 8.8 joint_back.5.refs_0_
  173.8 124.8 %plane_step.2 = (f32[2048,256]{1,0:T(8,128)}, bf16[2048,2048]{1,0:T(8,128)(2,1)}, bf16[4,512,768]{2,1,0:T(8,128)(2,1)}, bf16[4,512,768]{2,1,0:T(8,128)(2,1)}) custom-call(bf16[2,2,2,2048,256]{4,3,2,1,0:T(8,128)(2,1)} %joint_back.5.refs_0_, bf16[2048,256]{1,0:T(8,128)(2,1)} %refs_1_.1, f32[1,256]{1,0:T(1,128)} %reshape_convert_fusion.refs_2_.refs_5_, ...), custom_call_target="tpu_custom_call" | custom-call | flops 60000002048 | bytes 16777216 | tf_op jit(solution)/shard_map/plane_step/pallas_call | solution.py:490
  312.6 27.9 %expert_chunk.7 = (bf16[2048,512]{1,0:T(8,128)(2,1)}, bf16[2048,256]{1,0:T(8,128)(2,1)}, f32[2048,2]{1,0:T(8,128)}, bf16[2048,768]{1,0:T(8,128)(2,1)}, bf16[2048,768]{1,0:T(8,128)(2,1)}) custom-call(s32[1]{0:T(128)} %bitcast.17.z_ref, bf16[512,768]{1,0:T(8,128)(2,1)} %copy-done.29, bf16[512,768]{1,0:T(8,128)(2,1)} %collective-permute-done.refs_1_, ...), custom_call_target="tpu_custom_call" | custom-call | flops 12884901888 | bytes 46137344 | tf_op jit(solution)/shard_map/expert_chunk/pallas_call | solution.py:704
  372.9 27.9 %expert_chunk.6 = (bf16[2048,512]{1,0:T(8,128)(2,1)}, bf16[2048,256]{1,0:T(8,128)(2,1)}, f32[2048,2]{1,0:T(8,128)}, bf16[2048,768]{1,0:T(8,128)(2,1)}, bf16[2048,768]{1,0:T(8,128)(2,1)}) custom-call(s32[1]{0:T(128)} %bitcast.17.z_ref, bf16[512,768]{1,0:T(8,128)(2,1)} %pad_maximum_fusion.7.refs_3_.refs_0_, bf16[2048,768]{1,0:T(8,128)(2,1)} %bitcast.125, ...), custom_call_target="tpu_custom_call" | custom-call | flops 12884901888 | bytes 46137344 | tf_op jit(solution)/shard_map/expert_chunk/pallas_call | solution.py:704
  402.2 9.8 collective-permute-start.19
  440.6 27.9 %expert_chunk.8 = (bf16[2048,512]{1,0:T(8,128)(2,1)}, bf16[2048,256]{1,0:T(8,128)(2,1)}, f32[2048,2]{1,0:T(8,128)}, bf16[2048,768]{1,0:T(8,128)(2,1)}, bf16[2048,768]{1,0:T(8,128)(2,1)}) custom-call(s32[1]{0:T(128)} %bitcast.17.z_ref, bf16[512,768]{1,0:T(8,128)(2,1)} %pad_maximum_fusion.8.refs_4_.refs_0_, bf16[2048,768]{1,0:T(8,128)(2,1)} %bitcast.124, ...), custom_call_target="tpu_custom_call" | custom-call | flops 12884901888 | bytes 46137344 | tf_op jit(solution)/shard_map/expert_chunk/pallas_call | solution.py:704
  470.2 8.3 collective-permute-start.26
  502.0 37.3 %collective-permute-done.27 = bf16[512,768]{1,0:T(8,128)(2,1)S(1)} collective-permute-done((bf16[512,768]{1,0:T(8,128)(2,1)S(1)}, bf16[512,768]{1,0:T(8,128)(2,1)S(1)}, u32[]{:S(2)}, u32[]{:S(2)}) %collective-permute-start.27) | collective-permute-done | bytes 786464 | tf_op jit(solution)/shard_map/ppermute | solution.py:557
  543.7 39.5 %expert_chunk.9 = (bf16[2048,1024]{1,0:T(8,128)(2,1)}, bf16[2048,512]{1,0:T(8,128)(2,1)}, f32[2048,2]{1,0:T(8,128)}, bf16[2048,1536]{1,0:T(8,128)(2,1)}, bf16[2048,1536]{1,0:T(8,128)(2,1)}) custom-call(s32[1]{0:T(128)} %bitcast.17.z_ref, bf16[512,1536]{1,0:T(8,128)(2,1)} %pad_maximum_fusion.refs_0_, bf16[512,1536]{1,0:T(8,128)(2,1)} %collective-permute-done.4.refs_1_, ...), custom_call_target="tpu_custom_call" | custom-call | flops 25769803776 | bytes 58720256 | tf_op jit(solution)/shard_map/expert_chunk/pallas_call | solution.py:704
  586.2 29.5 %joint_back.6.refs_4_ = f32[2048,2048]{1,0:T(8,128)} custom-call(bf16[2048,512]{1,0:T(8,128)(2,1)} %get-tuple-element.99.refs_0_, bf16[2048,512]{1,0:T(8,128)(2,1)} %get-tuple-element.100.refs_1_, bf16[2048,512]{1,0:T(8,128)(2,1)} %get-tuple-element.101.refs_2_, bf16[2048,1024]{1,0:T(8,128)(2,1)} %get-tuple-element.102.refs_3_, ...), custom_call_target="tpu_custom_call" | custom-call | flops 21474836480 | bytes 37748736 | tf_op jit(solution)/shard_map/joint_back/pallas_call | solution.py:767
  640.4 39.5 %expert_chunk.10 = (bf16[2048,1024]{1,0:T(8,128)(2,1)}, bf16[2048,512]{1,0:T(8,128)(2,1)}, f32[2048,2]{1,0:T(8,128)}, bf16[2048,1536]{1,0:T(8,128)(2,1)}, bf16[2048,1536]{1,0:T(8,128)(2,1)}) custom-call(s32[1]{0:T(128)} %bitcast.17.z_ref, bf16[512,1536]{1,0:T(8,128)(2,1)} %pad_maximum_fusion.1.refs_0_, bf16[512,1536]{1,0:T(8,128)(2,1)} %collective-permute-done.17.refs_1_, ...), custom_call_target="tpu_custom_call" | custom-call | flops 25769803776 | bytes 58720256 | tf_op jit(solution)/shard_map/expert_chunk/pallas_call | solution.py:704
  682.4 22.1 %joint_back.7.refs_2_ = f32[2048,2048]{1,0:T(8,128)} custom-call(bf16[2048,256]{1,0:T(8,128)(2,1)} %get-tuple-element.88.refs_0_, bf16[2048,256]{1,0:T(8,128)(2,1)} %get-tuple-element.89.refs_1_, bf16[2048,256]{1,0:T(8,128)(2,1)} %get-tuple-element.93.refs_2_, bf16[2048,512]{1,0:T(8,128)(2,1)} %get-tuple-element.98.refs_3_, ...), custom_call_target="tpu_custom_call" | custom-call | flops 15032385536 | bytes 31457280 | tf_op jit(solution)/shard_map/joint_back/pallas_call | solution.py:767
  729.9 10.1 collective-permute-done.9.refs_4_
  741.8 13.4 %collective-permute-done.10.refs_5_ = bf16[512,1152]{1,0:T(8,128)(2,1)} collective-permute-done((bf16[512,1152]{1,0:T(8,128)(2,1)}, bf16[512,1152]{1,0:T(8,128)(2,1)}, u32[]{:S(2)}, u32[]{:S(2)}) %collective-permute-start.10) | collective-permute-done | bytes 1179680 | tf_op jit(solution)/shard_map/ppermute | solution.py:197
  757.4 36.2 %expert_chunk.11 = (bf16[2048,768]{1,0:T(8,128)(2,1)}, bf16[2048,384]{1,0:T(8,128)(2,1)}, f32[2048,2]{1,0:T(8,128)}, bf16[2048,1152]{1,0:T(8,128)(2,1)}, bf16[2048,1152]{1,0:T(8,128)(2,1)}) custom-call(s32[1]{0:T(128)} %bitcast.17.z_ref, bf16[512,1152]{1,0:T(8,128)(2,1)} %pad_maximum_fusion.5.refs_0_, bf16[512,1152]{1,0:T(8,128)(2,1)} %collective-permute-done.6.refs_1_, ...), custom_call_target="tpu_custom_call" | custom-call | flops 19327352832 | bytes 52428800 | tf_op jit(solution)/shard_map/expert_chunk/pallas_call | solution.py:704
  801.1 12.3 all-gather.1
  828.0 14.3 %joint_back.8 = bf16[2048,2048]{1,0:T(8,128)(2,1)} custom-call(bf16[2048,384]{1,0:T(8,128)(2,1)} %get-tuple-element.113.refs_0_, bf16[2048,1152]{1,0:T(8,128)(2,1)} %get-tuple-element.114.refs_1_.refs_3_, f32[2048,2048]{1,0:T(8,128)} %joint_back.7.refs_2_), custom_call_target="tpu_custom_call" | custom-call | flops 3221225472 | bytes 19922944 | tf_op jit(solution)/shard_map/joint_back/pallas_call | solution.py:767
  844.9 22.5 %joint_back.9.refs_0_ = bf16[2,2,2,2048,256]{4,3,2,1,0:T(8,128)(2,1)} custom-call(bf16[2048,1024]{1,0:T(8,128)(2,1)} %get-tuple-element.115.refs_0_, bf16[2048,768]{1,0:T(8,128)(2,1)} %get-tuple-element.118.refs_1_, bf16[2048,1536]{1,0:T(8,128)(2,1)} %get-tuple-element.110.refs_9_.refs_2_, bf16[2048,1152]{1,0:T(8,128)(2,1)} %get-tuple-element.114.refs_1_.refs_3_, ...), custom_call_target="tpu_custom_call" | custom-call | flops 15032385536 | bytes 31457280 | tf_op jit(solution)/shard_map/joint_back/pallas_call | solution.py:767
  867.4 82.2 %plane_step.3 = (f32[2048,256]{1,0:T(8,128)}, f32[2048,256]{1,0:T(8,128)}, bf16[2048,2048]{1,0:T(8,128)(2,1)}) custom-call(bf16[2,2,2,2048,256]{4,3,2,1,0:T(8,128)(2,1)} %joint_back.9.refs_0_, f32[2048,256]{1,0:T(8,128)} %fusion.29.refs_1_, bf16[2048,256]{1,0:T(8,128)(2,1)} %refs_2_.1, f32[2048,256]{1,0:T(8,128)} %get-tuple-element.81.refs_3_, ...), custom_call_target="tpu_custom_call" | custom-call | flops 60000002048 | bytes 16777216 | tf_op jit(solution)/shard_map/plane_step/pallas_call | solution.py:490
  964.2 17.0 %collective-permute-done.44 = bf16[512,1152]{1,0:T(8,128)(2,1)S(1)} collective-permute-done((bf16[512,1152]{1,0:T(8,128)(2,1)S(1)}, bf16[512,1152]{1,0:T(8,128)(2,1)S(1)}, u32[]{:S(2)}, u32[]{:S(2)}) %collective-permute-start.44) | collective-permute-done | bytes 1179680 | tf_op jit(solution)/shard_map/ppermute | solution.py:556
  990.2 16.1 %collective-permute-done.45 = bf16[512,1152]{1,0:T(8,128)(2,1)S(1)} collective-permute-done((bf16[512,1152]{1,0:T(8,128)(2,1)S(1)}, bf16[512,1152]{1,0:T(8,128)(2,1)S(1)}, u32[]{:S(2)}, u32[]{:S(2)}) %collective-permute-start.45) | collective-permute-done | bytes 1179680 | tf_op jit(solution)/shard_map/ppermute | solution.py:557
  1018.4 21.7 %collective-permute-done.43 = bf16[512,1536]{1,0:T(8,128)(2,1)S(1)} collective-permute-done((bf16[512,1536]{1,0:T(8,128)(2,1)S(1)}, bf16[512,1536]{1,0:T(8,128)(2,1)S(1)}, u32[]{:S(2)}, u32[]{:S(2)}) %collective-permute-start.43) | collective-permute-done | bytes 1572896 | tf_op jit(solution)/shard_map/ppermute | solution.py:580
  1041.2 28.4 %attend_backward.1 = (bf16[2048,768]{1,0:T(8,128)(2,1)}, f32[2048,1]{1,0:T(8,128)}) custom-call(s32[2]{0:T(128)} %dynamic_slice.122.length_ref, bf16[2048,768]{1,0:T(8,128)(2,1)} %get-tuple-element.126.qkv_ref, bf16[2048,256]{1,0:T(8,128)(2,1)} %convolution_convert_fusion.3.dcontext_ref, f32[2048,256]{1,0:T(8,128)} %get-tuple-element.129.lse_ref, ...), custom_call_target="tpu_custom_call" | custom-call | flops 4294967296 | bytes 12582912 | tf_op jit(solution)/shard_map/attend_backward/pallas_call | solution.py:151
  1069.6 11.5 convolution_convert_fusion
  1137.6 10.9 convolution_convert_fusion.1
  1158.8 12.0 psum.21
  1192.2 15.8 %collective-permute-start.53 = (bf16[512,768]{0,1:T(8,128)(2,1)}, bf16[512,768]{0,1:T(8,128)(2,1)}, u32[]{:S(2)}, u32[]{:S(2)}) collective-permute-start(bf16[512,768]{0,1:T(8,128)(2,1)} %add_convert_fusion.10), channel_id=1, source_target_pairs={{0,8},{8,0},{16,24},{24,16},{1,9},{9,1},{17,25},{25,17},{2,10},{10... | collective-permute-start | bytes 2359304 | tf_op jit(solution)/shard_map/ppermute | solution.py:580
  1230.3 10.9 all-reduce.4
  (436 shorter events, 374.0 us)
Async XLA Ops:
  7.2 128.1 %all-gather.5.cloned.1.call-start = ((), (), s32[]{:S(2)}) async-start(), calls=%async_computation.3 | async-start | bytes 9437184 | tf_op jit(solution)/shard_map/all_gather | solution.py:886
  8.0 165.8 %all-gather.7.cloned.1.call-start = ((), (), s32[]{:S(2)}) async-start(), calls=%async_computation.4 | async-start | bytes 9437184 | tf_op jit(solution)/shard_map/all_gather | solution.py:888
  8.7 1097.7 %reduce-scatter.8.cloned.1.call-start = ((), (), s32[]{:S(2)}) async-start(), calls=%async_computation.7 | async-start | bytes 163840 | tf_op jit(solution)/shard_map/reduce_scatter | solution.py:1001
  9.4 119.6 %collective-permute-start = (bf16[512,768]{1,0:T(8,128)(2,1)S(1)}, bf16[512,768]{1,0:T(8,128)(2,1)}, u32[]{:S(2)}, u32[]{:S(2)}) collective-permute-start(bf16[512,768]{1,0:T(8,128)(2,1)S(1)} %fusion.17.refs_0_), channel_id=1, source_target_pairs={{0,8},{8,0},{16,24},{24,16},{1,9},{9,1},{17,25},{25,17},{2,10},{10... | collective-permute-start | bytes 2359304 | tf_op jit(solution)/shard_map/ppermute | solution.py:184
  12.5 119.9 %collective-permute-start.1 = (bf16[512,768]{1,0:T(8,128)(2,1)S(1)}, bf16[512,768]{1,0:T(8,128)(2,1)}, u32[]{:S(2)}, u32[]{:S(2)}) collective-permute-start(bf16[512,768]{1,0:T(8,128)(2,1)S(1)} %fusion.17.refs_0_), channel_id=1, source_target_pairs={{8,16},{16,8},{9,17},{17,9},{10,18},{18,10},{11,19},{19,11},{12,20... | collective-permute-start | bytes 2359304 | tf_op jit(solution)/shard_map/ppermute | solution.py:185
  133.7 178.0 %collective-permute-start.11 = (bf16[512,768]{1,0:T(8,128)(2,1)}, bf16[512,768]{1,0:T(8,128)(2,1)S(1)}, u32[]{:S(2)}, u32[]{:S(2)}) collective-permute-start(bf16[512,768]{1,0:T(8,128)(2,1)} %collective-permute-done.2.refs_3_), channel_id=1, source_target_pairs={{8,0},{16,24},{9,1},{17,25},{10,2},{18,26},{11,3},{19,27},{12,4},{... | collective-permute-start | bytes 2359304 | tf_op jit(solution)/shard_map/ppermute | solution.py:197
  298.5 69.8 %collective-permute-start.4 = (bf16[512,1536]{1,0:T(8,128)(2,1)}, bf16[512,1536]{1,0:T(8,128)(2,1)}, u32[]{:S(2)}, u32[]{:S(2)}) collective-permute-start(bf16[512,1536]{1,0:T(8,128)(2,1)} %pad_maximum_fusion.refs_0_), channel_id=1, source_target_pairs={{0,8},{8,0},{16,24},{24,16},{1,9},{9,1},{17,25},{25,17},{2,10},{10... | collective-permute-start | bytes 4718600 | tf_op jit(solution)/shard_map/ppermute | solution.py:184
  298.6 69.7 %collective-permute-start.5 = (bf16[512,1536]{1,0:T(8,128)(2,1)}, bf16[512,1536]{1,0:T(8,128)(2,1)}, u32[]{:S(2)}, u32[]{:S(2)}) collective-permute-start(bf16[512,1536]{1,0:T(8,128)(2,1)} %pad_maximum_fusion.refs_0_), channel_id=1, source_target_pairs={{8,16},{16,8},{9,17},{17,9},{10,18},{18,10},{11,19},{19,11},{12,20... | collective-permute-start | bytes 4718600 | tf_op jit(solution)/shard_map/ppermute | solution.py:185
  367.6 69.9 %collective-permute-start.21 = (bf16[512,768]{1,0:T(8,128)(2,1)}, bf16[512,768]{1,0:T(8,128)(2,1)S(1)}, u32[]{:S(2)}, u32[]{:S(2)}) collective-permute-start(bf16[512,768]{1,0:T(8,128)(2,1)} %add_convert_fusion.21), channel_id=1, source_target_pairs={{8,16},{16,8},{9,17},{17,9},{10,18},{18,10},{11,19},{19,11},{12,20... | collective-permute-start | bytes 2359304 | tf_op jit(solution)/shard_map/ppermute | solution.py:572
  369.7 61.2 %collective-permute-start.12 = (bf16[512,1536]{1,0:T(8,128)(2,1)}, bf16[512,1536]{1,0:T(8,128)(2,1)}, u32[]{:S(2)}, u32[]{:S(2)}) collective-permute-start(bf16[512,1536]{1,0:T(8,128)(2,1)} %collective-permute-done.4.refs_1_), channel_id=1, source_target_pairs={{8,16},{16,8},{9,17},{17,9},{10,18},{18,10},{11,19},{19,11},{12,20... | collective-permute-start | bytes 4718600 | tf_op jit(solution)/shard_map/ppermute | solution.py:191
  371.6 61.2 %collective-permute-start.13 = (bf16[512,1536]{1,0:T(8,128)(2,1)}, bf16[512,1536]{1,0:T(8,128)(2,1)}, u32[]{:S(2)}, u32[]{:S(2)}) collective-permute-start(bf16[512,1536]{1,0:T(8,128)(2,1)} %collective-permute-done.5.refs_2_), channel_id=1, source_target_pairs={{8,0},{16,24},{9,1},{17,25},{10,2},{18,26},{11,3},{19,27},{12,4},{... | collective-permute-start | bytes 4718600 | tf_op jit(solution)/shard_map/ppermute | solution.py:190
  439.1 103.2 %collective-permute-start.16 = (bf16[512,1536]{1,0:T(8,128)(2,1)}, bf16[512,1536]{1,0:T(8,128)(2,1)}, u32[]{:S(2)}, u32[]{:S(2)}) collective-permute-start(bf16[512,1536]{1,0:T(8,128)(2,1)} %collective-permute-done.12.refs_3_), channel_id=1, source_target_pairs={{8,0},{16,24},{9,1},{17,25},{10,2},{18,26},{11,3},{19,27},{12,4},{... | collective-permute-start | bytes 4718600 | tf_op jit(solution)/shard_map/ppermute | solution.py:197
  480.8 134.9 %collective-permute-start.6 = (bf16[512,1152]{1,0:T(8,128)(2,1)S(1)}, bf16[512,1152]{1,0:T(8,128)(2,1)}, u32[]{:S(2)}, u32[]{:S(2)}) collective-permute-start(bf16[512,1152]{1,0:T(8,128)(2,1)S(1)} %copy-done.24), channel_id=1, source_target_pairs={{0,8},{8,0},{16,24},{24,16},{1,9},{9,1},{17,25},{25,17},{2,10},{10... | collective-permute-start | bytes 3538952 | tf_op jit(solution)/shard_map/ppermute | solution.py:184
  482.8 56.5 %collective-permute-start.27 = (bf16[512,768]{1,0:T(8,128)(2,1)S(1)}, bf16[512,768]{1,0:T(8,128)(2,1)S(1)}, u32[]{:S(2)}, u32[]{:S(2)}) collective-permute-start(bf16[512,768]{1,0:T(8,128)(2,1)S(1)} %get-tuple-element.219), channel_id=1, source_target_pairs={{0,8},{24,16},{1,9},{25,17},{2,10},{26,18},{3,11},{27,19},{4,12},{... | collective-permute-start | bytes 2359304 | tf_op jit(solution)/shard_map/ppermute | solution.py:557
  489.2 128.2 %collective-permute-start.7 = (bf16[512,1152]{1,0:T(8,128)(2,1)S(1)}, bf16[512,1152]{1,0:T(8,128)(2,1)}, u32[]{:S(2)}, u32[]{:S(2)}) collective-permute-start(bf16[512,1152]{1,0:T(8,128)(2,1)S(1)} %copy-done.24), channel_id=1, source_target_pairs={{8,16},{16,8},{9,17},{17,9},{10,18},{18,10},{11,19},{19,11},{12,20... | collective-permute-start | bytes 3538952 | tf_op jit(solution)/shard_map/ppermute | solution.py:185
  497.2 86.0 %collective-permute-start.30 = (bf16[512,768]{1,0:T(8,128)(2,1)}, bf16[512,768]{1,0:T(8,128)(2,1)S(1)}, u32[]{:S(2)}, u32[]{:S(2)}) collective-permute-start(bf16[512,768]{1,0:T(8,128)(2,1)} %add_convert_fusion.17), channel_id=1, source_target_pairs={{0,8},{8,0},{16,24},{24,16},{1,9},{9,1},{17,25},{25,17},{2,10},{10... | collective-permute-start | bytes 2359304 | tf_op jit(solution)/shard_map/ppermute | solution.py:580
  542.3 89.6 %collective-permute-start.24 = (bf16[512,1536]{1,0:T(8,128)(2,1)}, bf16[512,1536]{1,0:T(8,128)(2,1)}, u32[]{:S(2)}, u32[]{:S(2)}) collective-permute-start(bf16[512,1536]{1,0:T(8,128)(2,1)} %collective-permute-done.18.refs_2_), channel_id=1, source_target_pairs={{8,0},{16,24},{9,1},{17,25},{10,2},{18,26},{11,3},{19,27},{12,4},{... | collective-permute-start | bytes 4718600 | tf_op jit(solution)/shard_map/ppermute | solution.py:190
  615.7 94.5 %collective-permute-start.8 = (bf16[512,1152]{1,0:T(8,128)(2,1)}, bf16[512,1152]{1,0:T(8,128)(2,1)}, u32[]{:S(2)}, u32[]{:S(2)}) collective-permute-start(bf16[512,1152]{1,0:T(8,128)(2,1)} %collective-permute-done.6.refs_1_), channel_id=1, source_target_pairs={{8,16},{16,8},{9,17},{17,9},{10,18},{18,10},{11,19},{19,11},{12,20... | collective-permute-start | bytes 3538952 | tf_op jit(solution)/shard_map/ppermute | solution.py:191
  617.3 91.5 %collective-permute-start.35 = (bf16[512,768]{1,0:T(8,128)(2,1)}, bf16[512,768]{1,0:T(8,128)(2,1)}, u32[]{:S(2)}, u32[]{:S(2)}) collective-permute-start(bf16[512,768]{1,0:T(8,128)(2,1)} %add_convert_fusion.14), channel_id=1, source_target_pairs={{0,8},{8,0},{16,24},{24,16},{1,9},{9,1},{17,25},{25,17},{2,10},{10... | collective-permute-start | bytes 2359304 | tf_op jit(solution)/shard_map/ppermute | solution.py:580
  631.9 79.5 %collective-permute-start.34 = (bf16[512,768]{1,0:T(8,128)(2,1)}, bf16[512,768]{1,0:T(8,128)(2,1)}, u32[]{:S(2)}, u32[]{:S(2)}) collective-permute-start(bf16[512,768]{1,0:T(8,128)(2,1)} %add_convert_fusion.15), channel_id=1, source_target_pairs={{8,16},{16,8},{9,17},{17,9},{10,18},{18,10},{11,19},{19,11},{12,20... | collective-permute-start | bytes 2359304 | tf_op jit(solution)/shard_map/ppermute | solution.py:573
  633.5 82.7 %collective-permute-start.31 = (bf16[512,1536]{1,0:T(8,128)(2,1)}, bf16[512,1536]{1,0:T(8,128)(2,1)}, u32[]{:S(2)}, u32[]{:S(2)}) collective-permute-start(bf16[512,1536]{1,0:T(8,128)(2,1)} %get-tuple-element.208), channel_id=1, source_target_pairs={{0,8},{24,16},{1,9},{25,17},{2,10},{26,18},{3,11},{27,19},{4,12},{... | collective-permute-start | bytes 4718600 | tf_op jit(solution)/shard_map/ppermute | solution.py:556
  711.5 133.4 %collective-permute-start.40 = (bf16[512,768]{1,0:T(8,128)(2,1)}, bf16[512,768]{1,0:T(8,128)(2,1)}, u32[]{:S(2)}, u32[]{:S(2)}) collective-permute-start(bf16[512,768]{1,0:T(8,128)(2,1)} %add_convert_fusion.13), channel_id=1, source_target_pairs={{0,8},{8,0},{16,24},{24,16},{1,9},{9,1},{17,25},{25,17},{2,10},{10... | collective-permute-start | bytes 2359304 | tf_op jit(solution)/shard_map/ppermute | solution.py:580
  716.2 128.7 %collective-permute-start.36 = (bf16[512,1536]{1,0:T(8,128)(2,1)S(1)}, bf16[512,1536]{1,0:T(8,128)(2,1)}, u32[]{:S(2)}, u32[]{:S(2)}) collective-permute-start(bf16[512,1536]{1,0:T(8,128)(2,1)S(1)} %get-tuple-element.206), channel_id=1, source_target_pairs={{0,8},{24,16},{1,9},{25,17},{2,10},{26,18},{3,11},{27,19},{4,12},{... | collective-permute-start | bytes 4718600 | tf_op jit(solution)/shard_map/ppermute | solution.py:556
  719.2 125.6 %collective-permute-start.37 = (bf16[512,1536]{1,0:T(8,128)(2,1)S(1)}, bf16[512,1536]{1,0:T(8,128)(2,1)}, u32[]{:S(2)}, u32[]{:S(2)}) collective-permute-start(bf16[512,1536]{1,0:T(8,128)(2,1)S(1)} %get-tuple-element.205), channel_id=1, source_target_pairs={{0,8},{24,16},{1,9},{25,17},{2,10},{26,18},{3,11},{27,19},{4,12},{... | collective-permute-start | bytes 4718600 | tf_op jit(solution)/shard_map/ppermute | solution.py:557
  740.0 104.9 %collective-permute-start.38 = (bf16[512,1536]{1,0:T(8,128)(2,1)}, bf16[512,1536]{1,0:T(8,128)(2,1)}, u32[]{:S(2)}, u32[]{:S(2)}) collective-permute-start(bf16[512,1536]{1,0:T(8,128)(2,1)} %add_convert_fusion.5), channel_id=1, source_target_pairs={{8,16},{16,8},{9,17},{17,9},{10,18},{18,10},{11,19},{19,11},{12,20... | collective-permute-start | bytes 4718600 | tf_op jit(solution)/shard_map/ppermute | solution.py:572
  755.2 89.7 %collective-permute-start.39 = (bf16[512,1536]{1,0:T(8,128)(2,1)}, bf16[512,1536]{1,0:T(8,128)(2,1)}, u32[]{:S(2)}, u32[]{:S(2)}) collective-permute-start(bf16[512,1536]{1,0:T(8,128)(2,1)} %add_convert_fusion.4), channel_id=1, source_target_pairs={{8,16},{16,8},{9,17},{17,9},{10,18},{18,10},{11,19},{19,11},{12,20... | collective-permute-start | bytes 4718600 | tf_op jit(solution)/shard_map/ppermute | solution.py:573
  823.0 400.4 %reduce-scatter.4.cloned.1.call-start = ((), (), s32[]{:S(2)}) async-start(), calls=%async_computation.5 | async-start | bytes 9437184 | tf_op jit(solution)/shard_map/reduce_scatter | solution.py:1014
  949.7 277.7 %reduce-scatter.6.cloned.1.call-start = ((), (), s32[]{:S(2)}) async-start(), calls=%async_computation.6 | async-start | bytes 9437184 | tf_op jit(solution)/shard_map/reduce_scatter | solution.py:1025
  982.4 98.7 %collective-permute-start.46 = (bf16[512,1152]{1,0:T(8,128)(2,1)}, bf16[512,1152]{1,0:T(8,128)(2,1)}, u32[]{:S(2)}, u32[]{:S(2)}) collective-permute-start(bf16[512,1152]{1,0:T(8,128)(2,1)} %add_convert_fusion.8), channel_id=1, source_target_pairs={{8,16},{16,8},{9,17},{17,9},{10,18},{18,10},{11,19},{19,11},{12,20... | collective-permute-start | bytes 3538952 | tf_op jit(solution)/shard_map/ppermute | solution.py:572
  1007.7 73.4 %collective-permute-start.47 = (bf16[512,1152]{1,0:T(8,128)(2,1)}, bf16[512,1152]{1,0:T(8,128)(2,1)}, u32[]{:S(2)}, u32[]{:S(2)}) collective-permute-start(bf16[512,1152]{1,0:T(8,128)(2,1)} %add_convert_fusion.7), channel_id=1, source_target_pairs={{8,16},{16,8},{9,17},{17,9},{10,18},{18,10},{11,19},{19,11},{12,20... | collective-permute-start | bytes 3538952 | tf_op jit(solution)/shard_map/ppermute | solution.py:573
  1011.3 69.9 %collective-permute-start.48 = (bf16[512,1536]{1,0:T(8,128)(2,1)S(1)}, bf16[512,1536]{1,0:T(8,128)(2,1)S(1)}, u32[]{:S(2)}, u32[]{:S(2)}) collective-permute-start(bf16[512,1536]{1,0:T(8,128)(2,1)S(1)} %add_convert_fusion), channel_id=1, source_target_pairs={{0,8},{8,0},{16,24},{24,16},{1,9},{9,1},{17,25},{25,17},{2,10},{10... | collective-permute-start | bytes 4718600 | tf_op jit(solution)/shard_map/ppermute | solution.py:580
  1121.0 62.0 %collective-permute-start.59 = (bf16[512,1152]{1,0:T(8,128)(2,1)}, bf16[512,1152]{1,0:T(8,128)(2,1)}, u32[]{:S(2)}, u32[]{:S(2)}) collective-permute-start(bf16[512,1152]{1,0:T(8,128)(2,1)} %add_convert_fusion.6), channel_id=1, source_target_pairs={{0,8},{8,0},{16,24},{24,16},{1,9},{9,1},{17,25},{25,17},{2,10},{10... | collective-permute-start | bytes 3538952 | tf_op jit(solution)/shard_map/ppermute | solution.py:580
  (109 other events, 2100.4 us)
Sparse Core Ops, SparseCore 0:
  10.0 58.6 all-gather.4
  70.5 55.9 all-gather.6
  823.1 17.9 reduce-scatter.7
  949.8 70.0 reduce-scatter.3
  1081.3 70.7 reduce-scatter.5

commit v8 on v7

--- a/solution.py
+++ b/solution.py
@@ -295,6 +295,125 @@
                 self.hand_far(at).wait_recv()
 
 
+class RowReduce:
+    def __init__(self, grads, total, refs):
+        self.grads, self.total = grads, total
+        self.far_in, self.near_in, self.far_sum, self.near_sum, self.last = refs[:5]
+        self.held, self.more, self.send_sems, self.recv_sems, self.local_sems = refs[5:]
+        self.z = lax.axis_index("row")
+        self.own, self.partner, self.near, self.far = places(self.z)
+        self.across = 3 - self.z
+        self.in_middle = (self.z == 1) | (self.z == 2)
+        self.outside = jnp.logical_not(self.in_middle)
+
+    def copy_of(self, kind, source, target, device):
+        return pltpu.make_async_remote_copy(
+            src_ref=source,
+            dst_ref=target,
+            send_sem=self.send_sems.at[kind],
+            recv_sem=self.recv_sems.at[kind],
+            device_id={"row": device},
+            device_id_type=pl.DeviceIdType.MESH,
+        )
+
+    def send_far(self):
+        return self.copy_of(0, self.grads.at[self.far], self.far_in, self.partner)
+
+    def send_near(self):
+        return self.copy_of(1, self.grads.at[self.near], self.near_in, self.partner)
+
+    def cross_far(self):
+        return self.copy_of(2, self.far_in, self.far_sum, self.across)
+
+    def cross_near(self):
+        return self.copy_of(3, self.near_in, self.near_sum, self.across)
+
+    def swap_middle(self):
+        return self.copy_of(4, self.far_sum, self.last, self.partner)
+
+    def swap_outer(self):
+        return self.copy_of(4, self.grads.at[self.partner], self.last, self.partner)
+
+    def load(self, kind, block):
+        target = self.more if kind % 2 else self.held
+        return pltpu.make_async_copy(self.grads.at[block], target, self.local_sems.at[kind])
+
+    def add(self, target, source):
+        @pl.loop(0, target.shape[0], step=64)
+        def _(at):
+            tile = pl.ds(pl.multiple_of(at, 64), 64)
+            target[tile, :] = (target[tile, :].astype(f32) + source[tile, :].astype(f32)).astype(bf16)
+
+    def begin(self):
+        @pl.when(self.outside)
+        def _():
+            self.send_far().start()
+            self.send_near().start()
+            self.swap_outer().start()
+            self.load(3, self.own).start()
+
+        @pl.when(self.in_middle)
+        def _():
+            self.load(0, self.far).start()
+            self.load(1, self.near).start()
+
+    def second_far(self):
+        @pl.when(self.in_middle)
+        def _():
+            self.load(0, self.far).wait()
+            self.send_far().wait_recv()
+            self.add(self.far_in, self.held)
+            self.cross_far().start()
+            self.load(2, self.partner).start()
+
+    def second_near(self):
+        @pl.when(self.in_middle)
+        def _():
+            self.load(1, self.near).wait()
+            self.send_near().wait_recv()
+            self.add(self.near_in, self.more)
+            self.cross_near().start()
+            self.load(3, self.own).start()
+
+    def third(self):
+        @pl.when(self.in_middle)
+        def _():
+            self.load(2, self.partner).wait()
+            self.cross_far().wait_recv()
+            self.add(self.far_sum, self.held)
+            self.swap_middle().start()
+
+    def finish(self):
+        self.load(3, self.own).wait()
+        self.swap_outer().wait_recv()
+
+        @pl.when(self.in_middle)
+        def _():
+            self.cross_near().wait_recv()
+
+        @pl.loop(0, self.total.shape[0], step=64)
+        def _(at):
+            tile = pl.ds(pl.multiple_of(at, 64), 64)
+            self.total[tile, :] = self.more[tile, :].astype(f32) + self.last[tile, :].astype(f32)
+
+        @pl.when(self.in_middle)
+        def _():
+            @pl.loop(0, self.total.shape[0], step=64)
+            def _(at):
+                tile = pl.ds(pl.multiple_of(at, 64), 64)
+                self.total[tile, :] += self.near_sum[tile, :].astype(f32)
+
+            self.cross_far().wait_send()
+            self.cross_near().wait_send()
+            self.swap_middle().wait_send()
+
+        @pl.when(self.outside)
+        def _():
+            self.send_far().wait_send()
+            self.send_near().wait_send()
+            self.swap_outer().wait_send()
+
+
 def signal_to(barrier, device):
     pl.semaphore_signal(barrier, inc=1, device_id=device, device_id_type=pl.DeviceIdType.MESH)
 
@@ -313,13 +432,17 @@
 PIECES = 4
 
 
-def plane_kernel(pointwise, given, made, gather, count, *refs):
+def plane_kernel(pointwise, given, made, gather, count, reducing, *refs):
     p_ref, inputs = refs[0], refs[1 : 1 + given]
     at = 1 + given
     packs = refs[at : at + count]
     at += count
+    grads = refs[at] if reducing else None
+    at += reducing
     results = refs[at : at + made]
     at += made
+    total_ref = refs[at] if reducing else None
+    at += reducing
     whole_refs = refs[at : at + gather + count]
     at += gather + count
     mine, from_core, from_first, summed, from_second, shared, send_sems, recv_sems, local_sems = refs[
@@ -335,21 +458,29 @@
     barrier = pltpu.get_barrier_semaphore()
     for mate in (core_mate, x_mate, y_mate):
         signal_to(barrier, {"col": mate})
-    rows = None
-    if count:
-        rows = RowGather(packs, whole_refs[gather:], refs[at + 9 : at + 11])
-        signal_to(barrier, {"row": rows.partner})
-
-        @pl.when(rows.in_middle)
-        def _():
-            signal_to(barrier, {"row": rows.across})
+    rows, reduction = None, None
+    if count or reducing:
+        if count:
+            rows = RowGather(packs, whole_refs[gather:], refs[at + 9 : at + 11])
+            at += 2
+        if reducing:
+            reduction = RowReduce(grads, total_ref, refs[at + 9 : at + 19])
+        chain = rows or reduction
+        signal_to(barrier, {"row": chain.partner})
+
+        @pl.when(chain.in_middle)
+        def _():
+            signal_to(barrier, {"row": chain.across})
             pl.semaphore_wait(barrier, 5)
 
-        @pl.when(rows.outside)
+        @pl.when(chain.outside)
         def _():
             pl.semaphore_wait(barrier, 4)
 
-        rows.begin()
+        if count:
+            rows.begin()
+        if reducing:
+            reduction.begin()
     else:
         pl.semaphore_wait(barrier, 3)
 
@@ -424,6 +555,8 @@
     if count:
         for at in range(count):
             rows.hand_on(at)
+    if reducing:
+        reduction.second_far()
     for i in order:
         second_copy(i).wait_recv()
         total = summed[i, y if x_first(i) else x].astype(f32) + from_second[i].astype(f32)
@@ -443,6 +576,8 @@
             keep(i).start()
     if count:
         rows.hand_last(0)
+    if reducing and not gather:
+        reduction.second_near()
     if gather:
         for i in order:
             spread(5 if x_first(i) else 4, i, y_mate).wait_recv()
@@ -454,6 +589,10 @@
     if count:
         for at in range(1, count):
             rows.hand_last(at)
+    if reducing and gather:
+        reduction.second_near()
+    if reducing:
+        reduction.third()
     if gather:
         for i in order:
             forward(i).wait_recv()
@@ -476,22 +615,35 @@
                 pass_on(kind, i, device, core_mate).wait()
     if count:
         rows.finish()
-
-
-def plane_step(partial, pointwise, inputs, made, gather, number, packs=()):
+    if reducing:
+        reduction.finish()
+
+
+def plane_step(partial, pointwise, inputs, made, gather, number, packs=(), grads=None):
     tokens, share = partial.shape[3:]
     size = tokens // PIECES
     count = len(packs)
+    reducing = 0 if grads is None else 1
+    totals, more_scratch, given_grads = [], [], []
+    if reducing:
+        block, columns = grads.shape[0] // 4, grads.shape[1]
+        given_grads = [grads.reshape(4, block, columns)]
+        totals = [jax.ShapeDtypeStruct((block, columns), f32)]
+        more_scratch = [pltpu.VMEM((block, columns), bf16)] * 7 + [
+            pltpu.SemaphoreType.DMA((5,)),
+            pltpu.SemaphoreType.DMA((5,)),
+            pltpu.SemaphoreType.DMA((4,)),
+        ]
     anywhere = pl.BlockSpec(memory_space=pl.ANY)
     vmem = pl.BlockSpec(memory_space=pltpu.VMEM)
     whole_shapes = [jax.ShapeDtypeStruct((tokens, 8 * share), bf16)] * gather + [
         jax.ShapeDtypeStruct((4,) + pack.shape, bf16) for pack in packs
     ]
     outs = pl.pallas_call(
-        functools.partial(plane_kernel, pointwise, len(inputs), made, gather, count),
-        in_specs=[anywhere] + [vmem] * len(inputs) + [anywhere] * count,
-        out_specs=[vmem] * made + [anywhere] * (gather + count),
-        out_shape=[jax.ShapeDtypeStruct((tokens, share), f32)] * made + whole_shapes,
+        functools.partial(plane_kernel, pointwise, len(inputs), made, gather, count, reducing),
+        in_specs=[anywhere] + [vmem] * len(inputs) + [anywhere] * (count + reducing),
+        out_specs=[vmem] * (made + reducing) + [anywhere] * (gather + count),
+        out_shape=[jax.ShapeDtypeStruct((tokens, share), f32)] * made + totals + whole_shapes,
         scratch_shapes=[
             pltpu.VMEM((PIECES, 2, 2, size, share), bf16),
             pltpu.VMEM((PIECES, 2, 2, size, share), bf16),
@@ -503,15 +655,17 @@
             pltpu.SemaphoreType.DMA((10, PIECES)),
             pltpu.SemaphoreType.DMA((2, PIECES)),
         ]
-        + [pltpu.SemaphoreType.DMA((5, count))] * (2 if count else 0),
+        + [pltpu.SemaphoreType.DMA((5, count))] * (2 if count else 0)
+        + more_scratch,
         compiler_params=pltpu.CompilerParams(collective_id=number, has_side_effects=True),
         cost_estimate=pl.CostEstimate(
             flops=60 * 10**9, bytes_accessed=32 * tokens * share, transcendentals=0
         ),
         name="plane_step",
-    )(partial, *inputs, *packs)
-    wholes = [whole.reshape((4 * whole.shape[1],) + whole.shape[2:]) for whole in outs[made + gather :]]
-    return outs[:made], outs[made : made + gather], wholes
+    )(partial, *inputs, *packs, *given_grads)
+    at = made + reducing
+    wholes = [whole.reshape((4 * whole.shape[1],) + whole.shape[2:]) for whole in outs[at + gather :]]
+    return outs[:at], outs[at : at + gather], wholes
 
 
 def gather_now(packs, number):
@@ -545,45 +699,34 @@
 
 class Reduced:
     def __init__(self, grads):
-        n = lax.axis_size("row")
-        self.chained = n == 4
-        self.total = None
+        self.chained = lax.axis_size("row") == 4
         if not self.chained:
             self.total = lax.psum_scatter(grads, "row", scatter_dimension=0, tiled=True).astype(f32)
+            self.hops = ((), (), ())
             return
-        self.grads, self.size = grads, grads.shape[0] // n
-        self.own, self.partner, self.near, self.far = places(lax.axis_index("row"))
-        self.far_in = lax.ppermute(self.block(self.far), "row", INWARD)
-        self.near_in = lax.ppermute(self.block(self.near), "row", INWARD)
-
-    def block(self, at, *others):
-        piece = lax.dynamic_slice_in_dim(self.grads, at * self.size, self.size, 0)
-        if others:
-            piece = piece.astype(f32)
-            for other in others:
-                piece = piece + other.astype(f32)
-        return piece
-
-    def second(self, *groups):
-        if not self.chained:
-            return ()
-        far = self.block(self.far, after(self.far_in, *groups)).astype(bf16)
-        near = self.block(self.near, after(self.near_in, *groups)).astype(bf16)
-        self.far_sum = lax.ppermute(far, "row", MIDDLE)
-        self.near_sum = lax.ppermute(near, "row", MIDDLE)
-        return (far, near)
-
-    def third(self, *groups):
-        if not self.chained:
-            return ()
-        piece = self.block(self.partner, after(self.far_sum, *groups)).astype(bf16)
-        self.exchanged = lax.ppermute(piece, "row", PAIRS)
-        return (piece,)
-
-    def result(self, *groups):
-        if self.total is None:
-            self.total = self.block(self.own, after(self.near_sum, *groups), self.exchanged)
-        return self.total
+        z = lax.axis_index("row")
+        own, partner, _, _ = places(z)
+        size = grads.shape[0] // 4
+        other = (1 - z // 2) * 2 * size
+
+        def rows_of(value, at, count):
+            return lax.dynamic_slice_in_dim(value, at, count, 0)
+
+        pair = rows_of(grads, other, 2 * size)
+        first = lax.ppermute(pair, "row", INWARD)
+        second = lax.ppermute(
+            (pair.astype(f32) + first.astype(f32)).astype(bf16), "row", MIDDLE
+        )
+        swapped = rows_of(grads, partner * size, size).astype(f32) + rows_of(
+            second, lax.rem(partner, 2) * size, size
+        ).astype(f32)
+        third = lax.ppermute(swapped.astype(bf16), "row", PAIRS)
+        self.total = (
+            rows_of(grads, own * size, size).astype(f32)
+            + rows_of(second, lax.rem(own, 2) * size, size).astype(f32)
+            + third.astype(f32)
+        )
+        self.hops = ((first,), (second,), (third,))
 
 
 def after(value, *groups):
@@ -865,9 +1008,9 @@
     expert_cuts = [
         (local, a, b)
         for local in range(local_experts)
-        for a, b in cuts_of(gate_expert.shape[2], (256, 256, 512))
+        for a, b in cuts_of(gate_expert.shape[2], (512, 512))
     ]
-    chunks = shared_cuts[-1:] + expert_cuts[:2] + shared_cuts[:-1] + expert_cuts[2:]
+    chunks = shared_cuts[-1:] + expert_cuts[:-1] + shared_cuts[:-1] + expert_cuts[-1:]
 
     def pack(kind, a, b):
         if kind is None:
@@ -899,17 +1042,16 @@
         attn_part = joint_back([context], [out_weights], 0, bf16, planar=True)
         attn_part = after(attn_part, (cot_rows,))
         (stream,), (scaled,), wholes_now = plane_step(
-            attn_part, stream_step, [block_input, gain_b[None]], 1, 1, 1, packs[1:3]
+            attn_part, stream_step, [block_input, gain_b[None]], 1, 1, 1, packs[1:2]
         )
-        for at in (1, 2):
-            gathered[at] = (packs[at], wholes_now[at - 1])
+        gathered[1] = (packs[1], wholes_now[0])
     else:
         attn_part = mm_nt(context, out_full).astype(bf16)
         attn_sum = lax.psum_scatter(attn_part, "col", scatter_dimension=1, tiled=True)
         scaled_share, stream = stream_step(attn_sum.astype(f32), block_input, gain_b[None])
         scaled = lax.all_gather(scaled_share.astype(bf16), "col", axis=1, tiled=True)
     for at in range(1, len(chunks)):
-        if at not in gathered and (at <= 3 or not chained):
+        if at not in gathered:
             gathered[at] = Gathered(packs[at], (scaled,))
 
     def pieces_of(at):
@@ -937,52 +1079,40 @@
     last = len(chunks) - 1
     came, went = {}, {}
 
-    def gather_all(at, *groups):
-        gathered[at] = Gathered(packs[at], *groups)
-        came[at] = (gathered[at].second(), gathered[at].third())
-
     def hop(arrivals, at, which):
         return arrivals[at][which] if at in arrivals else ()
 
-    if planar:
-        came[3] = (gathered[3].second(), gathered[3].third())
+    for at in range(1, len(chunks)):
+        if not isinstance(gathered[at], tuple):
+            came[at] = (gathered[at].second(), gathered[at].third())
     for at, (kind, a, b) in enumerate(chunks):
         coef = jnp.concatenate([scale_b, shares[kind][:, None]], axis=1)
-        if planar:
-            if at == 1:
-                coef = after(coef, hop(came, 3, 0))
-                gather_all(4, (sums,))
-            if at == 2:
-                coef = after(coef, hop(came, 3, 1), hop(went, 0, 0))
-                gather_all(5, (sums,))
-            if at == 3:
-                coef = after(coef, hop(came, 4, 0), hop(went, 1, 0), hop(went, 0, 1))
-            if at == 4:
-                dscaled_early = joint_back(dpairs, wholes, 0, f32)
-                coef = after(
-                    coef, (dscaled_early,), hop(came, 5, 0), hop(went, 2, 0), hop(went, 1, 1), hop(went, 0, 2)
-                )
-            if at == 5:
-                moe_early = joint_back(hiddens, wholes, 2, f32)
-                coef = after(coef, (moe_early,), hop(went, 3, 0), hop(went, 2, 1), hop(went, 1, 2))
-        elif at == last:
+        if at == last:
             dscaled_early = joint_back(dpairs, wholes, 0, f32)
             moe_early = joint_back(hiddens, wholes, 2, f32)
+            coef = after(coef, (dscaled_early, moe_early))
+        if planar and at > 0:
+            coef = after(
+                coef,
+                hop(came, at + 1, 0),
+                hop(came, at, 1) if at < last else (),
+                hop(went, at - 2, 0),
+                hop(went, at - 3, 1),
+                hop(went, at - 4, 2),
+            )
         dpair, hidden, sums, grads, whole = expert_chunk(pieces_of(at), scaled, cot_rows, coef)
         dots[kind] = dots.get(kind, 0.0) + sums[:, 0]
         inner = inner + sums[:, 1]
         dpairs.append(dpair)
         hiddens.append(hidden)
         wholes.append(whole)
-        one = Reduced(grads)
-        reduced.append(one)
-        if chained:
-            went[at] = ((one.far_in, one.near_in), one.second(), one.third())
-            went[at] = (went[at][0], (one.far_sum, one.near_sum), (one.exchanged,))
-    first_late = 4 if planar else last
-    late_pairs, late_wholes = dpairs[first_late:], wholes[first_late:]
-    if planar:
-        late_pairs[-1] = after(late_pairs[-1], hop(went, 4, 0), hop(went, 3, 1), hop(went, 2, 2))
+        if at < last or not planar:
+            reduced.append(Reduced(grads))
+            went[at] = reduced[at].hops
+    late_pairs, late_wholes = dpairs[last:], wholes[last:]
+    late_pairs[-1] = after(
+        late_pairs[-1], hop(went, last - 1, 0), hop(went, last - 2, 1), hop(went, last - 3, 2)
+    )
     dscaled_part = joint_back(late_pairs, late_wholes, 0, bf16, dscaled_early, planar=planar)
     moe_part = joint_back(hiddens[last:], wholes[last:], 2, bf16, moe_early)
 
@@ -1004,7 +1134,9 @@
     damp = scale_b * scale_b * inner[:, None] / width
     step_inputs = [back_term, grad_output, stream, damp, gain_b[None]]
     if planar:
-        (dstream, dscaled), (dattn,), _ = plane_step(dscaled_part, dstream_step, step_inputs, 2, 1, 2)
+        (dstream, dscaled, last_grad), (dattn,), _ = plane_step(
+            dscaled_part, dstream_step, step_inputs, 2, 1, 2, (), grads
+        )
     else:
         dscaled_sum = lax.psum_scatter(dscaled_part, "col", scatter_dimension=1, tiled=True)
         dstream_low, dstream, dscaled = dstream_step(dscaled_sum.astype(f32), *step_inputs)
@@ -1015,22 +1147,27 @@
         after(moe_part, (dattn,)), "col", scatter_dimension=1, tiled=True
     ).astype(f32)
     block_output = (stream + moe_share).astype(bf16)
-    waits = hop(went, 4, 1) + hop(went, 3, 2) + hop(went, 5, 0)
-    out_reduced = Reduced(mm_tn(dattn, context).astype(bf16))
-    dcontext = after(mm(dattn, out_full).astype(bf16), waits)
+    out_part = mm_tn(dattn, context).astype(bf16)
+    dcontext = mm(dattn, out_full).astype(bf16)
+    dcontext = after(dcontext, hop(went, last - 1, 1), hop(went, last - 2, 2))
     dqkv, inner_a = attend_backward(qkv, dcontext, lse, lengths, cosine, sine)
-    waits = hop(went, 5, 1) + hop(went, 4, 2)
-    out_reduced.second()
-    dnormed_part = after(mm_nt(dqkv, qkv_full).astype(bf16), waits)
-    dnormed_sum = lax.psum_scatter(dnormed_part, "col", scatter_dimension=1, tiled=True)
-    qkv_reduced = Reduced(mm_tn(normed_a, dqkv).astype(bf16))
-    out_reduced.third()
-    qkv_reduced.second()
-    qkv_reduced.third()
     inner_a = lax.psum(inner_a[:, 0], "col")[:, None]
-    qkv_grad, out_grad = qkv_reduced.result(), out_reduced.result()
-    unit_grads = [one.result() for one in reduced]
-    dnormed_a = after(dnormed_sum, (inner_a,)).astype(f32)
+    attn_grads = jnp.concatenate([mm_tn(normed_a, dqkv).astype(bf16), out_part], axis=1)
+    if planar:
+        dnormed_part = joint_back([dqkv], [qkv_full], 0, bf16, planar=True)
+        dnormed_part = after(dnormed_part, hop(went, last - 1, 2))
+        (dnormed_a, attn_grad), _, _ = plane_step(
+            dnormed_part, lambda total: (total,), [], 1, 0, 3, (), attn_grads
+        )
+    else:
+        dnormed_a = lax.psum_scatter(
+            mm_nt(dqkv, qkv_full).astype(bf16), "col", scatter_dimension=1, tiled=True
+        ).astype(f32)
+        attn_grad = Reduced(attn_grads).total
+    qkv_grad, out_grad = attn_grad[:, : 3 * head_width], attn_grad[:, 3 * head_width :]
+    unit_grads = [one.total for one in reduced]
+    if planar:
+        unit_grads.append(last_grad)
     gain_a_share = input_gain.astype(f32)
     dinput = dstream + scale_a * gain_a_share * dnormed_a
     dinput = dinput - x_share * (scale_a * scale_a * inner_a / width)

time: 1260 us -> 1230 us (0.976)
  starting transfers between devices: 167 us -> 79.7 us
  Pallas kernels: 632 us -> 719 us
  other arithmetic: 114 us -> 85.9 us
    pallas_call x2 -> x3, Pallas kernels: 207 us -> 301 us  [plane_step(): pl.pallas_call(functools.partial(plane_kernel, pointwise, len(inputs), ma...]
    ppermute x40 -> x12, starting transfers between devices: 136 us -> 49.1 us  [the longest x4 21.1 us: __init__(): first = lax.ppermute(pair, 'row', INWARD)]
    ppermute x40 -> x12, waiting for transfers between devices: 123 us -> 61.9 us  [the longest x4 43.9 us: __init__(): third = lax.ppermute(swapped.astype(bf16), 'row', PAIRS)]
    ppermute x4, waiting for transfers between devices: 13.4 us -> 52 us  [third(): self.far_out = lax.ppermute(after(self.far_mid, *groups), 'row', OUTWARD)]
    ppermute x4, waiting for transfers between devices: 10.1 us -> 38.8 us  [second(): self.near_out = lax.ppermute(after(self.near_mid, *groups), 'row', OUTWARD)]
    convert_element_type x24 -> x8, other arithmetic: 45.5 us -> 28.5 us  [the longest x4 18.9 us: __init__(): (pair.astype(f32) + first.astype(f32)).astype(bf16)]
    pallas_call x6 -> x5, Pallas kernels: 199 us -> 183 us  [expert_chunk(): pl.pallas_call(functools.partial(expert_kernel, size, steps, count), grid...]
    pallas_call x5 -> x6, Pallas kernels: 97.2 us -> 112 us  [joint_back(): pl.pallas_call(functools.partial(joint_kernel, len(lefts), len(base) > 0,...]
  transfers between devices with their start and end apart: 65 -> 36, of which waited for: 14 -> 8; matrix products, arithmetic and copies ran while one was open for 18% -> 16% of each run, Pallas kernels for 51% -> 59%
where the time goes in v8:
time: 1230 us
  Pallas kernels  719 us (58%)
  waiting for transfers between devices  159 us (13%)
  other arithmetic  85.9 us (7%)
  starting transfers between devices  79.7 us (6%)
  local copies, waits for them, and re-layouts  73.8 us (6%)
  blocking collectives  48.4 us (4%)
  matrix products  44.6 us (4%)
  between operations  15.4 us (1%)
    pallas_call x3, Pallas kernels, plane_step(): pl.pallas_call(functools.partial(plane_kernel, pointwise, len(inputs), ma...  301 us
    pallas_call x5, Pallas kernels, expert_chunk(): pl.pallas_call(functools.partial(expert_kernel, size, steps, count), grid...  183 us
    pallas_call x6, Pallas kernels, joint_back(): pl.pallas_call(functools.partial(joint_kernel, len(lefts), len(base) > 0,...  112 us
    pallas_call x1, Pallas kernels, gather_now(): pl.pallas_call(functools.partial(gather_kernel, count), in_specs=[anywher...  81.1 us
    ppermute x4, waiting for transfers between devices, third(): self.far_out = lax.ppermute(after(self.far_mid, *groups), 'row', OUTWARD)  52 us
    ppermute x4, waiting for transfers between devices, __init__(): third = lax.ppermute(swapped.astype(bf16), 'row', PAIRS)  43.9 us
    ppermute x4, waiting for transfers between devices, second(): self.near_out = lax.ppermute(after(self.near_mid, *groups), 'row', OUTWARD)  38.8 us
    pallas_call x1, Pallas kernels, attend_backward(): pl.pallas_call(attend_backward_kernel, grid_spec=pltpu.PrefetchScalarGrid...  28.5 us
  transfers between devices with their start and end apart: 36, of which 8 were waited for; matrix products, arithmetic and copies ran while one was open for 16% of the time, Pallas kernels for 59%

profile of v8, /device:TPU:0, one launch (start us, length us, event | category | flops | bytes accessed | tf_op | source)
XLA Modules:
  0.0 1225.9 jit_solution(11278660823435175113)
XLA Ops:
  20.7 8.9 all_gather.16
  31.0 81.1 %gather_rows.1 = (bf16[4,512,768]{2,1,0:T(8,128)(2,1)}, bf16[4,512,384]{2,1,0:T(8,128)(2,1)}) custom-call(bf16[512,768]{1,0:T(8,128)(2,1)} %copy.135.refs_0_, bf16[512,384]{1,0:T(8,128)(2,1)} %fusion.18.refs_1_), custom_call_target="tpu_custom_call" | custom-call | flops 63700992000 | bytes 7077888 | tf_op jit(solution)/shard_map/gather_rows/pallas_call | solution.py:677
  131.2 10.5 fusion.4.raw_ref
  141.7 12.7 %attend_forward.1 = (bf16[2048,768]{1,0:T(8,128)(2,1)}, bf16[2048,256]{1,0:T(8,128)(2,1)}, f32[2048,256]{1,0:T(8,128)}) custom-call(s32[2]{0:T(128)} %dynamic_slice.70.length_ref, f32[2048,768]{1,0:T(8,128)} %fusion.4.raw_ref, f32[1024,128]{1,0:T(8,128)} %pad_maximum_fusion.9.cos_ref, f32[1024,128]{1,0:T(8,128)} %pad_maximum_fusion.10.sin_ref), custom_call_target="tpu_custom_call" | custom-call | flops 1610612736 | bytes 12582912 | tf_op jit(solution)/shard_map/attend_forward/pallas_call | solution.py:81
  154.4 8.7 joint_back.6.refs_0_
  163.2 124.3 %plane_step.3 = (f32[2048,256]{1,0:T(8,128)}, bf16[2048,2048]{1,0:T(8,128)(2,1)}, bf16[4,512,1536]{2,1,0:T(8,128)(2,1)}) custom-call(bf16[2,2,2,2048,256]{4,3,2,1,0:T(8,128)(2,1)} %joint_back.6.refs_0_, bf16[2048,256]{1,0:T(8,128)(2,1)} %refs_1_.1, f32[1,256]{1,0:T(1,128)} %reshape_convert_fusion.refs_2_.refs_5_, ...), custom_call_target="tpu_custom_call" | custom-call | flops 60000002048 | bytes 16777216 | tf_op jit(solution)/shard_map/plane_step/pallas_call | solution.py:642
  302.7 27.9 %expert_chunk.5 = (bf16[2048,512]{1,0:T(8,128)(2,1)}, bf16[2048,256]{1,0:T(8,128)(2,1)}, f32[2048,2]{1,0:T(8,128)}, bf16[2048,768]{1,0:T(8,128)(2,1)}, bf16[2048,768]{1,0:T(8,128)(2,1)}) custom-call(s32[1]{0:T(128)} %bitcast.13.z_ref, bf16[512,768]{1,0:T(8,128)(2,1)} %fusion.16.refs_0_, bf16[512,768]{1,0:T(8,128)(2,1)} %collective-permute-done.refs_1_, ...), custom_call_target="tpu_custom_call" | custom-call | flops 12884901888 | bytes 46137344 | tf_op jit(solution)/shard_map/expert_chunk/pallas_call | solution.py:847
  355.5 18.0 %collective-permute-done.17 = bf16[1024,768]{1,0:T(8,128)(2,1)} collective-permute-done((bf16[1024,768]{1,0:T(8,128)(2,1)}, bf16[1024,768]{1,0:T(8,128)(2,1)}, u32[]{:S(2)}, u32[]{:S(2)}) %collective-permute-start.17) | collective-permute-done | bytes 1572896 | tf_op jit(solution)/shard_map/ppermute | solution.py:716
  378.4 39.5 %expert_chunk.6 = (bf16[2048,1024]{1,0:T(8,128)(2,1)}, bf16[2048,512]{1,0:T(8,128)(2,1)}, f32[2048,2]{1,0:T(8,128)}, bf16[2048,1536]{1,0:T(8,128)(2,1)}, bf16[2048,1536]{1,0:T(8,128)(2,1)}) custom-call(s32[1]{0:T(128)} %bitcast.13.z_ref, bf16[512,1536]{1,0:T(8,128)(2,1)} %pad_maximum_fusion.1.refs_3_.refs_0_, bf16[2048,1536]{1,0:T(8,128)(2,1)} %bitcast.114, ...), custom_call_target="tpu_custom_call" | custom-call | flops 25769803776 | bytes 58720256 | tf_op jit(solution)/shard_map/expert_chunk/pallas_call | solution.py:847
  434.5 16.3 %collective-permute-start.25 = (bf16[512,768]{1,0:T(8,128)(2,1)S(1)}, bf16[512,768]{1,0:T(8,128)(2,1)}, u32[]{:S(2)}, u32[]{:S(2)}) collective-permute-start(bf16[512,768]{1,0:T(8,128)(2,1)S(1)} %add_convert_fusion.8), channel_id=1, source_target_pairs={{0,8},{8,0},{16,24},{24,16},{1,9},{9,1},{17,25},{25,17},{2,10},{10... | collective-permute-start | bytes 2359304 | tf_op jit(solution)/shard_map/ppermute | solution.py:723
  454.0 29.9 %collective-permute-done.13.refs_4_ = bf16[512,1536]{1,0:T(8,128)(2,1)} collective-permute-done((bf16[512,1536]{1,0:T(8,128)(2,1)}, bf16[512,1536]{1,0:T(8,128)(2,1)}, u32[]{:S(2)}, u32[]{:S(2)}) %collective-permute-start.13) | collective-permute-done | bytes 1572896 | tf_op jit(solution)/shard_map/ppermute | solution.py:190
  485.6 26.5 %collective-permute-done.25 = bf16[512,768]{1,0:T(8,128)(2,1)} collective-permute-done((bf16[512,768]{1,0:T(8,128)(2,1)S(1)}, bf16[512,768]{1,0:T(8,128)(2,1)}, u32[]{:S(2)}, u32[]{:S(2)}) %collective-permute-start.25) | collective-permute-done | bytes 786464 | tf_op jit(solution)/shard_map/ppermute | solution.py:723
  525.6 8.9 collective-permute-done.19.refs_4_
  544.8 23.4 %collective-permute-done.14.refs_5_ = bf16[512,1536]{1,0:T(8,128)(2,1)} collective-permute-done((bf16[512,1536]{1,0:T(8,128)(2,1)}, bf16[512,1536]{1,0:T(8,128)(2,1)}, u32[]{:S(2)}, u32[]{:S(2)}) %collective-permute-start.14) | collective-permute-done | bytes 1572896 | tf_op jit(solution)/shard_map/ppermute | solution.py:197
  568.2 39.5 %expert_chunk.7 = (bf16[2048,1024]{1,0:T(8,128)(2,1)}, bf16[2048,512]{1,0:T(8,128)(2,1)}, f32[2048,2]{1,0:T(8,128)}, bf16[2048,1536]{1,0:T(8,128)(2,1)}, bf16[2048,1536]{1,0:T(8,128)(2,1)}) custom-call(s32[1]{0:T(128)} %bitcast.13.z_ref, bf16[512,1536]{1,0:T(8,128)(2,1)} %pad_maximum_fusion.2.refs_0_, bf16[512,1536]{1,0:T(8,128)(2,1)} %collective-permute-done.10.refs_1_, ...), custom_call_target="tpu_custom_call" | custom-call | flops 25769803776 | bytes 58720256 | tf_op jit(solution)/shard_map/expert_chunk/pallas_call | solution.py:847
  613.1 28.6 %collective-permute-done.20.refs_5_ = bf16[512,1536]{1,0:T(8,128)(2,1)} collective-permute-done((bf16[512,1536]{1,0:T(8,128)(2,1)}, bf16[512,1536]{1,0:T(8,128)(2,1)}, u32[]{:S(2)}, u32[]{:S(2)}) %collective-permute-start.20) | collective-permute-done | bytes 1572896 | tf_op jit(solution)/shard_map/ppermute | solution.py:197
  641.7 39.5 %expert_chunk.8 = (bf16[2048,1024]{1,0:T(8,128)(2,1)}, bf16[2048,512]{1,0:T(8,128)(2,1)}, f32[2048,2]{1,0:T(8,128)}, bf16[2048,1536]{1,0:T(8,128)(2,1)}, bf16[2048,1536]{1,0:T(8,128)(2,1)}) custom-call(s32[1]{0:T(128)} %bitcast.13.z_ref, bf16[512,1536]{1,0:T(8,128)(2,1)} %pad_maximum_fusion.3.refs_0_, bf16[512,1536]{1,0:T(8,128)(2,1)} %collective-permute-done.15.refs_1_, ...), custom_call_target="tpu_custom_call" | custom-call | flops 25769803776 | bytes 58720256 | tf_op jit(solution)/shard_map/expert_chunk/pallas_call | solution.py:847
  681.3 21.9 %joint_back.8.refs_2_ = f32[2048,2048]{1,0:T(8,128)} custom-call(bf16[2048,256]{1,0:T(8,128)(2,1)} %get-tuple-element.97.refs_0_, bf16[2048,512]{1,0:T(8,128)(2,1)} %get-tuple-element.98.refs_1_, bf16[2048,512]{1,0:T(8,128)(2,1)} %get-tuple-element.99.refs_2_, bf16[2048,512]{1,0:T(8,128)(2,1)} %get-tuple-element.100.refs_3_, ...), custom_call_target="tpu_custom_call" | custom-call | flops 15032385536 | bytes 31457280 | tf_op jit(solution)/shard_map/joint_back/pallas_call | solution.py:910
  703.2 39.5 %joint_back.7.refs_2_ = f32[2048,2048]{1,0:T(8,128)} custom-call(bf16[2048,512]{1,0:T(8,128)(2,1)} %get-tuple-element.81.refs_0_, bf16[2048,1024]{1,0:T(8,128)(2,1)} %get-tuple-element.85.refs_1_, bf16[2048,1024]{1,0:T(8,128)(2,1)} %get-tuple-element.89.refs_2_, bf16[2048,1024]{1,0:T(8,128)(2,1)} %get-tuple-element.92.refs_3_, ...), custom_call_target="tpu_custom_call" | custom-call | flops 30064771072 | bytes 46137344 | tf_op jit(solution)/shard_map/joint_back/pallas_call | solution.py:910
  762.5 36.2 %expert_chunk.9 = (bf16[2048,768]{1,0:T(8,128)(2,1)}, bf16[2048,384]{1,0:T(8,128)(2,1)}, f32[2048,2]{1,0:T(8,128)}, bf16[2048,1152]{1,0:T(8,128)(2,1)}, bf16[2048,1152]{1,0:T(8,128)(2,1)}) custom-call(s32[1]{0:T(128)} %bitcast.13.z_ref, bf16[512,1152]{1,0:T(8,128)(2,1)} %pad_maximum_fusion.7.refs_0_, bf16[512,1152]{1,0:T(8,128)(2,1)} %collective-permute-done.4.refs_1_, ...), custom_call_target="tpu_custom_call" | custom-call | flops 19327352832 | bytes 52428800 | tf_op jit(solution)/shard_map/expert_chunk/pallas_call | solution.py:847
  803.6 13.2 %all-gather.1 = f32[8,3,2048]{2,1,0:T(4,128)S(1)} all-gather(f32[1,3,2048]{2,1,0:T(4,128)S(1)} %maximum_bitcast_fusion.3), channel_id=2, replica_groups=mesh['row'=4,'col'=8] {'col'}, dimensions={0}, use_global_device_ids=true | all-gather | bytes 221184 | tf_op jit(solution)/shard_map/all_gather | solution.py:1120
  831.1 14.3 %joint_back.9 = bf16[2048,2048]{1,0:T(8,128)(2,1)} custom-call(bf16[2048,384]{1,0:T(8,128)(2,1)} %get-tuple-element.104.refs_0_, bf16[2048,1152]{1,0:T(8,128)(2,1)} %get-tuple-element.105.refs_1_, f32[2048,2048]{1,0:T(8,128)} %joint_back.8.refs_2_), custom_call_target="tpu_custom_call" | custom-call | flops 3221225472 | bytes 19922944 | tf_op jit(solution)/shard_map/joint_back/pallas_call | solution.py:910
  856.2 15.7 %joint_back.10.refs_0_ = bf16[2,2,2,2048,256]{4,3,2,1,0:T(8,128)(2,1)} custom-call(bf16[2048,768]{1,0:T(8,128)(2,1)} %get-tuple-element.108.refs_0_, bf16[2048,1152]{1,0:T(8,128)(2,1)} %get-tuple-element.105.refs_1_, f32[2048,2048]{1,0:T(8,128)} %joint_back.7.refs_2_), custom_call_target="tpu_custom_call" | custom-call | flops 6442450944 | bytes 23068672 | tf_op jit(solution)/shard_map/joint_back/pallas_call | solution.py:910
  871.9 97.6 %plane_step.4 = (f32[2048,256]{1,0:T(8,128)}, f32[2048,256]{1,0:T(8,128)}, f32[512,1152]{1,0:T(8,128)}, bf16[2048,2048]{1,0:T(8,128)(2,1)}) custom-call(bf16[2,2,2,2048,256]{4,3,2,1,0:T(8,128)(2,1)} %joint_back.10.refs_0_, f32[2048,256]{1,0:T(8,128)} %fusion.28.refs_1_, bf16[2048,256]{1,0:T(8,128)(2,1)} %refs_2_.1, f32[2048,256]{1,0:T(8,128)} %get-tuple-element.78.refs_3_, ...), custom_call_target="tpu_custom_call" | custom-call | flops 60000002048 | bytes 16777216 | tf_op jit(solution)/shard_map/plane_step/pallas_call | solution.py:642
  979.2 9.3 convolution_convert_fusion.2.dcontext_ref
  991.9 17.3 %collective-permute-done.30 = bf16[512,1536]{1,0:T(8,128)(2,1)S(1)} collective-permute-done((bf16[512,1536]{1,0:T(8,128)(2,1)S(1)}, bf16[512,1536]{1,0:T(8,128)(2,1)S(1)}, u32[]{:S(2)}, u32[]{:S(2)}) %collective-permute-start.30) | collective-permute-done | bytes 1572896 | tf_op jit(solution)/shard_map/ppermute | solution.py:723
  1010.4 28.5 %attend_backward.1 = (bf16[2048,768]{1,0:T(8,128)(2,1)}, f32[2048,1]{1,0:T(8,128)}) custom-call(s32[2]{0:T(128)} %dynamic_slice.70.length_ref, bf16[2048,768]{1,0:T(8,128)(2,1)} %get-tuple-element.118.qkv_ref, bf16[2048,256]{1,0:T(8,128)(2,1)} %convolution_convert_fusion.2.dcontext_ref, f32[2048,256]{1,0:T(8,128)} %get-tuple-element.120.lse_ref, ...), custom_call_target="tpu_custom_call" | custom-call | flops 4294967296 | bytes 12582912 | tf_op jit(solution)/shard_map/attend_backward/pallas_call | solution.py:151
  1038.8 12.2 joint_back.11.refs_0_
  1051.0 11.5 convolution_convert_fusion
  1071.2 79.4 %plane_step.5 = (f32[2048,256]{1,0:T(8,128)}, f32[512,1024]{1,0:T(8,128)}) custom-call(bf16[2,2,2,2048,256]{4,3,2,1,0:T(8,128)(2,1)} %joint_back.11.refs_0_, bf16[4,512,1024]{2,1,0:T(8,128)(2,1)} %bitcast.86), custom_call_target="tpu_custom_call" | custom-call | flops 60000002048 | bytes 16777216 | tf_op jit(solution)/shard_map/plane_step/pallas_call | solution.py:642
  1180.6 14.1 %psum.21 = f32[2048]{0:T(1024)S(1)} all-reduce(f32[2048]{0:T(1024)S(1)} %reduce.5), channel_id=1, replica_groups=mesh['row'=4,'col'=8] {'col'}, use_global_device_ids=true, to_apply=%region_10.11 | all-reduce | flops 2048 | bytes 16384 | tf_op jit(solution)/shard_map/psum | solution.py:1154
  1207.0 12.1 all-reduce.4
  (345 shorter events, 243.3 us)
Async XLA Ops:
  7.2 117.5 %all-gather.5.cloned.1.call-start = ((), (), s32[]{:S(2)}) async-start(), calls=%async_computation.2 | async-start | bytes 9437184 | tf_op jit(solution)/shard_map/all_gather | solution.py:1029
  8.0 155.2 %all-gather.7.cloned.1.call-start = ((), (), s32[]{:S(2)}) async-start(), calls=%async_computation.3 | async-start | bytes 9437184 | tf_op jit(solution)/shard_map/all_gather | solution.py:1031
  8.7 844.8 %reduce-scatter.5.cloned.1.call-start = ((), (), s32[]{:S(2)}) async-start(), calls=%async_computation.5 | async-start | bytes 163840 | tf_op jit(solution)/shard_map/reduce_scatter | solution.py:1131
  11.2 108.1 %collective-permute-start = (bf16[512,768]{1,0:T(8,128)(2,1)}, bf16[512,768]{1,0:T(8,128)(2,1)}, u32[]{:S(2)}, u32[]{:S(2)}) collective-permute-start(bf16[512,768]{1,0:T(8,128)(2,1)} %fusion.16.refs_0_), channel_id=1, source_target_pairs={{0,8},{8,0},{16,24},{24,16},{1,9},{9,1},{17,25},{25,17},{2,10},{10... | collective-permute-start | bytes 2359304 | tf_op jit(solution)/shard_map/ppermute | solution.py:184
  14.2 107.6 %collective-permute-start.1 = (bf16[512,768]{1,0:T(8,128)(2,1)}, bf16[512,768]{1,0:T(8,128)(2,1)}, u32[]{:S(2)}, u32[]{:S(2)}) collective-permute-start(bf16[512,768]{1,0:T(8,128)(2,1)} %fusion.16.refs_0_), channel_id=1, source_target_pairs={{8,16},{16,8},{9,17},{17,9},{10,18},{18,10},{11,19},{19,11},{12,20... | collective-permute-start | bytes 2359304 | tf_op jit(solution)/shard_map/ppermute | solution.py:185
  123.2 178.6 %collective-permute-start.9 = (bf16[512,768]{1,0:T(8,128)(2,1)S(1)}, bf16[512,768]{1,0:T(8,128)(2,1)S(1)}, u32[]{:S(2)}, u32[]{:S(2)}) collective-permute-start(bf16[512,768]{1,0:T(8,128)(2,1)S(1)} %collective-permute-done.2.refs_3_), channel_id=1, source_target_pairs={{8,0},{16,24},{9,1},{17,25},{10,2},{18,26},{11,3},{19,27},{12,4},{... | collective-permute-start | bytes 2359304 | tf_op jit(solution)/shard_map/ppermute | solution.py:197
  287.5 60.7 %collective-permute-start.10 = (bf16[512,1536]{1,0:T(8,128)(2,1)}, bf16[512,1536]{1,0:T(8,128)(2,1)}, u32[]{:S(2)}, u32[]{:S(2)}) collective-permute-start(bf16[512,1536]{1,0:T(8,128)(2,1)} %pad_maximum_fusion.2.refs_0_), channel_id=1, source_target_pairs={{0,8},{8,0},{16,24},{24,16},{1,9},{9,1},{17,25},{25,17},{2,10},{10... | collective-permute-start | bytes 4718600 | tf_op jit(solution)/shard_map/ppermute | solution.py:184
  287.6 64.0 %collective-permute-start.11 = (bf16[512,1536]{1,0:T(8,128)(2,1)}, bf16[512,1536]{1,0:T(8,128)(2,1)}, u32[]{:S(2)}, u32[]{:S(2)}) collective-permute-start(bf16[512,1536]{1,0:T(8,128)(2,1)} %pad_maximum_fusion.2.refs_0_), channel_id=1, source_target_pairs={{8,16},{16,8},{9,17},{17,9},{10,18},{18,10},{11,19},{19,11},{12,20... | collective-permute-start | bytes 4718600 | tf_op jit(solution)/shard_map/ppermute | solution.py:185
  333.3 40.2 %collective-permute-start.17 = (bf16[1024,768]{1,0:T(8,128)(2,1)}, bf16[1024,768]{1,0:T(8,128)(2,1)}, u32[]{:S(2)}, u32[]{:S(2)}) collective-permute-start(bf16[1024,768]{1,0:T(8,128)(2,1)} %constant_dynamic-slice_fusion.4), channel_id=1, source_target_pairs={{0,8},{24,16},{1,9},{25,17},{2,10},{26,18},{3,11},{27,19},{4,12},{... | collective-permute-start | bytes 4718600 | tf_op jit(solution)/shard_map/ppermute | solution.py:716
  346.5 71.5 %collective-permute-start.4 = (bf16[512,1152]{1,0:T(8,128)(2,1)}, bf16[512,1152]{1,0:T(8,128)(2,1)}, u32[]{:S(2)}, u32[]{:S(2)}) collective-permute-start(bf16[512,1152]{1,0:T(8,128)(2,1)} %pad_maximum_fusion.7.refs_0_), channel_id=1, source_target_pairs={{0,8},{8,0},{16,24},{24,16},{1,9},{9,1},{17,25},{25,17},{2,10},{10... | collective-permute-start | bytes 3538952 | tf_op jit(solution)/shard_map/ppermute | solution.py:184
  346.5 77.0 %collective-permute-start.5 = (bf16[512,1152]{1,0:T(8,128)(2,1)}, bf16[512,1152]{1,0:T(8,128)(2,1)}, u32[]{:S(2)}, u32[]{:S(2)}) collective-permute-start(bf16[512,1152]{1,0:T(8,128)(2,1)} %pad_maximum_fusion.7.refs_0_), channel_id=1, source_target_pairs={{8,16},{16,8},{9,17},{17,9},{10,18},{18,10},{11,19},{19,11},{12,20... | collective-permute-start | bytes 3538952 | tf_op jit(solution)/shard_map/ppermute | solution.py:185
  348.2 86.4 %collective-permute-start.15 = (bf16[512,1536]{1,0:T(8,128)(2,1)}, bf16[512,1536]{1,0:T(8,128)(2,1)}, u32[]{:S(2)}, u32[]{:S(2)}) collective-permute-start(bf16[512,1536]{1,0:T(8,128)(2,1)} %pad_maximum_fusion.3.refs_0_), channel_id=1, source_target_pairs={{0,8},{8,0},{16,24},{24,16},{1,9},{9,1},{17,25},{25,17},{2,10},{10... | collective-permute-start | bytes 4718600 | tf_op jit(solution)/shard_map/ppermute | solution.py:184
  351.6 99.3 %collective-permute-start.16 = (bf16[512,1536]{1,0:T(8,128)(2,1)}, bf16[512,1536]{1,0:T(8,128)(2,1)}, u32[]{:S(2)}, u32[]{:S(2)}) collective-permute-start(bf16[512,1536]{1,0:T(8,128)(2,1)} %pad_maximum_fusion.3.refs_0_), channel_id=1, source_target_pairs={{8,16},{16,8},{9,17},{17,9},{10,18},{18,10},{11,19},{19,11},{12,20... | collective-permute-start | bytes 4718600 | tf_op jit(solution)/shard_map/ppermute | solution.py:185
  376.4 55.5 %collective-permute-start.22 = (bf16[1024,768]{1,0:T(8,128)(2,1)}, bf16[1024,768]{1,0:T(8,128)(2,1)}, u32[]{:S(2)}, u32[]{:S(2)}) collective-permute-start(bf16[1024,768]{1,0:T(8,128)(2,1)} %add_convert_fusion.6), channel_id=1, source_target_pairs={{8,16},{16,8},{9,17},{17,9},{10,18},{18,10},{11,19},{19,11},{12,20... | collective-permute-start | bytes 4718600 | tf_op jit(solution)/shard_map/ppermute | solution.py:717
  423.5 112.2 %collective-permute-start.21 = (bf16[1024,1536]{1,0:T(8,128)(2,1)}, bf16[1024,1536]{1,0:T(8,128)(2,1)}, u32[]{:S(2)}, u32[]{:S(2)}) collective-permute-start(bf16[1024,1536]{1,0:T(8,128)(2,1)} %constant_dynamic-slice_fusion.3), channel_id=1, source_target_pairs={{0,8},{24,16},{1,9},{25,17},{2,10},{26,18},{3,11},{27,19},{4,12},{... | collective-permute-start | bytes 9437192 | tf_op jit(solution)/shard_map/ppermute | solution.py:716
  431.9 52.0 %collective-permute-start.13 = (bf16[512,1536]{1,0:T(8,128)(2,1)}, bf16[512,1536]{1,0:T(8,128)(2,1)}, u32[]{:S(2)}, u32[]{:S(2)}) collective-permute-start(bf16[512,1536]{1,0:T(8,128)(2,1)} %collective-permute-done.11.refs_2_), channel_id=1, source_target_pairs={{8,0},{16,24},{9,1},{17,25},{10,2},{18,26},{11,3},{19,27},{12,4},{... | collective-permute-start | bytes 4718600 | tf_op jit(solution)/shard_map/ppermute | solution.py:190
  434.5 77.6 %collective-permute-start.25 = (bf16[512,768]{1,0:T(8,128)(2,1)S(1)}, bf16[512,768]{1,0:T(8,128)(2,1)}, u32[]{:S(2)}, u32[]{:S(2)}) collective-permute-start(bf16[512,768]{1,0:T(8,128)(2,1)S(1)} %add_convert_fusion.8), channel_id=1, source_target_pairs={{0,8},{8,0},{16,24},{24,16},{1,9},{9,1},{17,25},{25,17},{2,10},{10... | collective-permute-start | bytes 2359304 | tf_op jit(solution)/shard_map/ppermute | solution.py:723
  450.9 73.4 %collective-permute-start.18 = (bf16[512,1536]{1,0:T(8,128)(2,1)}, bf16[512,1536]{1,0:T(8,128)(2,1)}, u32[]{:S(2)}, u32[]{:S(2)}) collective-permute-start(bf16[512,1536]{1,0:T(8,128)(2,1)} %collective-permute-done.15.refs_1_), channel_id=1, source_target_pairs={{8,16},{16,8},{9,17},{17,9},{10,18},{18,10},{11,19},{19,11},{12,20... | collective-permute-start | bytes 4718600 | tf_op jit(solution)/shard_map/ppermute | solution.py:191
  452.7 81.7 %collective-permute-start.19 = (bf16[512,1536]{1,0:T(8,128)(2,1)}, bf16[512,1536]{1,0:T(8,128)(2,1)}, u32[]{:S(2)}, u32[]{:S(2)}) collective-permute-start(bf16[512,1536]{1,0:T(8,128)(2,1)} %collective-permute-done.16.refs_2_), channel_id=1, source_target_pairs={{8,0},{16,24},{9,1},{17,25},{10,2},{18,26},{11,3},{19,27},{12,4},{... | collective-permute-start | bytes 4718600 | tf_op jit(solution)/shard_map/ppermute | solution.py:190
  483.9 39.1 %collective-permute-start.6 = (bf16[512,1152]{1,0:T(8,128)(2,1)}, bf16[512,1152]{1,0:T(8,128)(2,1)}, u32[]{:S(2)}, u32[]{:S(2)}) collective-permute-start(bf16[512,1152]{1,0:T(8,128)(2,1)} %collective-permute-done.4.refs_1_), channel_id=1, source_target_pairs={{8,16},{16,8},{9,17},{17,9},{10,18},{18,10},{11,19},{19,11},{12,20... | collective-permute-start | bytes 3538952 | tf_op jit(solution)/shard_map/ppermute | solution.py:191
  512.1 56.0 %collective-permute-start.14 = (bf16[512,1536]{1,0:T(8,128)(2,1)}, bf16[512,1536]{1,0:T(8,128)(2,1)}, u32[]{:S(2)}, u32[]{:S(2)}) collective-permute-start(bf16[512,1536]{1,0:T(8,128)(2,1)} %collective-permute-done.12.refs_3_), channel_id=1, source_target_pairs={{8,0},{16,24},{9,1},{17,25},{10,2},{18,26},{11,3},{19,27},{12,4},{... | collective-permute-start | bytes 4718600 | tf_op jit(solution)/shard_map/ppermute | solution.py:197
  523.0 239.5 %collective-permute-start.7 = (bf16[512,1152]{1,0:T(8,128)(2,1)}, bf16[512,1152]{1,0:T(8,128)(2,1)}, u32[]{:S(2)}, u32[]{:S(2)}) collective-permute-start(bf16[512,1152]{1,0:T(8,128)(2,1)} %collective-permute-done.5.refs_2_), channel_id=1, source_target_pairs={{8,0},{16,24},{9,1},{17,25},{10,2},{18,26},{11,3},{19,27},{12,4},{... | collective-permute-start | bytes 3538952 | tf_op jit(solution)/shard_map/ppermute | solution.py:190
  524.3 238.2 %collective-permute-start.8 = (bf16[512,1152]{1,0:T(8,128)(2,1)}, bf16[512,1152]{1,0:T(8,128)(2,1)}, u32[]{:S(2)}, u32[]{:S(2)}) collective-permute-start(bf16[512,1152]{1,0:T(8,128)(2,1)} %collective-permute-done.6.refs_3_), channel_id=1, source_target_pairs={{8,0},{16,24},{9,1},{17,25},{10,2},{18,26},{11,3},{19,27},{12,4},{... | collective-permute-start | bytes 3538952 | tf_op jit(solution)/shard_map/ppermute | solution.py:197
  534.5 107.2 %collective-permute-start.20 = (bf16[512,1536]{1,0:T(8,128)(2,1)}, bf16[512,1536]{1,0:T(8,128)(2,1)}, u32[]{:S(2)}, u32[]{:S(2)}) collective-permute-start(bf16[512,1536]{1,0:T(8,128)(2,1)} %collective-permute-done.18.refs_3_), channel_id=1, source_target_pairs={{8,0},{16,24},{9,1},{17,25},{10,2},{18,26},{11,3},{19,27},{12,4},{... | collective-permute-start | bytes 4718600 | tf_op jit(solution)/shard_map/ppermute | solution.py:197
  542.5 207.1 %collective-permute-start.24 = (bf16[1024,1536]{1,0:T(8,128)(2,1)}, bf16[1024,1536]{1,0:T(8,128)(2,1)}, u32[]{:S(2)}, u32[]{:S(2)}) collective-permute-start(bf16[1024,1536]{1,0:T(8,128)(2,1)} %add_convert_fusion.2), channel_id=1, source_target_pairs={{8,16},{16,8},{9,17},{17,9},{10,18},{18,10},{11,19},{19,11},{12,20... | collective-permute-start | bytes 9437192 | tf_op jit(solution)/shard_map/ppermute | solution.py:717
  609.8 143.2 %collective-permute-start.23 = (bf16[1024,1536]{1,0:T(8,128)(2,1)S(1)}, bf16[1024,1536]{1,0:T(8,128)(2,1)}, u32[]{:S(2)}, u32[]{:S(2)}) collective-permute-start(bf16[1024,1536]{1,0:T(8,128)(2,1)S(1)} %constant_dynamic-slice_fusion.2), channel_id=1, source_target_pairs={{0,8},{24,16},{1,9},{25,17},{2,10},{26,18},{3,11},{27,19},{4,12},{... | collective-permute-start | bytes 9437192 | tf_op jit(solution)/shard_map/ppermute | solution.py:716
  746.4 71.2 %collective-permute-start.26 = (bf16[1024,1536]{1,0:T(8,128)(2,1)}, bf16[1024,1536]{1,0:T(8,128)(2,1)}, u32[]{:S(2)}, u32[]{:S(2)}) collective-permute-start(bf16[1024,1536]{1,0:T(8,128)(2,1)} %constant_dynamic-slice_fusion.1), channel_id=1, source_target_pairs={{0,8},{24,16},{1,9},{25,17},{2,10},{26,18},{3,11},{27,19},{4,12},{... | collective-permute-start | bytes 9437192 | tf_op jit(solution)/shard_map/ppermute | solution.py:716
  753.0 103.2 %collective-permute-start.28 = (bf16[512,1536]{1,0:T(8,128)(2,1)}, bf16[512,1536]{1,0:T(8,128)(2,1)}, u32[]{:S(2)}, u32[]{:S(2)}) collective-permute-start(bf16[512,1536]{1,0:T(8,128)(2,1)} %add_convert_fusion.5), channel_id=1, source_target_pairs={{0,8},{8,0},{16,24},{24,16},{1,9},{9,1},{17,25},{25,17},{2,10},{10... | collective-permute-start | bytes 4718600 | tf_op jit(solution)/shard_map/ppermute | solution.py:723
  759.7 96.5 %collective-permute-start.27 = (bf16[1024,1536]{1,0:T(8,128)(2,1)}, bf16[1024,1536]{1,0:T(8,128)(2,1)}, u32[]{:S(2)}, u32[]{:S(2)}) collective-permute-start(bf16[1024,1536]{1,0:T(8,128)(2,1)} %add_convert_fusion.1), channel_id=1, source_target_pairs={{8,16},{16,8},{9,17},{17,9},{10,18},{18,10},{11,19},{19,11},{12,20... | collective-permute-start | bytes 9437192 | tf_op jit(solution)/shard_map/ppermute | solution.py:717
  823.0 151.1 %collective-permute-start.29 = (bf16[1024,1536]{1,0:T(8,128)(2,1)}, bf16[1024,1536]{1,0:T(8,128)(2,1)}, u32[]{:S(2)}, u32[]{:S(2)}) collective-permute-start(bf16[1024,1536]{1,0:T(8,128)(2,1)} %add_convert_fusion), channel_id=1, source_target_pairs={{8,16},{16,8},{9,17},{17,9},{10,18},{18,10},{11,19},{19,11},{12,20... | collective-permute-start | bytes 9437192 | tf_op jit(solution)/shard_map/ppermute | solution.py:717
  831.0 372.6 %reduce-scatter.3.cloned.1.call-start = ((), (), s32[]{:S(2)}) async-start(), calls=%async_computation.4 | async-start | bytes 9437184 | tf_op jit(solution)/shard_map/reduce_scatter | solution.py:1146
  976.7 74.3 %collective-permute-start.31 = (bf16[512,1536]{1,0:T(8,128)(2,1)S(1)}, bf16[512,1536]{1,0:T(8,128)(2,1)S(1)}, u32[]{:S(2)}, u32[]{:S(2)}) collective-permute-start(bf16[512,1536]{1,0:T(8,128)(2,1)S(1)} %add_convert_fusion.3), channel_id=1, source_target_pairs={{0,8},{8,0},{16,24},{24,16},{1,9},{9,1},{17,25},{25,17},{2,10},{10... | collective-permute-start | bytes 4718600 | tf_op jit(solution)/shard_map/ppermute | solution.py:723
  (77 other events, 946.8 us)
Sparse Core Ops, SparseCore 0:
  9.9 58.6 all-gather.4
  70.5 55.9 all-gather.6
  831.1 22.4 reduce-scatter.4
  969.7 70.8 reduce-scatter.2

commit v9 on v8

--- a/solution.py
+++ b/solution.py
@@ -702,31 +702,47 @@
         self.chained = lax.axis_size("row") == 4
         if not self.chained:
             self.total = lax.psum_scatter(grads, "row", scatter_dimension=0, tiled=True).astype(f32)
-            self.hops = ((), (), ())
             return
         z = lax.axis_index("row")
-        own, partner, _, _ = places(z)
-        size = grads.shape[0] // 4
-        other = (1 - z // 2) * 2 * size
-
-        def rows_of(value, at, count):
-            return lax.dynamic_slice_in_dim(value, at, count, 0)
-
-        pair = rows_of(grads, other, 2 * size)
-        first = lax.ppermute(pair, "row", INWARD)
-        second = lax.ppermute(
-            (pair.astype(f32) + first.astype(f32)).astype(bf16), "row", MIDDLE
-        )
-        swapped = rows_of(grads, partner * size, size).astype(f32) + rows_of(
-            second, lax.rem(partner, 2) * size, size
-        ).astype(f32)
-        third = lax.ppermute(swapped.astype(bf16), "row", PAIRS)
-        self.total = (
-            rows_of(grads, own * size, size).astype(f32)
-            + rows_of(second, lax.rem(own, 2) * size, size).astype(f32)
-            + third.astype(f32)
-        )
-        self.hops = ((first,), (second,), (third,))
+        self.own, self.partner, _, _ = places(z)
+        self.grads, self.size = grads, grads.shape[0] // 4
+        self.pair = self.rows_of(grads, (1 - z // 2) * 2, 2)
+        self.first = lax.ppermute(self.pair, "row", INWARD)
+
+    def rows_of(self, value, at, count):
+        return lax.dynamic_slice_in_dim(value, at * self.size, count * self.size, 0)
+
+    def two(self, at):
+        mine = self.rows_of(self.grads, at, 1).astype(f32)
+        return mine + self.rows_of(self.crossed, lax.rem(at, 2), 1).astype(f32)
+
+    def second(self, *groups):
+        if not self.chained:
+            return ()
+        first = after(self.first, *groups)
+        value = (self.pair.astype(f32) + first.astype(f32)).astype(bf16)
+        self.crossed = lax.ppermute(value, "row", MIDDLE)
+        return (value,)
+
+    def third(self, *groups):
+        if not self.chained:
+            return ()
+        self.crossed = after(self.crossed, *groups)
+        value = self.two(self.partner).astype(bf16)
+        self.swapped = lax.ppermute(value, "row", PAIRS)
+        return (value,)
+
+    def result(self):
+        if self.chained:
+            return self.two(self.own) + self.swapped.astype(f32)
+        return self.total
+
+
+def one_reduction(grads):
+    one = Reduced(grads)
+    one.second()
+    one.third()
+    return one.result()
 
 
 def after(value, *groups):
@@ -1050,7 +1066,7 @@
         attn_sum = lax.psum_scatter(attn_part, "col", scatter_dimension=1, tiled=True)
         scaled_share, stream = stream_step(attn_sum.astype(f32), block_input, gain_b[None])
         scaled = lax.all_gather(scaled_share.astype(bf16), "col", axis=1, tiled=True)
-    for at in range(1, len(chunks)):
+    for at in range(1, 3 if planar else len(chunks)):
         if at not in gathered:
             gathered[at] = Gathered(packs[at], (scaled,))
 
@@ -1077,44 +1093,68 @@
         shares[local] = jnp.where(members[local], column, 0.0)
     dpairs, hiddens, wholes, reduced = [], [], [], []
     last = len(chunks) - 1
-    came, went = {}, {}
-
-    def hop(arrivals, at, which):
-        return arrivals[at][which] if at in arrivals else ()
-
-    for at in range(1, len(chunks)):
-        if not isinstance(gathered[at], tuple):
-            came[at] = (gathered[at].second(), gathered[at].third())
+    waits = ()
+    if not planar:
+        for at in range(1, len(chunks)):
+            gathered[at].second()
+            gathered[at].third()
+
+    def joints(*base):
+        return (
+            joint_back(dpairs[-2:], wholes[-2:], 0, f32, *base[:1]),
+            joint_back(hiddens[-2:], wholes[-2:], 2, f32, *base[1:]),
+        )
+
     for at, (kind, a, b) in enumerate(chunks):
         coef = jnp.concatenate([scale_b, shares[kind][:, None]], axis=1)
-        if at == last:
-            dscaled_early = joint_back(dpairs, wholes, 0, f32)
-            moe_early = joint_back(hiddens, wholes, 2, f32)
-            coef = after(coef, (dscaled_early, moe_early))
-        if planar and at > 0:
-            coef = after(
-                coef,
-                hop(came, at + 1, 0),
-                hop(came, at, 1) if at < last else (),
-                hop(went, at - 2, 0),
-                hop(went, at - 3, 1),
-                hop(went, at - 4, 2),
-            )
+        coef = after(coef, waits)
         dpair, hidden, sums, grads, whole = expert_chunk(pieces_of(at), scaled, cot_rows, coef)
         dots[kind] = dots.get(kind, 0.0) + sums[:, 0]
         inner = inner + sums[:, 1]
         dpairs.append(dpair)
         hiddens.append(hidden)
         wholes.append(whole)
-        if at < last or not planar:
+        now = (sums,)
+        waits = ()
+        if at == 1:
+            early, joined = joints(), 2
+            waits += early
+        elif at == 3 and at < last:
+            early, joined = joints(*early), 4
+            waits += early
+        if planar and at + 2 <= last:
+            if at == 0:
+                waits += gathered[2].second(now)
+            elif at == 1:
+                gathered[2].third(now)
+                gathered[3] = Gathered(packs[3], (gathered[2].far_mid,))
+            elif at == 2:
+                gathered[3].second(now)
+                gathered[3].third()
+                gathered[4] = Gathered(packs[4], (gathered[3].far_mid,))
+        if planar and at == 3:
+            gathered[4].second(now)
+            gathered[4].third()
+        if not planar:
             reduced.append(Reduced(grads))
-            went[at] = reduced[at].hops
-    late_pairs, late_wholes = dpairs[last:], wholes[last:]
-    late_pairs[-1] = after(
-        late_pairs[-1], hop(went, last - 1, 0), hop(went, last - 2, 1), hop(went, last - 3, 2)
-    )
-    dscaled_part = joint_back(late_pairs, late_wholes, 0, bf16, dscaled_early, planar=planar)
-    moe_part = joint_back(hiddens[last:], wholes[last:], 2, bf16, moe_early)
+        elif at < last:
+            if at >= 1:
+                waits += reduced[at - 1].second(now)
+            if at >= 2:
+                waits += reduced[at - 2].third(now)
+            reduced.append(Reduced(grads))
+    now = (sums,)
+    if planar:
+        waits = reduced[3].second(now)
+        waits += reduced[2].third(now)
+    else:
+        waits = ()
+        for one in reduced:
+            one.second()
+            one.third()
+    late_pairs, late_wholes, late_hiddens = dpairs[joined:], wholes[joined:], hiddens[joined:]
+    late_pairs[-1] = after(late_pairs[-1], waits)
+    dscaled_part = joint_back(late_pairs, late_wholes, 0, bf16, early[0], planar=planar)
 
     named = [jnp.where(members[local], dots[local], 0.0) for local in range(local_experts)]
     table = lax.all_gather(jnp.stack(named + [dots[None], inner]), "col", axis=0)
@@ -1126,9 +1166,6 @@
     inner = inner + jnp.sum(dboth * both_logits, axis=1)
     dboth = scale_b * dboth
     parts = split_three(dboth)
-    stacked = mm_tn(jnp.concatenate(parts, axis=1), scaled)
-    grad_router_part = stacked.reshape(3, experts + 1, width).sum(axis=0)
-    grad_router_both = lax.psum_scatter(grad_router_part, "row", scatter_dimension=1, tiled=True)
     router_rows = lax.dynamic_slice_in_dim(router_full, col_id * share, share, 0)
     back_term = mm_nt(jnp.concatenate(parts, axis=1), jnp.concatenate([router_rows] * 3, axis=1))
     damp = scale_b * scale_b * inner[:, None] / width
@@ -1143,19 +1180,23 @@
         dattn = lax.all_gather(dstream_low.astype(bf16), "col", axis=1, tiled=True)
     gain_b_grad = jnp.sum(dscaled * stream, axis=0)
 
-    moe_share = lax.psum_scatter(
-        after(moe_part, (dattn,)), "col", scatter_dimension=1, tiled=True
-    ).astype(f32)
+    late_hiddens[-1] = after(late_hiddens[-1], (dattn,))
+    moe_part = joint_back(late_hiddens, late_wholes, 2, bf16, early[1])
+    moe_share = lax.psum_scatter(moe_part, "col", scatter_dimension=1, tiled=True).astype(f32)
     block_output = (stream + moe_share).astype(bf16)
     out_part = mm_tn(dattn, context).astype(bf16)
     dcontext = mm(dattn, out_full).astype(bf16)
-    dcontext = after(dcontext, hop(went, last - 1, 1), hop(went, last - 2, 2))
+    if planar:
+        dcontext = after(dcontext, reduced[3].third((dattn,)))
+    router_left = after(jnp.concatenate(parts, axis=1), (dattn,))
+    grad_router_part = mm_tn(router_left, scaled).reshape(3, experts + 1, width).sum(axis=0)
+    grad_router_both = lax.psum_scatter(grad_router_part, "row", scatter_dimension=1, tiled=True)
     dqkv, inner_a = attend_backward(qkv, dcontext, lse, lengths, cosine, sine)
     inner_a = lax.psum(inner_a[:, 0], "col")[:, None]
     attn_grads = jnp.concatenate([mm_tn(normed_a, dqkv).astype(bf16), out_part], axis=1)
     if planar:
         dnormed_part = joint_back([dqkv], [qkv_full], 0, bf16, planar=True)
-        dnormed_part = after(dnormed_part, hop(went, last - 1, 2))
+        dnormed_part = after(dnormed_part, (inner_a,))
         (dnormed_a, attn_grad), _, _ = plane_step(
             dnormed_part, lambda total: (total,), [], 1, 0, 3, (), attn_grads
         )
@@ -1163,9 +1204,9 @@
         dnormed_a = lax.psum_scatter(
             mm_nt(dqkv, qkv_full).astype(bf16), "col", scatter_dimension=1, tiled=True
         ).astype(f32)
-        attn_grad = Reduced(attn_grads).total
+        attn_grad = one_reduction(attn_grads)
     qkv_grad, out_grad = attn_grad[:, : 3 * head_width], attn_grad[:, 3 * head_width :]
-    unit_grads = [one.total for one in reduced]
+    unit_grads = [one.result() for one in reduced]
     if planar:
         unit_grads.append(last_grad)
     gain_a_share = input_gain.astype(f32)

time: 1230 us -> 1250 us (1.016)
  waiting for transfers between devices: 159 us -> 127 us
  Pallas kernels: 719 us -> 746 us
    ppermute x4, waiting for transfers between devices: 0.01 us -> 38.5 us  [__init__(): self.partner = lax.ppermute(part, 'row', PAIRS)]
    ppermute x4, waiting for transfers between devices: 38.8 us -> 11.9 us  [second(): self.near_out = lax.ppermute(after(self.near_mid, *groups), 'row', OUTWARD)]
    ppermute x12, waiting for transfers between devices: 61.9 us -> 41.4 us  [the longest x4 41.4 us: third(): self.swapped = lax.ppermute(value, 'row', PAIRS)]
    ppermute x4, waiting for transfers between devices: 52 us -> 34 us  [third(): self.far_out = lax.ppermute(after(self.far_mid, *groups), 'row', OUTWARD)]
    pallas_call x6 -> x8, Pallas kernels: 112 us -> 129 us  [joint_back(): pl.pallas_call(functools.partial(joint_kernel, len(lefts), len(base) > 0,...]
    unnamed x155 -> x149, local copies, waits for them, and re-layouts: 23.3 us -> 26.1 us
  transfers between devices with their start and end apart: 36 -> 36, of which waited for: 8 -> 5; matrix products, arithmetic and copies ran while one was open for 16% -> 17% of each run, Pallas kernels for 59% -> 60%
where the time goes in v9:
time: 1250 us; the launch traced here: 1240 us
  Pallas kernels  746 us (60%)
  waiting for transfers between devices  127 us (10%)
  starting transfers between devices  90.9 us (7%)
  other arithmetic  89.5 us (7%)
  local copies, waits for them, and re-layouts  84.2 us (7%)
  matrix products  45.9 us (4%)
  blocking collectives  45.4 us (4%)
  between operations  15.2 us (1%)
    pallas_call x3, Pallas kernels, plane_step(): pl.pallas_call(functools.partial(plane_kernel, pointwise, len(inputs), ma...  308 us
    pallas_call x5, Pallas kernels, expert_chunk(): pl.pallas_call(functools.partial(expert_kernel, size, steps, count), grid...  183 us
    pallas_call x8, Pallas kernels, joint_back(): pl.pallas_call(functools.partial(joint_kernel, len(lefts), len(base) > 0,...  129 us
    pallas_call x1, Pallas kernels, gather_now(): pl.pallas_call(functools.partial(gather_kernel, count), in_specs=[anywher...  85.1 us
    ppermute x4, waiting for transfers between devices, third(): self.swapped = lax.ppermute(value, 'row', PAIRS)  41.4 us
    ppermute x4, waiting for transfers between devices, __init__(): self.partner = lax.ppermute(part, 'row', PAIRS)  38.5 us
    ppermute x4, waiting for transfers between devices, third(): self.far_out = lax.ppermute(after(self.far_mid, *groups), 'row', OUTWARD)  34 us
    ppermute x4, starting transfers between devices, __init__(): self.first = lax.ppermute(self.pair, 'row', INWARD)  28.6 us
  transfers between devices with their start and end apart: 36, of which 5 were waited for; matrix products, arithmetic and copies ran while one was open for 17% of the time, Pallas kernels for 60%

profile of v9, /device:TPU:0, one launch (start us, length us, event | category | flops | bytes accessed | tf_op | source)
XLA Modules:
  0.0 1244.5 jit_solution(7745336456234675906)
XLA Ops:
  23.0 85.1 %gather_rows.1 = (bf16[4,512,768]{2,1,0:T(8,128)(2,1)}, bf16[4,512,384]{2,1,0:T(8,128)(2,1)}) custom-call(bf16[512,768]{1,0:T(8,128)(2,1)} %copy.135.refs_0_, bf16[512,384]{1,0:T(8,128)(2,1)} %fusion.18.refs_1_), custom_call_target="tpu_custom_call" | custom-call | flops 63700992000 | bytes 7077888 | tf_op jit(solution)/shard_map/gather_rows/pallas_call | solution.py:677
  120.3 9.1 all_gather.16
  140.1 10.5 fusion.4.raw_ref
  150.6 12.7 %attend_forward.1 = (bf16[2048,768]{1,0:T(8,128)(2,1)}, bf16[2048,256]{1,0:T(8,128)(2,1)}, f32[2048,256]{1,0:T(8,128)}) custom-call(s32[2]{0:T(128)} %dynamic_slice.70.length_ref, f32[2048,768]{1,0:T(8,128)} %fusion.4.raw_ref, f32[1024,128]{1,0:T(8,128)} %get-tuple-element.271.cos_ref, f32[1024,128]{1,0:T(8,128)} %get-tuple-element.272.sin_ref), custom_call_target="tpu_custom_call" | custom-call | flops 1610612736 | bytes 12582912 | tf_op jit(solution)/shard_map/attend_forward/pallas_call | solution.py:81
  172.0 113.4 %plane_step.3 = (f32[2048,256]{1,0:T(8,128)}, bf16[2048,2048]{1,0:T(8,128)(2,1)}, bf16[4,512,1536]{2,1,0:T(8,128)(2,1)}) custom-call(bf16[2,2,2,2048,256]{4,3,2,1,0:T(8,128)(2,1)} %joint_back.8.refs_0_, bf16[2048,256]{1,0:T(8,128)(2,1)} %refs_1_.1, f32[1,256]{1,0:T(1,128)} %reshape_convert_fusion.refs_2_.refs_5_, ...), custom_call_target="tpu_custom_call" | custom-call | flops 60000002048 | bytes 16777216 | tf_op jit(solution)/shard_map/plane_step/pallas_call | solution.py:642
  298.8 27.9 %expert_chunk.5 = (bf16[2048,512]{1,0:T(8,128)(2,1)}, bf16[2048,256]{1,0:T(8,128)(2,1)}, f32[2048,2]{1,0:T(8,128)}, bf16[2048,768]{1,0:T(8,128)(2,1)}, bf16[2048,768]{1,0:T(8,128)(2,1)}) custom-call(s32[1]{0:T(128)} %bitcast.13.z_ref, bf16[512,768]{1,0:T(8,128)(2,1)} %fusion.16.refs_0_, bf16[512,768]{1,0:T(8,128)(2,1)} %collective-permute-done.refs_1_, ...), custom_call_target="tpu_custom_call" | custom-call | flops 12884901888 | bytes 46137344 | tf_op jit(solution)/shard_map/expert_chunk/pallas_call | solution.py:863
  338.3 39.7 %expert_chunk.6 = (bf16[2048,1024]{1,0:T(8,128)(2,1)}, bf16[2048,512]{1,0:T(8,128)(2,1)}, f32[2048,2]{1,0:T(8,128)}, bf16[2048,1536]{1,0:T(8,128)(2,1)}, bf16[2048,1536]{1,0:T(8,128)(2,1)}) custom-call(s32[1]{0:T(128)} %bitcast.13.z_ref, bf16[512,1536]{1,0:T(8,128)(2,1)} %get-tuple-element.269.refs_3_.refs_0_, bf16[2048,1536]{1,0:T(8,128)(2,1)} %bitcast.118, ...), custom_call_target="tpu_custom_call" | custom-call | flops 25769803776 | bytes 58720256 | tf_op jit(solution)/shard_map/expert_chunk/pallas_call | solution.py:863
  385.6 13.0 %joint_back.10.refs_4_ = f32[2048,2048]{1,0:T(8,128)} custom-call(bf16[2048,256]{1,0:T(8,128)(2,1)} %get-tuple-element.107.refs_0_, bf16[2048,512]{1,0:T(8,128)(2,1)} %get-tuple-element.108.refs_1_, bf16[2048,768]{1,0:T(8,128)(2,1)} %get-tuple-element.105.refs_2_, bf16[2048,1536]{1,0:T(8,128)(2,1)} %get-tuple-element.106.refs_3_), custom_call_target="tpu_custom_call" | custom-call | flops 6442450944 | bytes 23068672 | tf_op jit(solution)/shard_map/joint_back/pallas_call | solution.py:926
  398.6 19.2 %joint_back.9.refs_4_ = f32[2048,2048]{1,0:T(8,128)} custom-call(bf16[2048,512]{1,0:T(8,128)(2,1)} %get-tuple-element.103.refs_0_, bf16[2048,1024]{1,0:T(8,128)(2,1)} %get-tuple-element.104.refs_1_, bf16[2048,768]{1,0:T(8,128)(2,1)} %get-tuple-element.105.refs_2_, bf16[2048,1536]{1,0:T(8,128)(2,1)} %get-tuple-element.106.refs_3_), custom_call_target="tpu_custom_call" | custom-call | flops 12884901888 | bytes 29360128 | tf_op jit(solution)/shard_map/joint_back/pallas_call | solution.py:926
  422.9 10.2 collective-permute-start.18
  434.9 16.3 %collective-permute-done.10.refs_5_ = bf16[512,1536]{1,0:T(8,128)(2,1)} collective-permute-done((bf16[512,1536]{1,0:T(8,128)(2,1)}, bf16[512,1536]{1,0:T(8,128)(2,1)}, u32[]{:S(2)}, u32[]{:S(2)}) %collective-permute-start.10) | collective-permute-done | bytes 1572896 | tf_op jit(solution)/shard_map/ppermute | solution.py:197
  451.2 39.5 %expert_chunk.7 = (bf16[2048,1024]{1,0:T(8,128)(2,1)}, bf16[2048,512]{1,0:T(8,128)(2,1)}, f32[2048,2]{1,0:T(8,128)}, bf16[2048,1536]{1,0:T(8,128)(2,1)}, bf16[2048,1536]{1,0:T(8,128)(2,1)}) custom-call(s32[1]{0:T(128)} %bitcast.13.z_ref, bf16[512,1536]{1,0:T(8,128)(2,1)} %get-tuple-element.94.refs_0_, bf16[512,1536]{1,0:T(8,128)(2,1)} %collective-permute-done.4.refs_1_, ...), custom_call_target="tpu_custom_call" | custom-call | flops 25769803776 | bytes 58720256 | tf_op jit(solution)/shard_map/expert_chunk/pallas_call | solution.py:863
  490.8 38.5 %collective-permute-done.7.refs_1_ = bf16[512,1536]{1,0:T(8,128)(2,1)} collective-permute-done((bf16[512,1536]{1,0:T(8,128)(2,1)}, bf16[512,1536]{1,0:T(8,128)(2,1)}, u32[]{:S(2)}, u32[]{:S(2)}) %collective-permute-start.7) | collective-permute-done | bytes 1572896 | tf_op jit(solution)/shard_map/ppermute | solution.py:184
  548.0 22.3 %collective-permute-start.29 = (bf16[512,768]{1,0:T(8,128)(2,1)}, bf16[512,768]{1,0:T(8,128)(2,1)}, u32[]{:S(2)}, u32[]{:S(2)}) collective-permute-start(bf16[512,768]{1,0:T(8,128)(2,1)} %add_convert_fusion.8), channel_id=1, source_target_pairs={{0,8},{8,0},{16,24},{24,16},{1,9},{9,1},{17,25},{25,17},{2,10},{10... | collective-permute-start | bytes 2359304 | tf_op jit(solution)/shard_map/ppermute | solution.py:732
  586.6 41.4 %collective-permute-done.29 = bf16[512,768]{1,0:T(8,128)(2,1)} collective-permute-done((bf16[512,768]{1,0:T(8,128)(2,1)}, bf16[512,768]{1,0:T(8,128)(2,1)}, u32[]{:S(2)}, u32[]{:S(2)}) %collective-permute-start.29) | collective-permute-done | bytes 786464 | tf_op jit(solution)/shard_map/ppermute | solution.py:732
  634.4 39.5 %expert_chunk.8 = (bf16[2048,1024]{1,0:T(8,128)(2,1)}, bf16[2048,512]{1,0:T(8,128)(2,1)}, f32[2048,2]{1,0:T(8,128)}, bf16[2048,1536]{1,0:T(8,128)(2,1)}, bf16[2048,1536]{1,0:T(8,128)(2,1)}) custom-call(s32[1]{0:T(128)} %bitcast.13.z_ref, bf16[512,1536]{1,0:T(8,128)(2,1)} %pad_maximum_fusion.2.refs_0_, bf16[512,1536]{1,0:T(8,128)(2,1)} %collective-permute-done.7.refs_1_, ...), custom_call_target="tpu_custom_call" | custom-call | flops 25769803776 | bytes 58720256 | tf_op jit(solution)/shard_map/expert_chunk/pallas_call | solution.py:863
  686.1 25.9 %joint_back.11.refs_2_ = f32[2048,2048]{1,0:T(8,128)} custom-call(bf16[2048,1024]{1,0:T(8,128)(2,1)} %get-tuple-element.123.refs_0_, bf16[2048,1024]{1,0:T(8,128)(2,1)} %get-tuple-element.124.refs_1_, bf16[2048,1536]{1,0:T(8,128)(2,1)} %get-tuple-element.125.refs_2_, bf16[2048,1536]{1,0:T(8,128)(2,1)} %get-tuple-element.126.refs_3_, ...), custom_call_target="tpu_custom_call" | custom-call | flops 17179869184 | bytes 33554432 | tf_op jit(solution)/shard_map/joint_back/pallas_call | solution.py:926
  712.0 20.2 %joint_back.12.refs_2_ = f32[2048,2048]{1,0:T(8,128)} custom-call(bf16[2048,512]{1,0:T(8,128)(2,1)} %get-tuple-element.127.refs_0_, bf16[2048,512]{1,0:T(8,128)(2,1)} %get-tuple-element.128.refs_1_, bf16[2048,1536]{1,0:T(8,128)(2,1)} %get-tuple-element.125.refs_2_, bf16[2048,1536]{1,0:T(8,128)(2,1)} %get-tuple-element.126.refs_3_, ...), custom_call_target="tpu_custom_call" | custom-call | flops 8589934592 | bytes 25165824 | tf_op jit(solution)/shard_map/joint_back/pallas_call | solution.py:926
  739.9 9.2 collective-permute-start.25
  753.4 11.9 collective-permute-done.21.refs_4_
  765.3 17.6 %collective-permute-done.22.refs_5_ = bf16[512,1152]{1,0:T(8,128)(2,1)} collective-permute-done((bf16[512,1152]{1,0:T(8,128)(2,1)}, bf16[512,1152]{1,0:T(8,128)(2,1)}, u32[]{:S(2)}, u32[]{:S(2)}) %collective-permute-start.22) | collective-permute-done | bytes 1179680 | tf_op jit(solution)/shard_map/ppermute | solution.py:197
  783.0 36.2 %expert_chunk.9 = (bf16[2048,768]{1,0:T(8,128)(2,1)}, bf16[2048,384]{1,0:T(8,128)(2,1)}, f32[2048,2]{1,0:T(8,128)}, bf16[2048,1152]{1,0:T(8,128)(2,1)}, bf16[2048,1152]{1,0:T(8,128)(2,1)}) custom-call(s32[1]{0:T(128)} %bitcast.13.z_ref, bf16[512,1152]{1,0:T(8,128)(2,1)} %pad_maximum_fusion.7.refs_0_, bf16[512,1152]{1,0:T(8,128)(2,1)} %collective-permute-done.13.refs_1_, ...), custom_call_target="tpu_custom_call" | custom-call | flops 19327352832 | bytes 52428800 | tf_op jit(solution)/shard_map/expert_chunk/pallas_call | solution.py:863
  823.9 13.0 %all-gather.1 = f32[8,3,2048]{2,1,0:T(4,128)S(1)} all-gather(f32[1,3,2048]{2,1,0:T(4,128)S(1)} %maximum_bitcast_fusion.3), channel_id=2, replica_groups=mesh['row'=4,'col'=8] {'col'}, dimensions={0}, use_global_device_ids=true | all-gather | bytes 221184 | tf_op jit(solution)/shard_map/all_gather | solution.py:1160
  853.4 15.7 %joint_back.13.refs_0_ = bf16[2,2,2,2048,256]{4,3,2,1,0:T(8,128)(2,1)} custom-call(bf16[2048,768]{1,0:T(8,128)(2,1)} %get-tuple-element.139.refs_0_, bf16[2048,1152]{1,0:T(8,128)(2,1)} %get-tuple-element.140.refs_1_, f32[2048,2048]{1,0:T(8,128)} %joint_back.11.refs_2_), custom_call_target="tpu_custom_call" | custom-call | flops 6442450944 | bytes 23068672 | tf_op jit(solution)/shard_map/joint_back/pallas_call | solution.py:926
  869.1 111.1 %plane_step.4 = (f32[2048,256]{1,0:T(8,128)}, f32[2048,256]{1,0:T(8,128)}, f32[512,1152]{1,0:T(8,128)}, bf16[2048,2048]{1,0:T(8,128)(2,1)}) custom-call(bf16[2,2,2,2048,256]{4,3,2,1,0:T(8,128)(2,1)} %joint_back.13.refs_0_, f32[2048,256]{1,0:T(8,128)} %fusion.27.refs_1_, bf16[2048,256]{1,0:T(8,128)(2,1)} %refs_2_.1, f32[2048,256]{1,0:T(8,128)} %get-tuple-element.92.refs_3_, ...), custom_call_target="tpu_custom_call" | custom-call | flops 60000002048 | bytes 16777216 | tf_op jit(solution)/shard_map/plane_step/pallas_call | solution.py:642
  993.1 14.4 %joint_back.14 = bf16[2048,2048]{1,0:T(8,128)(2,1)} custom-call(bf16[2048,384]{1,0:T(8,128)(2,1)} %get-tuple-element.143.refs_0_, bf16[2048,1152]{1,0:T(8,128)(2,1)} %get-tuple-element.140.refs_1_, f32[2048,2048]{1,0:T(8,128)} %joint_back.12.refs_2_), custom_call_target="tpu_custom_call" | custom-call | flops 3221225472 | bytes 19922944 | tf_op jit(solution)/shard_map/joint_back/pallas_call | solution.py:926
  1037.8 28.3 %attend_backward.1 = (bf16[2048,768]{1,0:T(8,128)(2,1)}, f32[2048,1]{1,0:T(8,128)}) custom-call(s32[2]{0:T(128)} %dynamic_slice.70.length_ref, bf16[2048,768]{1,0:T(8,128)(2,1)} %get-tuple-element.145.qkv_ref, bf16[2048,256]{1,0:T(8,128)(2,1)} %convolution_convert_fusion.2.dcontext_ref, f32[2048,256]{1,0:T(8,128)} %get-tuple-element.148.lse_ref, ...), custom_call_target="tpu_custom_call" | custom-call | flops 4294967296 | bytes 12582912 | tf_op jit(solution)/shard_map/attend_backward/pallas_call | solution.py:151
  1066.1 11.2 convolution_convert_fusion
  1086.1 12.1 joint_back.15.refs_0_
  1098.2 83.6 %plane_step.5 = (f32[2048,256]{1,0:T(8,128)}, f32[512,1024]{1,0:T(8,128)}) custom-call(bf16[2,2,2,2048,256]{4,3,2,1,0:T(8,128)(2,1)} %joint_back.15.refs_0_, bf16[4,512,1024]{2,1,0:T(8,128)(2,1)} %bitcast.90), custom_call_target="tpu_custom_call" | custom-call | flops 60000002048 | bytes 16777216 | tf_op jit(solution)/shard_map/plane_step/pallas_call | solution.py:642
  1196.7 13.6 %psum.21 = f32[2048]{0:T(1024)S(1)} all-reduce(f32[2048]{0:T(1024)S(1)} %reduce.5), channel_id=1, replica_groups=mesh['row'=4,'col'=8] {'col'}, use_global_device_ids=true, to_apply=%region_10.11 | all-reduce | flops 2048 | bytes 16384 | tf_op jit(solution)/shard_map/psum | solution.py:1195
  1228.1 9.7 all-reduce.4
  (340 shorter events, 257.4 us)
Async XLA Ops:
  7.2 127.1 %all-gather.5.cloned.1.call-start = ((), (), s32[]{:S(2)}) async-start(), calls=%async_computation.2 | async-start | bytes 9437184 | tf_op jit(solution)/shard_map/all_gather | solution.py:1045
  8.0 164.1 %all-gather.7.cloned.1.call-start = ((), (), s32[]{:S(2)}) async-start(), calls=%async_computation.3 | async-start | bytes 9437184 | tf_op jit(solution)/shard_map/all_gather | solution.py:1047
  8.7 1008.6 %reduce-scatter.5.cloned.1.call-start = ((), (), s32[]{:S(2)}) async-start(), calls=%async_computation.5 | async-start | bytes 163840 | tf_op jit(solution)/shard_map/reduce_scatter | solution.py:1193
  11.2 104.8 %collective-permute-start = (bf16[512,768]{1,0:T(8,128)(2,1)}, bf16[512,768]{1,0:T(8,128)(2,1)}, u32[]{:S(2)}, u32[]{:S(2)}) collective-permute-start(bf16[512,768]{1,0:T(8,128)(2,1)} %fusion.16.refs_0_), channel_id=1, source_target_pairs={{0,8},{8,0},{16,24},{24,16},{1,9},{9,1},{17,25},{25,17},{2,10},{10... | collective-permute-start | bytes 2359304 | tf_op jit(solution)/shard_map/ppermute | solution.py:184
  14.2 116.9 %collective-permute-start.1 = (bf16[512,768]{1,0:T(8,128)(2,1)}, bf16[512,768]{1,0:T(8,128)(2,1)}, u32[]{:S(2)}, u32[]{:S(2)}) collective-permute-start(bf16[512,768]{1,0:T(8,128)(2,1)} %fusion.16.refs_0_), channel_id=1, source_target_pairs={{8,16},{16,8},{9,17},{17,9},{10,18},{18,10},{11,19},{19,11},{12,20... | collective-permute-start | bytes 2359304 | tf_op jit(solution)/shard_map/ppermute | solution.py:185
  132.4 166.3 %collective-permute-start.5 = (bf16[512,768]{1,0:T(8,128)(2,1)}, bf16[512,768]{1,0:T(8,128)(2,1)}, u32[]{:S(2)}, u32[]{:S(2)}) collective-permute-start(bf16[512,768]{1,0:T(8,128)(2,1)} %collective-permute-done.2.refs_3_), channel_id=1, source_target_pairs={{8,0},{16,24},{9,1},{17,25},{10,2},{18,26},{11,3},{19,27},{12,4},{... | collective-permute-start | bytes 2359304 | tf_op jit(solution)/shard_map/ppermute | solution.py:197
  285.5 49.6 %collective-permute-start.4 = (bf16[512,1536]{1,0:T(8,128)(2,1)S(1)}, bf16[512,1536]{1,0:T(8,128)(2,1)}, u32[]{:S(2)}, u32[]{:S(2)}) collective-permute-start(bf16[512,1536]{1,0:T(8,128)(2,1)S(1)} %copy-done.27), channel_id=1, source_target_pairs={{0,8},{8,0},{16,24},{24,16},{1,9},{9,1},{17,25},{25,17},{2,10},{10... | collective-permute-start | bytes 4718600 | tf_op jit(solution)/shard_map/ppermute | solution.py:184
  285.5 49.6 %collective-permute-start.8 = (bf16[512,1536]{1,0:T(8,128)(2,1)S(1)}, bf16[512,1536]{1,0:T(8,128)(2,1)}, u32[]{:S(2)}, u32[]{:S(2)}) collective-permute-start(bf16[512,1536]{1,0:T(8,128)(2,1)S(1)} %copy-done.27), channel_id=1, source_target_pairs={{8,16},{16,8},{9,17},{17,9},{10,18},{18,10},{11,19},{19,11},{12,20... | collective-permute-start | bytes 4718600 | tf_op jit(solution)/shard_map/ppermute | solution.py:185
  329.4 48.6 %collective-permute-start.11 = (bf16[1024,768]{1,0:T(8,128)(2,1)}, bf16[1024,768]{1,0:T(8,128)(2,1)}, u32[]{:S(2)}, u32[]{:S(2)}) collective-permute-start(bf16[1024,768]{1,0:T(8,128)(2,1)} %constant_dynamic-slice_fusion.4), channel_id=1, source_target_pairs={{0,8},{24,16},{1,9},{25,17},{2,10},{26,18},{3,11},{27,19},{4,12},{... | collective-permute-start | bytes 4718600 | tf_op jit(solution)/shard_map/ppermute | solution.py:710
  336.5 47.6 %collective-permute-start.6 = (bf16[512,1536]{1,0:T(8,128)(2,1)}, bf16[512,1536]{1,0:T(8,128)(2,1)}, u32[]{:S(2)}, u32[]{:S(2)}) collective-permute-start(bf16[512,1536]{1,0:T(8,128)(2,1)} %collective-permute-done.4.refs_1_), channel_id=1, source_target_pairs={{8,16},{16,8},{9,17},{17,9},{10,18},{18,10},{11,19},{19,11},{12,20... | collective-permute-start | bytes 4718600 | tf_op jit(solution)/shard_map/ppermute | solution.py:191
  378.0 56.9 %collective-permute-start.9 = (bf16[512,1536]{1,0:T(8,128)(2,1)}, bf16[512,1536]{1,0:T(8,128)(2,1)}, u32[]{:S(2)}, u32[]{:S(2)}) collective-permute-start(bf16[512,1536]{1,0:T(8,128)(2,1)} %collective-permute-done.8.refs_2_), channel_id=1, source_target_pairs={{8,0},{16,24},{9,1},{17,25},{10,2},{18,26},{11,3},{19,27},{12,4},{... | collective-permute-start | bytes 4718600 | tf_op jit(solution)/shard_map/ppermute | solution.py:190
  382.3 160.9 %collective-permute-start.19 = (bf16[1024,768]{1,0:T(8,128)(2,1)}, bf16[1024,768]{1,0:T(8,128)(2,1)}, u32[]{:S(2)}, u32[]{:S(2)}) collective-permute-start(bf16[1024,768]{1,0:T(8,128)(2,1)} %add_convert_fusion.6), channel_id=1, source_target_pairs={{8,16},{16,8},{9,17},{17,9},{10,18},{18,10},{11,19},{19,11},{12,20... | collective-permute-start | bytes 4718600 | tf_op jit(solution)/shard_map/ppermute | solution.py:724
  384.1 67.1 %collective-permute-start.10 = (bf16[512,1536]{1,0:T(8,128)(2,1)}, bf16[512,1536]{1,0:T(8,128)(2,1)}, u32[]{:S(2)}, u32[]{:S(2)}) collective-permute-start(bf16[512,1536]{1,0:T(8,128)(2,1)} %collective-permute-done.6.refs_3_), channel_id=1, source_target_pairs={{8,0},{16,24},{9,1},{17,25},{10,2},{18,26},{11,3},{19,27},{12,4},{... | collective-permute-start | bytes 4718600 | tf_op jit(solution)/shard_map/ppermute | solution.py:197
  422.9 125.1 %collective-permute-start.18 = (bf16[1024,1536]{1,0:T(8,128)(2,1)}, bf16[1024,1536]{1,0:T(8,128)(2,1)}, u32[]{:S(2)}, u32[]{:S(2)}) collective-permute-start(bf16[1024,1536]{1,0:T(8,128)(2,1)} %constant_dynamic-slice_fusion.3), channel_id=1, source_target_pairs={{0,8},{24,16},{1,9},{25,17},{2,10},{26,18},{3,11},{27,19},{4,12},{... | collective-permute-start | bytes 9437192 | tf_op jit(solution)/shard_map/ppermute | solution.py:710
  433.1 110.1 %collective-permute-start.15 = (bf16[512,1536]{1,0:T(8,128)(2,1)}, bf16[512,1536]{1,0:T(8,128)(2,1)}, u32[]{:S(2)}, u32[]{:S(2)}) collective-permute-start(bf16[512,1536]{1,0:T(8,128)(2,1)} %pad_maximum_fusion.2.refs_0_), channel_id=1, source_target_pairs={{8,16},{16,8},{9,17},{17,9},{10,18},{18,10},{11,19},{19,11},{12,20... | collective-permute-start | bytes 4718600 | tf_op jit(solution)/shard_map/ppermute | solution.py:185
  434.9 94.4 %collective-permute-start.7 = (bf16[512,1536]{1,0:T(8,128)(2,1)}, bf16[512,1536]{1,0:T(8,128)(2,1)}, u32[]{:S(2)}, u32[]{:S(2)}) collective-permute-start(bf16[512,1536]{1,0:T(8,128)(2,1)} %pad_maximum_fusion.2.refs_0_), channel_id=1, source_target_pairs={{0,8},{8,0},{16,24},{24,16},{1,9},{9,1},{17,25},{25,17},{2,10},{10... | collective-permute-start | bytes 4718600 | tf_op jit(solution)/shard_map/ppermute | solution.py:184
  543.2 89.6 %collective-permute-start.16 = (bf16[512,1536]{1,0:T(8,128)(2,1)}, bf16[512,1536]{1,0:T(8,128)(2,1)}, u32[]{:S(2)}, u32[]{:S(2)}) collective-permute-start(bf16[512,1536]{1,0:T(8,128)(2,1)} %collective-permute-done.15.refs_2_), channel_id=1, source_target_pairs={{8,0},{16,24},{9,1},{17,25},{10,2},{18,26},{11,3},{19,27},{12,4},{... | collective-permute-start | bytes 4718600 | tf_op jit(solution)/shard_map/ppermute | solution.py:190
  544.5 89.9 %collective-permute-start.17 = (bf16[512,1536]{1,0:T(8,128)(2,1)}, bf16[512,1536]{1,0:T(8,128)(2,1)}, u32[]{:S(2)}, u32[]{:S(2)}) collective-permute-start(bf16[512,1536]{1,0:T(8,128)(2,1)} %collective-permute-done.12.refs_3_), channel_id=1, source_target_pairs={{8,0},{16,24},{9,1},{17,25},{10,2},{18,26},{11,3},{19,27},{12,4},{... | collective-permute-start | bytes 4718600 | tf_op jit(solution)/shard_map/ppermute | solution.py:197
  548.0 79.9 %collective-permute-start.29 = (bf16[512,768]{1,0:T(8,128)(2,1)}, bf16[512,768]{1,0:T(8,128)(2,1)}, u32[]{:S(2)}, u32[]{:S(2)}) collective-permute-start(bf16[512,768]{1,0:T(8,128)(2,1)} %add_convert_fusion.8), channel_id=1, source_target_pairs={{0,8},{8,0},{16,24},{24,16},{1,9},{9,1},{17,25},{25,17},{2,10},{10... | collective-permute-start | bytes 2359304 | tf_op jit(solution)/shard_map/ppermute | solution.py:732
  575.7 98.2 %collective-permute-start.24 = (bf16[1024,1536]{1,0:T(8,128)(2,1)}, bf16[1024,1536]{1,0:T(8,128)(2,1)}, u32[]{:S(2)}, u32[]{:S(2)}) collective-permute-start(bf16[1024,1536]{1,0:T(8,128)(2,1)} %add_convert_fusion.2), channel_id=1, source_target_pairs={{8,16},{16,8},{9,17},{17,9},{10,18},{18,10},{11,19},{19,11},{12,20... | collective-permute-start | bytes 9437192 | tf_op jit(solution)/shard_map/ppermute | solution.py:724
  583.1 93.7 %collective-permute-start.23 = (bf16[1024,1536]{1,0:T(8,128)(2,1)}, bf16[1024,1536]{1,0:T(8,128)(2,1)}, u32[]{:S(2)}, u32[]{:S(2)}) collective-permute-start(bf16[1024,1536]{1,0:T(8,128)(2,1)} %constant_dynamic-slice_fusion.2), channel_id=1, source_target_pairs={{0,8},{24,16},{1,9},{25,17},{2,10},{26,18},{3,11},{27,19},{4,12},{... | collective-permute-start | bytes 9437192 | tf_op jit(solution)/shard_map/ppermute | solution.py:710
  630.8 102.7 %collective-permute-start.14 = (bf16[512,1152]{1,0:T(8,128)(2,1)}, bf16[512,1152]{1,0:T(8,128)(2,1)}, u32[]{:S(2)}, u32[]{:S(2)}) collective-permute-start(bf16[512,1152]{1,0:T(8,128)(2,1)} %pad_maximum_fusion.7.refs_0_), channel_id=1, source_target_pairs={{8,16},{16,8},{9,17},{17,9},{10,18},{18,10},{11,19},{19,11},{12,20... | collective-permute-start | bytes 3538952 | tf_op jit(solution)/shard_map/ppermute | solution.py:185
  632.9 49.2 %collective-permute-start.13 = (bf16[512,1152]{1,0:T(8,128)(2,1)}, bf16[512,1152]{1,0:T(8,128)(2,1)}, u32[]{:S(2)}, u32[]{:S(2)}) collective-permute-start(bf16[512,1152]{1,0:T(8,128)(2,1)} %pad_maximum_fusion.7.refs_0_), channel_id=1, source_target_pairs={{0,8},{8,0},{16,24},{24,16},{1,9},{9,1},{17,25},{25,17},{2,10},{10... | collective-permute-start | bytes 3538952 | tf_op jit(solution)/shard_map/ppermute | solution.py:184
  676.2 72.9 %collective-permute-start.30 = (bf16[512,1536]{1,0:T(8,128)(2,1)S(1)}, bf16[512,1536]{1,0:T(8,128)(2,1)S(1)}, u32[]{:S(2)}, u32[]{:S(2)}) collective-permute-start(bf16[512,1536]{1,0:T(8,128)(2,1)S(1)} %add_convert_fusion.5), channel_id=1, source_target_pairs={{0,8},{8,0},{16,24},{24,16},{1,9},{9,1},{17,25},{25,17},{2,10},{10... | collective-permute-start | bytes 4718600 | tf_op jit(solution)/shard_map/ppermute | solution.py:732
  682.1 52.7 %collective-permute-start.20 = (bf16[512,1152]{1,0:T(8,128)(2,1)}, bf16[512,1152]{1,0:T(8,128)(2,1)}, u32[]{:S(2)}, u32[]{:S(2)}) collective-permute-start(bf16[512,1152]{1,0:T(8,128)(2,1)} %collective-permute-done.13.refs_1_), channel_id=1, source_target_pairs={{8,16},{16,8},{9,17},{17,9},{10,18},{18,10},{11,19},{19,11},{12,20... | collective-permute-start | bytes 3538952 | tf_op jit(solution)/shard_map/ppermute | solution.py:191
  683.8 158.7 %collective-permute-start.26 = (bf16[1024,1536]{1,0:T(8,128)(2,1)}, bf16[1024,1536]{1,0:T(8,128)(2,1)}, u32[]{:S(2)}, u32[]{:S(2)}) collective-permute-start(bf16[1024,1536]{1,0:T(8,128)(2,1)} %add_convert_fusion.1), channel_id=1, source_target_pairs={{8,16},{16,8},{9,17},{17,9},{10,18},{18,10},{11,19},{19,11},{12,20... | collective-permute-start | bytes 9437192 | tf_op jit(solution)/shard_map/ppermute | solution.py:724
  734.8 48.2 %collective-permute-start.22 = (bf16[512,1152]{1,0:T(8,128)(2,1)}, bf16[512,1152]{1,0:T(8,128)(2,1)}, u32[]{:S(2)}, u32[]{:S(2)}) collective-permute-start(bf16[512,1152]{1,0:T(8,128)(2,1)} %collective-permute-done.20.refs_3_), channel_id=1, source_target_pairs={{8,0},{16,24},{9,1},{17,25},{10,2},{18,26},{11,3},{19,27},{12,4},{... | collective-permute-start | bytes 3538952 | tf_op jit(solution)/shard_map/ppermute | solution.py:197
  739.9 106.6 %collective-permute-start.25 = (bf16[1024,1536]{1,0:T(8,128)(2,1)}, bf16[1024,1536]{1,0:T(8,128)(2,1)}, u32[]{:S(2)}, u32[]{:S(2)}) collective-permute-start(bf16[1024,1536]{1,0:T(8,128)(2,1)} %constant_dynamic-slice_fusion.1), channel_id=1, source_target_pairs={{0,8},{24,16},{1,9},{25,17},{2,10},{26,18},{3,11},{27,19},{4,12},{... | collective-permute-start | bytes 9437192 | tf_op jit(solution)/shard_map/ppermute | solution.py:710
  846.4 173.5 %collective-permute-start.31 = (bf16[512,1536]{1,0:T(8,128)(2,1)}, bf16[512,1536]{1,0:T(8,128)(2,1)}, u32[]{:S(2)}, u32[]{:S(2)}) collective-permute-start(bf16[512,1536]{1,0:T(8,128)(2,1)} %add_convert_fusion.4), channel_id=1, source_target_pairs={{0,8},{8,0},{16,24},{24,16},{1,9},{9,1},{17,25},{25,17},{2,10},{10... | collective-permute-start | bytes 4718600 | tf_op jit(solution)/shard_map/ppermute | solution.py:732
  851.0 183.3 %collective-permute-start.27 = (bf16[1024,1536]{1,0:T(8,128)(2,1)}, bf16[1024,1536]{1,0:T(8,128)(2,1)}, u32[]{:S(2)}, u32[]{:S(2)}) collective-permute-start(bf16[1024,1536]{1,0:T(8,128)(2,1)} %add_convert_fusion), channel_id=1, source_target_pairs={{8,16},{16,8},{9,17},{17,9},{10,18},{18,10},{11,19},{19,11},{12,20... | collective-permute-start | bytes 9437192 | tf_op jit(solution)/shard_map/ppermute | solution.py:724
  992.6 231.6 %reduce-scatter.3.cloned.1.call-start = ((), (), s32[]{:S(2)}) async-start(), calls=%async_computation.4 | async-start | bytes 9437184 | tf_op jit(solution)/shard_map/reduce_scatter | solution.py:1185
  1037.8 175.8 %collective-permute-start.28 = (bf16[512,1536]{1,0:T(8,128)(2,1)}, bf16[512,1536]{1,0:T(8,128)(2,1)}, u32[]{:S(2)}, u32[]{:S(2)}) collective-permute-start(bf16[512,1536]{1,0:T(8,128)(2,1)} %add_convert_fusion.3), channel_id=1, source_target_pairs={{0,8},{8,0},{16,24},{24,16},{1,9},{9,1},{17,25},{25,17},{2,10},{10... | collective-permute-start | bytes 4718600 | tf_op jit(solution)/shard_map/ppermute | solution.py:732
  (73 other events, 1576.5 us)
Sparse Core Ops, SparseCore 0:
  9.9 58.6 all-gather.4
  70.5 55.9 all-gather.6
  992.7 18.5 reduce-scatter.4
  1015.0 69.4 reduce-scatter.2

commit v10 on v9

--- a/solution.py
+++ b/solution.py
@@ -750,12 +750,26 @@
     return lax.optimization_barrier((value,) + others)[0] if others else value
 
 
-def expert_kernel(size, steps, count, z_ref, *refs):
+def expert_kernel(size, steps, count, ahead, *refs):
     pieces = refs[:count]
     (x_ref, cot_ref, x_cols, cot_cols, coef_ref) = refs[count : count + 5]
-    (dpair_ref, hidden_ref, sums_ref, grads_ref, whole_ref) = refs[count + 5 : count + 10]
-    weights, dpair, hidden, sems, out_sem = refs[count + 10 :]
+    at = count + 5 + ahead
+    (dpair_ref, hidden_ref, sums_ref, grads_ref, whole_ref) = refs[at : at + 5]
+    weights, dpair, hidden, sems, out_sem = refs[at + 5 + ahead : at + 10 + ahead]
     step = pl.program_id(0)
+    final = pl.num_programs(0) - 1
+    if ahead:
+        rows = RowGather(refs[count + 5 : count + 6], refs[at + 5 : at + 6], refs[at + 10 + ahead :])
+
+        @pl.when(step == 0)
+        def _():
+            rows.greet(pltpu.get_barrier_semaphore())
+            rows.begin()
+
+        @pl.when(step == final - 2)
+        def _():
+            rows.hand_on(0)
+
     write = pltpu.make_async_copy(weights, whole_ref, out_sem)
 
     @pl.when(step == 0)
@@ -768,7 +782,7 @@
             block = pieces[0].shape[0]
 
             def block_copy(back):
-                at = pl.multiple_of(lax.rem(z_ref[0] + back, 4) * block, block)
+                at = pl.multiple_of(lax.rem(lax.axis_index("row") + back, 4) * block, block)
                 source = pieces[1].at[pl.ds(at, block)] if back else pieces[0]
                 return pltpu.make_async_copy(source, weights.at[pl.ds(at, block)], sems.at[back])
 
@@ -777,7 +791,7 @@
             for back in range(4):
                 block_copy(back).wait()
         else:
-            z = z_ref[0]
+            z = lax.axis_index("row")
             block = pieces[0].shape[0]
 
             def copy_of(piece, which):
@@ -846,25 +860,33 @@
                 cot_cols[...], hidden[:, a:b]
             ).astype(bf16)
 
-    @pl.when(step == pl.num_programs(0) - 1)
+    @pl.when(step == final)
     def _():
         write.wait()
-
-
-def expert_chunk(pieces, scaled, cots, coef):
+        if ahead:
+            rows.hand_last(0)
+            rows.finish()
+
+
+def expert_chunk(pieces, scaled, cots, coef, pack=None, number=None):
     tokens, width = scaled.shape
     size = pieces[0].shape[1] // 3
-    steps, more = tokens // TILE, width // TILE
+    steps, more_steps = tokens // TILE, width // TILE
     count = len(pieces)
-    rows = lambda i, _: (jnp.minimum(i, steps - 1), 0)
-    cols = lambda i, _: (0, jnp.maximum(i - steps, 0))
-    down = lambda i, _: (jnp.maximum(i - steps, 0), 0)
-    z = jnp.reshape(lax.axis_index("row"), (1,)).astype(jnp.int32)
-    return pl.pallas_call(
-        functools.partial(expert_kernel, size, steps, count),
-        grid_spec=pltpu.PrefetchScalarGridSpec(
-            num_scalar_prefetch=1,
-            grid=(steps + more,),
+    rows = lambda i: (jnp.minimum(i, steps - 1), 0)
+    cols = lambda i: (0, jnp.maximum(i - steps, 0))
+    down = lambda i: (jnp.maximum(i - steps, 0), 0)
+    anywhere = pl.BlockSpec(memory_space=pl.ANY)
+    ahead, more, more_shapes, more_scratch, params = 0, [], [], [], {}
+    if pack is not None:
+        ahead, more = 1, [pack]
+        more_shapes = [jax.ShapeDtypeStruct((4,) + pack.shape, bf16)]
+        more_scratch = [pltpu.SemaphoreType.DMA((5, 1))] * 2
+        params = dict(collective_id=number, has_side_effects=True)
+    outs = pl.pallas_call(
+        functools.partial(expert_kernel, size, steps, count, ahead),
+        grid_spec=pl.GridSpec(
+            grid=(steps + more_steps,),
             in_specs=[pl.BlockSpec(memory_space=pl.ANY)] * count
             + [
                 pl.BlockSpec((TILE, width), rows),
@@ -872,21 +894,24 @@
                 pl.BlockSpec((tokens, TILE), cols),
                 pl.BlockSpec((tokens, TILE), cols),
                 pl.BlockSpec((TILE, 2), rows),
-            ],
+            ]
+            + [anywhere] * ahead,
             out_specs=[
                 pl.BlockSpec((TILE, 2 * size), rows),
                 pl.BlockSpec((TILE, size), rows),
                 pl.BlockSpec((TILE, 2), rows),
                 pl.BlockSpec((TILE, 3 * size), down),
-                pl.BlockSpec(memory_space=pl.ANY),
-            ],
+                anywhere,
+            ]
+            + [anywhere] * ahead,
             scratch_shapes=[
                 pltpu.VMEM((width, 3 * size), bf16),
                 pltpu.VMEM((tokens, 2 * size), bf16),
                 pltpu.VMEM((tokens, size), bf16),
                 pltpu.SemaphoreType.DMA((4,)),
                 pltpu.SemaphoreType.DMA,
-            ],
+            ]
+            + more_scratch,
         ),
         out_shape=[
             jax.ShapeDtypeStruct((tokens, 2 * size), bf16),
@@ -894,14 +919,19 @@
             jax.ShapeDtypeStruct((tokens, 2), f32),
             jax.ShapeDtypeStruct((width, 3 * size), bf16),
             jax.ShapeDtypeStruct((width, 3 * size), bf16),
-        ],
+        ]
+        + more_shapes,
+        compiler_params=pltpu.CompilerParams(**params),
         cost_estimate=pl.CostEstimate(
             flops=12 * tokens * width * size,
             bytes_accessed=8 * tokens * width + 24 * width * size,
             transcendentals=tokens * size,
         ),
         name="expert_chunk",
-    )(z, *pieces, scaled, cots, scaled, cots, coef)
+    )(*pieces, scaled, cots, scaled, cots, coef, *more)
+    if ahead:
+        return outs[:5], (pack, outs[5].reshape(4 * pack.shape[0], pack.shape[1]))
+    return outs, None
 
 
 def joint_kernel(count, based, planar, *refs):
@@ -1066,7 +1096,7 @@
         attn_sum = lax.psum_scatter(attn_part, "col", scatter_dimension=1, tiled=True)
         scaled_share, stream = stream_step(attn_sum.astype(f32), block_input, gain_b[None])
         scaled = lax.all_gather(scaled_share.astype(bf16), "col", axis=1, tiled=True)
-    for at in range(1, 3 if planar else len(chunks)):
+    for at in range(1, 1 if planar else len(chunks)):
         if at not in gathered:
             gathered[at] = Gathered(packs[at], (scaled,))
 
@@ -1108,7 +1138,17 @@
     for at, (kind, a, b) in enumerate(chunks):
         coef = jnp.concatenate([scale_b, shares[kind][:, None]], axis=1)
         coef = after(coef, waits)
-        dpair, hidden, sums, grads, whole = expert_chunk(pieces_of(at), scaled, cot_rows, coef)
+        later = at + 2 if planar and at + 2 <= last else None
+        (dpair, hidden, sums, grads, whole), found = expert_chunk(
+            pieces_of(at),
+            scaled,
+            cot_rows,
+            coef,
+            None if later is None else packs[later],
+            4 + at,
+        )
+        if later is not None:
+            gathered[later] = found
         dots[kind] = dots.get(kind, 0.0) + sums[:, 0]
         inner = inner + sums[:, 1]
         dpairs.append(dpair)
@@ -1122,27 +1162,17 @@
         elif at == 3 and at < last:
             early, joined = joints(*early), 4
             waits += early
-        if planar and at + 2 <= last:
-            if at == 0:
-                waits += gathered[2].second(now)
-            elif at == 1:
-                gathered[2].third(now)
-                gathered[3] = Gathered(packs[3], (gathered[2].far_mid,))
-            elif at == 2:
-                gathered[3].second(now)
-                gathered[3].third()
-                gathered[4] = Gathered(packs[4], (gathered[3].far_mid,))
-        if planar and at == 3:
-            gathered[4].second(now)
-            gathered[4].third()
+        if at == 3:
+            now = early
         if not planar:
             reduced.append(Reduced(grads))
         elif at < last:
             if at >= 1:
                 waits += reduced[at - 1].second(now)
             if at >= 2:
-                waits += reduced[at - 2].third(now)
+                waits += reduced[at - 2].third((sums,))
             reduced.append(Reduced(grads))
+            waits += (reduced[at].pair,)
     now = (sums,)
     if planar:
         waits = reduced[3].second(now)

time: 1250 us -> 1300 us (1.040)
  Pallas kernels: 746 us -> 977 us
  waiting for transfers between devices: 127 us -> 1.48 us
  starting transfers between devices: 90.9 us -> 34.5 us
    pallas_call x5, Pallas kernels: 183 us -> 411 us  [expert_chunk(): pl.pallas_call(functools.partial(expert_kernel, size, steps, count, ahead...]
    ppermute x4, waiting for transfers between devices: 41.4 us -> 0.01 us  [third(): self.swapped = lax.ppermute(value, 'row', PAIRS)]
    ppermute x4 -> x1, waiting for transfers between devices: 38.5 us -> 0.01 us  [__init__(): self.partner = lax.ppermute(part, 'row', PAIRS)]
    ppermute x4 -> x1, waiting for transfers between devices: 34 us -> 0.01 us  [third(): self.far_out = lax.ppermute(after(self.far_mid, *groups), 'row', OUTWARD)]
    ppermute x4, starting transfers between devices: 22.9 us -> 3.09 us  [third(): self.swapped = lax.ppermute(value, 'row', PAIRS)]
    ppermute x4, starting transfers between devices: 28.6 us -> 15 us  [__init__(): self.first = lax.ppermute(self.pair, 'row', INWARD)]
    unnamed x149 -> x143, local copies, waits for them, and re-layouts: 26.1 us -> 21.7 us
  transfers between devices with their start and end apart: 36 -> 21, of which waited for: 5 -> 0; matrix products, arithmetic and copies ran while one was open for 17% -> 15% of each run, Pallas kernels for 60% -> 68%
where the time goes in v10:
time: 1300 us; the launch traced here: 1290 us
  Pallas kernels  977 us (75%)
  other arithmetic  91.2 us (7%)
  local copies, waits for them, and re-layouts  80.7 us (6%)
  blocking collectives  50.3 us (4%)
  matrix products  39.3 us (3%)
  starting transfers between devices  34.5 us (3%)
  between operations  15.2 us (1%)
    pallas_call x5, Pallas kernels, expert_chunk(): pl.pallas_call(functools.partial(expert_kernel, size, steps, count, ahead...  411 us
    pallas_call x3, Pallas kernels, plane_step(): pl.pallas_call(functools.partial(plane_kernel, pointwise, len(inputs), ma...  314 us
    pallas_call x8, Pallas kernels, joint_back(): pl.pallas_call(functools.partial(joint_kernel, len(lefts), len(base) > 0,...  129 us
    pallas_call x1, Pallas kernels, gather_now(): pl.pallas_call(functools.partial(gather_kernel, count), in_specs=[anywher...  81.9 us
    pallas_call x1, Pallas kernels, attend_backward(): pl.pallas_call(attend_backward_kernel, grid_spec=pltpu.PrefetchScalarGrid...  28.3 us
  transfers between devices with their start and end apart: 21, of which 0 were waited for; matrix products, arithmetic and copies ran while one was open for 15% of the time, Pallas kernels for 68%

profile of v10, /device:TPU:0, one launch (start us, length us, event | category | flops | bytes accessed | tf_op | source)
XLA Modules:
  0.0 1289.9 jit_solution(9780503350129729303)
XLA Ops:
  26.2 81.9 %gather_rows.1 = (bf16[4,512,768]{2,1,0:T(8,128)(2,1)}, bf16[4,512,384]{2,1,0:T(8,128)(2,1)}) custom-call(bf16[512,768]{1,0:T(8,128)(2,1)} %copy.135.refs_0_, bf16[512,384]{1,0:T(8,128)(2,1)} %fusion.18.refs_1_), custom_call_target="tpu_custom_call" | custom-call | flops 63700992000 | bytes 7077888 | tf_op jit(solution)/shard_map/gather_rows/pallas_call | solution.py:677
  114.6 9.3 all_gather.16
  144.4 10.5 fusion.4.raw_ref
  154.9 12.7 attend_forward.1
  167.6 8.7 joint_back.8.refs_0_
  176.4 127.4 %plane_step.3 = (f32[2048,256]{1,0:T(8,128)}, bf16[2048,2048]{1,0:T(8,128)(2,1)}, bf16[4,512,1536]{2,1,0:T(8,128)(2,1)}) custom-call(bf16[2,2,2,2048,256]{4,3,2,1,0:T(8,128)(2,1)} %joint_back.8.refs_0_, bf16[2048,256]{1,0:T(8,128)(2,1)} %refs_1_.1, f32[1,256]{1,0:T(1,128)} %reshape_convert_fusion.refs_2_.refs_5_, ...), custom_call_target="tpu_custom_call" | custom-call | flops 60000002048 | bytes 16777216 | tf_op jit(solution)/shard_map/plane_step/pallas_call | solution.py:642
  303.8 5.8 multiply_reduce_fusion
  315.1 104.8 %expert_chunk.5 = (bf16[2048,512]{1,0:T(8,128)(2,1)}, bf16[2048,256]{1,0:T(8,128)(2,1)}, f32[2048,2]{1,0:T(8,128)}, bf16[2048,768]{1,0:T(8,128)(2,1)}, bf16[2048...) custom-call(bf16[512,768]{1,0:T(8,128)(2,1)} %fusion.16.refs_0_, bf16[512,768]{1,0:T(8,128)(2,1)} %collective-permute-done.refs_1_, ...), custom_call_target="tpu_custom_call" | custom-call | flops 12884901888 | bytes 46137344 | tf_op jit(solution)/shard_map/expert_chunk/pallas_call | solution.py:886
  426.8 129.2 %expert_chunk.6 = (bf16[2048,1024]{1,0:T(8,128)(2,1)}, bf16[2048,512]{1,0:T(8,128)(2,1)}, f32[2048,2]{1,0:T(8,128)}, bf16[2048,1536]{1,0:T(8,128)(2,1)}, bf16[20...) custom-call(bf16[512,1536]{1,0:T(8,128)(2,1)} %pad_maximum_fusion.1.refs_3_.refs_0_, bf16[2048,1536]{1,0:T(8,128)(2,1)} %bitcast.120, ...), custom_call_target="tpu_custom_call" | custom-call | flops 25769803776 | bytes 58720256 | tf_op jit(solution)/shard_map/expert_chunk/pallas_call | solution.py:886
  562.8 19.1 %joint_back.9.refs_4_ = f32[2048,2048]{1,0:T(8,128)} custom-call(bf16[2048,512]{1,0:T(8,128)(2,1)} %get-tuple-element.88.refs_0_, bf16[2048,1024]{1,0:T(8,128)(2,1)} %get-tuple-element.92.refs_1_, bf16[2048,768]{1,0:T(8,128)(2,1)} %get-tuple-element.93.refs_2_, bf16[2048,1536]{1,0:T(8,128)(2,1)} %get-tuple-element.94.refs_3_), custom_call_target="tpu_custom_call" | custom-call | flops 12884901888 | bytes 29360128 | tf_op jit(solution)/shard_map/joint_back/pallas_call | solution.py:956
  582.0 13.0 %joint_back.10.refs_4_ = f32[2048,2048]{1,0:T(8,128)} custom-call(bf16[2048,256]{1,0:T(8,128)(2,1)} %get-tuple-element.95.refs_0_, bf16[2048,512]{1,0:T(8,128)(2,1)} %get-tuple-element.96.refs_1_, bf16[2048,768]{1,0:T(8,128)(2,1)} %get-tuple-element.93.refs_2_, bf16[2048,1536]{1,0:T(8,128)(2,1)} %get-tuple-element.94.refs_3_), custom_call_target="tpu_custom_call" | custom-call | flops 6442450944 | bytes 23068672 | tf_op jit(solution)/shard_map/joint_back/pallas_call | solution.py:956
  602.5 100.8 %expert_chunk.7 = (bf16[2048,1024]{1,0:T(8,128)(2,1)}, bf16[2048,512]{1,0:T(8,128)(2,1)}, f32[2048,2]{1,0:T(8,128)}, bf16[2048,1536]{1,0:T(8,128)(2,1)}, bf16[20...) custom-call(bf16[512,1536]{1,0:T(8,128)(2,1)} %pad_maximum_fusion.2.refs_11_.refs_0_, bf16[2048,1536]{1,0:T(8,128)(2,1)} %bitcast.119, ...), custom_call_target="tpu_custom_call" | custom-call | flops 25769803776 | bytes 58720256 | tf_op jit(solution)/shard_map/expert_chunk/pallas_call | solution.py:886
  710.7 5.4 add_convert_fusion.2
  722.0 39.7 %expert_chunk.8 = (bf16[2048,1024]{1,0:T(8,128)(2,1)}, bf16[2048,512]{1,0:T(8,128)(2,1)}, f32[2048,2]{1,0:T(8,128)}, bf16[2048,1536]{1,0:T(8,128)(2,1)}, bf16[2048,1536]{1,0:T(8,128)(2,1)}) custom-call(bf16[512,1536]{1,0:T(8,128)(2,1)} %pad_maximum_fusion.3.refs_7_.refs_0_, bf16[2048,1536]{1,0:T(8,128)(2,1)} %bitcast.118, ...), custom_call_target="tpu_custom_call" | custom-call | flops 25769803776 | bytes 58720256 | tf_op jit(solution)/shard_map/expert_chunk/pallas_call | solution.py:886
  765.3 5.6 collective-permute-start.10
  770.9 25.9 %joint_back.11.refs_2_ = f32[2048,2048]{1,0:T(8,128)} custom-call(bf16[2048,1024]{1,0:T(8,128)(2,1)} %get-tuple-element.102.refs_0_, bf16[2048,1024]{1,0:T(8,128)(2,1)} %get-tuple-element.109.refs_1_, bf16[2048,1536]{1,0:T(8,128)(2,1)} %get-tuple-element.110.refs_2_, bf16[2048,1536]{1,0:T(8,128)(2,1)} %get-tuple-element.111.refs_3_, ...), custom_call_target="tpu_custom_call" | custom-call | flops 17179869184 | bytes 33554432 | tf_op jit(solution)/shard_map/joint_back/pallas_call | solution.py:956
  796.7 20.2 %joint_back.12.refs_2_ = f32[2048,2048]{1,0:T(8,128)} custom-call(bf16[2048,512]{1,0:T(8,128)(2,1)} %get-tuple-element.112.refs_0_, bf16[2048,512]{1,0:T(8,128)(2,1)} %get-tuple-element.113.refs_1_, bf16[2048,1536]{1,0:T(8,128)(2,1)} %get-tuple-element.110.refs_2_, bf16[2048,1536]{1,0:T(8,128)(2,1)} %get-tuple-element.111.refs_3_, ...), custom_call_target="tpu_custom_call" | custom-call | flops 8589934592 | bytes 25165824 | tf_op jit(solution)/shard_map/joint_back/pallas_call | solution.py:956
  819.7 5.3 add_convert_fusion.1
  832.3 37.0 %expert_chunk.9 = (bf16[2048,768]{1,0:T(8,128)(2,1)}, bf16[2048,384]{1,0:T(8,128)(2,1)}, f32[2048,2]{1,0:T(8,128)}, bf16[2048,1152]{1,0:T(8,128)(2,1)}, bf16[2048,1152]{1,0:T(8,128)(2,1)}) custom-call(bf16[512,1152]{1,0:T(8,128)(2,1)} %pad_maximum_fusion.7.refs_7_.refs_0_, bf16[2048,1152]{1,0:T(8,128)(2,1)} %bitcast.121, ...), custom_call_target="tpu_custom_call" | custom-call | flops 19327352832 | bytes 52428800 | tf_op jit(solution)/shard_map/expert_chunk/pallas_call | solution.py:886
  874.1 15.6 %all-gather.1 = f32[8,3,2048]{2,1,0:T(4,128)S(1)} all-gather(f32[1,3,2048]{2,1,0:T(4,128)S(1)} %maximum_bitcast_fusion.3), channel_id=2, replica_groups=mesh['row'=4,'col'=8] {'col'}, dimensions={0}, use_global_device_ids=true | all-gather | bytes 221184 | tf_op jit(solution)/shard_map/all_gather | solution.py:1190
  893.4 5.3 add_convert_fusion
  906.1 15.7 %joint_back.13.refs_0_ = bf16[2,2,2,2048,256]{4,3,2,1,0:T(8,128)(2,1)} custom-call(bf16[2048,768]{1,0:T(8,128)(2,1)} %get-tuple-element.124.refs_0_, bf16[2048,1152]{1,0:T(8,128)(2,1)} %get-tuple-element.125.refs_1_, f32[2048,2048]{1,0:T(8,128)} %joint_back.11.refs_2_), custom_call_target="tpu_custom_call" | custom-call | flops 6442450944 | bytes 23068672 | tf_op jit(solution)/shard_map/joint_back/pallas_call | solution.py:956
  921.8 106.6 %plane_step.4 = (f32[2048,256]{1,0:T(8,128)}, f32[2048,256]{1,0:T(8,128)}, f32[512,1152]{1,0:T(8,128)}, bf16[2048,2048]{1,0:T(8,128)(2,1)}) custom-call(bf16[2,2,2,2048,256]{4,3,2,1,0:T(8,128)(2,1)} %joint_back.13.refs_0_, f32[2048,256]{1,0:T(8,128)} %fusion.27.refs_1_, bf16[2048,256]{1,0:T(8,128)(2,1)} %refs_2_.1, f32[2048,256]{1,0:T(8,128)} %get-tuple-element.85.refs_3_, ...), custom_call_target="tpu_custom_call" | custom-call | flops 60000002048 | bytes 16777216 | tf_op jit(solution)/shard_map/plane_step/pallas_call | solution.py:642
  1028.4 5.6 fusion.41
  1036.2 14.4 %joint_back.14 = bf16[2048,2048]{1,0:T(8,128)(2,1)} custom-call(bf16[2048,384]{1,0:T(8,128)(2,1)} %get-tuple-element.129.refs_0_, bf16[2048,1152]{1,0:T(8,128)(2,1)} %get-tuple-element.125.refs_1_, f32[2048,2048]{1,0:T(8,128)} %joint_back.12.refs_2_), custom_call_target="tpu_custom_call" | custom-call | flops 3221225472 | bytes 19922944 | tf_op jit(solution)/shard_map/joint_back/pallas_call | solution.py:956
  1072.7 28.3 %attend_backward.1 = (bf16[2048,768]{1,0:T(8,128)(2,1)}, f32[2048,1]{1,0:T(8,128)}) custom-call(s32[2]{0:T(128)} %dynamic_slice.70.length_ref, bf16[2048,768]{1,0:T(8,128)(2,1)} %get-tuple-element.131.qkv_ref, bf16[2048,256]{1,0:T(8,128)(2,1)} %convolution_convert_fusion.2.dcontext_ref, f32[2048,256]{1,0:T(8,128)} %get-tuple-element.134.lse_ref, ...), custom_call_target="tpu_custom_call" | custom-call | flops 4294967296 | bytes 12582912 | tf_op jit(solution)/shard_map/attend_backward/pallas_call | solution.py:151
  1101.0 11.3 convolution_convert_fusion
  1114.5 6.4 copy.157
  1121.0 12.1 joint_back.15.refs_0_
  1133.1 79.8 %plane_step.5 = (f32[2048,256]{1,0:T(8,128)}, f32[512,1024]{1,0:T(8,128)}) custom-call(bf16[2,2,2,2048,256]{4,3,2,1,0:T(8,128)(2,1)} %joint_back.15.refs_0_, bf16[4,512,1024]{2,1,0:T(8,128)(2,1)} %bitcast.90), custom_call_target="tpu_custom_call" | custom-call | flops 60000002048 | bytes 16777216 | tf_op jit(solution)/shard_map/plane_step/pallas_call | solution.py:642
  1234.3 14.8 %psum.21 = f32[2048]{0:T(1024)S(1)} all-reduce(f32[2048]{0:T(1024)S(1)} %reduce.5), channel_id=1, replica_groups=mesh['row'=4,'col'=8] {'col'}, use_global_device_ids=true, to_apply=%region_10.11 | all-reduce | flops 2048 | bytes 16384 | tf_op jit(solution)/shard_map/psum | solution.py:1225
  1272.4 10.7 all-reduce.4
  (304 shorter events, 186.0 us)
Async XLA Ops:
  7.2 106.2 %copy-start = (s32[8]{0:T(128)S(1)}, s32[8]{0:T(128)}, u32[]{:S(2)}) copy-start(s32[8]{0:T(128)} %param.20) | copy-start | bytes 100
  7.2 131.4 %all-gather.5.cloned.1.call-start = ((), (), s32[]{:S(2)}) async-start(), calls=%async_computation.2 | async-start | bytes 9437184 | tf_op jit(solution)/shard_map/all_gather | solution.py:1075
  8.0 168.4 %all-gather.7.cloned.1.call-start = ((), (), s32[]{:S(2)}) async-start(), calls=%async_computation.3 | async-start | bytes 9437184 | tf_op jit(solution)/shard_map/all_gather | solution.py:1077
  8.7 1056.9 %reduce-scatter.5.cloned.1.call-start = ((), (), s32[]{:S(2)}) async-start(), calls=%async_computation.5 | async-start | bytes 163840 | tf_op jit(solution)/shard_map/reduce_scatter | solution.py:1223
  11.2 121.8 %collective-permute-start = (bf16[512,768]{1,0:T(8,128)(2,1)}, bf16[512,768]{1,0:T(8,128)(2,1)}, u32[]{:S(2)}, u32[]{:S(2)}) collective-permute-start(bf16[512,768]{1,0:T(8,128)(2,1)} %fusion.16.refs_0_), channel_id=1, source_target_pairs={{0,8},{8,0},{16,24},{24,16},{1,9},{9,1},{17,25},{25,17},{2,10},{10... | collective-permute-start | bytes 2359304 | tf_op jit(solution)/shard_map/ppermute | solution.py:184
  14.2 121.2 %collective-permute-start.1 = (bf16[512,768]{1,0:T(8,128)(2,1)}, bf16[512,768]{1,0:T(8,128)(2,1)}, u32[]{:S(2)}, u32[]{:S(2)}) collective-permute-start(bf16[512,768]{1,0:T(8,128)(2,1)} %fusion.16.refs_0_), channel_id=1, source_target_pairs={{8,16},{16,8},{9,17},{17,9},{10,18},{18,10},{11,19},{19,11},{12,20... | collective-permute-start | bytes 2359304 | tf_op jit(solution)/shard_map/ppermute | solution.py:185
  26.2 87.1 %copy-start.56 = (s32[8]{0:T(128)S(1)}, s32[8]{0:T(128)}, u32[]{:S(2)}) copy-start(s32[8]{0:T(128)} %param.21) | copy-start | bytes 100
  124.7 188.3 %copy-start.46 = (pred[2048]{0:T(1024)(128)(4,1)}, pred[2048]{0:T(1024)(128)(4,1)S(1)}, u32[]{:S(2)}) copy-start(pred[2048]{0:T(1024)(128)(4,1)S(1)} %compare_reduce_fusion) | copy-start | bytes 6148
  133.0 3.7 collective-permute-start.2
  135.5 32.2 %collective-permute-start.3 = (bf16[512,768]{1,0:T(8,128)(2,1)}, bf16[512,768]{1,0:T(8,128)(2,1)S(1)}, u32[]{:S(2)}, u32[]{:S(2)}) collective-permute-start(bf16[512,768]{1,0:T(8,128)(2,1)} %collective-permute-done.1.refs_2_), channel_id=1, source_target_pairs={{8,0},{16,24},{9,1},{17,25},{10,2},{18,26},{11,3},{19,27},{12,4},{... | collective-permute-start | bytes 2359304 | tf_op jit(solution)/shard_map/ppermute | solution.py:190
  136.8 178.3 %collective-permute-start.4 = (bf16[512,768]{1,0:T(8,128)(2,1)S(1)}, bf16[512,768]{1,0:T(8,128)(2,1)}, u32[]{:S(2)}, u32[]{:S(2)}) collective-permute-start(bf16[512,768]{1,0:T(8,128)(2,1)S(1)} %collective-permute-done.2.refs_3_), channel_id=1, source_target_pairs={{8,0},{16,24},{9,1},{17,25},{10,2},{18,26},{11,3},{19,27},{12,4},{... | collective-permute-start | bytes 2359304 | tf_op jit(solution)/shard_map/ppermute | solution.py:197
  422.6 173.8 %collective-permute-start.5 = (bf16[1024,768]{1,0:T(8,128)(2,1)}, bf16[1024,768]{1,0:T(8,128)(2,1)}, u32[]{:S(2)}, u32[]{:S(2)}) collective-permute-start(bf16[1024,768]{1,0:T(8,128)(2,1)} %constant_dynamic-slice_fusion.4), channel_id=1, source_target_pairs={{0,8},{24,16},{1,9},{25,17},{2,10},{26,18},{3,11},{27,19},{4,12},{... | collective-permute-start | bytes 4718600 | tf_op jit(solution)/shard_map/ppermute | solution.py:710
  559.7 151.0 %collective-permute-start.6 = (bf16[1024,1536]{1,0:T(8,128)(2,1)}, bf16[1024,1536]{1,0:T(8,128)(2,1)}, u32[]{:S(2)}, u32[]{:S(2)}) collective-permute-start(bf16[1024,1536]{1,0:T(8,128)(2,1)} %constant_dynamic-slice_fusion.3), channel_id=1, source_target_pairs={{0,8},{24,16},{1,9},{25,17},{2,10},{26,18},{3,11},{27,19},{4,12},{... | collective-permute-start | bytes 9437192 | tf_op jit(solution)/shard_map/ppermute | solution.py:710
  599.4 119.0 %collective-permute-start.7 = (bf16[1024,768]{1,0:T(8,128)(2,1)}, bf16[1024,768]{1,0:T(8,128)(2,1)}, u32[]{:S(2)}, u32[]{:S(2)}) collective-permute-start(bf16[1024,768]{1,0:T(8,128)(2,1)} %add_convert_fusion.6), channel_id=1, source_target_pairs={{8,16},{16,8},{9,17},{17,9},{10,18},{18,10},{11,19},{19,11},{12,20... | collective-permute-start | bytes 4718600 | tf_op jit(solution)/shard_map/ppermute | solution.py:724
  707.1 112.6 %collective-permute-start.8 = (bf16[1024,1536]{1,0:T(8,128)(2,1)}, bf16[1024,1536]{1,0:T(8,128)(2,1)}, u32[]{:S(2)}, u32[]{:S(2)}) collective-permute-start(bf16[1024,1536]{1,0:T(8,128)(2,1)} %constant_dynamic-slice_fusion.2), channel_id=1, source_target_pairs={{0,8},{24,16},{1,9},{25,17},{2,10},{26,18},{3,11},{27,19},{4,12},{... | collective-permute-start | bytes 9437192 | tf_op jit(solution)/shard_map/ppermute | solution.py:710
  716.1 111.4 %collective-permute-start.9 = (bf16[1024,1536]{1,0:T(8,128)(2,1)}, bf16[1024,1536]{1,0:T(8,128)(2,1)}, u32[]{:S(2)}, u32[]{:S(2)}) collective-permute-start(bf16[1024,1536]{1,0:T(8,128)(2,1)} %add_convert_fusion.2), channel_id=1, source_target_pairs={{8,16},{16,8},{9,17},{17,9},{10,18},{18,10},{11,19},{19,11},{12,20... | collective-permute-start | bytes 9437192 | tf_op jit(solution)/shard_map/ppermute | solution.py:724
  720.6 96.3 %collective-permute-start.14 = (bf16[512,768]{1,0:T(8,128)(2,1)}, bf16[512,768]{1,0:T(8,128)(2,1)}, u32[]{:S(2)}, u32[]{:S(2)}) collective-permute-start(bf16[512,768]{1,0:T(8,128)(2,1)} %add_convert_fusion.8), channel_id=1, source_target_pairs={{0,8},{8,0},{16,24},{24,16},{1,9},{9,1},{17,25},{25,17},{2,10},{10... | collective-permute-start | bytes 2359304 | tf_op jit(solution)/shard_map/ppermute | solution.py:732
  765.3 128.1 %collective-permute-start.10 = (bf16[1024,1536]{1,0:T(8,128)(2,1)}, bf16[1024,1536]{1,0:T(8,128)(2,1)}, u32[]{:S(2)}, u32[]{:S(2)}) collective-permute-start(bf16[1024,1536]{1,0:T(8,128)(2,1)} %constant_dynamic-slice_fusion.1), channel_id=1, source_target_pairs={{0,8},{24,16},{1,9},{25,17},{2,10},{26,18},{3,11},{27,19},{4,12},{... | collective-permute-start | bytes 9437192 | tf_op jit(solution)/shard_map/ppermute | solution.py:710
  825.0 74.6 %collective-permute-start.11 = (bf16[1024,1536]{1,0:T(8,128)(2,1)}, bf16[1024,1536]{1,0:T(8,128)(2,1)}, u32[]{:S(2)}, u32[]{:S(2)}) collective-permute-start(bf16[1024,1536]{1,0:T(8,128)(2,1)} %add_convert_fusion.1), channel_id=1, source_target_pairs={{8,16},{16,8},{9,17},{17,9},{10,18},{18,10},{11,19},{19,11},{12,20... | collective-permute-start | bytes 9437192 | tf_op jit(solution)/shard_map/ppermute | solution.py:724
  831.0 222.9 %collective-permute-start.15 = (bf16[512,1536]{1,0:T(8,128)(2,1)}, bf16[512,1536]{1,0:T(8,128)(2,1)}, u32[]{:S(2)}, u32[]{:S(2)}) collective-permute-start(bf16[512,1536]{1,0:T(8,128)(2,1)} %add_convert_fusion.5), channel_id=1, source_target_pairs={{0,8},{8,0},{16,24},{24,16},{1,9},{9,1},{17,25},{25,17},{2,10},{10... | collective-permute-start | bytes 4718600 | tf_op jit(solution)/shard_map/ppermute | solution.py:732
  832.3 37.0 %copy-start.9 = (f32[2048,2]{1,0:T(8,128)S(1)}, f32[2048,2]{1,0:T(8,128)}, u32[]{:S(2)}) copy-start(f32[2048,2]{1,0:T(8,128)} %get-tuple-element.126) | copy-start | bytes 49156
  832.3 37.0 %copy-start.10 = (f32[2048,2]{1,0:T(8,128)S(1)}, f32[2048,2]{1,0:T(8,128)}, u32[]{:S(2)}) copy-start(f32[2048,2]{1,0:T(8,128)} %get-tuple-element.97) | copy-start | bytes 49156
  832.3 37.0 %copy-start.11 = (f32[2048,2]{1,0:T(8,128)S(1)}, f32[2048,2]{1,0:T(8,128)}, u32[]{:S(2)}) copy-start(f32[2048,2]{1,0:T(8,128)} %get-tuple-element.104) | copy-start | bytes 49156
  898.8 169.5 %collective-permute-start.12 = (bf16[1024,1536]{1,0:T(8,128)(2,1)}, bf16[1024,1536]{1,0:T(8,128)(2,1)S(1)}, u32[]{:S(2)}, u32[]{:S(2)}) collective-permute-start(bf16[1024,1536]{1,0:T(8,128)(2,1)} %add_convert_fusion), channel_id=1, source_target_pairs={{8,16},{16,8},{9,17},{17,9},{10,18},{18,10},{11,19},{19,11},{12,20... | collective-permute-start | bytes 9437192 | tf_op jit(solution)/shard_map/ppermute | solution.py:724
  903.0 313.0 %collective-permute-start.16 = (bf16[512,1536]{1,0:T(8,128)(2,1)}, bf16[512,1536]{1,0:T(8,128)(2,1)}, u32[]{:S(2)}, u32[]{:S(2)}) collective-permute-start(bf16[512,1536]{1,0:T(8,128)(2,1)} %add_convert_fusion.4), channel_id=1, source_target_pairs={{0,8},{8,0},{16,24},{24,16},{1,9},{9,1},{17,25},{25,17},{2,10},{10... | collective-permute-start | bytes 4718600 | tf_op jit(solution)/shard_map/ppermute | solution.py:732
  1035.8 232.6 %reduce-scatter.3.cloned.1.call-start = ((), (), s32[]{:S(2)}) async-start(), calls=%async_computation.4 | async-start | bytes 9437184 | tf_op jit(solution)/shard_map/reduce_scatter | solution.py:1215
  1068.3 32.7 %copy-start.18 = (bf16[1024,1536]{1,0:T(8,128)(2,1)}, bf16[1024,1536]{1,0:T(8,128)(2,1)S(1)}, u32[]{:S(2)}) copy-start(bf16[1024,1536]{1,0:T(8,128)(2,1)S(1)} %collective-permute-done.12) | copy-start | bytes 9437188
  1072.7 185.2 %collective-permute-start.13 = (bf16[512,1536]{1,0:T(8,128)(2,1)}, bf16[512,1536]{1,0:T(8,128)(2,1)}, u32[]{:S(2)}, u32[]{:S(2)}) collective-permute-start(bf16[512,1536]{1,0:T(8,128)(2,1)} %add_convert_fusion.3), channel_id=1, source_target_pairs={{0,8},{8,0},{16,24},{24,16},{1,9},{9,1},{17,25},{25,17},{2,10},{10... | collective-permute-start | bytes 4718600 | tf_op jit(solution)/shard_map/ppermute | solution.py:732
  1072.7 28.3 %copy-start.45 = (f32[2048]{0:T(1024)S(1)}, f32[2048]{0:T(1024)}, u32[]{:S(2)}) copy-start(f32[2048]{0:T(1024)} %copy-done.44) | copy-start | bytes 24580
  1072.7 28.3 %copy-start.50 = (f32[1,2048]{1,0:T(1,128)S(1)}, f32[1,2048]{1,0:T(1,128)}, u32[]{:S(2)}) copy-start(f32[1,2048]{1,0:T(1,128)} %copy-done.49) | copy-start | bytes 24580
  1225.4 23.6 %copy-start.42 = (f32[2048]{0:T(1024)S(1)}, f32[2048]{0:T(1024)}, u32[]{:S(2)}) copy-start(f32[2048]{0:T(1024)} %copy-done.41) | copy-start | bytes 24580
  1225.4 23.6 %copy-start.13 = (f32[512,512]{1,0:T(8,128)S(1)}, f32[512,512]{1,0:T(8,128)}, u32[]{:S(2)}) copy-start(f32[512,512]{1,0:T(8,128)} %get-tuple-element.216) | copy-start | bytes 3145732
  (55 other events, 410.4 us)
Sparse Core Ops, SparseCore 0:
  9.9 58.6 all-gather.4
  70.5 55.9 all-gather.6
  1035.9 17.2 reduce-scatter.4
  1056.9 69.3 reduce-scatter.2

commit v11 on v10

--- a/solution.py
+++ b/solution.py
@@ -412,6 +412,115 @@
             self.send_far().wait_send()
             self.send_near().wait_send()
             self.swap_outer().wait_send()
+
+
+class RowHop:
+    def __init__(self, kind, given, found, sems):
+        self.kind, self.given, self.found, (self.send_sems, self.recv_sems) = kind, given, found, sems
+        self.z = lax.axis_index("row")
+        self.partner, self.across = places(self.z)[1], 3 - self.z
+        self.in_middle = (self.z == 1) | (self.z == 2)
+        self.outside = jnp.logical_not(self.in_middle)
+
+    def copy_of(self, at, source, target, device):
+        return pltpu.make_async_remote_copy(
+            src_ref=source,
+            dst_ref=target,
+            send_sem=self.send_sems.at[at],
+            recv_sem=self.recv_sems.at[at],
+            device_id={"row": device},
+            device_id_type=pl.DeviceIdType.MESH,
+        )
+
+    def across_copy(self):
+        if self.kind == 1:
+            return self.copy_of(0, self.given[0], self.found[1], self.across)
+        return self.copy_of(0, self.given[0], self.found[0], self.across)
+
+    def outward_copy(self):
+        if self.kind == 1:
+            return self.copy_of(1, self.given[0], self.found[0], self.partner)
+        if self.kind == 3:
+            return self.copy_of(1, self.given[0], self.found[0], self.partner)
+        return self.copy_of(1, self.given[1], self.found[1], self.partner)
+
+    def last_copy(self):
+        return self.copy_of(2, self.found[0], self.found[2], self.partner)
+
+    def begin(self):
+        barrier = pltpu.get_barrier_semaphore()
+        signal_to(barrier, {"row": self.partner})
+
+        @pl.when(self.in_middle)
+        def _():
+            signal_to(barrier, {"row": self.across})
+            pl.semaphore_wait(barrier, 2)
+            if self.kind != 3:
+                self.across_copy().start()
+            self.outward_copy().start()
+
+        @pl.when(self.outside)
+        def _():
+            pl.semaphore_wait(barrier, 1)
+            if self.kind == 1:
+                self.outward_copy().start()
+
+    def finish(self):
+        @pl.when(self.in_middle)
+        def _():
+            if self.kind != 3:
+                self.across_copy().wait()
+            if self.kind == 23:
+                self.last_copy().start()
+            if self.kind == 1:
+                self.outward_copy().wait()
+            else:
+                self.outward_copy().wait_send()
+            if self.kind == 23:
+                self.last_copy().wait_send()
+
+        @pl.when(self.outside)
+        def _():
+            if self.kind == 1:
+                self.outward_copy().wait()
+            else:
+                self.outward_copy().wait_recv()
+            if self.kind == 23:
+                self.last_copy().wait_recv()
+
+
+HOP_COUNTS = {1: (1, 2), 2: (2, 2), 3: (1, 1), 23: (2, 3), None: (0, 0)}
+
+
+def hop_parts(hop, number):
+    if hop is None:
+        return [], [], [], pltpu.CompilerParams()
+    kind, given = hop
+    shape = jax.ShapeDtypeStruct(given[0].shape, bf16)
+    scratch = [pltpu.SemaphoreType.DMA((3,)), pltpu.SemaphoreType.DMA((3,))]
+    params = pltpu.CompilerParams(collective_id=number, has_side_effects=True)
+    return list(given), [shape] * HOP_COUNTS[kind][1], scratch, params
+
+
+def hop_kernel(kind, *refs):
+    given, found = HOP_COUNTS[kind]
+    hop = RowHop(kind, refs[:given], refs[given : given + found], refs[given + found :])
+    hop.begin()
+    hop.finish()
+
+
+def hop_now(hop, number):
+    given, shapes, scratch, params = hop_parts(hop, number)
+    anywhere = pl.BlockSpec(memory_space=pl.ANY)
+    return pl.pallas_call(
+        functools.partial(hop_kernel, hop[0]),
+        in_specs=[anywhere] * len(given),
+        out_specs=[anywhere] * len(shapes),
+        out_shape=shapes,
+        scratch_shapes=scratch,
+        compiler_params=params,
+        name="gather_hops",
+    )(*given)
 
 
 def signal_to(barrier, device):
@@ -750,25 +859,23 @@
     return lax.optimization_barrier((value,) + others)[0] if others else value
 
 
-def expert_kernel(size, steps, count, ahead, *refs):
+def expert_kernel(size, steps, count, kind, *refs):
     pieces = refs[:count]
     (x_ref, cot_ref, x_cols, cot_cols, coef_ref) = refs[count : count + 5]
-    at = count + 5 + ahead
+    taken, found = HOP_COUNTS[kind]
+    at = count + 5 + taken
     (dpair_ref, hidden_ref, sums_ref, grads_ref, whole_ref) = refs[at : at + 5]
-    weights, dpair, hidden, sems, out_sem = refs[at + 5 + ahead : at + 10 + ahead]
+    weights, dpair, hidden, sems, out_sem = refs[at + 5 + found : at + 10 + found]
     step = pl.program_id(0)
     final = pl.num_programs(0) - 1
-    if ahead:
-        rows = RowGather(refs[count + 5 : count + 6], refs[at + 5 : at + 6], refs[at + 10 + ahead :])
+    if kind:
+        hop = RowHop(
+            kind, refs[count + 5 : at], refs[at + 5 : at + 5 + found], refs[at + 10 + found :]
+        )
 
         @pl.when(step == 0)
         def _():
-            rows.greet(pltpu.get_barrier_semaphore())
-            rows.begin()
-
-        @pl.when(step == final - 2)
-        def _():
-            rows.hand_on(0)
+            hop.begin()
 
     write = pltpu.make_async_copy(weights, whole_ref, out_sem)
 
@@ -863,12 +970,11 @@
     @pl.when(step == final)
     def _():
         write.wait()
-        if ahead:
-            rows.hand_last(0)
-            rows.finish()
-
-
-def expert_chunk(pieces, scaled, cots, coef, pack=None, number=None):
+        if kind:
+            hop.finish()
+
+
+def expert_chunk(pieces, scaled, cots, coef, hop=None, number=None):
     tokens, width = scaled.shape
     size = pieces[0].shape[1] // 3
     steps, more_steps = tokens // TILE, width // TILE
@@ -877,14 +983,9 @@
     cols = lambda i: (0, jnp.maximum(i - steps, 0))
     down = lambda i: (jnp.maximum(i - steps, 0), 0)
     anywhere = pl.BlockSpec(memory_space=pl.ANY)
-    ahead, more, more_shapes, more_scratch, params = 0, [], [], [], {}
-    if pack is not None:
-        ahead, more = 1, [pack]
-        more_shapes = [jax.ShapeDtypeStruct((4,) + pack.shape, bf16)]
-        more_scratch = [pltpu.SemaphoreType.DMA((5, 1))] * 2
-        params = dict(collective_id=number, has_side_effects=True)
+    more, more_shapes, more_scratch, params = hop_parts(hop, number)
     outs = pl.pallas_call(
-        functools.partial(expert_kernel, size, steps, count, ahead),
+        functools.partial(expert_kernel, size, steps, count, hop and hop[0]),
         grid_spec=pl.GridSpec(
             grid=(steps + more_steps,),
             in_specs=[pl.BlockSpec(memory_space=pl.ANY)] * count
@@ -895,7 +996,7 @@
                 pl.BlockSpec((tokens, TILE), cols),
                 pl.BlockSpec((TILE, 2), rows),
             ]
-            + [anywhere] * ahead,
+            + [anywhere] * len(more),
             out_specs=[
                 pl.BlockSpec((TILE, 2 * size), rows),
                 pl.BlockSpec((TILE, size), rows),
@@ -903,7 +1004,7 @@
                 pl.BlockSpec((TILE, 3 * size), down),
                 anywhere,
             ]
-            + [anywhere] * ahead,
+            + [anywhere] * len(more_shapes),
             scratch_shapes=[
                 pltpu.VMEM((width, 3 * size), bf16),
                 pltpu.VMEM((tokens, 2 * size), bf16),
@@ -921,7 +1022,7 @@
             jax.ShapeDtypeStruct((width, 3 * size), bf16),
         ]
         + more_shapes,
-        compiler_params=pltpu.CompilerParams(**params),
+        compiler_params=params,
         cost_estimate=pl.CostEstimate(
             flops=12 * tokens * width * size,
             bytes_accessed=8 * tokens * width + 24 * width * size,
@@ -929,13 +1030,20 @@
         ),
         name="expert_chunk",
     )(*pieces, scaled, cots, scaled, cots, coef, *more)
-    if ahead:
-        return outs[:5], (pack, outs[5].reshape(4 * pack.shape[0], pack.shape[1]))
-    return outs, None
-
-
-def joint_kernel(count, based, planar, *refs):
-    out_ref = refs[-1]
+    return outs[:5], outs[5:]
+
+
+def joint_kernel(count, based, planar, kind, *refs):
+    taken, found = HOP_COUNTS[kind]
+    at = 2 * count + based + taken
+    out_ref = refs[at]
+    if kind:
+        hop = RowHop(kind, refs[at - taken : at], refs[at + 1 : at + 1 + found], refs[at + 1 + found :])
+
+        @pl.when(pl.program_id(0) == 0)
+        def _():
+            hop.begin()
+
     for a in range(0, refs[count].shape[0], TILE):
         total = refs[2 * count][:, a : a + TILE] if based else None
         for left, weights in zip(refs[:count], refs[count : 2 * count]):
@@ -946,33 +1054,47 @@
             out_ref[at // 4, at // 2 % 2, at % 2] = total.astype(out_ref.dtype)
         else:
             out_ref[:, a : a + TILE] = total.astype(out_ref.dtype)
-
-
-def joint_back(lefts, weights, column, kind, *base, planar=False):
+    if kind:
+        @pl.when(pl.program_id(0) == pl.num_programs(0) - 1)
+        def _():
+            hop.finish()
+
+
+def joint_back(lefts, weights, column, kind, *base, planar=False, hop=None, number=None):
     tokens, width = lefts[0].shape[0], weights[0].shape[0]
     row = lambda i: (i, 0)
     fixed = lambda i: (0, column)
     depth = sum(left.shape[1] for left in lefts)
-    return pl.pallas_call(
-        functools.partial(joint_kernel, len(lefts), len(base) > 0, planar),
+    more, more_shapes, more_scratch, params = hop_parts(hop, number)
+    anywhere = pl.BlockSpec(memory_space=pl.ANY)
+    out_spec = pl.BlockSpec((TILE, width), row)
+    if planar:
+        out_spec = pl.BlockSpec((2, 2, 2, TILE, TILE), lambda i: (0, 0, 0, i, 0))
+    outs = pl.pallas_call(
+        functools.partial(joint_kernel, len(lefts), len(base), planar, hop and hop[0]),
         grid=(tokens // TILE,),
         in_specs=[pl.BlockSpec((TILE, left.shape[1]), row) for left in lefts]
         + [
             pl.BlockSpec((width, left.shape[1]), fixed, pipeline_mode=pl.Buffered(1))
             for left in lefts
         ]
-        + [pl.BlockSpec((TILE, width), row)] * len(base),
-        out_specs=pl.BlockSpec((2, 2, 2, TILE, TILE), lambda i: (0, 0, 0, i, 0))
-        if planar
-        else pl.BlockSpec((TILE, width), row),
-        out_shape=jax.ShapeDtypeStruct((2, 2, 2, tokens, TILE) if planar else (tokens, width), kind),
+        + [pl.BlockSpec((TILE, width), row)] * len(base)
+        + [anywhere] * len(more),
+        out_specs=[out_spec] + [anywhere] * len(more_shapes),
+        out_shape=[
+            jax.ShapeDtypeStruct((2, 2, 2, tokens, TILE) if planar else (tokens, width), kind)
+        ]
+        + more_shapes,
+        scratch_shapes=more_scratch,
+        compiler_params=params,
         cost_estimate=pl.CostEstimate(
             flops=2 * tokens * width * depth,
             bytes_accessed=2 * (tokens + width) * depth + 4 * tokens * width,
             transcendentals=0,
         ),
         name="joint_back",
-    )(*lefts, *weights, *base)
+    )(*lefts, *weights, *base, *more)
+    return outs[0] if hop is None else outs
 
 
 def split_three(values):
@@ -1129,26 +1251,17 @@
             gathered[at].second()
             gathered[at].third()
 
-    def joints(*base):
-        return (
-            joint_back(dpairs[-2:], wholes[-2:], 0, f32, *base[:1]),
-            joint_back(hiddens[-2:], wholes[-2:], 2, f32, *base[1:]),
-        )
-
+    carried = []
     for at, (kind, a, b) in enumerate(chunks):
         coef = jnp.concatenate([scale_b, shares[kind][:, None]], axis=1)
         coef = after(coef, waits)
-        later = at + 2 if planar and at + 2 <= last else None
+        hop = None
+        if planar:
+            hop = {0: (1, packs[2:3]), 1: (2, carried), 2: (1, packs[3:4]), 3: (1, packs[4:5])}.get(at)
         (dpair, hidden, sums, grads, whole), found = expert_chunk(
-            pieces_of(at),
-            scaled,
-            cot_rows,
-            coef,
-            None if later is None else packs[later],
-            4 + at,
+            pieces_of(at), scaled, cot_rows, coef, hop, 4 + at
         )
-        if later is not None:
-            gathered[later] = found
+        carried = carried + list(found) if at == 1 else list(found)
         dots[kind] = dots.get(kind, 0.0) + sums[:, 0]
         inner = inner + sums[:, 1]
         dpairs.append(dpair)
@@ -1156,14 +1269,28 @@
         wholes.append(whole)
         now = (sums,)
         waits = ()
-        if at == 1:
-            early, joined = joints(), 2
-            waits += early
-        elif at == 3 and at < last:
-            early, joined = joints(*early), 4
-            waits += early
-        if at == 3:
+        early = ()
+        if planar and at == 1:
+            dscaled_early, last_piece = joint_back(
+                dpairs, wholes, 0, f32, hop=(3, carried[2:3]), number=9
+            )
+            gathered[2] = (packs[2], *carried[:2], carried[2], carried[3], last_piece)
+            early = (dscaled_early,)
+        elif planar and at == 2:
+            rest = hop_now((23, [after(carried[0], now), carried[1]]), 10)
+            gathered[3] = (packs[3], *carried, *rest)
+            early = (rest[2],)
+        elif planar and at == 3:
+            dscaled_early, *next_pieces = joint_back(
+                dpairs[2:], wholes[2:], 0, f32, dscaled_early, hop=(2, carried), number=11
+            )
+            moe_early, last_piece = joint_back(
+                hiddens, wholes, 2, f32, hop=(3, next_pieces[:1]), number=12
+            )
+            gathered[4] = (packs[4], *carried, *next_pieces, last_piece)
+            early = (dscaled_early, moe_early)
             now = early
+        waits += early
         if not planar:
             reduced.append(Reduced(grads))
         elif at < last:
@@ -1182,9 +1309,11 @@
         for one in reduced:
             one.second()
             one.third()
+    joined = 4 if planar else 0
+    bases = ((dscaled_early,), (moe_early,)) if planar else ((), ())
     late_pairs, late_wholes, late_hiddens = dpairs[joined:], wholes[joined:], hiddens[joined:]
     late_pairs[-1] = after(late_pairs[-1], waits)
-    dscaled_part = joint_back(late_pairs, late_wholes, 0, bf16, early[0], planar=planar)
+    dscaled_part = joint_back(late_pairs, late_wholes, 0, bf16, *bases[0], planar=planar)
 
     named = [jnp.where(members[local], dots[local], 0.0) for local in range(local_experts)]
     table = lax.all_gather(jnp.stack(named + [dots[None], inner]), "col", axis=0)
@@ -1211,7 +1340,7 @@
     gain_b_grad = jnp.sum(dscaled * stream, axis=0)
 
     late_hiddens[-1] = after(late_hiddens[-1], (dattn,))
-    moe_part = joint_back(late_hiddens, late_wholes, 2, bf16, early[1])
+    moe_part = joint_back(late_hiddens, late_wholes, 2, bf16, *bases[1])
     moe_share = lax.psum_scatter(moe_part, "col", scatter_dimension=1, tiled=True).astype(f32)
     block_output = (stream + moe_share).astype(bf16)
     out_part = mm_tn(dattn, context).astype(bf16)

time: 1300 us -> 1220 us (0.938)
  Pallas kernels: 977 us -> 840 us
  starting transfers between devices: 34.5 us -> 96.8 us
    pallas_call x13, Pallas kernels: 540 us -> 418 us  [the longest x5 211 us: expert_chunk(): pl.pallas_call(functools.partial(expert_kernel, size, steps, count, hop a...]
    ppermute x4, starting transfers between devices: 15 us -> 74.2 us  [__init__(): self.first = lax.ppermute(self.pair, 'row', INWARD)]
    pallas_call x3, Pallas kernels: 314 us -> 298 us  [plane_step(): pl.pallas_call(functools.partial(plane_kernel, pointwise, len(inputs), ma...]
    unnamed x143 -> x147, local copies, waits for them, and re-layouts: 21.7 us -> 27.1 us
  transfers between devices with their start and end apart: 21 -> 21, of which waited for: 0 -> 0; matrix products, arithmetic and copies ran while one was open for 15% -> 17% of each run, Pallas kernels for 68% -> 66%
where the time goes in v11:
time: 1220 us; the launch traced here: 1210 us
  Pallas kernels  840 us (69%)
  starting transfers between devices  96.8 us (8%)
  other arithmetic  90.4 us (7%)
  local copies, waits for them, and re-layouts  83.4 us (7%)
  blocking collectives  45.1 us (4%)
  matrix products  39.3 us (3%)
  between operations  15.2 us (1%)
    pallas_call x3, Pallas kernels, plane_step(): pl.pallas_call(functools.partial(plane_kernel, pointwise, len(inputs), ma...  298 us
    pallas_call x5, Pallas kernels, expert_chunk(): pl.pallas_call(functools.partial(expert_kernel, size, steps, count, hop a...  211 us
    pallas_call x7, Pallas kernels, joint_back(): pl.pallas_call(functools.partial(joint_kernel, len(lefts), len(base), pla...  143 us
    pallas_call x1, Pallas kernels, gather_now(): pl.pallas_call(functools.partial(gather_kernel, count), in_specs=[anywher...  82.9 us
    ppermute x4, starting transfers between devices, __init__(): self.first = lax.ppermute(self.pair, 'row', INWARD)  74.2 us
    pallas_call x1, Pallas kernels, hop_now(): pl.pallas_call(functools.partial(hop_kernel, hop[0]), in_specs=[anywhere]...  64.4 us
    pallas_call x1, Pallas kernels, attend_backward(): pl.pallas_call(attend_backward_kernel, grid_spec=pltpu.PrefetchScalarGrid...  28.3 us
    unnamed x147, local copies, waits for them, and re-layouts  27.1 us
  transfers between devices with their start and end apart: 21, of which 0 were waited for; matrix products, arithmetic and copies ran while one was open for 17% of the time, Pallas kernels for 66%

profile of v11, /device:TPU:0, one launch (start us, length us, event | category | flops | bytes accessed | tf_op | source)
XLA Modules:
  0.0 1211.7 jit_solution(15843604479162606681)
XLA Ops:
  25.2 82.9 %gather_rows.1 = (bf16[4,512,768]{2,1,0:T(8,128)(2,1)}, bf16[4,512,384]{2,1,0:T(8,128)(2,1)}) custom-call(bf16[512,768]{1,0:T(8,128)(2,1)} %copy.135.refs_0_, bf16[512,384]{1,0:T(8,128)(2,1)} %fusion.18.refs_1_), custom_call_target="tpu_custom_call" | custom-call | flops 63700992000 | bytes 7077888 | tf_op jit(solution)/shard_map/gather_rows/pallas_call | solution.py:786
  127.5 9.0 all_gather.16
  147.2 10.5 fusion.4.raw_ref
  157.7 12.7 %attend_forward.1 = (bf16[2048,768]{1,0:T(8,128)(2,1)}, bf16[2048,256]{1,0:T(8,128)(2,1)}, f32[2048,256]{1,0:T(8,128)}) custom-call(s32[2]{0:T(128)} %dynamic_slice.70.length_ref, f32[2048,768]{1,0:T(8,128)} %fusion.4.raw_ref, f32[1024,128]{1,0:T(8,128)} %get-tuple-element.289.cos_ref, f32[1024,128]{1,0:T(8,128)} %get-tuple-element.290.sin_ref), custom_call_target="tpu_custom_call" | custom-call | flops 1610612736 | bytes 12582912 | tf_op jit(solution)/shard_map/attend_forward/pallas_call | solution.py:81
  170.4 8.7 joint_back.7.refs_0_
  179.2 113.2 %plane_step.3 = (f32[2048,256]{1,0:T(8,128)}, bf16[2048,2048]{1,0:T(8,128)(2,1)}, bf16[4,512,1536]{2,1,0:T(8,128)(2,1)}) custom-call(bf16[2,2,2,2048,256]{4,3,2,1,0:T(8,128)(2,1)} %joint_back.7.refs_0_, bf16[2048,256]{1,0:T(8,128)(2,1)} %refs_1_.1, f32[1,256]{1,0:T(1,128)} %reshape_convert_fusion.refs_2_.refs_5_, ...), custom_call_target="tpu_custom_call" | custom-call | flops 60000002048 | bytes 16777216 | tf_op jit(solution)/shard_map/plane_step/pallas_call | solution.py:751
  292.3 5.8 multiply_reduce_fusion
  304.4 37.8 %expert_chunk.5 = (bf16[2048,512]{1,0:T(8,128)(2,1)}, bf16[2048,256]{1,0:T(8,128)(2,1)}, f32[2048,2]{1,0:T(8,128)}, bf16[2048,768]{1,0:T(8,128)(2,1)}, bf16[2048...) custom-call(bf16[512,768]{1,0:T(8,128)(2,1)} %fusion.16.refs_0_, ...), custom_call_target="tpu_custom_call" | custom-call | flops 12884901888 | bytes 46137344 | tf_op jit(solution)/shard_map/expert_chunk/pallas_call | solution.py:987
  350.7 40.5 %expert_chunk.6 = (bf16[2048,1024]{1,0:T(8,128)(2,1)}, bf16[2048,512]{1,0:T(8,128)(2,1)}, f32[2048,2]{1,0:T(8,128)}, bf16[2048,1536]{1,0:T(8,128)(2,1)}, bf16[20...) custom-call(bf16[512,1536]{1,0:T(8,128)(2,1)} %get-tuple-element.287.refs_3_.refs_0_, ...), custom_call_target="tpu_custom_call" | custom-call | flops 25769803776 | bytes 58720256 | tf_op jit(solution)/shard_map/expert_chunk/pallas_call | solution.py:987
  395.1 5.4 collective-permute-start.6
  400.5 37.3 %joint_back.8 = (f32[2048,2048]{1,0:T(8,128)}, bf16[512,1536]{1,0:T(8,128)(2,1)}) custom-call(bf16[2048,512]{1,0:T(8,128)(2,1)} %get-tuple-element.110.refs_0_, bf16[2048,1024]{1,0:T(8,128)(2,1)} %get-tuple-element.111.refs_1_, bf16[2048,768]{1,0:T(8,128)(2,1)} %get-tuple-element.112.refs_2_.refs_4_, bf16[2048,1536]{1,0:T(8,128)(2,1)} %get-tuple-element.113.refs_3_.refs_5_, ...), custom_call_target="tpu_custom_call" | custom-call | flops 12884901888 | bytes 29360128 | tf_op jit(solution)/shard_map/joint_back/pallas_call | solution.py:1073
  445.4 52.8 %expert_chunk.7 = (bf16[2048,1024]{1,0:T(8,128)(2,1)}, bf16[2048,512]{1,0:T(8,128)(2,1)}, f32[2048,2]{1,0:T(8,128)}, bf16[2048,1536]{1,0:T(8,128)(2,1)}, bf16[20...) custom-call(bf16[512,1536]{1,0:T(8,128)(2,1)} %get-tuple-element.288.refs_11_.refs_0_, ...), custom_call_target="tpu_custom_call" | custom-call | flops 25769803776 | bytes 58720256 | tf_op jit(solution)/shard_map/expert_chunk/pallas_call | solution.py:987
  501.9 15.9 %collective-permute-start.8 = (bf16[1024,1536]{1,0:T(8,128)(2,1)}, bf16[1024,1536]{1,0:T(8,128)(2,1)}, u32[]{:S(2)}, u32[]{:S(2)}) collective-permute-start(bf16[1024,1536]{1,0:T(8,128)(2,1)} %constant_dynamic-slice_fusion.2), channel_id=1, source_target_pairs={{0,8},{24,16},{1,9},{25,17},{2,10},{26,18},{3,11},{27,19},{4,12},{... | collective-permute-start | bytes 9437192 | tf_op jit(solution)/shard_map/ppermute | solution.py:819
  517.9 64.4 %gather_hops.1 = (bf16[512,1536]{1,0:T(8,128)(2,1)}, bf16[512,1536]{1,0:T(8,128)(2,1)}, bf16[512,1536]{1,0:T(8,128)(2,1)}) custom-call(bf16[512,1536]{1,0:T(8,128)(2,1)} %get-tuple-element.123.refs_0_.refs_1_, bf16[512,1536]{1,0:T(8,128)(2,1)} %get-tuple-element.121.refs_1_.refs_2_), custom_call_target="tpu_custom_call" | custom-call | tf_op jit(solution)/shard_map/gather_hops/pallas_call | solution.py:515
  594.0 42.4 %expert_chunk.8 = (bf16[2048,1024]{1,0:T(8,128)(2,1)}, bf16[2048,512]{1,0:T(8,128)(2,1)}, f32[2048,2]{1,0:T(8,128)}, bf16[2048,1536]{1,0:T(8,128)(2,1)}, bf16[20...) custom-call(bf16[512,1536]{1,0:T(8,128)(2,1)} %pad_maximum_fusion.2.refs_11_.refs_0_, ...), custom_call_target="tpu_custom_call" | custom-call | flops 25769803776 | bytes 58720256 | tf_op jit(solution)/shard_map/expert_chunk/pallas_call | solution.py:987
  640.2 48.4 %collective-permute-start.10 = (bf16[1024,1536]{1,0:T(8,128)(2,1)}, bf16[1024,1536]{1,0:T(8,128)(2,1)}, u32[]{:S(2)}, u32[]{:S(2)}) collective-permute-start(bf16[1024,1536]{1,0:T(8,128)(2,1)} %constant_dynamic-slice_fusion.1), channel_id=1, source_target_pairs={{0,8},{24,16},{1,9},{25,17},{2,10},{26,18},{3,11},{27,19},{4,12},{... | collective-permute-start | bytes 9437192 | tf_op jit(solution)/shard_map/ppermute | solution.py:819
  688.6 28.2 %joint_back.9 = (f32[2048,2048]{1,0:T(8,128)}, bf16[512,1152]{1,0:T(8,128)(2,1)}, bf16[512,1152]{1,0:T(8,128)(2,1)}) custom-call(bf16[2048,1024]{1,0:T(8,128)(2,1)} %get-tuple-element.133.refs_0_, bf16[2048,1024]{1,0:T(8,128)(2,1)} %get-tuple-element.134.refs_1_, bf16[2048,1536]{1,0:T(8,128)(2,1)} %get-tuple-element.135.refs_2_.refs_6_, ...), custom_call_target="tpu_custom_call" | custom-call | flops 17179869184 | bytes 33554432 | tf_op jit(solution)/shard_map/joint_back/pallas_call | solution.py:1073
  716.8 26.8 %joint_back.10 = (f32[2048,2048]{1,0:T(8,128)}, bf16[512,1152]{1,0:T(8,128)(2,1)}) custom-call(bf16[2048,256]{1,0:T(8,128)(2,1)} %get-tuple-element.139.refs_0_, bf16[2048,512]{1,0:T(8,128)(2,1)} %get-tuple-element.140.refs_1_, bf16[2048,512]{1,0:T(8,128)(2,1)} %get-tuple-element.141.refs_2_, bf16[2048,512]{1,0:T(8,128)(2,1)} %get-tuple-element.142.refs_3_, ...), custom_call_target="tpu_custom_call" | custom-call | flops 15032385536 | bytes 31457280 | tf_op jit(solution)/shard_map/joint_back/pallas_call | solution.py:1073
  760.0 37.0 %expert_chunk.9 = (bf16[2048,768]{1,0:T(8,128)(2,1)}, bf16[2048,384]{1,0:T(8,128)(2,1)}, f32[2048,2]{1,0:T(8,128)}, bf16[2048,1152]{1,0:T(8,128)(2,1)}, bf16[2048,1152]{1,0:T(8,128)(2,1)}) custom-call(bf16[512,1152]{1,0:T(8,128)(2,1)} %pad_maximum_fusion.7.refs_11_.refs_0_, bf16[512,1152]{1,0:T(8,128)(2,1)} %get-tuple-element.131.refs_5_.refs_1_, ...), custom_call_target="tpu_custom_call" | custom-call | flops 19327352832 | bytes 52428800 | tf_op jit(solution)/shard_map/expert_chunk/pallas_call | solution.py:987
  801.7 10.4 all-gather.1
  815.9 5.4 add_convert_fusion
  829.5 15.7 %joint_back.11.refs_0_ = bf16[2,2,2,2048,256]{4,3,2,1,0:T(8,128)(2,1)} custom-call(bf16[2048,768]{1,0:T(8,128)(2,1)} %get-tuple-element.156.refs_0_, bf16[2048,1152]{1,0:T(8,128)(2,1)} %get-tuple-element.157.refs_1_, f32[2048,2048]{1,0:T(8,128)} %get-tuple-element.144.refs_2_), custom_call_target="tpu_custom_call" | custom-call | flops 6442450944 | bytes 23068672 | tf_op jit(solution)/shard_map/joint_back/pallas_call | solution.py:1073
  845.2 104.9 %plane_step.4 = (f32[2048,256]{1,0:T(8,128)}, f32[2048,256]{1,0:T(8,128)}, f32[512,1152]{1,0:T(8,128)}, bf16[2048,2048]{1,0:T(8,128)(2,1)}) custom-call(bf16[2,2,2,2048,256]{4,3,2,1,0:T(8,128)(2,1)} %joint_back.11.refs_0_, f32[2048,256]{1,0:T(8,128)} %fusion.27.refs_1_, bf16[2048,256]{1,0:T(8,128)(2,1)} %refs_2_.1, f32[2048,256]{1,0:T(8,128)} %get-tuple-element.101.refs_3_, ...), custom_call_target="tpu_custom_call" | custom-call | flops 60000002048 | bytes 16777216 | tf_op jit(solution)/shard_map/plane_step/pallas_call | solution.py:751
  950.2 5.6 fusion.41
  958.0 14.3 %joint_back.12 = bf16[2048,2048]{1,0:T(8,128)(2,1)} custom-call(bf16[2048,384]{1,0:T(8,128)(2,1)} %get-tuple-element.161.refs_0_, bf16[2048,1152]{1,0:T(8,128)(2,1)} %get-tuple-element.157.refs_1_, f32[2048,2048]{1,0:T(8,128)} %get-tuple-element.145.refs_2_), custom_call_target="tpu_custom_call" | custom-call | flops 3221225472 | bytes 19922944 | tf_op jit(solution)/shard_map/joint_back/pallas_call | solution.py:1073
  994.4 28.3 %attend_backward.1 = (bf16[2048,768]{1,0:T(8,128)(2,1)}, f32[2048,1]{1,0:T(8,128)}) custom-call(s32[2]{0:T(128)} %dynamic_slice.70.length_ref, bf16[2048,768]{1,0:T(8,128)(2,1)} %get-tuple-element.163.qkv_ref, bf16[2048,256]{1,0:T(8,128)(2,1)} %convolution_convert_fusion.2.dcontext_ref, f32[2048,256]{1,0:T(8,128)} %get-tuple-element.166.lse_ref, ...), custom_call_target="tpu_custom_call" | custom-call | flops 4294967296 | bytes 12582912 | tf_op jit(solution)/shard_map/attend_backward/pallas_call | solution.py:151
  1022.7 11.3 convolution_convert_fusion
  1036.3 6.4 copy.157
  1042.7 12.2 %joint_back.13.refs_0_ = bf16[2,2,2,2048,256]{4,3,2,1,0:T(8,128)(2,1)} custom-call(bf16[2048,768]{1,0:T(8,128)(2,1)} %get-tuple-element.167.refs_0_, bf16[2048,768]{1,0:T(8,128)(2,1)} %constant_dynamic-update-slice_fusion.1.refs_1_), custom_call_target="tpu_custom_call" | custom-call | flops 6442450944 | bytes 23068672 | tf_op jit(solution)/shard_map/joint_back/pallas_call | solution.py:1073
  1054.9 79.8 %plane_step.5 = (f32[2048,256]{1,0:T(8,128)}, f32[512,1024]{1,0:T(8,128)}) custom-call(bf16[2,2,2,2048,256]{4,3,2,1,0:T(8,128)(2,1)} %joint_back.13.refs_0_, bf16[4,512,1024]{2,1,0:T(8,128)(2,1)} %bitcast.87), custom_call_target="tpu_custom_call" | custom-call | flops 60000002048 | bytes 16777216 | tf_op jit(solution)/shard_map/plane_step/pallas_call | solution.py:751
  1156.1 15.5 %psum.21 = f32[2048]{0:T(1024)S(1)} all-reduce(f32[2048]{0:T(1024)S(1)} %reduce.5), channel_id=1, replica_groups=mesh['row'=4,'col'=8] {'col'}, use_global_device_ids=true, to_apply=%region_10.11 | all-reduce | flops 2048 | bytes 16384 | tf_op jit(solution)/shard_map/psum | solution.py:1354
  1194.8 10.2 all-reduce.4
  (309 shorter events, 196.7 us)
Async XLA Ops:
  7.2 119.1 %copy-start = (s32[8]{0:T(128)S(1)}, s32[8]{0:T(128)}, u32[]{:S(2)}) copy-start(s32[8]{0:T(128)} %param.20) | copy-start | bytes 100
  7.2 134.2 %all-gather.5.cloned.1.call-start = ((), (), s32[]{:S(2)}) async-start(), calls=%async_computation.2 | async-start | bytes 9437184 | tf_op jit(solution)/shard_map/all_gather | solution.py:1197
  8.0 171.2 %all-gather.7.cloned.1.call-start = ((), (), s32[]{:S(2)}) async-start(), calls=%async_computation.3 | async-start | bytes 9437184 | tf_op jit(solution)/shard_map/all_gather | solution.py:1199
  8.7 978.6 %reduce-scatter.5.cloned.1.call-start = ((), (), s32[]{:S(2)}) async-start(), calls=%async_computation.5 | async-start | bytes 163840 | tf_op jit(solution)/shard_map/reduce_scatter | solution.py:1352
  11.2 109.7 %collective-permute-start = (bf16[512,768]{1,0:T(8,128)(2,1)}, bf16[512,768]{1,0:T(8,128)(2,1)}, u32[]{:S(2)}, u32[]{:S(2)}) collective-permute-start(bf16[512,768]{1,0:T(8,128)(2,1)} %fusion.16.refs_0_), channel_id=1, source_target_pairs={{0,8},{8,0},{16,24},{24,16},{1,9},{9,1},{17,25},{25,17},{2,10},{10... | collective-permute-start | bytes 2359304 | tf_op jit(solution)/shard_map/ppermute | solution.py:184
  14.2 124.1 %collective-permute-start.1 = (bf16[512,768]{1,0:T(8,128)(2,1)}, bf16[512,768]{1,0:T(8,128)(2,1)}, u32[]{:S(2)}, u32[]{:S(2)}) collective-permute-start(bf16[512,768]{1,0:T(8,128)(2,1)} %fusion.16.refs_0_), channel_id=1, source_target_pairs={{8,16},{16,8},{9,17},{17,9},{10,18},{18,10},{11,19},{19,11},{12,20... | collective-permute-start | bytes 2359304 | tf_op jit(solution)/shard_map/ppermute | solution.py:185
  25.2 85.4 %copy-start.58 = (s32[8]{0:T(128)S(1)}, s32[8]{0:T(128)}, u32[]{:S(2)}) copy-start(s32[8]{0:T(128)} %param.21) | copy-start | bytes 100
  25.2 86.8 %copy-start.20 = (bf16[512,768]{1,0:T(8,128)(2,1)S(1)}, bf16[512,768]{1,0:T(8,128)(2,1)}, u32[]{:S(2)}) copy-start(bf16[512,768]{1,0:T(8,128)(2,1)} %copy.135.refs_0_) | copy-start | bytes 2359300
  111.4 190.2 %copy-start.47 = (pred[2048]{0:T(1024)(128)(4,1)}, pred[2048]{0:T(1024)(128)(4,1)S(1)}, u32[]{:S(2)}) copy-start(pred[2048]{0:T(1024)(128)(4,1)S(1)} %compare_reduce_fusion) | copy-start | bytes 6148
  120.8 18.8 %collective-permute-start.2 = (bf16[512,768]{1,0:T(8,128)(2,1)}, bf16[512,768]{1,0:T(8,128)(2,1)}, u32[]{:S(2)}, u32[]{:S(2)}) collective-permute-start(bf16[512,768]{1,0:T(8,128)(2,1)} %collective-permute-done.refs_1_), channel_id=1, source_target_pairs={{8,16},{16,8},{9,17},{17,9},{10,18},{18,10},{11,19},{19,11},{12,20... | collective-permute-start | bytes 2359304 | tf_op jit(solution)/shard_map/ppermute | solution.py:191
  138.3 32.1 %collective-permute-start.3 = (bf16[512,768]{1,0:T(8,128)(2,1)}, bf16[512,768]{1,0:T(8,128)(2,1)S(1)}, u32[]{:S(2)}, u32[]{:S(2)}) collective-permute-start(bf16[512,768]{1,0:T(8,128)(2,1)} %collective-permute-done.1.refs_2_), channel_id=1, source_target_pairs={{8,0},{16,24},{9,1},{17,25},{10,2},{18,26},{11,3},{19,27},{12,4},{... | collective-permute-start | bytes 2359304 | tf_op jit(solution)/shard_map/ppermute | solution.py:190
  139.6 164.0 %collective-permute-start.4 = (bf16[512,768]{1,0:T(8,128)(2,1)}, bf16[512,768]{1,0:T(8,128)(2,1)S(1)}, u32[]{:S(2)}, u32[]{:S(2)}) collective-permute-start(bf16[512,768]{1,0:T(8,128)(2,1)} %collective-permute-done.2.refs_3_), channel_id=1, source_target_pairs={{8,0},{16,24},{9,1},{17,25},{10,2},{18,26},{11,3},{19,27},{12,4},{... | collective-permute-start | bytes 2359304 | tf_op jit(solution)/shard_map/ppermute | solution.py:197
  344.9 94.3 %collective-permute-start.5 = (bf16[1024,768]{1,0:T(8,128)(2,1)}, bf16[1024,768]{1,0:T(8,128)(2,1)}, u32[]{:S(2)}, u32[]{:S(2)}) collective-permute-start(bf16[1024,768]{1,0:T(8,128)(2,1)} %constant_dynamic-slice_fusion.4), channel_id=1, source_target_pairs={{0,8},{24,16},{1,9},{25,17},{2,10},{26,18},{3,11},{27,19},{4,12},{... | collective-permute-start | bytes 4718600 | tf_op jit(solution)/shard_map/ppermute | solution.py:819
  395.1 187.2 %collective-permute-start.6 = (bf16[1024,1536]{1,0:T(8,128)(2,1)}, bf16[1024,1536]{1,0:T(8,128)(2,1)}, u32[]{:S(2)}, u32[]{:S(2)}) collective-permute-start(bf16[1024,1536]{1,0:T(8,128)(2,1)} %constant_dynamic-slice_fusion.3), channel_id=1, source_target_pairs={{0,8},{24,16},{1,9},{25,17},{2,10},{26,18},{3,11},{27,19},{4,12},{... | collective-permute-start | bytes 9437192 | tf_op jit(solution)/shard_map/ppermute | solution.py:819
  400.5 38.7 %copy-start.4 = (bf16[2048,768]{1,0:T(8,128)(2,1)S(1)}, bf16[2048,768]{1,0:T(8,128)(2,1)}, u32[]{:S(2)}) copy-start(bf16[2048,768]{1,0:T(8,128)(2,1)} %get-tuple-element.106) | copy-start | bytes 9437188
  442.2 148.3 %collective-permute-start.7 = (bf16[1024,768]{1,0:T(8,128)(2,1)}, bf16[1024,768]{1,0:T(8,128)(2,1)}, u32[]{:S(2)}, u32[]{:S(2)}) collective-permute-start(bf16[1024,768]{1,0:T(8,128)(2,1)} %add_convert_fusion.6), channel_id=1, source_target_pairs={{8,16},{16,8},{9,17},{17,9},{10,18},{18,10},{11,19},{19,11},{12,20... | collective-permute-start | bytes 4718600 | tf_op jit(solution)/shard_map/ppermute | solution.py:833
  501.9 244.6 %collective-permute-start.8 = (bf16[1024,1536]{1,0:T(8,128)(2,1)}, bf16[1024,1536]{1,0:T(8,128)(2,1)}, u32[]{:S(2)}, u32[]{:S(2)}) collective-permute-start(bf16[1024,1536]{1,0:T(8,128)(2,1)} %constant_dynamic-slice_fusion.2), channel_id=1, source_target_pairs={{0,8},{24,16},{1,9},{25,17},{2,10},{26,18},{3,11},{27,19},{4,12},{... | collective-permute-start | bytes 9437192 | tf_op jit(solution)/shard_map/ppermute | solution.py:819
  587.7 166.7 %collective-permute-start.9 = (bf16[1024,1536]{1,0:T(8,128)(2,1)}, bf16[1024,1536]{1,0:T(8,128)(2,1)}, u32[]{:S(2)}, u32[]{:S(2)}) collective-permute-start(bf16[1024,1536]{1,0:T(8,128)(2,1)} %add_convert_fusion.2), channel_id=1, source_target_pairs={{8,16},{16,8},{9,17},{17,9},{10,18},{18,10},{11,19},{19,11},{12,20... | collective-permute-start | bytes 9437192 | tf_op jit(solution)/shard_map/ppermute | solution.py:833
  592.6 151.0 %collective-permute-start.14 = (bf16[512,768]{1,0:T(8,128)(2,1)}, bf16[512,768]{1,0:T(8,128)(2,1)}, u32[]{:S(2)}, u32[]{:S(2)}) collective-permute-start(bf16[512,768]{1,0:T(8,128)(2,1)} %add_convert_fusion.8), channel_id=1, source_target_pairs={{0,8},{8,0},{16,24},{24,16},{1,9},{9,1},{17,25},{25,17},{2,10},{10... | collective-permute-start | bytes 2359304 | tf_op jit(solution)/shard_map/ppermute | solution.py:841
  640.2 175.7 %collective-permute-start.10 = (bf16[1024,1536]{1,0:T(8,128)(2,1)}, bf16[1024,1536]{1,0:T(8,128)(2,1)}, u32[]{:S(2)}, u32[]{:S(2)}) collective-permute-start(bf16[1024,1536]{1,0:T(8,128)(2,1)} %constant_dynamic-slice_fusion.1), channel_id=1, source_target_pairs={{0,8},{24,16},{1,9},{25,17},{2,10},{26,18},{3,11},{27,19},{4,12},{... | collective-permute-start | bytes 9437192 | tf_op jit(solution)/shard_map/ppermute | solution.py:819
  751.9 70.3 %collective-permute-start.11 = (bf16[1024,1536]{1,0:T(8,128)(2,1)}, bf16[1024,1536]{1,0:T(8,128)(2,1)}, u32[]{:S(2)}, u32[]{:S(2)}) collective-permute-start(bf16[1024,1536]{1,0:T(8,128)(2,1)} %add_convert_fusion.1), channel_id=1, source_target_pairs={{8,16},{16,8},{9,17},{17,9},{10,18},{18,10},{11,19},{19,11},{12,20... | collective-permute-start | bytes 9437192 | tf_op jit(solution)/shard_map/ppermute | solution.py:833
  757.8 217.8 %collective-permute-start.15 = (bf16[512,1536]{1,0:T(8,128)(2,1)}, bf16[512,1536]{1,0:T(8,128)(2,1)}, u32[]{:S(2)}, u32[]{:S(2)}) collective-permute-start(bf16[512,1536]{1,0:T(8,128)(2,1)} %add_convert_fusion.5), channel_id=1, source_target_pairs={{0,8},{8,0},{16,24},{24,16},{1,9},{9,1},{17,25},{25,17},{2,10},{10... | collective-permute-start | bytes 4718600 | tf_op jit(solution)/shard_map/ppermute | solution.py:841
  760.0 37.0 %copy-start.9 = (f32[2048,2]{1,0:T(8,128)S(1)}, f32[2048,2]{1,0:T(8,128)}, u32[]{:S(2)}) copy-start(f32[2048,2]{1,0:T(8,128)} %get-tuple-element.158) | copy-start | bytes 49156
  760.0 37.0 %copy-start.10 = (f32[2048,2]{1,0:T(8,128)S(1)}, f32[2048,2]{1,0:T(8,128)}, u32[]{:S(2)}) copy-start(f32[2048,2]{1,0:T(8,128)} %get-tuple-element.116) | copy-start | bytes 49156
  760.0 37.0 %copy-start.11 = (f32[2048,2]{1,0:T(8,128)S(1)}, f32[2048,2]{1,0:T(8,128)}, u32[]{:S(2)}) copy-start(f32[2048,2]{1,0:T(8,128)} %get-tuple-element.122) | copy-start | bytes 49156
  821.3 168.7 %collective-permute-start.12 = (bf16[1024,1536]{1,0:T(8,128)(2,1)}, bf16[1024,1536]{1,0:T(8,128)(2,1)S(1)}, u32[]{:S(2)}, u32[]{:S(2)}) collective-permute-start(bf16[1024,1536]{1,0:T(8,128)(2,1)} %add_convert_fusion), channel_id=1, source_target_pairs={{8,16},{16,8},{9,17},{17,9},{10,18},{18,10},{11,19},{19,11},{12,20... | collective-permute-start | bytes 9437192 | tf_op jit(solution)/shard_map/ppermute | solution.py:833
  825.6 312.2 %collective-permute-start.16 = (bf16[512,1536]{1,0:T(8,128)(2,1)}, bf16[512,1536]{1,0:T(8,128)(2,1)}, u32[]{:S(2)}, u32[]{:S(2)}) collective-permute-start(bf16[512,1536]{1,0:T(8,128)(2,1)} %add_convert_fusion.4), channel_id=1, source_target_pairs={{0,8},{8,0},{16,24},{24,16},{1,9},{9,1},{17,25},{25,17},{2,10},{10... | collective-permute-start | bytes 4718600 | tf_op jit(solution)/shard_map/ppermute | solution.py:841
  957.5 233.4 %reduce-scatter.3.cloned.1.call-start = ((), (), s32[]{:S(2)}) async-start(), calls=%async_computation.4 | async-start | bytes 9437184 | tf_op jit(solution)/shard_map/reduce_scatter | solution.py:1344
  990.0 32.7 %copy-start.18 = (bf16[1024,1536]{1,0:T(8,128)(2,1)}, bf16[1024,1536]{1,0:T(8,128)(2,1)S(1)}, u32[]{:S(2)}) copy-start(bf16[1024,1536]{1,0:T(8,128)(2,1)S(1)} %collective-permute-done.12) | copy-start | bytes 9437188
  994.4 186.1 %collective-permute-start.13 = (bf16[512,1536]{1,0:T(8,128)(2,1)}, bf16[512,1536]{1,0:T(8,128)(2,1)}, u32[]{:S(2)}, u32[]{:S(2)}) collective-permute-start(bf16[512,1536]{1,0:T(8,128)(2,1)} %add_convert_fusion.3), channel_id=1, source_target_pairs={{0,8},{8,0},{16,24},{24,16},{1,9},{9,1},{17,25},{25,17},{2,10},{10... | collective-permute-start | bytes 4718600 | tf_op jit(solution)/shard_map/ppermute | solution.py:841
  994.4 28.3 %copy-start.46 = (f32[2048]{0:T(1024)S(1)}, f32[2048]{0:T(1024)}, u32[]{:S(2)}) copy-start(f32[2048]{0:T(1024)} %copy-done.45) | copy-start | bytes 24580
  994.4 28.3 %copy-start.51 = (f32[1,2048]{1,0:T(1,128)S(1)}, f32[1,2048]{1,0:T(1,128)}, u32[]{:S(2)}) copy-start(f32[1,2048]{1,0:T(1,128)} %copy-done.50) | copy-start | bytes 24580
  (58 other events, 385.1 us)
Sparse Core Ops, SparseCore 0:
  9.9 58.6 all-gather.4
  70.5 55.9 all-gather.6
  957.6 18.5 reduce-scatter.4
  979.9 69.4 reduce-scatter.2

commit v12 on v11

--- a/solution.py
+++ b/solution.py
@@ -1269,41 +1269,35 @@
         wholes.append(whole)
         now = (sums,)
         waits = ()
-        early = ()
-        if planar and at == 1:
+        if at < last or not planar:
+            reduced.append(Reduced(grads))
+        if planar and at == 0:
+            waits = (reduced[0].pair,)
+        elif planar and at == 1:
+            first_pair = after(dpairs[0], reduced[0].second(now), (reduced[1].pair,))
             dscaled_early, last_piece = joint_back(
-                dpairs, wholes, 0, f32, hop=(3, carried[2:3]), number=9
+                [first_pair, dpair], wholes, 0, f32, hop=(3, carried[2:3]), number=9
             )
             gathered[2] = (packs[2], *carried[:2], carried[2], carried[3], last_piece)
-            early = (dscaled_early,)
+            waits = (dscaled_early,)
         elif planar and at == 2:
-            rest = hop_now((23, [after(carried[0], now), carried[1]]), 10)
+            rest = hop_now((23, [after(carried[0], now, (reduced[2].pair,)), carried[1]]), 10)
             gathered[3] = (packs[3], *carried, *rest)
-            early = (rest[2],)
+            waits = (rest[2],)
         elif planar and at == 3:
+            third_pair = after(dpairs[2], (reduced[3].pair,))
             dscaled_early, *next_pieces = joint_back(
-                dpairs[2:], wholes[2:], 0, f32, dscaled_early, hop=(2, carried), number=11
+                [third_pair, dpair], wholes[2:], 0, f32, dscaled_early, hop=(2, carried), number=11
             )
+            first_hidden = after(hiddens[0], reduced[1].second((dscaled_early,)))
             moe_early, last_piece = joint_back(
-                hiddens, wholes, 2, f32, hop=(3, next_pieces[:1]), number=12
+                [first_hidden] + hiddens[1:], wholes, 2, f32, hop=(3, next_pieces[:1]), number=12
             )
             gathered[4] = (packs[4], *carried, *next_pieces, last_piece)
-            early = (dscaled_early, moe_early)
-            now = early
-        waits += early
-        if not planar:
-            reduced.append(Reduced(grads))
-        elif at < last:
-            if at >= 1:
-                waits += reduced[at - 1].second(now)
-            if at >= 2:
-                waits += reduced[at - 2].third((sums,))
-            reduced.append(Reduced(grads))
-            waits += (reduced[at].pair,)
+            waits = (dscaled_early, moe_early)
     now = (sums,)
     if planar:
-        waits = reduced[3].second(now)
-        waits += reduced[2].third(now)
+        waits = reduced[2].second(now) + reduced[0].third(now) + reduced[1].third(now)
     else:
         waits = ()
         for one in reduced:
@@ -1346,11 +1340,13 @@
     out_part = mm_tn(dattn, context).astype(bf16)
     dcontext = mm(dattn, out_full).astype(bf16)
     if planar:
-        dcontext = after(dcontext, reduced[3].third((dattn,)))
+        dcontext = after(dcontext, reduced[3].second((dattn,)), reduced[2].third((dattn,)))
     router_left = after(jnp.concatenate(parts, axis=1), (dattn,))
     grad_router_part = mm_tn(router_left, scaled).reshape(3, experts + 1, width).sum(axis=0)
     grad_router_both = lax.psum_scatter(grad_router_part, "row", scatter_dimension=1, tiled=True)
     dqkv, inner_a = attend_backward(qkv, dcontext, lse, lengths, cosine, sine)
+    if planar:
+        dqkv = after(dqkv, reduced[3].third((inner_a,)))
     inner_a = lax.psum(inner_a[:, 0], "col")[:, None]
     attn_grads = jnp.concatenate([mm_tn(normed_a, dqkv).astype(bf16), out_part], axis=1)
     if planar:

time: 1220 us -> 1190 us (0.975)
  starting transfers between devices: 96.8 us -> 43.3 us
  waiting for transfers between devices: 1.48 us -> 18.4 us
    ppermute x4, starting transfers between devices: 74.2 us -> 21.4 us  [__init__(): self.first = lax.ppermute(self.pair, 'row', INWARD)]
    ppermute x4, waiting for transfers between devices: 0.01 us -> 16.9 us  [third(): self.swapped = lax.ppermute(value, 'row', PAIRS)]
    unnamed x147 -> x149, local copies, waits for them, and re-layouts: 27.1 us -> 27.7 us
  transfers between devices with their start and end apart: 21 -> 21, of which waited for: 0 -> 1; matrix products, arithmetic and copies ran while one was open for 17% -> 17% of each run, Pallas kernels for 66% -> 69%
where the time goes in v12:
time: 1190 us; the launch traced here: 1180 us
  Pallas kernels  846 us (71%)
  other arithmetic  91.5 us (8%)
  local copies, waits for them, and re-layouts  82 us (7%)
  starting transfers between devices  43.3 us (4%)
  matrix products  41.1 us (3%)
  blocking collectives  40.2 us (3%)
  waiting for transfers between devices  18.4 us (2%)
  between operations  15.2 us (1%)
    pallas_call x3, Pallas kernels, plane_step(): pl.pallas_call(functools.partial(plane_kernel, pointwise, len(inputs), ma...  300 us
    pallas_call x5, Pallas kernels, expert_chunk(): pl.pallas_call(functools.partial(expert_kernel, size, steps, count, hop a...  209 us
    pallas_call x7, Pallas kernels, joint_back(): pl.pallas_call(functools.partial(joint_kernel, len(lefts), len(base), pla...  147 us
    pallas_call x1, Pallas kernels, gather_now(): pl.pallas_call(functools.partial(gather_kernel, count), in_specs=[anywher...  82.9 us
    pallas_call x1, Pallas kernels, hop_now(): pl.pallas_call(functools.partial(hop_kernel, hop[0]), in_specs=[anywhere]...  66 us
    pallas_call x1, Pallas kernels, attend_backward(): pl.pallas_call(attend_backward_kernel, grid_spec=pltpu.PrefetchScalarGrid...  28.9 us
    unnamed x149, local copies, waits for them, and re-layouts  27.7 us
  transfers between devices with their start and end apart: 21, of which 1 were waited for; matrix products, arithmetic and copies ran while one was open for 17% of the time, Pallas kernels for 69%

profile of v12, /device:TPU:0, one launch (start us, length us, event | category | flops | bytes accessed | tf_op | source)
XLA Modules:
  0.0 1177.6 jit_solution(10180200907077466154)
XLA Ops:
  25.1 82.9 %gather_rows.1 = (bf16[4,512,768]{2,1,0:T(8,128)(2,1)}, bf16[4,512,384]{2,1,0:T(8,128)(2,1)}) custom-call(bf16[512,768]{1,0:T(8,128)(2,1)} %copy.135.refs_0_, bf16[512,384]{1,0:T(8,128)(2,1)} %fusion.18.refs_1_), custom_call_target="tpu_custom_call" | custom-call | flops 63700992000 | bytes 7077888 | tf_op jit(solution)/shard_map/gather_rows/pallas_call | solution.py:786
  127.3 9.1 all_gather.16
  147.1 10.5 fusion.4.raw_ref
  157.5 12.7 %attend_forward.1 = (bf16[2048,768]{1,0:T(8,128)(2,1)}, bf16[2048,256]{1,0:T(8,128)(2,1)}, f32[2048,256]{1,0:T(8,128)}) custom-call(s32[2]{0:T(128)} %dynamic_slice.70.length_ref, f32[2048,768]{1,0:T(8,128)} %fusion.4.raw_ref, f32[1024,128]{1,0:T(8,128)} %get-tuple-element.297.cos_ref, f32[1024,128]{1,0:T(8,128)} %get-tuple-element.298.sin_ref), custom_call_target="tpu_custom_call" | custom-call | flops 1610612736 | bytes 12582912 | tf_op jit(solution)/shard_map/attend_forward/pallas_call | solution.py:81
  170.2 8.7 joint_back.7.refs_0_
  178.9 113.2 %plane_step.3 = (f32[2048,256]{1,0:T(8,128)}, bf16[2048,2048]{1,0:T(8,128)(2,1)}, bf16[4,512,1536]{2,1,0:T(8,128)(2,1)}) custom-call(bf16[2,2,2,2048,256]{4,3,2,1,0:T(8,128)(2,1)} %joint_back.7.refs_0_, bf16[2048,256]{1,0:T(8,128)(2,1)} %refs_1_.1, f32[1,256]{1,0:T(1,128)} %reshape_convert_fusion.refs_2_.refs_5_, ...), custom_call_target="tpu_custom_call" | custom-call | flops 60000002048 | bytes 16777216 | tf_op jit(solution)/shard_map/plane_step/pallas_call | solution.py:751
  292.2 5.8 multiply_reduce_fusion
  304.3 37.8 %expert_chunk.5 = (bf16[2048,512]{1,0:T(8,128)(2,1)}, bf16[2048,256]{1,0:T(8,128)(2,1)}, f32[2048,2]{1,0:T(8,128)}, bf16[2048,768]{1,0:T(8,128)(2,1)}, bf16[2048...) custom-call(bf16[512,768]{1,0:T(8,128)(2,1)} %fusion.16.refs_0_, ...), custom_call_target="tpu_custom_call" | custom-call | flops 12884901888 | bytes 46137344 | tf_op jit(solution)/shard_map/expert_chunk/pallas_call | solution.py:987
  350.7 40.6 %expert_chunk.6 = (bf16[2048,1024]{1,0:T(8,128)(2,1)}, bf16[2048,512]{1,0:T(8,128)(2,1)}, f32[2048,2]{1,0:T(8,128)}, bf16[2048,1536]{1,0:T(8,128)(2,1)}, bf16[20...) custom-call(bf16[512,1536]{1,0:T(8,128)(2,1)} %get-tuple-element.295.refs_3_.refs_0_, ...), custom_call_target="tpu_custom_call" | custom-call | flops 25769803776 | bytes 58720256 | tf_op jit(solution)/shard_map/expert_chunk/pallas_call | solution.py:987
  395.1 5.5 collective-permute-start.6
  406.8 37.2 %joint_back.8 = (f32[2048,2048]{1,0:T(8,128)}, bf16[512,1536]{1,0:T(8,128)(2,1)}) custom-call(bf16[2048,512]{1,0:T(8,128)(2,1)} %get-tuple-element.118.refs_0_, bf16[2048,1024]{1,0:T(8,128)(2,1)} %get-tuple-element.119.refs_1_, bf16[2048,768]{1,0:T(8,128)(2,1)} %get-tuple-element.120.refs_2_.refs_4_, bf16[2048,1536]{1,0:T(8,128)(2,1)} %get-tuple-element.121.refs_3_.refs_5_, ...), custom_call_target="tpu_custom_call" | custom-call | flops 12884901888 | bytes 29360128 | tf_op jit(solution)/shard_map/joint_back/pallas_call | solution.py:1073
  445.4 52.7 %expert_chunk.7 = (bf16[2048,1024]{1,0:T(8,128)(2,1)}, bf16[2048,512]{1,0:T(8,128)(2,1)}, f32[2048,2]{1,0:T(8,128)}, bf16[2048,1536]{1,0:T(8,128)(2,1)}, bf16[20...) custom-call(bf16[512,1536]{1,0:T(8,128)(2,1)} %get-tuple-element.296.refs_11_.refs_0_, ...), custom_call_target="tpu_custom_call" | custom-call | flops 25769803776 | bytes 58720256 | tf_op jit(solution)/shard_map/expert_chunk/pallas_call | solution.py:987
  501.9 6.0 collective-permute-start.7
  507.9 66.0 %gather_hops.1 = (bf16[512,1536]{1,0:T(8,128)(2,1)}, bf16[512,1536]{1,0:T(8,128)(2,1)}, bf16[512,1536]{1,0:T(8,128)(2,1)}) custom-call(bf16[512,1536]{1,0:T(8,128)(2,1)} %get-tuple-element.129.refs_0_.refs_1_, bf16[512,1536]{1,0:T(8,128)(2,1)} %get-tuple-element.126.refs_1_.refs_2_), custom_call_target="tpu_custom_call" | custom-call | tf_op jit(solution)/shard_map/gather_hops/pallas_call | solution.py:515
  575.3 40.5 %expert_chunk.8 = (bf16[2048,1024]{1,0:T(8,128)(2,1)}, bf16[2048,512]{1,0:T(8,128)(2,1)}, f32[2048,2]{1,0:T(8,128)}, bf16[2048,1536]{1,0:T(8,128)(2,1)}, bf16[20...) custom-call(bf16[512,1536]{1,0:T(8,128)(2,1)} %pad_maximum_fusion.2.refs_11_.refs_0_, ...), custom_call_target="tpu_custom_call" | custom-call | flops 25769803776 | bytes 58720256 | tf_op jit(solution)/shard_map/expert_chunk/pallas_call | solution.py:987
  625.0 30.1 %joint_back.9 = (f32[2048,2048]{1,0:T(8,128)}, bf16[512,1152]{1,0:T(8,128)(2,1)}, bf16[512,1152]{1,0:T(8,128)(2,1)}) custom-call(bf16[2048,1024]{1,0:T(8,128)(2,1)} %get-tuple-element.138.refs_0_, bf16[2048,1024]{1,0:T(8,128)(2,1)} %get-tuple-element.139.refs_1_, bf16[2048,1536]{1,0:T(8,128)(2,1)} %get-tuple-element.140.refs_2_.refs_6_, ...), custom_call_target="tpu_custom_call" | custom-call | flops 17179869184 | bytes 33554432 | tf_op jit(solution)/shard_map/joint_back/pallas_call | solution.py:1073
  662.9 29.1 %joint_back.10 = (f32[2048,2048]{1,0:T(8,128)}, bf16[512,1152]{1,0:T(8,128)(2,1)}) custom-call(bf16[2048,256]{1,0:T(8,128)(2,1)} %get-tuple-element.147.refs_0_, bf16[2048,512]{1,0:T(8,128)(2,1)} %get-tuple-element.148.refs_1_, bf16[2048,512]{1,0:T(8,128)(2,1)} %get-tuple-element.149.refs_2_, bf16[2048,512]{1,0:T(8,128)(2,1)} %get-tuple-element.150.refs_3_, ...), custom_call_target="tpu_custom_call" | custom-call | flops 15032385536 | bytes 31457280 | tf_op jit(solution)/shard_map/joint_back/pallas_call | solution.py:1073
  693.4 37.0 %expert_chunk.9 = (bf16[2048,768]{1,0:T(8,128)(2,1)}, bf16[2048,384]{1,0:T(8,128)(2,1)}, f32[2048,2]{1,0:T(8,128)}, bf16[2048,1152]{1,0:T(8,128)(2,1)}, bf16[2048,1152]{1,0:T(8,128)(2,1)}) custom-call(bf16[512,1152]{1,0:T(8,128)(2,1)} %pad_maximum_fusion.7.refs_11_.refs_0_, bf16[512,1152]{1,0:T(8,128)(2,1)} %get-tuple-element.134.refs_5_.refs_1_, ...), custom_call_target="tpu_custom_call" | custom-call | flops 19327352832 | bytes 52428800 | tf_op jit(solution)/shard_map/expert_chunk/pallas_call | solution.py:987
  735.2 9.1 all-gather.1
  750.8 16.9 %collective-permute-done.14 = bf16[512,768]{1,0:T(8,128)(2,1)S(1)} collective-permute-done((bf16[512,768]{1,0:T(8,128)(2,1)S(1)}, bf16[512,768]{1,0:T(8,128)(2,1)S(1)}, u32[]{:S(2)}, u32[]{:S(2)}) %collective-permute-start.14) | collective-permute-done | bytes 786464 | tf_op jit(solution)/shard_map/ppermute | solution.py:841
  781.7 15.7 %joint_back.11.refs_0_ = bf16[2,2,2,2048,256]{4,3,2,1,0:T(8,128)(2,1)} custom-call(bf16[2048,768]{1,0:T(8,128)(2,1)} %get-tuple-element.160.refs_0_, bf16[2048,1152]{1,0:T(8,128)(2,1)} %get-tuple-element.161.refs_1_, f32[2048,2048]{1,0:T(8,128)} %get-tuple-element.145.refs_2_), custom_call_target="tpu_custom_call" | custom-call | flops 6442450944 | bytes 23068672 | tf_op jit(solution)/shard_map/joint_back/pallas_call | solution.py:1073
  797.4 104.5 %plane_step.4 = (f32[2048,256]{1,0:T(8,128)}, f32[2048,256]{1,0:T(8,128)}, f32[512,1152]{1,0:T(8,128)}, bf16[2048,2048]{1,0:T(8,128)(2,1)}) custom-call(bf16[2,2,2,2048,256]{4,3,2,1,0:T(8,128)(2,1)} %joint_back.11.refs_0_, f32[2048,256]{1,0:T(8,128)} %fusion.27.refs_1_, bf16[2048,256]{1,0:T(8,128)(2,1)} %refs_2_.1, f32[2048,256]{1,0:T(8,128)} %get-tuple-element.105.refs_3_, ...), custom_call_target="tpu_custom_call" | custom-call | flops 60000002048 | bytes 16777216 | tf_op jit(solution)/shard_map/plane_step/pallas_call | solution.py:751
  915.8 6.8 convolution_convert_fusion.2.dcontext_ref
  922.6 5.8 convolution_convert_fusion.1
  928.4 14.4 %joint_back.12 = bf16[2048,2048]{1,0:T(8,128)(2,1)} custom-call(bf16[2048,384]{1,0:T(8,128)(2,1)} %get-tuple-element.166.refs_0_, bf16[2048,1152]{1,0:T(8,128)(2,1)} %get-tuple-element.161.refs_1_, f32[2048,2048]{1,0:T(8,128)} %get-tuple-element.152.refs_2_), custom_call_target="tpu_custom_call" | custom-call | flops 3221225472 | bytes 19922944 | tf_op jit(solution)/shard_map/joint_back/pallas_call | solution.py:1073
  952.6 28.9 %attend_backward.1 = (bf16[2048,768]{1,0:T(8,128)(2,1)}, f32[2048,1]{1,0:T(8,128)}) custom-call(s32[2]{0:T(128)} %dynamic_slice.70.length_ref, bf16[2048,768]{1,0:T(8,128)(2,1)} %get-tuple-element.168.qkv_ref, bf16[2048,256]{1,0:T(8,128)(2,1)} %convolution_convert_fusion.2.dcontext_ref, f32[2048,256]{1,0:T(8,128)} %get-tuple-element.172.lse_ref, ...), custom_call_target="tpu_custom_call" | custom-call | flops 4294967296 | bytes 12582912 | tf_op jit(solution)/shard_map/attend_backward/pallas_call | solution.py:151
  983.1 12.6 %psum.21 = f32[2048]{0:T(1024)S(1)} all-reduce(f32[2048]{0:T(1024)S(1)} %reduce.5), channel_id=1, replica_groups=mesh['row'=4,'col'=8] {'col'}, use_global_device_ids=true, to_apply=%region_10.11 | all-reduce | flops 2048 | bytes 16384 | tf_op jit(solution)/shard_map/psum | solution.py:1350
  1007.1 8.0 convolution_convert_fusion
  1017.4 6.4 copy.157
  1023.8 12.1 %joint_back.13.refs_0_ = bf16[2,2,2,2048,256]{4,3,2,1,0:T(8,128)(2,1)} custom-call(bf16[2048,768]{1,0:T(8,128)(2,1)} %get-tuple-element.176.refs_0_, bf16[2048,768]{1,0:T(8,128)(2,1)} %constant_dynamic-update-slice_fusion.1.refs_1_), custom_call_target="tpu_custom_call" | custom-call | flops 6442450944 | bytes 23068672 | tf_op jit(solution)/shard_map/joint_back/pallas_call | solution.py:1073
  1035.8 81.8 %plane_step.5 = (f32[2048,256]{1,0:T(8,128)}, f32[512,1024]{1,0:T(8,128)}) custom-call(bf16[2,2,2,2048,256]{4,3,2,1,0:T(8,128)(2,1)} %joint_back.13.refs_0_, bf16[4,512,1024]{2,1,0:T(8,128)(2,1)} %bitcast.91), custom_call_target="tpu_custom_call" | custom-call | flops 60000002048 | bytes 16777216 | tf_op jit(solution)/shard_map/plane_step/pallas_call | solution.py:751
  1161.3 9.5 all-reduce.4
  (312 shorter events, 204.6 us)
Async XLA Ops:
  7.2 118.9 %copy-start = (s32[8]{0:T(128)S(1)}, s32[8]{0:T(128)}, u32[]{:S(2)}) copy-start(s32[8]{0:T(128)} %param.20) | copy-start | bytes 100
  7.2 134.1 %all-gather.5.cloned.1.call-start = ((), (), s32[]{:S(2)}) async-start(), calls=%async_computation.2 | async-start | bytes 9437184 | tf_op jit(solution)/shard_map/all_gather | solution.py:1197
  8.0 171.0 %all-gather.7.cloned.1.call-start = ((), (), s32[]{:S(2)}) async-start(), calls=%async_computation.3 | async-start | bytes 9437184 | tf_op jit(solution)/shard_map/all_gather | solution.py:1199
  8.7 937.2 %reduce-scatter.5.cloned.1.call-start = ((), (), s32[]{:S(2)}) async-start(), calls=%async_computation.5 | async-start | bytes 163840 | tf_op jit(solution)/shard_map/reduce_scatter | solution.py:1346
  11.2 109.6 %collective-permute-start = (bf16[512,768]{1,0:T(8,128)(2,1)}, bf16[512,768]{1,0:T(8,128)(2,1)}, u32[]{:S(2)}, u32[]{:S(2)}) collective-permute-start(bf16[512,768]{1,0:T(8,128)(2,1)} %fusion.16.refs_0_), channel_id=1, source_target_pairs={{0,8},{8,0},{16,24},{24,16},{1,9},{9,1},{17,25},{25,17},{2,10},{10... | collective-permute-start | bytes 2359304 | tf_op jit(solution)/shard_map/ppermute | solution.py:184
  14.2 123.9 %collective-permute-start.1 = (bf16[512,768]{1,0:T(8,128)(2,1)}, bf16[512,768]{1,0:T(8,128)(2,1)}, u32[]{:S(2)}, u32[]{:S(2)}) collective-permute-start(bf16[512,768]{1,0:T(8,128)(2,1)} %fusion.16.refs_0_), channel_id=1, source_target_pairs={{8,16},{16,8},{9,17},{17,9},{10,18},{18,10},{11,19},{19,11},{12,20... | collective-permute-start | bytes 2359304 | tf_op jit(solution)/shard_map/ppermute | solution.py:185
  25.1 85.4 %copy-start.56 = (s32[8]{0:T(128)S(1)}, s32[8]{0:T(128)}, u32[]{:S(2)}) copy-start(s32[8]{0:T(128)} %param.21) | copy-start | bytes 100
  25.1 86.9 %copy-start.17 = (bf16[512,768]{1,0:T(8,128)(2,1)S(1)}, bf16[512,768]{1,0:T(8,128)(2,1)}, u32[]{:S(2)}) copy-start(bf16[512,768]{1,0:T(8,128)(2,1)} %copy.135.refs_0_) | copy-start | bytes 2359300
  111.4 190.1 %copy-start.45 = (pred[2048]{0:T(1024)(128)(4,1)}, pred[2048]{0:T(1024)(128)(4,1)S(1)}, u32[]{:S(2)}) copy-start(pred[2048]{0:T(1024)(128)(4,1)S(1)} %compare_reduce_fusion) | copy-start | bytes 6148
  120.8 18.6 %collective-permute-start.2 = (bf16[512,768]{1,0:T(8,128)(2,1)}, bf16[512,768]{1,0:T(8,128)(2,1)}, u32[]{:S(2)}, u32[]{:S(2)}) collective-permute-start(bf16[512,768]{1,0:T(8,128)(2,1)} %collective-permute-done.refs_1_), channel_id=1, source_target_pairs={{8,16},{16,8},{9,17},{17,9},{10,18},{18,10},{11,19},{19,11},{12,20... | collective-permute-start | bytes 2359304 | tf_op jit(solution)/shard_map/ppermute | solution.py:191
  138.1 32.1 %collective-permute-start.3 = (bf16[512,768]{1,0:T(8,128)(2,1)}, bf16[512,768]{1,0:T(8,128)(2,1)S(1)}, u32[]{:S(2)}, u32[]{:S(2)}) collective-permute-start(bf16[512,768]{1,0:T(8,128)(2,1)} %collective-permute-done.1.refs_2_), channel_id=1, source_target_pairs={{8,0},{16,24},{9,1},{17,25},{10,2},{18,26},{11,3},{19,27},{12,4},{... | collective-permute-start | bytes 2359304 | tf_op jit(solution)/shard_map/ppermute | solution.py:190
  139.4 164.0 %collective-permute-start.4 = (bf16[512,768]{1,0:T(8,128)(2,1)}, bf16[512,768]{1,0:T(8,128)(2,1)S(1)}, u32[]{:S(2)}, u32[]{:S(2)}) collective-permute-start(bf16[512,768]{1,0:T(8,128)(2,1)} %collective-permute-done.2.refs_3_), channel_id=1, source_target_pairs={{8,0},{16,24},{9,1},{17,25},{10,2},{18,26},{11,3},{19,27},{12,4},{... | collective-permute-start | bytes 2359304 | tf_op jit(solution)/shard_map/ppermute | solution.py:197
  344.8 57.1 %collective-permute-start.5 = (bf16[1024,768]{1,0:T(8,128)(2,1)}, bf16[1024,768]{1,0:T(8,128)(2,1)}, u32[]{:S(2)}, u32[]{:S(2)}) collective-permute-start(bf16[1024,768]{1,0:T(8,128)(2,1)} %constant_dynamic-slice_fusion.4), channel_id=1, source_target_pairs={{0,8},{24,16},{1,9},{25,17},{2,10},{26,18},{3,11},{27,19},{4,12},{... | collective-permute-start | bytes 4718600 | tf_op jit(solution)/shard_map/ppermute | solution.py:819
  395.1 260.0 %collective-permute-start.6 = (bf16[1024,1536]{1,0:T(8,128)(2,1)}, bf16[1024,1536]{1,0:T(8,128)(2,1)}, u32[]{:S(2)}, u32[]{:S(2)}) collective-permute-start(bf16[1024,1536]{1,0:T(8,128)(2,1)} %constant_dynamic-slice_fusion.3), channel_id=1, source_target_pairs={{0,8},{24,16},{1,9},{25,17},{2,10},{26,18},{3,11},{27,19},{4,12},{... | collective-permute-start | bytes 9437192 | tf_op jit(solution)/shard_map/ppermute | solution.py:819
  405.0 341.1 %collective-permute-start.8 = (bf16[1024,768]{1,0:T(8,128)(2,1)}, bf16[1024,768]{1,0:T(8,128)(2,1)}, u32[]{:S(2)}, u32[]{:S(2)}) collective-permute-start(bf16[1024,768]{1,0:T(8,128)(2,1)} %add_convert_fusion.6), channel_id=1, source_target_pairs={{8,16},{16,8},{9,17},{17,9},{10,18},{18,10},{11,19},{19,11},{12,20... | collective-permute-start | bytes 4718600 | tf_op jit(solution)/shard_map/ppermute | solution.py:833
  501.9 268.6 %collective-permute-start.7 = (bf16[1024,1536]{1,0:T(8,128)(2,1)}, bf16[1024,1536]{1,0:T(8,128)(2,1)}, u32[]{:S(2)}, u32[]{:S(2)}) collective-permute-start(bf16[1024,1536]{1,0:T(8,128)(2,1)} %constant_dynamic-slice_fusion.2), channel_id=1, source_target_pairs={{0,8},{24,16},{1,9},{25,17},{2,10},{26,18},{3,11},{27,19},{4,12},{... | collective-permute-start | bytes 9437192 | tf_op jit(solution)/shard_map/ppermute | solution.py:819
  619.6 282.3 %collective-permute-start.10 = (bf16[1024,1536]{1,0:T(8,128)(2,1)}, bf16[1024,1536]{1,0:T(8,128)(2,1)}, u32[]{:S(2)}, u32[]{:S(2)}) collective-permute-start(bf16[1024,1536]{1,0:T(8,128)(2,1)} %constant_dynamic-slice_fusion.1), channel_id=1, source_target_pairs={{0,8},{24,16},{1,9},{25,17},{2,10},{26,18},{3,11},{27,19},{4,12},{... | collective-permute-start | bytes 9437192 | tf_op jit(solution)/shard_map/ppermute | solution.py:819
  660.4 117.1 %collective-permute-start.9 = (bf16[1024,1536]{1,0:T(8,128)(2,1)}, bf16[1024,1536]{1,0:T(8,128)(2,1)}, u32[]{:S(2)}, u32[]{:S(2)}) collective-permute-start(bf16[1024,1536]{1,0:T(8,128)(2,1)} %add_convert_fusion.2), channel_id=1, source_target_pairs={{8,16},{16,8},{9,17},{17,9},{10,18},{18,10},{11,19},{19,11},{12,20... | collective-permute-start | bytes 9437192 | tf_op jit(solution)/shard_map/ppermute | solution.py:833
  693.4 37.0 %copy-start.9 = (f32[2048,2]{1,0:T(8,128)S(1)}, f32[2048,2]{1,0:T(8,128)}, u32[]{:S(2)}) copy-start(f32[2048,2]{1,0:T(8,128)} %get-tuple-element.162) | copy-start | bytes 49156
  693.4 37.0 %copy-start.10 = (f32[2048,2]{1,0:T(8,128)S(1)}, f32[2048,2]{1,0:T(8,128)}, u32[]{:S(2)}) copy-start(f32[2048,2]{1,0:T(8,128)} %get-tuple-element.115) | copy-start | bytes 49156
  693.4 37.0 %copy-start.11 = (f32[2048,2]{1,0:T(8,128)S(1)}, f32[2048,2]{1,0:T(8,128)}, u32[]{:S(2)}) copy-start(f32[2048,2]{1,0:T(8,128)} %get-tuple-element.127) | copy-start | bytes 49156
  730.4 14.2 %copy-start.32 = (f32[2048]{0:T(1024)S(1)}, f32[2048]{0:T(1024)}, u32[]{:S(2)}) copy-start(f32[2048]{0:T(1024)} %copy-done.31) | copy-start | bytes 24580
  744.7 25.8 %slice-start = ((s8[6291456]{0:T(1024)(128)(4,1)}), s8[2097152]{0:T(1024)(128)(4,1)S(1)}, s32[]{:S(2)}) async-start(s8[6291456]{0:T(1024)(128)(4,1)} %bitcast.85), calls=%async_computation.6 | async-start | bytes 4194304
  747.8 19.9 %collective-permute-start.14 = (bf16[512,768]{1,0:T(8,128)(2,1)S(1)}, bf16[512,768]{1,0:T(8,128)(2,1)S(1)}, u32[]{:S(2)}, u32[]{:S(2)}) collective-permute-start(bf16[512,768]{1,0:T(8,128)(2,1)S(1)} %add_convert_fusion.8), channel_id=1, source_target_pairs={{0,8},{8,0},{16,24},{24,16},{1,9},{9,1},{17,25},{25,17},{2,10},{10... | collective-permute-start | bytes 2359304 | tf_op jit(solution)/shard_map/ppermute | solution.py:841
  749.7 20.8 %slice-start.1 = ((s8[6291456]{0:T(1024)(128)(4,1)}), s8[4194304]{0:T(1024)(128)(4,1)S(1)}, s32[]{:S(2)}) async-start(s8[6291456]{0:T(1024)(128)(4,1)} %bitcast.85), calls=%async_computation.7 | async-start | bytes 8388608
  775.1 173.4 %collective-permute-start.11 = (bf16[1024,1536]{1,0:T(8,128)(2,1)}, bf16[1024,1536]{1,0:T(8,128)(2,1)}, u32[]{:S(2)}, u32[]{:S(2)}) collective-permute-start(bf16[1024,1536]{1,0:T(8,128)(2,1)} %add_convert_fusion.1), channel_id=1, source_target_pairs={{8,16},{16,8},{9,17},{17,9},{10,18},{18,10},{11,19},{19,11},{12,20... | collective-permute-start | bytes 9437192 | tf_op jit(solution)/shard_map/ppermute | solution.py:833
  781.0 214.8 %collective-permute-start.15 = (bf16[512,1536]{1,0:T(8,128)(2,1)}, bf16[512,1536]{1,0:T(8,128)(2,1)}, u32[]{:S(2)}, u32[]{:S(2)}) collective-permute-start(bf16[512,1536]{1,0:T(8,128)(2,1)} %add_convert_fusion.5), channel_id=1, source_target_pairs={{0,8},{8,0},{16,24},{24,16},{1,9},{9,1},{17,25},{25,17},{2,10},{10... | collective-permute-start | bytes 4718600 | tf_op jit(solution)/shard_map/ppermute | solution.py:841
  907.2 93.6 %collective-permute-start.12 = (bf16[1024,1536]{1,0:T(8,128)(2,1)}, bf16[1024,1536]{1,0:T(8,128)(2,1)}, u32[]{:S(2)}, u32[]{:S(2)}) collective-permute-start(bf16[1024,1536]{1,0:T(8,128)(2,1)} %add_convert_fusion), channel_id=1, source_target_pairs={{8,16},{16,8},{9,17},{17,9},{10,18},{18,10},{11,19},{19,11},{12,20... | collective-permute-start | bytes 9437192 | tf_op jit(solution)/shard_map/ppermute | solution.py:833
  915.3 242.1 %reduce-scatter.3.cloned.1.call-start = ((), (), s32[]{:S(2)}) async-start(), calls=%async_computation.4 | async-start | bytes 9437184 | tf_op jit(solution)/shard_map/reduce_scatter | solution.py:1338
  952.6 181.4 %collective-permute-start.16 = (bf16[512,1536]{1,0:T(8,128)(2,1)}, bf16[512,1536]{1,0:T(8,128)(2,1)}, u32[]{:S(2)}, u32[]{:S(2)}) collective-permute-start(bf16[512,1536]{1,0:T(8,128)(2,1)} %add_convert_fusion.4), channel_id=1, source_target_pairs={{0,8},{8,0},{16,24},{24,16},{1,9},{9,1},{17,25},{25,17},{2,10},{10... | collective-permute-start | bytes 4718600 | tf_op jit(solution)/shard_map/ppermute | solution.py:841
  952.6 43.1 %copy-start.41 = (f32[2048]{0:T(1024)S(1)}, f32[2048]{0:T(1024)}, u32[]{:S(2)}) copy-start(f32[2048]{0:T(1024)} %copy-done.40) | copy-start | bytes 24580
  1004.9 141.9 %collective-permute-start.13 = (bf16[512,1536]{1,0:T(8,128)(2,1)}, bf16[512,1536]{1,0:T(8,128)(2,1)}, u32[]{:S(2)}, u32[]{:S(2)}) collective-permute-start(bf16[512,1536]{1,0:T(8,128)(2,1)} %add_convert_fusion.3), channel_id=1, source_target_pairs={{0,8},{8,0},{16,24},{24,16},{1,9},{9,1},{17,25},{25,17},{2,10},{10... | collective-permute-start | bytes 4718600 | tf_op jit(solution)/shard_map/ppermute | solution.py:841
  (59 other events, 349.9 us)
Sparse Core Ops, SparseCore 0:
  9.9 58.6 all-gather.4
  70.5 55.9 all-gather.6
  915.4 17.5 reduce-scatter.4
  942.9 69.9 reduce-scatter.2

commit v13 on v12

--- a/solution.py
+++ b/solution.py
@@ -841,9 +841,9 @@
         self.swapped = lax.ppermute(value, "row", PAIRS)
         return (value,)
 
-    def result(self):
+    def result(self, *groups):
         if self.chained:
-            return self.two(self.own) + self.swapped.astype(f32)
+            return self.two(self.own) + after(self.swapped, *groups).astype(f32)
         return self.total
 
 
@@ -1192,10 +1192,13 @@
     chained = lax.axis_size("row") == 4
     planar = chained and cols == 8 and share == TILE
     gathered = {}
-    gathered[0] = Gathered(packs[0])
-
-    rows_in = lax.all_gather(block_input, "col", axis=1, tiled=True)
-    gains = lax.all_gather(jnp.stack([input_gain, mlp_gain]), "col", axis=1, tiled=True).astype(f32)
+    gathered[0] = Gathered(packs[0], (qkv_whole,))
+
+    gain_rows = jnp.pad(jnp.stack([input_gain, mlp_gain]), ((0, 14), (0, 0)))
+    both_in = lax.all_gather(
+        jnp.concatenate([block_input, gain_rows], axis=0), "col", axis=1, tiled=True
+    )
+    rows_in, gains = both_in[:tokens], both_in[tokens : tokens + 2].astype(f32)
     cot_rows = lax.all_gather(grad_output, "col", axis=1, tiled=True)
     rows_f = rows_in.astype(f32)
     scale_a = lax.rsqrt(jnp.mean(rows_f * rows_f, axis=-1, keepdims=True) + norm_eps)
@@ -1340,28 +1343,32 @@
     out_part = mm_tn(dattn, context).astype(bf16)
     dcontext = mm(dattn, out_full).astype(bf16)
     if planar:
-        dcontext = after(dcontext, reduced[3].second((dattn,)), reduced[2].third((dattn,)))
+        out_reduced = Reduced(out_part)
+        dcontext = after(
+            dcontext, reduced[3].second((dattn,)), reduced[2].third((dattn,)), (out_reduced.pair,)
+        )
     router_left = after(jnp.concatenate(parts, axis=1), (dattn,))
     grad_router_part = mm_tn(router_left, scaled).reshape(3, experts + 1, width).sum(axis=0)
     grad_router_both = lax.psum_scatter(grad_router_part, "row", scatter_dimension=1, tiled=True)
     dqkv, inner_a = attend_backward(qkv, dcontext, lse, lengths, cosine, sine)
     if planar:
-        dqkv = after(dqkv, reduced[3].third((inner_a,)))
+        dqkv = after(dqkv, reduced[3].third((inner_a,)), out_reduced.second((inner_a,)))
     inner_a = lax.psum(inner_a[:, 0], "col")[:, None]
-    attn_grads = jnp.concatenate([mm_tn(normed_a, dqkv).astype(bf16), out_part], axis=1)
+    qkv_part = mm_tn(normed_a, dqkv).astype(bf16)
     if planar:
+        dqkv = after(dqkv, out_reduced.third((qkv_part,)))
         dnormed_part = joint_back([dqkv], [qkv_full], 0, bf16, planar=True)
         dnormed_part = after(dnormed_part, (inner_a,))
-        (dnormed_a, attn_grad), _, _ = plane_step(
-            dnormed_part, lambda total: (total,), [], 1, 0, 3, (), attn_grads
+        (dnormed_a, qkv_grad), _, _ = plane_step(
+            dnormed_part, lambda total: (total,), [], 1, 0, 3, (), qkv_part
         )
+        out_grad = out_reduced.result((dnormed_a,))
     else:
         dnormed_a = lax.psum_scatter(
             mm_nt(dqkv, qkv_full).astype(bf16), "col", scatter_dimension=1, tiled=True
         ).astype(f32)
-        attn_grad = one_reduction(attn_grads)
-    qkv_grad, out_grad = attn_grad[:, : 3 * head_width], attn_grad[:, 3 * head_width :]
-    unit_grads = [one.result() for one in reduced]
+        qkv_grad, out_grad = one_reduction(qkv_part), one_reduction(out_part)
+    unit_grads = [one.result((dnormed_a,)) for one in reduced]
     if planar:
         unit_grads.append(last_grad)
     gain_a_share = input_gain.astype(f32)

time: 1190 us -> 1160 us (0.975)
  waiting for transfers between devices: 18.4 us -> 1.87 us
  Pallas kernels: 846 us -> 834 us
    ppermute x4 -> x5, waiting for transfers between devices: 16.9 us -> 0.01 us  [third(): self.swapped = lax.ppermute(value, 'row', PAIRS)]
    unnamed x149 -> x147, local copies, waits for them, and re-layouts: 27.7 us -> 23.5 us
    ppermute x4 -> x5, starting transfers between devices: 21.4 us -> 24.6 us  [__init__(): self.first = lax.ppermute(self.pair, 'row', INWARD)]
  transfers between devices with their start and end apart: 21 -> 24, of which waited for: 1 -> 1; matrix products, arithmetic and copies ran while one was open for 17% -> 18% of each run, Pallas kernels for 69% -> 69%
where the time goes in v13:
time: 1160 us; the launch traced here: 1150 us
  Pallas kernels  834 us (72%)
  other arithmetic  97.6 us (8%)
  local copies, waits for them, and re-layouts  78.7 us (7%)
  starting transfers between devices  46.2 us (4%)
  matrix products  45.1 us (4%)
  blocking collectives  35.5 us (3%)
  between operations  15.4 us (1%)
    pallas_call x3, Pallas kernels, plane_step(): pl.pallas_call(functools.partial(plane_kernel, pointwise, len(inputs), ma...  292 us
    pallas_call x5, Pallas kernels, expert_chunk(): pl.pallas_call(functools.partial(expert_kernel, size, steps, count, hop a...  207 us
    pallas_call x7, Pallas kernels, joint_back(): pl.pallas_call(functools.partial(joint_kernel, len(lefts), len(base), pla...  147 us
    pallas_call x1, Pallas kernels, gather_now(): pl.pallas_call(functools.partial(gather_kernel, count), in_specs=[anywher...  81.4 us
    pallas_call x1, Pallas kernels, hop_now(): pl.pallas_call(functools.partial(hop_kernel, hop[0]), in_specs=[anywhere]...  65.6 us
    pallas_call x1, Pallas kernels, attend_backward(): pl.pallas_call(attend_backward_kernel, grid_spec=pltpu.PrefetchScalarGrid...  28.8 us
    ppermute x5, starting transfers between devices, __init__(): self.first = lax.ppermute(self.pair, 'row', INWARD)  24.6 us
    unnamed x147, local copies, waits for them, and re-layouts  23.5 us
  transfers between devices with their start and end apart: 24, of which 1 were waited for; matrix products, arithmetic and copies ran while one was open for 18% of the time, Pallas kernels for 69%

profile of v13, /device:TPU:0, one launch (start us, length us, event | category | flops | bytes accessed | tf_op | source)
XLA Modules:
  0.0 1154.1 jit_solution(6384582195336613703)
XLA Ops:
  16.2 81.4 %gather_rows.1 = (bf16[4,512,768]{2,1,0:T(8,128)(2,1)}, bf16[4,512,384]{2,1,0:T(8,128)(2,1)}) custom-call(bf16[512,768]{1,0:T(8,128)(2,1)} %copy.132.refs_0_, bf16[512,384]{1,0:T(8,128)(2,1)} %fusion.18.refs_1_), custom_call_target="tpu_custom_call" | custom-call | flops 63700992000 | bytes 7077888 | tf_op jit(solution)/shard_map/gather_rows/pallas_call | solution.py:786
  140.2 10.5 fusion.12.raw_ref
  150.7 12.7 %attend_forward.1 = (bf16[2048,768]{1,0:T(8,128)(2,1)}, bf16[2048,256]{1,0:T(8,128)(2,1)}, f32[2048,256]{1,0:T(8,128)}) custom-call(s32[2]{0:T(128)} %dynamic_slice.85.length_ref, f32[2048,768]{1,0:T(8,128)} %fusion.12.raw_ref, f32[1024,128]{1,0:T(8,128)} %get-tuple-element.315.cos_ref, f32[1024,128]{1,0:T(8,128)} %get-tuple-element.316.sin_ref), custom_call_target="tpu_custom_call" | custom-call | flops 1610612736 | bytes 12582912 | tf_op jit(solution)/shard_map/attend_forward/pallas_call | solution.py:81
  163.4 8.7 joint_back.7.refs_0_
  172.1 113.5 %plane_step.3 = (f32[2048,256]{1,0:T(8,128)}, bf16[2048,2048]{1,0:T(8,128)(2,1)}, bf16[4,512,1536]{2,1,0:T(8,128)(2,1)}) custom-call(bf16[2,2,2,2048,256]{4,3,2,1,0:T(8,128)(2,1)} %joint_back.7.refs_0_, bf16[2048,256]{1,0:T(8,128)(2,1)} %refs_1_.1, f32[1,256]{1,0:T(1,128)} %reshape_convert_fusion.refs_2_.refs_5_, ...), custom_call_target="tpu_custom_call" | custom-call | flops 60000002048 | bytes 16777216 | tf_op jit(solution)/shard_map/plane_step/pallas_call | solution.py:751
  285.7 5.8 multiply_reduce_fusion
  297.8 37.0 %expert_chunk.5 = (bf16[2048,512]{1,0:T(8,128)(2,1)}, bf16[2048,256]{1,0:T(8,128)(2,1)}, f32[2048,2]{1,0:T(8,128)}, bf16[2048,768]{1,0:T(8,128)(2,1)}, bf16[2048...) custom-call(bf16[512,768]{1,0:T(8,128)(2,1)} %fusion.16.refs_0_, ...), custom_call_target="tpu_custom_call" | custom-call | flops 12884901888 | bytes 46137344 | tf_op jit(solution)/shard_map/expert_chunk/pallas_call | solution.py:987
  343.7 40.4 %expert_chunk.6 = (bf16[2048,1024]{1,0:T(8,128)(2,1)}, bf16[2048,512]{1,0:T(8,128)(2,1)}, f32[2048,2]{1,0:T(8,128)}, bf16[2048,1536]{1,0:T(8,128)(2,1)}, bf16[20...) custom-call(bf16[512,1536]{1,0:T(8,128)(2,1)} %get-tuple-element.313.refs_3_.refs_0_, ...), custom_call_target="tpu_custom_call" | custom-call | flops 25769803776 | bytes 58720256 | tf_op jit(solution)/shard_map/expert_chunk/pallas_call | solution.py:987
  388.1 5.5 collective-permute-start.6
  399.8 37.0 %joint_back.8 = (f32[2048,2048]{1,0:T(8,128)}, bf16[512,1536]{1,0:T(8,128)(2,1)}) custom-call(bf16[2048,512]{1,0:T(8,128)(2,1)} %get-tuple-element.128.refs_0_, bf16[2048,1024]{1,0:T(8,128)(2,1)} %get-tuple-element.129.refs_1_, bf16[2048,768]{1,0:T(8,128)(2,1)} %get-tuple-element.130.refs_2_.refs_4_, bf16[2048,1536]{1,0:T(8,128)(2,1)} %get-tuple-element.131.refs_3_.refs_5_, ...), custom_call_target="tpu_custom_call" | custom-call | flops 12884901888 | bytes 29360128 | tf_op jit(solution)/shard_map/joint_back/pallas_call | solution.py:1073
  438.2 52.8 %expert_chunk.7 = (bf16[2048,1024]{1,0:T(8,128)(2,1)}, bf16[2048,512]{1,0:T(8,128)(2,1)}, f32[2048,2]{1,0:T(8,128)}, bf16[2048,1536]{1,0:T(8,128)(2,1)}, bf16[20...) custom-call(bf16[512,1536]{1,0:T(8,128)(2,1)} %get-tuple-element.314.refs_11_.refs_0_, ...), custom_call_target="tpu_custom_call" | custom-call | flops 25769803776 | bytes 58720256 | tf_op jit(solution)/shard_map/expert_chunk/pallas_call | solution.py:987
  494.7 6.0 collective-permute-start.7
  500.7 65.6 %gather_hops.1 = (bf16[512,1536]{1,0:T(8,128)(2,1)}, bf16[512,1536]{1,0:T(8,128)(2,1)}, bf16[512,1536]{1,0:T(8,128)(2,1)}) custom-call(bf16[512,1536]{1,0:T(8,128)(2,1)} %get-tuple-element.139.refs_0_.refs_1_, bf16[512,1536]{1,0:T(8,128)(2,1)} %get-tuple-element.136.refs_1_.refs_2_), custom_call_target="tpu_custom_call" | custom-call | tf_op jit(solution)/shard_map/gather_hops/pallas_call | solution.py:515
  567.6 40.5 %expert_chunk.8 = (bf16[2048,1024]{1,0:T(8,128)(2,1)}, bf16[2048,512]{1,0:T(8,128)(2,1)}, f32[2048,2]{1,0:T(8,128)}, bf16[2048,1536]{1,0:T(8,128)(2,1)}, bf16[20...) custom-call(bf16[512,1536]{1,0:T(8,128)(2,1)} %pad_maximum_fusion.1.refs_11_.refs_0_, ...), custom_call_target="tpu_custom_call" | custom-call | flops 25769803776 | bytes 58720256 | tf_op jit(solution)/shard_map/expert_chunk/pallas_call | solution.py:987
  611.9 5.4 collective-permute-start.10
  617.3 30.0 %joint_back.9 = (f32[2048,2048]{1,0:T(8,128)}, bf16[512,1152]{1,0:T(8,128)(2,1)}, bf16[512,1152]{1,0:T(8,128)(2,1)}) custom-call(bf16[2048,1024]{1,0:T(8,128)(2,1)} %get-tuple-element.148.refs_0_, bf16[2048,1024]{1,0:T(8,128)(2,1)} %get-tuple-element.149.refs_1_, bf16[2048,1536]{1,0:T(8,128)(2,1)} %get-tuple-element.150.refs_2_.refs_6_, ...), custom_call_target="tpu_custom_call" | custom-call | flops 17179869184 | bytes 33554432 | tf_op jit(solution)/shard_map/joint_back/pallas_call | solution.py:1073
  655.4 28.8 %joint_back.10 = (f32[2048,2048]{1,0:T(8,128)}, bf16[512,1152]{1,0:T(8,128)(2,1)}) custom-call(bf16[2048,256]{1,0:T(8,128)(2,1)} %get-tuple-element.157.refs_0_, bf16[2048,512]{1,0:T(8,128)(2,1)} %get-tuple-element.158.refs_1_, bf16[2048,512]{1,0:T(8,128)(2,1)} %get-tuple-element.159.refs_2_, bf16[2048,512]{1,0:T(8,128)(2,1)} %get-tuple-element.160.refs_3_, ...), custom_call_target="tpu_custom_call" | custom-call | flops 15032385536 | bytes 31457280 | tf_op jit(solution)/shard_map/joint_back/pallas_call | solution.py:1073
  685.6 36.3 %expert_chunk.9 = (bf16[2048,768]{1,0:T(8,128)(2,1)}, bf16[2048,384]{1,0:T(8,128)(2,1)}, f32[2048,2]{1,0:T(8,128)}, bf16[2048,1152]{1,0:T(8,128)(2,1)}, bf16[2048,1152]{1,0:T(8,128)(2,1)}) custom-call(bf16[512,1152]{1,0:T(8,128)(2,1)} %pad_maximum_fusion.6.refs_11_.refs_0_, bf16[512,1152]{1,0:T(8,128)(2,1)} %get-tuple-element.144.refs_5_.refs_1_, ...), custom_call_target="tpu_custom_call" | custom-call | flops 19327352832 | bytes 52428800 | tf_op jit(solution)/shard_map/expert_chunk/pallas_call | solution.py:987
  721.9 6.6 add_reduce_fusion.2
  728.5 11.7 %all-gather.1 = f32[8,3,2048]{2,1,0:T(4,128)S(1)} all-gather(f32[1,3,2048]{2,1,0:T(4,128)S(1)} %maximum_bitcast_fusion.3), channel_id=2, replica_groups=mesh['row'=4,'col'=8] {'col'}, dimensions={0}, use_global_device_ids=true | all-gather | bytes 221184 | tf_op jit(solution)/shard_map/all_gather | solution.py:1316
  761.3 15.7 %joint_back.11.refs_0_ = bf16[2,2,2,2048,256]{4,3,2,1,0:T(8,128)(2,1)} custom-call(bf16[2048,768]{1,0:T(8,128)(2,1)} %get-tuple-element.170.refs_0_, bf16[2048,1152]{1,0:T(8,128)(2,1)} %get-tuple-element.171.refs_1_, f32[2048,2048]{1,0:T(8,128)} %get-tuple-element.155.refs_2_), custom_call_target="tpu_custom_call" | custom-call | flops 6442450944 | bytes 23068672 | tf_op jit(solution)/shard_map/joint_back/pallas_call | solution.py:1073
  777.0 106.6 %plane_step.4 = (f32[2048,256]{1,0:T(8,128)}, f32[2048,256]{1,0:T(8,128)}, f32[512,1152]{1,0:T(8,128)}, bf16[2048,2048]{1,0:T(8,128)(2,1)}) custom-call(bf16[2,2,2,2048,256]{4,3,2,1,0:T(8,128)(2,1)} %joint_back.11.refs_0_, f32[2048,256]{1,0:T(8,128)} %fusion.29.refs_1_, bf16[2048,256]{1,0:T(8,128)(2,1)} %refs_2_.1, f32[2048,256]{1,0:T(8,128)} %get-tuple-element.115.refs_3_, ...), custom_call_target="tpu_custom_call" | custom-call | flops 60000002048 | bytes 16777216 | tf_op jit(solution)/shard_map/plane_step/pallas_call | solution.py:751
  883.6 5.9 convolution_convert_fusion.1
  900.4 5.6 fusion.44
  907.9 14.4 %joint_back.12 = bf16[2048,2048]{1,0:T(8,128)(2,1)} custom-call(bf16[2048,384]{1,0:T(8,128)(2,1)} %get-tuple-element.176.refs_0_, bf16[2048,1152]{1,0:T(8,128)(2,1)} %get-tuple-element.171.refs_1_, f32[2048,2048]{1,0:T(8,128)} %get-tuple-element.162.refs_2_), custom_call_target="tpu_custom_call" | custom-call | flops 3221225472 | bytes 19922944 | tf_op jit(solution)/shard_map/joint_back/pallas_call | solution.py:1073
  925.6 6.7 convolution_convert_fusion.2.dcontext_ref
  939.0 28.8 %attend_backward.1 = (bf16[2048,768]{1,0:T(8,128)(2,1)}, f32[2048,1]{1,0:T(8,128)}) custom-call(s32[2]{0:T(128)} %dynamic_slice.85.length_ref, bf16[2048,768]{1,0:T(8,128)(2,1)} %get-tuple-element.178.qkv_ref, bf16[2048,256]{1,0:T(8,128)(2,1)} %convolution_convert_fusion.2.dcontext_ref, f32[2048,256]{1,0:T(8,128)} %get-tuple-element.182.lse_ref, ...), custom_call_target="tpu_custom_call" | custom-call | flops 4294967296 | bytes 12582912 | tf_op jit(solution)/shard_map/attend_backward/pallas_call | solution.py:151
  973.1 12.3 %psum.21 = f32[2048]{0:T(1024)S(1)} all-reduce(f32[2048]{0:T(1024)S(1)} %reduce.5), channel_id=1, replica_groups=mesh['row'=4,'col'=8] {'col'}, use_global_device_ids=true, to_apply=%region_10.11 | all-reduce | flops 2048 | bytes 16384 | tf_op jit(solution)/shard_map/psum | solution.py:1356
  992.4 11.3 convolution_convert_fusion
  1004.9 12.1 %joint_back.13.refs_0_ = bf16[2,2,2,2048,256]{4,3,2,1,0:T(8,128)(2,1)} custom-call(bf16[2048,768]{1,0:T(8,128)(2,1)} %get-tuple-element.189.refs_0_, bf16[2048,768]{1,0:T(8,128)(2,1)} %constant_dynamic-update-slice_fusion.1.refs_1_), custom_call_target="tpu_custom_call" | custom-call | flops 6442450944 | bytes 23068672 | tf_op jit(solution)/shard_map/joint_back/pallas_call | solution.py:1073
  1016.9 71.5 %plane_step.5 = (f32[2048,256]{1,0:T(8,128)}, f32[512,768]{1,0:T(8,128)}) custom-call(bf16[2,2,2,2048,256]{4,3,2,1,0:T(8,128)(2,1)} %joint_back.13.refs_0_, bf16[4,512,768]{2,1,0:T(8,128)(2,1)} %bitcast.116), custom_call_target="tpu_custom_call" | custom-call | flops 60000002048 | bytes 16777216 | tf_op jit(solution)/shard_map/plane_step/pallas_call | solution.py:751
  1135.6 11.4 all-reduce.5
  (315 shorter events, 200.1 us)
Async XLA Ops:
  7.2 118.6 %copy-start = (s32[8]{0:T(128)S(1)}, s32[8]{0:T(128)}, u32[]{:S(2)}) copy-start(s32[8]{0:T(128)} %param.20) | copy-start | bytes 100
  7.2 126.9 %all-gather.5.cloned.1.call-start = ((), (), s32[]{:S(2)}) async-start(), calls=%async_computation.2 | async-start | bytes 9510912 | tf_op jit(solution)/shard_map/all_gather | solution.py:1198
  11.1 161.1 %all-gather.7.cloned.1.call-start = ((), (), s32[]{:S(2)}) async-start(), calls=%async_computation.3 | async-start | bytes 9437184 | tf_op jit(solution)/shard_map/all_gather | solution.py:1202
  11.8 920.5 %reduce-scatter.5.cloned.1.call-start = ((), (), s32[]{:S(2)}) async-start(), calls=%async_computation.5 | async-start | bytes 163840 | tf_op jit(solution)/shard_map/reduce_scatter | solution.py:1352
  97.6 18.8 %collective-permute-start = (bf16[512,768]{1,0:T(8,128)(2,1)}, bf16[512,768]{1,0:T(8,128)(2,1)}, u32[]{:S(2)}, u32[]{:S(2)}) collective-permute-start(bf16[512,768]{1,0:T(8,128)(2,1)} %fusion.16.refs_0_), channel_id=1, source_target_pairs={{0,8},{8,0},{16,24},{24,16},{1,9},{9,1},{17,25},{25,17},{2,10},{10... | collective-permute-start | bytes 2359304 | tf_op jit(solution)/shard_map/ppermute | solution.py:184
  97.7 33.6 %collective-permute-start.1 = (bf16[512,768]{1,0:T(8,128)(2,1)}, bf16[512,768]{1,0:T(8,128)(2,1)}, u32[]{:S(2)}, u32[]{:S(2)}) collective-permute-start(bf16[512,768]{1,0:T(8,128)(2,1)} %fusion.16.refs_0_), channel_id=1, source_target_pairs={{8,16},{16,8},{9,17},{17,9},{10,18},{18,10},{11,19},{19,11},{12,20... | collective-permute-start | bytes 2359304 | tf_op jit(solution)/shard_map/ppermute | solution.py:185
  104.4 190.5 %copy-start.50 = (pred[2048]{0:T(1024)(128)(4,1)}, pred[2048]{0:T(1024)(128)(4,1)S(1)}, u32[]{:S(2)}) copy-start(pred[2048]{0:T(1024)(128)(4,1)S(1)} %compare_reduce_fusion) | copy-start | bytes 6148
  116.4 16.1 %collective-permute-start.2 = (bf16[512,768]{1,0:T(8,128)(2,1)}, bf16[512,768]{1,0:T(8,128)(2,1)}, u32[]{:S(2)}, u32[]{:S(2)}) collective-permute-start(bf16[512,768]{1,0:T(8,128)(2,1)} %collective-permute-done.refs_1_), channel_id=1, source_target_pairs={{8,16},{16,8},{9,17},{17,9},{10,18},{18,10},{11,19},{19,11},{12,20... | collective-permute-start | bytes 2359304 | tf_op jit(solution)/shard_map/ppermute | solution.py:191
  131.2 32.2 %collective-permute-start.3 = (bf16[512,768]{1,0:T(8,128)(2,1)}, bf16[512,768]{1,0:T(8,128)(2,1)S(1)}, u32[]{:S(2)}, u32[]{:S(2)}) collective-permute-start(bf16[512,768]{1,0:T(8,128)(2,1)} %collective-permute-done.1.refs_2_), channel_id=1, source_target_pairs={{8,0},{16,24},{9,1},{17,25},{10,2},{18,26},{11,3},{19,27},{12,4},{... | collective-permute-start | bytes 2359304 | tf_op jit(solution)/shard_map/ppermute | solution.py:190
  132.5 164.4 %collective-permute-start.4 = (bf16[512,768]{1,0:T(8,128)(2,1)}, bf16[512,768]{1,0:T(8,128)(2,1)S(1)}, u32[]{:S(2)}, u32[]{:S(2)}) collective-permute-start(bf16[512,768]{1,0:T(8,128)(2,1)} %collective-permute-done.2.refs_3_), channel_id=1, source_target_pairs={{8,0},{16,24},{9,1},{17,25},{10,2},{18,26},{11,3},{19,27},{12,4},{... | collective-permute-start | bytes 2359304 | tf_op jit(solution)/shard_map/ppermute | solution.py:197
  337.5 57.4 %collective-permute-start.5 = (bf16[1024,768]{1,0:T(8,128)(2,1)}, bf16[1024,768]{1,0:T(8,128)(2,1)}, u32[]{:S(2)}, u32[]{:S(2)}) collective-permute-start(bf16[1024,768]{1,0:T(8,128)(2,1)} %constant_dynamic-slice_fusion.5), channel_id=1, source_target_pairs={{0,8},{24,16},{1,9},{25,17},{2,10},{26,18},{3,11},{27,19},{4,12},{... | collective-permute-start | bytes 4718600 | tf_op jit(solution)/shard_map/ppermute | solution.py:819
  388.1 259.3 %collective-permute-start.6 = (bf16[1024,1536]{1,0:T(8,128)(2,1)}, bf16[1024,1536]{1,0:T(8,128)(2,1)}, u32[]{:S(2)}, u32[]{:S(2)}) collective-permute-start(bf16[1024,1536]{1,0:T(8,128)(2,1)} %constant_dynamic-slice_fusion.4), channel_id=1, source_target_pairs={{0,8},{24,16},{1,9},{25,17},{2,10},{26,18},{3,11},{27,19},{4,12},{... | collective-permute-start | bytes 9437192 | tf_op jit(solution)/shard_map/ppermute | solution.py:819
  397.9 347.1 %collective-permute-start.8 = (bf16[1024,768]{1,0:T(8,128)(2,1)}, bf16[1024,768]{1,0:T(8,128)(2,1)}, u32[]{:S(2)}, u32[]{:S(2)}) collective-permute-start(bf16[1024,768]{1,0:T(8,128)(2,1)} %add_convert_fusion.6), channel_id=1, source_target_pairs={{8,16},{16,8},{9,17},{17,9},{10,18},{18,10},{11,19},{19,11},{12,20... | collective-permute-start | bytes 4718600 | tf_op jit(solution)/shard_map/ppermute | solution.py:833
  494.7 252.5 %collective-permute-start.7 = (bf16[1024,1536]{1,0:T(8,128)(2,1)}, bf16[1024,1536]{1,0:T(8,128)(2,1)}, u32[]{:S(2)}, u32[]{:S(2)}) collective-permute-start(bf16[1024,1536]{1,0:T(8,128)(2,1)} %constant_dynamic-slice_fusion.3), channel_id=1, source_target_pairs={{0,8},{24,16},{1,9},{25,17},{2,10},{26,18},{3,11},{27,19},{4,12},{... | collective-permute-start | bytes 9437192 | tf_op jit(solution)/shard_map/ppermute | solution.py:819
  611.9 277.6 %collective-permute-start.10 = (bf16[1024,1536]{1,0:T(8,128)(2,1)}, bf16[1024,1536]{1,0:T(8,128)(2,1)}, u32[]{:S(2)}, u32[]{:S(2)}) collective-permute-start(bf16[1024,1536]{1,0:T(8,128)(2,1)} %constant_dynamic-slice_fusion.2), channel_id=1, source_target_pairs={{0,8},{24,16},{1,9},{25,17},{2,10},{26,18},{3,11},{27,19},{4,12},{... | collective-permute-start | bytes 9437192 | tf_op jit(solution)/shard_map/ppermute | solution.py:819
  652.7 102.1 %collective-permute-start.9 = (bf16[1024,1536]{1,0:T(8,128)(2,1)}, bf16[1024,1536]{1,0:T(8,128)(2,1)}, u32[]{:S(2)}, u32[]{:S(2)}) collective-permute-start(bf16[1024,1536]{1,0:T(8,128)(2,1)} %add_convert_fusion.2), channel_id=1, source_target_pairs={{8,16},{16,8},{9,17},{17,9},{10,18},{18,10},{11,19},{19,11},{12,20... | collective-permute-start | bytes 9437192 | tf_op jit(solution)/shard_map/ppermute | solution.py:833
  721.8 18.6 %copy-start.12 = (f32[2048,9]{0,1:T(8,128)S(1)}, f32[2048,9]{0,1:T(8,128)}, u32[]{:S(2)}) copy-start(f32[2048,9]{0,1:T(8,128)} %copy-done.11) | copy-start | bytes 221188
  721.9 18.7 %copy-start.35 = (f32[2048]{0:T(1024)S(1)}, f32[2048]{0:T(1024)}, u32[]{:S(2)}) copy-start(f32[2048]{0:T(1024)} %copy-done.34) | copy-start | bytes 24580
  747.2 341.3 %collective-permute-start.17 = (bf16[512,768]{1,0:T(8,128)(2,1)}, bf16[512,768]{1,0:T(8,128)(2,1)}, u32[]{:S(2)}, u32[]{:S(2)}) collective-permute-start(bf16[512,768]{1,0:T(8,128)(2,1)} %add_convert_fusion.8), channel_id=1, source_target_pairs={{0,8},{8,0},{16,24},{24,16},{1,9},{9,1},{17,25},{25,17},{2,10},{10... | collective-permute-start | bytes 2359304 | tf_op jit(solution)/shard_map/ppermute | solution.py:841
  752.6 182.4 %collective-permute-start.11 = (bf16[1024,1536]{1,0:T(8,128)(2,1)}, bf16[1024,1536]{1,0:T(8,128)(2,1)}, u32[]{:S(2)}, u32[]{:S(2)}) collective-permute-start(bf16[1024,1536]{1,0:T(8,128)(2,1)} %add_convert_fusion.1), channel_id=1, source_target_pairs={{8,16},{16,8},{9,17},{17,9},{10,18},{18,10},{11,19},{19,11},{12,20... | collective-permute-start | bytes 9437192 | tf_op jit(solution)/shard_map/ppermute | solution.py:833
  758.3 330.2 %collective-permute-start.18 = (bf16[512,1536]{1,0:T(8,128)(2,1)}, bf16[512,1536]{1,0:T(8,128)(2,1)}, u32[]{:S(2)}, u32[]{:S(2)}) collective-permute-start(bf16[512,1536]{1,0:T(8,128)(2,1)} %add_convert_fusion.5), channel_id=1, source_target_pairs={{0,8},{8,0},{16,24},{24,16},{1,9},{9,1},{17,25},{25,17},{2,10},{10... | collective-permute-start | bytes 4718600 | tf_op jit(solution)/shard_map/ppermute | solution.py:841
  777.0 106.6 %copy-start.33 = (bf16[2048,256]{1,0:T(8,128)(2,1)S(1)}, bf16[2048,256]{1,0:T(8,128)(2,1)}, u32[]{:S(2)}) copy-start(bf16[2048,256]{1,0:T(8,128)(2,1)} %get-tuple-element.112.refs_0_) | copy-start | bytes 3145732
  891.3 76.5 %collective-permute-start.13 = (bf16[1024,256]{1,0:T(8,128)(2,1)}, bf16[1024,256]{1,0:T(8,128)(2,1)}, u32[]{:S(2)}, u32[]{:S(2)}) collective-permute-start(bf16[1024,256]{1,0:T(8,128)(2,1)} %constant_dynamic-slice_fusion), channel_id=1, source_target_pairs={{0,8},{24,16},{1,9},{25,17},{2,10},{26,18},{3,11},{27,19},{4,12},{... | collective-permute-start | bytes 1572872 | tf_op jit(solution)/shard_map/ppermute | solution.py:819
  899.5 86.0 %collective-permute-start.12 = (bf16[1024,1536]{1,0:T(8,128)(2,1)}, bf16[1024,1536]{1,0:T(8,128)(2,1)S(1)}, u32[]{:S(2)}, u32[]{:S(2)}) collective-permute-start(bf16[1024,1536]{1,0:T(8,128)(2,1)} %add_convert_fusion), channel_id=1, source_target_pairs={{8,16},{16,8},{9,17},{17,9},{10,18},{18,10},{11,19},{19,11},{12,20... | collective-permute-start | bytes 9437192 | tf_op jit(solution)/shard_map/ppermute | solution.py:833
  907.7 224.1 %reduce-scatter.3.cloned.1.call-start = ((), (), s32[]{:S(2)}) async-start(), calls=%async_computation.4 | async-start | bytes 9437184 | tf_op jit(solution)/shard_map/reduce_scatter | solution.py:1341
  939.0 165.7 %collective-permute-start.19 = (bf16[512,1536]{1,0:T(8,128)(2,1)}, bf16[512,1536]{1,0:T(8,128)(2,1)}, u32[]{:S(2)}, u32[]{:S(2)}) collective-permute-start(bf16[512,1536]{1,0:T(8,128)(2,1)} %add_convert_fusion.4), channel_id=1, source_target_pairs={{0,8},{8,0},{16,24},{24,16},{1,9},{9,1},{17,25},{25,17},{2,10},{10... | collective-permute-start | bytes 4718600 | tf_op jit(solution)/shard_map/ppermute | solution.py:841
  939.0 46.5 %copy-start.45 = (f32[2048]{0:T(1024)S(1)}, f32[2048]{0:T(1024)}, u32[]{:S(2)}) copy-start(f32[2048]{0:T(1024)} %copy-done.44) | copy-start | bytes 24580
  969.9 22.5 %copy-start.48 = (f32[2048]{0:T(1024)S(1)}, f32[2048]{0:T(1024)}, u32[]{:S(2)}) copy-start(f32[2048]{0:T(1024)} %copy-done.47) | copy-start | bytes 24580
  969.9 22.5 %copy-start.54 = (f32[1,2048]{1,0:T(1,128)S(1)}, f32[1,2048]{1,0:T(1,128)}, u32[]{:S(2)}) copy-start(f32[1,2048]{1,0:T(1,128)} %copy-done.53) | copy-start | bytes 24580
  969.9 33.8 %collective-permute-start.14 = (bf16[1024,256]{1,0:T(8,128)(2,1)}, bf16[1024,256]{1,0:T(8,128)(2,1)}, u32[]{:S(2)}, u32[]{:S(2)}) collective-permute-start(bf16[1024,256]{1,0:T(8,128)(2,1)} %add_convert_fusion.9), channel_id=1, source_target_pairs={{8,16},{16,8},{9,17},{17,9},{10,18},{18,10},{11,19},{19,11},{12,20... | collective-permute-start | bytes 1572872 | tf_op jit(solution)/shard_map/ppermute | solution.py:833
  989.8 131.7 %collective-permute-start.16 = (bf16[512,1536]{1,0:T(8,128)(2,1)}, bf16[512,1536]{1,0:T(8,128)(2,1)}, u32[]{:S(2)}, u32[]{:S(2)}) collective-permute-start(bf16[512,1536]{1,0:T(8,128)(2,1)} %add_convert_fusion.3), channel_id=1, source_target_pairs={{0,8},{8,0},{16,24},{24,16},{1,9},{9,1},{17,25},{25,17},{2,10},{10... | collective-permute-start | bytes 4718600 | tf_op jit(solution)/shard_map/ppermute | solution.py:841
  1004.8 112.4 %collective-permute-start.15 = (bf16[512,256]{1,0:T(8,128)(2,1)S(1)}, bf16[512,256]{1,0:T(8,128)(2,1)}, u32[]{:S(2)}, u32[]{:S(2)}) collective-permute-start(bf16[512,256]{1,0:T(8,128)(2,1)S(1)} %add_convert_fusion.10), channel_id=1, source_target_pairs={{0,8},{8,0},{16,24},{24,16},{1,9},{9,1},{17,25},{25,17},{2,10},{10... | collective-permute-start | bytes 786440 | tf_op jit(solution)/shard_map/ppermute | solution.py:841
  (61 other events, 319.0 us)
Sparse Core Ops, SparseCore 0:
  11.2 58.9 all-gather.4
  72.0 55.9 all-gather.6
  907.8 17.7 reduce-scatter.4
  929.3 69.5 reduce-scatter.2

commit v14 on v13

--- a/solution.py
+++ b/solution.py
@@ -798,6 +798,17 @@
     return [whole.reshape((4 * whole.shape[1],) + whole.shape[2:]) for whole in wholes]
 
 
+def join_rows(pieces):
+    if len(pieces) == 1:
+        return pieces[0]
+    part = pieces[0]
+    whole = jnp.zeros((4,) + part.shape, part.dtype)
+    blocks = (part, pieces[1], pieces[2] + pieces[4], pieces[3] + pieces[5])
+    for at, piece in zip(places(lax.axis_index("row")), blocks):
+        whole = lax.dynamic_update_slice_in_dim(whole, piece[None], at, 0)
+    return whole.reshape((4 * part.shape[0],) + part.shape[1:])
+
+
 def put_own(whole, part):
     if lax.axis_size("row") != 4:
         return whole
@@ -821,9 +832,9 @@
     def rows_of(self, value, at, count):
         return lax.dynamic_slice_in_dim(value, at * self.size, count * self.size, 0)
 
-    def two(self, at):
-        mine = self.rows_of(self.grads, at, 1).astype(f32)
-        return mine + self.rows_of(self.crossed, lax.rem(at, 2), 1).astype(f32)
+    def two(self, at, cut=slice(None)):
+        mine = self.rows_of(self.grads, at, 1)[:, cut].astype(f32)
+        return mine + self.rows_of(self.crossed, lax.rem(at, 2), 1)[:, cut].astype(f32)
 
     def second(self, *groups):
         if not self.chained:
@@ -842,16 +853,17 @@
         return (value,)
 
     def result(self, *groups):
-        if self.chained:
-            return self.two(self.own) + after(self.swapped, *groups).astype(f32)
-        return self.total
+        if not self.chained:
+            return lambda cut: self.total[:, cut]
+        swapped = after(self.swapped, *groups)
+        return lambda cut: self.two(self.own, cut) + swapped[:, cut].astype(f32)
 
 
 def one_reduction(grads):
     one = Reduced(grads)
     one.second()
     one.third()
-    return one.result()
+    return one.result()(slice(None))
 
 
 def after(value, *groups):
@@ -1168,8 +1180,12 @@
     router_pack = jnp.concatenate([router_weight, score_shared[:, None]], axis=1)
     router_pack = jnp.pad(router_pack, ((0, 0), (0, -router_pack.shape[1] % 128)))
     out_pack = jnp.concatenate([output_weight.T, router_pack], axis=1)
-    qkv_whole, out_whole = gather_now([qkv_pack, out_pack], 0)
-    qkv_full, out_weights = put_own(qkv_whole, qkv_pack), put_own(out_whole, out_pack)
+    (qkv_whole,) = gather_now([qkv_pack], 0)
+    qkv_full = put_own(qkv_whole, qkv_pack)
+    out_gathered = Gathered(out_pack, (qkv_whole,))
+    out_gathered.second()
+    out_gathered.third()
+    out_weights = join_rows(out_gathered.pieces)
     out_full = out_weights[:, :head_width]
     router_full = out_weights[:, head_width : head_width + experts + 1]
     shared_cuts = [(None, a, b) for a, b in cuts_of(gate_shared.shape[1], (512,))]
@@ -1292,7 +1308,9 @@
             dscaled_early, *next_pieces = joint_back(
                 [third_pair, dpair], wholes[2:], 0, f32, dscaled_early, hop=(2, carried), number=11
             )
-            first_hidden = after(hiddens[0], reduced[1].second((dscaled_early,)))
+            first_hidden = after(
+                hiddens[0], reduced[1].second((dscaled_early,)), reduced[2].second((dscaled_early,))
+            )
             moe_early, last_piece = joint_back(
                 [first_hidden] + hiddens[1:], wholes, 2, f32, hop=(3, next_pieces[:1]), number=12
             )
@@ -1300,7 +1318,7 @@
             waits = (dscaled_early, moe_early)
     now = (sums,)
     if planar:
-        waits = reduced[2].second(now) + reduced[0].third(now) + reduced[1].third(now)
+        waits = reduced[0].third(now)
     else:
         waits = ()
         for one in reduced:
@@ -1345,7 +1363,11 @@
     if planar:
         out_reduced = Reduced(out_part)
         dcontext = after(
-            dcontext, reduced[3].second((dattn,)), reduced[2].third((dattn,)), (out_reduced.pair,)
+            dcontext,
+            reduced[3].second((dattn,)),
+            reduced[1].third((dattn,)),
+            reduced[2].third((dattn,)),
+            (out_reduced.pair,),
         )
     router_left = after(jnp.concatenate(parts, axis=1), (dattn,))
     grad_router_part = mm_tn(router_left, scaled).reshape(3, experts + 1, width).sum(axis=0)
@@ -1362,7 +1384,7 @@
         (dnormed_a, qkv_grad), _, _ = plane_step(
             dnormed_part, lambda total: (total,), [], 1, 0, 3, (), qkv_part
         )
-        out_grad = out_reduced.result((dnormed_a,))
+        out_grad = out_reduced.result((dnormed_a,))(slice(None))
     else:
         dnormed_a = lax.psum_scatter(
             mm_nt(dqkv, qkv_full).astype(bf16), "col", scatter_dimension=1, tiled=True
@@ -1370,7 +1392,7 @@
         qkv_grad, out_grad = one_reduction(qkv_part), one_reduction(out_part)
     unit_grads = [one.result((dnormed_a,)) for one in reduced]
     if planar:
-        unit_grads.append(last_grad)
+        unit_grads.append(lambda cut: last_grad[:, cut])
     gain_a_share = input_gain.astype(f32)
     dinput = dstream + scale_a * gain_a_share * dnormed_a
     dinput = dinput - x_share * (scale_a * scale_a * inner_a / width)
@@ -1385,8 +1407,8 @@
         found = []
         for (of, a, b), grad in zip(chunks, unit_grads):
             if of == kind:
-                size = grad.shape[1] // 3
-                part = grad[:, which * size : which * size + b - a]
+                size = b - a + -(b - a) % 128
+                part = grad(slice(which * size, which * size + b - a))
                 found.append((a, part.T if which == 2 else part))
         found = [part for _, part in sorted(found, key=lambda item: item[0])]
         return jnp.concatenate(found, axis=0 if which == 2 else 1)

time: 1160 us -> 1160 us (level)
  Pallas kernels: 834 us -> 812 us
    pallas_call x1, Pallas kernels: 81.4 us -> 57.7 us  [gather_now(): pl.pallas_call(functools.partial(gather_kernel, count), in_specs=[anywher...]
    transpose x0 -> x4, other arithmetic: none -> 15.6 us  [unpack(): found.append((a, part.T if which == 2 else part))]
    unnamed x147 -> x136, local copies, waits for them, and re-layouts: 23.5 us -> 20.3 us
  transfers between devices with their start and end apart: 24 -> 29, of which waited for: 1 -> 2; matrix products, arithmetic and copies ran while one was open for 18% -> 18% of each run, Pallas kernels for 69% -> 67%
where the time goes in v14:
time: 1160 us; the launch traced here: 1150 us
  Pallas kernels  812 us (70%)
  other arithmetic  105 us (9%)
  local copies, waits for them, and re-layouts  68.7 us (6%)
  starting transfers between devices  53.8 us (5%)
  matrix products  45.4 us (4%)
  blocking collectives  35.7 us (3%)
  between operations  15.5 us (1%)
  waiting for transfers between devices  12.9 us (1%)
    pallas_call x3, Pallas kernels, plane_step(): pl.pallas_call(functools.partial(plane_kernel, pointwise, len(inputs), ma...  293 us
    pallas_call x5, Pallas kernels, expert_chunk(): pl.pallas_call(functools.partial(expert_kernel, size, steps, count, hop a...  208 us
    pallas_call x7, Pallas kernels, joint_back(): pl.pallas_call(functools.partial(joint_kernel, len(lefts), len(base), pla...  147 us
    pallas_call x1, Pallas kernels, hop_now(): pl.pallas_call(functools.partial(hop_kernel, hop[0]), in_specs=[anywhere]...  65.5 us
    pallas_call x1, Pallas kernels, gather_now(): pl.pallas_call(functools.partial(gather_kernel, count), in_specs=[anywher...  57.7 us
    pallas_call x1, Pallas kernels, attend_backward(): pl.pallas_call(attend_backward_kernel, grid_spec=pltpu.PrefetchScalarGrid...  28.1 us
    ppermute x5, starting transfers between devices, __init__(): self.first = lax.ppermute(self.pair, 'row', INWARD)  24.5 us
  transfers between devices with their start and end apart: 29, of which 2 were waited for; matrix products, arithmetic and copies ran while one was open for 18% of the time, Pallas kernels for 67%

profile of v14, /device:TPU:0, one launch (start us, length us, event | category | flops | bytes accessed | tf_op | source)
XLA Modules:
  0.0 1148.9 jit_solution(11583587130951967522)
XLA Ops:
  14.4 57.7 %gather_rows.1 = bf16[4,512,768]{2,1,0:T(8,128)(2,1)} custom-call(bf16[512,768]{1,0:T(8,128)(2,1)} %copy.135.refs_0_), custom_call_target="tpu_custom_call" | custom-call | flops 42467328000 | bytes 4718592 | tf_op jit(solution)/shard_map/gather_rows/pallas_call | solution.py:786
  108.2 6.3 collective-permute-done.6
  117.1 5.8 collective-permute-done.8
  132.9 10.5 fusion.12.raw_ref
  143.4 12.7 %attend_forward.1 = (bf16[2048,768]{1,0:T(8,128)(2,1)}, bf16[2048,256]{1,0:T(8,128)(2,1)}, f32[2048,256]{1,0:T(8,128)}) custom-call(s32[2]{0:T(128)} %dynamic_slice.101.length_ref, f32[2048,768]{1,0:T(8,128)} %fusion.12.raw_ref, f32[1024,128]{1,0:T(8,128)} %get-tuple-element.315.cos_ref, f32[1024,128]{1,0:T(8,128)} %get-tuple-element.316.sin_ref), custom_call_target="tpu_custom_call" | custom-call | flops 1610612736 | bytes 12582912 | tf_op jit(solution)/shard_map/attend_forward/pallas_call | solution.py:81
  156.1 8.7 joint_back.7.refs_0_
  164.8 112.3 %plane_step.3 = (f32[2048,256]{1,0:T(8,128)}, bf16[2048,2048]{1,0:T(8,128)(2,1)}, bf16[4,512,1536]{2,1,0:T(8,128)(2,1)}) custom-call(bf16[2,2,2,2048,256]{4,3,2,1,0:T(8,128)(2,1)} %joint_back.7.refs_0_, bf16[2048,256]{1,0:T(8,128)(2,1)} %refs_1_.1, f32[1,256]{1,0:T(1,128)} %reshape_convert_fusion.refs_2_.refs_5_, ...), custom_call_target="tpu_custom_call" | custom-call | flops 60000002048 | bytes 16777216 | tf_op jit(solution)/shard_map/plane_step/pallas_call | solution.py:751
  277.0 5.8 multiply_reduce_fusion
  289.2 37.5 %expert_chunk.5 = (bf16[2048,512]{1,0:T(8,128)(2,1)}, bf16[2048,256]{1,0:T(8,128)(2,1)}, f32[2048,2]{1,0:T(8,128)}, bf16[2048,768]{1,0:T(8,128)(2,1)}, bf16[2048...) custom-call(bf16[512,768]{1,0:T(8,128)(2,1)} %fusion.16.refs_0_, ...), custom_call_target="tpu_custom_call" | custom-call | flops 12884901888 | bytes 46137344 | tf_op jit(solution)/shard_map/expert_chunk/pallas_call | solution.py:999
  334.5 40.4 %expert_chunk.6 = (bf16[2048,1024]{1,0:T(8,128)(2,1)}, bf16[2048,512]{1,0:T(8,128)(2,1)}, f32[2048,2]{1,0:T(8,128)}, bf16[2048,1536]{1,0:T(8,128)(2,1)}, bf16[20...) custom-call(bf16[512,1536]{1,0:T(8,128)(2,1)} %get-tuple-element.313.refs_3_.refs_0_, ...), custom_call_target="tpu_custom_call" | custom-call | flops 25769803776 | bytes 58720256 | tf_op jit(solution)/shard_map/expert_chunk/pallas_call | solution.py:999
  390.4 36.9 %joint_back.8 = (f32[2048,2048]{1,0:T(8,128)}, bf16[512,1536]{1,0:T(8,128)(2,1)}) custom-call(bf16[2048,512]{1,0:T(8,128)(2,1)} %get-tuple-element.126.refs_0_, bf16[2048,1024]{1,0:T(8,128)(2,1)} %get-tuple-element.127.refs_1_, bf16[2048,768]{1,0:T(8,128)(2,1)} %get-tuple-element.128.refs_2_.refs_4_, bf16[2048,1536]{1,0:T(8,128)(2,1)} %get-tuple-element.129.refs_3_.refs_5_, ...), custom_call_target="tpu_custom_call" | custom-call | flops 12884901888 | bytes 29360128 | tf_op jit(solution)/shard_map/joint_back/pallas_call | solution.py:1085
  428.7 52.9 %expert_chunk.7 = (bf16[2048,1024]{1,0:T(8,128)(2,1)}, bf16[2048,512]{1,0:T(8,128)(2,1)}, f32[2048,2]{1,0:T(8,128)}, bf16[2048,1536]{1,0:T(8,128)(2,1)}, bf16[20...) custom-call(bf16[512,1536]{1,0:T(8,128)(2,1)} %get-tuple-element.314.refs_11_.refs_0_, ...), custom_call_target="tpu_custom_call" | custom-call | flops 25769803776 | bytes 58720256 | tf_op jit(solution)/shard_map/expert_chunk/pallas_call | solution.py:999
  485.4 6.1 collective-permute-start.12
  491.5 65.5 %gather_hops.1 = (bf16[512,1536]{1,0:T(8,128)(2,1)}, bf16[512,1536]{1,0:T(8,128)(2,1)}, bf16[512,1536]{1,0:T(8,128)(2,1)}) custom-call(bf16[512,1536]{1,0:T(8,128)(2,1)} %get-tuple-element.137.refs_0_.refs_1_, bf16[512,1536]{1,0:T(8,128)(2,1)} %get-tuple-element.134.refs_1_.refs_2_), custom_call_target="tpu_custom_call" | custom-call | tf_op jit(solution)/shard_map/gather_hops/pallas_call | solution.py:515
  558.3 40.5 %expert_chunk.8 = (bf16[2048,1024]{1,0:T(8,128)(2,1)}, bf16[2048,512]{1,0:T(8,128)(2,1)}, f32[2048,2]{1,0:T(8,128)}, bf16[2048,1536]{1,0:T(8,128)(2,1)}, bf16[20...) custom-call(bf16[512,1536]{1,0:T(8,128)(2,1)} %pad_maximum_fusion.1.refs_11_.refs_0_, ...), custom_call_target="tpu_custom_call" | custom-call | flops 25769803776 | bytes 58720256 | tf_op jit(solution)/shard_map/expert_chunk/pallas_call | solution.py:999
  608.1 30.4 %joint_back.9 = (f32[2048,2048]{1,0:T(8,128)}, bf16[512,1152]{1,0:T(8,128)(2,1)}, bf16[512,1152]{1,0:T(8,128)(2,1)}) custom-call(bf16[2048,1024]{1,0:T(8,128)(2,1)} %get-tuple-element.146.refs_0_, bf16[2048,1024]{1,0:T(8,128)(2,1)} %get-tuple-element.147.refs_1_, bf16[2048,1536]{1,0:T(8,128)(2,1)} %get-tuple-element.148.refs_2_.refs_6_, ...), custom_call_target="tpu_custom_call" | custom-call | flops 17179869184 | bytes 33554432 | tf_op jit(solution)/shard_map/joint_back/pallas_call | solution.py:1085
  654.2 29.2 %joint_back.10 = (f32[2048,2048]{1,0:T(8,128)}, bf16[512,1152]{1,0:T(8,128)(2,1)}) custom-call(bf16[2048,256]{1,0:T(8,128)(2,1)} %get-tuple-element.156.refs_0_, bf16[2048,512]{1,0:T(8,128)(2,1)} %get-tuple-element.157.refs_1_, bf16[2048,512]{1,0:T(8,128)(2,1)} %get-tuple-element.158.refs_2_, bf16[2048,512]{1,0:T(8,128)(2,1)} %get-tuple-element.159.refs_3_, ...), custom_call_target="tpu_custom_call" | custom-call | flops 15032385536 | bytes 31457280 | tf_op jit(solution)/shard_map/joint_back/pallas_call | solution.py:1085
  684.7 36.3 %expert_chunk.9 = (bf16[2048,768]{1,0:T(8,128)(2,1)}, bf16[2048,384]{1,0:T(8,128)(2,1)}, f32[2048,2]{1,0:T(8,128)}, bf16[2048,1152]{1,0:T(8,128)(2,1)}, bf16[2048,1152]{1,0:T(8,128)(2,1)}) custom-call(bf16[512,1152]{1,0:T(8,128)(2,1)} %pad_maximum_fusion.6.refs_11_.refs_0_, bf16[512,1152]{1,0:T(8,128)(2,1)} %get-tuple-element.142.refs_5_.refs_1_, ...), custom_call_target="tpu_custom_call" | custom-call | flops 19327352832 | bytes 52428800 | tf_op jit(solution)/shard_map/expert_chunk/pallas_call | solution.py:999
  721.0 6.6 add_reduce_fusion.2
  727.7 13.1 %all-gather.1 = f32[8,3,2048]{2,1,0:T(4,128)S(1)} all-gather(f32[1,3,2048]{2,1,0:T(4,128)S(1)} %maximum_bitcast_fusion.3), channel_id=2, replica_groups=mesh['row'=4,'col'=8] {'col'}, dimensions={0}, use_global_device_ids=true | all-gather | bytes 221184 | tf_op jit(solution)/shard_map/all_gather | solution.py:1334
  747.9 15.7 %joint_back.11.refs_0_ = bf16[2,2,2,2048,256]{4,3,2,1,0:T(8,128)(2,1)} custom-call(bf16[2048,768]{1,0:T(8,128)(2,1)} %get-tuple-element.167.refs_0_, bf16[2048,1152]{1,0:T(8,128)(2,1)} %get-tuple-element.168.refs_1_, f32[2048,2048]{1,0:T(8,128)} %get-tuple-element.153.refs_2_), custom_call_target="tpu_custom_call" | custom-call | flops 6442450944 | bytes 23068672 | tf_op jit(solution)/shard_map/joint_back/pallas_call | solution.py:1085
  763.6 100.1 %plane_step.4 = (f32[2048,256]{1,0:T(8,128)}, f32[2048,256]{1,0:T(8,128)}, f32[512,1152]{1,0:T(8,128)}, bf16[2048,2048]{1,0:T(8,128)(2,1)}) custom-call(bf16[2,2,2,2048,256]{4,3,2,1,0:T(8,128)(2,1)} %joint_back.11.refs_0_, f32[2048,256]{1,0:T(8,128)} %fusion.30.refs_1_, bf16[2048,256]{1,0:T(8,128)(2,1)} %refs_2_.1, f32[2048,256]{1,0:T(8,128)} %get-tuple-element.113.refs_3_, ...), custom_call_target="tpu_custom_call" | custom-call | flops 60000002048 | bytes 16777216 | tf_op jit(solution)/shard_map/plane_step/pallas_call | solution.py:751
  863.7 5.9 convolution_convert_fusion.1
  881.5 5.6 fusion.46
  889.1 14.4 %joint_back.12 = bf16[2048,2048]{1,0:T(8,128)(2,1)} custom-call(bf16[2048,384]{1,0:T(8,128)(2,1)} %get-tuple-element.173.refs_0_, bf16[2048,1152]{1,0:T(8,128)(2,1)} %get-tuple-element.168.refs_1_, f32[2048,2048]{1,0:T(8,128)} %get-tuple-element.161.refs_2_), custom_call_target="tpu_custom_call" | custom-call | flops 3221225472 | bytes 19922944 | tf_op jit(solution)/shard_map/joint_back/pallas_call | solution.py:1085
  906.8 6.7 convolution_convert_fusion.2.dcontext_ref
  926.3 28.1 %attend_backward.1 = (bf16[2048,768]{1,0:T(8,128)(2,1)}, f32[2048,1]{1,0:T(8,128)}) custom-call(s32[2]{0:T(128)} %dynamic_slice.101.length_ref, bf16[2048,768]{1,0:T(8,128)(2,1)} %get-tuple-element.175.qkv_ref, bf16[2048,256]{1,0:T(8,128)(2,1)} %convolution_convert_fusion.2.dcontext_ref, f32[2048,256]{1,0:T(8,128)} %get-tuple-element.180.lse_ref, ...), custom_call_target="tpu_custom_call" | custom-call | flops 4294967296 | bytes 12582912 | tf_op jit(solution)/shard_map/attend_backward/pallas_call | solution.py:151
  963.1 11.6 %convolution_convert_fusion = bf16[2048,768]{1,0:T(8,128)(2,1)} fusion(bf16[2048,768]{1,0:T(8,128)(2,1)S(1)} %copy-done.57, f32[2048]{0:T(1024)S(1)} %bitcast.120, f32[2048]{0:T(1024)S(1)} %copy-done.43, bf16[2064,2048]{1,0:T(8,128)(2,1)} %all-gather.5.cloned.1.call-done), kind=kOutput, calls=%fused_computation.10 | convolution fusion | flops 6460801024 | bytes 14696448 | tf_op jit(solution)/shard_map/dot_general | solution.py:30
  976.3 12.0 %psum.21 = f32[2048]{0:T(1024)S(1)} all-reduce(f32[2048]{0:T(1024)S(1)} %reduce.5), channel_id=1, replica_groups=mesh['row'=4,'col'=8] {'col'}, use_global_device_ids=true, to_apply=%region_10.11 | all-reduce | flops 2048 | bytes 16384 | tf_op jit(solution)/shard_map/psum | solution.py:1378
  990.7 12.1 %joint_back.13.refs_0_ = bf16[2,2,2,2048,256]{4,3,2,1,0:T(8,128)(2,1)} custom-call(bf16[2048,768]{1,0:T(8,128)(2,1)} %get-tuple-element.187.refs_0_, bf16[2048,768]{1,0:T(8,128)(2,1)} %constant_dynamic-update-slice_fusion.4.refs_1_), custom_call_target="tpu_custom_call" | custom-call | flops 6442450944 | bytes 23068672 | tf_op jit(solution)/shard_map/joint_back/pallas_call | solution.py:1085
  1002.8 80.3 %plane_step.5 = (f32[2048,256]{1,0:T(8,128)}, f32[512,768]{1,0:T(8,128)}) custom-call(bf16[2,2,2,2048,256]{4,3,2,1,0:T(8,128)(2,1)} %joint_back.13.refs_0_, bf16[4,512,768]{2,1,0:T(8,128)(2,1)} %bitcast.125), custom_call_target="tpu_custom_call" | custom-call | flops 60000002048 | bytes 16777216 | tf_op jit(solution)/shard_map/plane_step/pallas_call | solution.py:751
  1131.4 10.5 all-reduce.5
  (320 shorter events, 215.2 us)
Async XLA Ops:
  7.2 93.0 %copy-start = (s32[8]{0:T(128)S(1)}, s32[8]{0:T(128)}, u32[]{:S(2)}) copy-start(s32[8]{0:T(128)} %param.20) | copy-start | bytes 100
  7.2 119.5 %all-gather.5.cloned.1.call-start = ((), (), s32[]{:S(2)}) async-start(), calls=%async_computation.2 | async-start | bytes 9510912 | tf_op jit(solution)/shard_map/all_gather | solution.py:1214
  11.0 153.8 %all-gather.7.cloned.1.call-start = ((), (), s32[]{:S(2)}) async-start(), calls=%async_computation.3 | async-start | bytes 9437184 | tf_op jit(solution)/shard_map/all_gather | solution.py:1218
  11.7 901.7 %reduce-scatter.5.cloned.1.call-start = ((), (), s32[]{:S(2)}) async-start(), calls=%async_computation.5 | async-start | bytes 163840 | tf_op jit(solution)/shard_map/reduce_scatter | solution.py:1374
  72.0 25.9 %collective-permute-start.4 = (bf16[512,384]{0,1:T(8,128)(2,1)}, bf16[512,384]{0,1:T(8,128)(2,1)}, u32[]{:S(2)}, u32[]{:S(2)}) collective-permute-start(bf16[512,384]{0,1:T(8,128)(2,1)} %get-tuple-element.111), channel_id=1, source_target_pairs={{0,8},{8,0},{16,24},{24,16},{1,9},{9,1},{17,25},{25,17},{2,10},{10... | collective-permute-start | bytes 1179656 | tf_op jit(solution)/shard_map/ppermute | solution.py:184
  72.1 29.4 %collective-permute-start.5 = (bf16[512,384]{0,1:T(8,128)(2,1)}, bf16[512,384]{0,1:T(8,128)(2,1)}, u32[]{:S(2)}, u32[]{:S(2)}) collective-permute-start(bf16[512,384]{0,1:T(8,128)(2,1)} %get-tuple-element.111), channel_id=1, source_target_pairs={{8,16},{16,8},{9,17},{17,9},{10,18},{18,10},{11,19},{19,11},{12,20... | collective-permute-start | bytes 1179656 | tf_op jit(solution)/shard_map/ppermute | solution.py:185
  75.0 31.6 %collective-permute-start = (bf16[512,768]{1,0:T(8,128)(2,1)}, bf16[512,768]{1,0:T(8,128)(2,1)}, u32[]{:S(2)}, u32[]{:S(2)}) collective-permute-start(bf16[512,768]{1,0:T(8,128)(2,1)} %fusion.16.refs_0_), channel_id=1, source_target_pairs={{0,8},{8,0},{16,24},{24,16},{1,9},{9,1},{17,25},{25,17},{2,10},{10... | collective-permute-start | bytes 2359304 | tf_op jit(solution)/shard_map/ppermute | solution.py:184
  79.0 36.7 %collective-permute-start.1 = (bf16[512,768]{1,0:T(8,128)(2,1)}, bf16[512,768]{1,0:T(8,128)(2,1)}, u32[]{:S(2)}, u32[]{:S(2)}) collective-permute-start(bf16[512,768]{1,0:T(8,128)(2,1)} %fusion.16.refs_0_), channel_id=1, source_target_pairs={{8,16},{16,8},{9,17},{17,9},{10,18},{18,10},{11,19},{19,11},{12,20... | collective-permute-start | bytes 2359304 | tf_op jit(solution)/shard_map/ppermute | solution.py:185
  98.0 7.2 collective-permute-start.7
  101.5 184.8 %copy-start.45 = (pred[2048]{0:T(1024)(128)(4,1)}, pred[2048]{0:T(1024)(128)(4,1)S(1)}, u32[]{:S(2)}) copy-start(pred[2048]{0:T(1024)(128)(4,1)S(1)} %compare_reduce_fusion) | copy-start | bytes 6148
  101.5 12.9 %collective-permute-start.6 = (bf16[512,384]{0,1:T(8,128)(2,1)}, bf16[512,384]{0,1:T(8,128)(2,1)S(1)}, u32[]{:S(2)}, u32[]{:S(2)}) collective-permute-start(bf16[512,384]{0,1:T(8,128)(2,1)} %collective-permute-done.5), channel_id=1, source_target_pairs={{8,0},{16,24},{9,1},{17,25},{10,2},{18,26},{11,3},{19,27},{12,4},{... | collective-permute-start | bytes 1179656 | tf_op jit(solution)/shard_map/ppermute | solution.py:190
  105.2 17.7 %collective-permute-start.8 = (bf16[512,384]{0,1:T(8,128)(2,1)}, bf16[512,384]{0,1:T(8,128)(2,1)S(1)}, u32[]{:S(2)}, u32[]{:S(2)}) collective-permute-start(bf16[512,384]{0,1:T(8,128)(2,1)} %collective-permute-done.7), channel_id=1, source_target_pairs={{8,0},{16,24},{9,1},{17,25},{10,2},{18,26},{11,3},{19,27},{12,4},{... | collective-permute-start | bytes 1179656 | tf_op jit(solution)/shard_map/ppermute | solution.py:197
  106.6 18.6 %collective-permute-start.2 = (bf16[512,768]{1,0:T(8,128)(2,1)}, bf16[512,768]{1,0:T(8,128)(2,1)}, u32[]{:S(2)}, u32[]{:S(2)}) collective-permute-start(bf16[512,768]{1,0:T(8,128)(2,1)} %collective-permute-done.refs_1_), channel_id=1, source_target_pairs={{8,16},{16,8},{9,17},{17,9},{10,18},{18,10},{11,19},{19,11},{12,20... | collective-permute-start | bytes 2359304 | tf_op jit(solution)/shard_map/ppermute | solution.py:191
  115.7 40.3 %collective-permute-start.3 = (bf16[512,768]{1,0:T(8,128)(2,1)}, bf16[512,768]{1,0:T(8,128)(2,1)S(1)}, u32[]{:S(2)}, u32[]{:S(2)}) collective-permute-start(bf16[512,768]{1,0:T(8,128)(2,1)} %collective-permute-done.1.refs_2_), channel_id=1, source_target_pairs={{8,0},{16,24},{9,1},{17,25},{10,2},{18,26},{11,3},{19,27},{12,4},{... | collective-permute-start | bytes 2359304 | tf_op jit(solution)/shard_map/ppermute | solution.py:190
  125.2 163.1 %collective-permute-start.9 = (bf16[512,768]{1,0:T(8,128)(2,1)}, bf16[512,768]{1,0:T(8,128)(2,1)S(1)}, u32[]{:S(2)}, u32[]{:S(2)}) collective-permute-start(bf16[512,768]{1,0:T(8,128)(2,1)} %collective-permute-done.2.refs_3_), channel_id=1, source_target_pairs={{8,0},{16,24},{9,1},{17,25},{10,2},{18,26},{11,3},{19,27},{12,4},{... | collective-permute-start | bytes 2359304 | tf_op jit(solution)/shard_map/ppermute | solution.py:197
  329.4 56.2 %collective-permute-start.10 = (bf16[1024,768]{1,0:T(8,128)(2,1)}, bf16[1024,768]{1,0:T(8,128)(2,1)}, u32[]{:S(2)}, u32[]{:S(2)}) collective-permute-start(bf16[1024,768]{1,0:T(8,128)(2,1)} %constant_dynamic-slice_fusion.5), channel_id=1, source_target_pairs={{0,8},{24,16},{1,9},{25,17},{2,10},{26,18},{3,11},{27,19},{4,12},{... | collective-permute-start | bytes 4718600 | tf_op jit(solution)/shard_map/ppermute | solution.py:830
  378.9 259.6 %collective-permute-start.11 = (bf16[1024,1536]{1,0:T(8,128)(2,1)}, bf16[1024,1536]{1,0:T(8,128)(2,1)}, u32[]{:S(2)}, u32[]{:S(2)}) collective-permute-start(bf16[1024,1536]{1,0:T(8,128)(2,1)} %constant_dynamic-slice_fusion.4), channel_id=1, source_target_pairs={{0,8},{24,16},{1,9},{25,17},{2,10},{26,18},{3,11},{27,19},{4,12},{... | collective-permute-start | bytes 9437192 | tf_op jit(solution)/shard_map/ppermute | solution.py:830
  388.6 353.9 %collective-permute-start.13 = (bf16[1024,768]{1,0:T(8,128)(2,1)}, bf16[1024,768]{1,0:T(8,128)(2,1)}, u32[]{:S(2)}, u32[]{:S(2)}) collective-permute-start(bf16[1024,768]{1,0:T(8,128)(2,1)} %add_convert_fusion.6), channel_id=1, source_target_pairs={{8,16},{16,8},{9,17},{17,9},{10,18},{18,10},{11,19},{19,11},{12,20... | collective-permute-start | bytes 4718600 | tf_op jit(solution)/shard_map/ppermute | solution.py:844
  485.4 160.8 %collective-permute-start.12 = (bf16[1024,1536]{1,0:T(8,128)(2,1)}, bf16[1024,1536]{1,0:T(8,128)(2,1)}, u32[]{:S(2)}, u32[]{:S(2)}) collective-permute-start(bf16[1024,1536]{1,0:T(8,128)(2,1)} %constant_dynamic-slice_fusion.3), channel_id=1, source_target_pairs={{0,8},{24,16},{1,9},{25,17},{2,10},{26,18},{3,11},{27,19},{4,12},{... | collective-permute-start | bytes 9437192 | tf_op jit(solution)/shard_map/ppermute | solution.py:830
  602.6 267.0 %collective-permute-start.14 = (bf16[1024,1536]{1,0:T(8,128)(2,1)}, bf16[1024,1536]{1,0:T(8,128)(2,1)}, u32[]{:S(2)}, u32[]{:S(2)}) collective-permute-start(bf16[1024,1536]{1,0:T(8,128)(2,1)} %constant_dynamic-slice_fusion.2), channel_id=1, source_target_pairs={{0,8},{24,16},{1,9},{25,17},{2,10},{26,18},{3,11},{27,19},{4,12},{... | collective-permute-start | bytes 9437192 | tf_op jit(solution)/shard_map/ppermute | solution.py:830
  643.8 272.3 %collective-permute-start.15 = (bf16[1024,1536]{1,0:T(8,128)(2,1)}, bf16[1024,1536]{1,0:T(8,128)(2,1)}, u32[]{:S(2)}, u32[]{:S(2)}) collective-permute-start(bf16[1024,1536]{1,0:T(8,128)(2,1)} %add_convert_fusion.2), channel_id=1, source_target_pairs={{8,16},{16,8},{9,17},{17,9},{10,18},{18,10},{11,19},{19,11},{12,20... | collective-permute-start | bytes 9437192 | tf_op jit(solution)/shard_map/ppermute | solution.py:844
  651.4 268.8 %collective-permute-start.16 = (bf16[1024,1536]{1,0:T(8,128)(2,1)}, bf16[1024,1536]{1,0:T(8,128)(2,1)}, u32[]{:S(2)}, u32[]{:S(2)}) collective-permute-start(bf16[1024,1536]{1,0:T(8,128)(2,1)} %add_convert_fusion.1), channel_id=1, source_target_pairs={{8,16},{16,8},{9,17},{17,9},{10,18},{18,10},{11,19},{19,11},{12,20... | collective-permute-start | bytes 9437192 | tf_op jit(solution)/shard_map/ppermute | solution.py:844
  744.9 345.5 %collective-permute-start.22 = (bf16[512,768]{1,0:T(8,128)(2,1)}, bf16[512,768]{1,0:T(8,128)(2,1)}, u32[]{:S(2)}, u32[]{:S(2)}) collective-permute-start(bf16[512,768]{1,0:T(8,128)(2,1)} %add_convert_fusion.8), channel_id=1, source_target_pairs={{0,8},{8,0},{16,24},{24,16},{1,9},{9,1},{17,25},{25,17},{2,10},{10... | collective-permute-start | bytes 2359304 | tf_op jit(solution)/shard_map/ppermute | solution.py:852
  763.6 100.1 %copy-start.28 = (bf16[2048,256]{1,0:T(8,128)(2,1)S(1)}, bf16[2048,256]{1,0:T(8,128)(2,1)}, u32[]{:S(2)}) copy-start(bf16[2048,256]{1,0:T(8,128)(2,1)} %get-tuple-element.110.refs_0_) | copy-start | bytes 3145732
  871.4 83.0 %collective-permute-start.18 = (bf16[1024,256]{1,0:T(8,128)(2,1)}, bf16[1024,256]{1,0:T(8,128)(2,1)}, u32[]{:S(2)}, u32[]{:S(2)}) collective-permute-start(bf16[1024,256]{1,0:T(8,128)(2,1)} %constant_dynamic-slice_fusion), channel_id=1, source_target_pairs={{0,8},{24,16},{1,9},{25,17},{2,10},{26,18},{3,11},{27,19},{4,12},{... | collective-permute-start | bytes 1572872 | tf_op jit(solution)/shard_map/ppermute | solution.py:830
  880.7 76.0 %collective-permute-start.17 = (bf16[1024,1536]{1,0:T(8,128)(2,1)}, bf16[1024,1536]{1,0:T(8,128)(2,1)S(1)}, u32[]{:S(2)}, u32[]{:S(2)}) collective-permute-start(bf16[1024,1536]{1,0:T(8,128)(2,1)} %add_convert_fusion), channel_id=1, source_target_pairs={{8,16},{16,8},{9,17},{17,9},{10,18},{18,10},{11,19},{19,11},{12,20... | collective-permute-start | bytes 9437192 | tf_op jit(solution)/shard_map/ppermute | solution.py:844
  888.9 238.3 %reduce-scatter.3.cloned.1.call-start = ((), (), s32[]{:S(2)}) async-start(), calls=%async_computation.4 | async-start | bytes 9437184 | tf_op jit(solution)/shard_map/reduce_scatter | solution.py:1359
  920.3 162.8 %collective-permute-start.23 = (bf16[512,1536]{1,0:T(8,128)(2,1)}, bf16[512,1536]{1,0:T(8,128)(2,1)}, u32[]{:S(2)}, u32[]{:S(2)}) collective-permute-start(bf16[512,1536]{1,0:T(8,128)(2,1)} %add_convert_fusion.5), channel_id=1, source_target_pairs={{0,8},{8,0},{16,24},{24,16},{1,9},{9,1},{17,25},{25,17},{2,10},{10... | collective-permute-start | bytes 4718600 | tf_op jit(solution)/shard_map/ppermute | solution.py:852
  924.3 179.6 %collective-permute-start.24 = (bf16[512,1536]{1,0:T(8,128)(2,1)}, bf16[512,1536]{1,0:T(8,128)(2,1)}, u32[]{:S(2)}, u32[]{:S(2)}) collective-permute-start(bf16[512,1536]{1,0:T(8,128)(2,1)} %add_convert_fusion.4), channel_id=1, source_target_pairs={{0,8},{8,0},{16,24},{24,16},{1,9},{9,1},{17,25},{25,17},{2,10},{10... | collective-permute-start | bytes 4718600 | tf_op jit(solution)/shard_map/ppermute | solution.py:852
  956.7 31.7 %collective-permute-start.19 = (bf16[1024,256]{1,0:T(8,128)(2,1)}, bf16[1024,256]{1,0:T(8,128)(2,1)}, u32[]{:S(2)}, u32[]{:S(2)}) collective-permute-start(bf16[1024,256]{1,0:T(8,128)(2,1)} %add_convert_fusion.9), channel_id=1, source_target_pairs={{8,16},{16,8},{9,17},{17,9},{10,18},{18,10},{11,19},{19,11},{12,20... | collective-permute-start | bytes 1572872 | tf_op jit(solution)/shard_map/ppermute | solution.py:844
  961.9 149.0 %collective-permute-start.21 = (bf16[512,1536]{1,0:T(8,128)(2,1)}, bf16[512,1536]{1,0:T(8,128)(2,1)}, u32[]{:S(2)}, u32[]{:S(2)}) collective-permute-start(bf16[512,1536]{1,0:T(8,128)(2,1)} %add_convert_fusion.3), channel_id=1, source_target_pairs={{0,8},{8,0},{16,24},{24,16},{1,9},{9,1},{17,25},{25,17},{2,10},{10... | collective-permute-start | bytes 4718600 | tf_op jit(solution)/shard_map/ppermute | solution.py:852
  990.2 111.5 %collective-permute-start.20 = (bf16[512,256]{1,0:T(8,128)(2,1)}, bf16[512,256]{1,0:T(8,128)(2,1)}, u32[]{:S(2)}, u32[]{:S(2)}) collective-permute-start(bf16[512,256]{1,0:T(8,128)(2,1)} %add_convert_fusion.10), channel_id=1, source_target_pairs={{0,8},{8,0},{16,24},{24,16},{1,9},{9,1},{17,25},{25,17},{2,10},{10... | collective-permute-start | bytes 786440 | tf_op jit(solution)/shard_map/ppermute | solution.py:852
  (62 other events, 558.1 us)
Sparse Core Ops, SparseCore 0:
  11.1 58.9 all-gather.4
  71.9 55.9 all-gather.6
  889.0 17.5 reduce-scatter.4
  910.3 69.4 reduce-scatter.2

commit v15 on v14

--- a/solution.py
+++ b/solution.py
@@ -818,7 +818,7 @@
 
 
 class Reduced:
-    def __init__(self, grads):
+    def __init__(self, grads, halves=False):
         self.chained = lax.axis_size("row") == 4
         if not self.chained:
             self.total = lax.psum_scatter(grads, "row", scatter_dimension=0, tiled=True).astype(f32)
@@ -827,7 +827,15 @@
         self.own, self.partner, _, _ = places(z)
         self.grads, self.size = grads, grads.shape[0] // 4
         self.pair = self.rows_of(grads, (1 - z // 2) * 2, 2)
-        self.first = lax.ppermute(self.pair, "row", INWARD)
+        if halves:
+            self.first = lax.ppermute(self.pair[: self.size], "row", INWARD)
+        else:
+            self.first = lax.ppermute(self.pair, "row", INWARD)
+
+    def first_rest(self, *groups):
+        rest = after(self.pair[self.size :], *groups)
+        self.first = jnp.concatenate([self.first, lax.ppermute(rest, "row", INWARD)], axis=0)
+        return (rest,)
 
     def rows_of(self, value, at, count):
         return lax.dynamic_slice_in_dim(value, at * self.size, count * self.size, 0)
@@ -1057,7 +1065,7 @@
             hop.begin()
 
     for a in range(0, refs[count].shape[0], TILE):
-        total = refs[2 * count][:, a : a + TILE] if based else None
+        total = refs[2 * count][:, a : a + TILE].astype(f32) if based else None
         for left, weights in zip(refs[:count], refs[count : 2 * count]):
             part = mm_nt(left[...], weights[a : a + TILE, :])
             total = part if total is None else total + part
@@ -1289,7 +1297,7 @@
         now = (sums,)
         waits = ()
         if at < last or not planar:
-            reduced.append(Reduced(grads))
+            reduced.append(Reduced(grads, planar and at == 1))
         if planar and at == 0:
             waits = (reduced[0].pair,)
         elif planar and at == 1:
@@ -1304,15 +1312,15 @@
             gathered[3] = (packs[3], *carried, *rest)
             waits = (rest[2],)
         elif planar and at == 3:
-            third_pair = after(dpairs[2], (reduced[3].pair,))
+            third_pair = after(dpairs[2], reduced[1].first_rest(now), (reduced[3].pair,))
             dscaled_early, *next_pieces = joint_back(
-                [third_pair, dpair], wholes[2:], 0, f32, dscaled_early, hop=(2, carried), number=11
+                [third_pair, dpair], wholes[2:], 0, bf16, dscaled_early, hop=(2, carried), number=11
             )
             first_hidden = after(
                 hiddens[0], reduced[1].second((dscaled_early,)), reduced[2].second((dscaled_early,))
             )
             moe_early, last_piece = joint_back(
-                [first_hidden] + hiddens[1:], wholes, 2, f32, hop=(3, next_pieces[:1]), number=12
+                [first_hidden] + hiddens[1:], wholes, 2, bf16, hop=(3, next_pieces[:1]), number=12
             )
             gathered[4] = (packs[4], *carried, *next_pieces, last_piece)
             waits = (dscaled_early, moe_early)

time: 1160 us -> 1140 us (0.983)
  Pallas kernels: 812 us -> 793 us
    pallas_call x5, Pallas kernels: 208 us -> 195 us  [expert_chunk(): pl.pallas_call(functools.partial(expert_kernel, size, steps, count, hop a...]
    ppermute x5 -> x4, starting transfers between devices: 24.5 us -> 16 us  [__init__(): self.first = lax.ppermute(self.pair, 'row', INWARD)]
  transfers between devices with their start and end apart: 29 -> 30, of which waited for: 2 -> 2; matrix products, arithmetic and copies ran while one was open for 18% -> 18% of each run, Pallas kernels for 67% -> 67%
where the time goes in v15:
time: 1140 us; the launch traced here: 1130 us
  Pallas kernels  793 us (70%)
  other arithmetic  105 us (9%)
  local copies, waits for them, and re-layouts  68.7 us (6%)
  starting transfers between devices  56 us (5%)
  matrix products  45.1 us (4%)
  blocking collectives  35.4 us (3%)
  between operations  15.5 us (1%)
  waiting for transfers between devices  12.8 us (1%)
    pallas_call x3, Pallas kernels, plane_step(): pl.pallas_call(functools.partial(plane_kernel, pointwise, len(inputs), ma...  293 us
    pallas_call x5, Pallas kernels, expert_chunk(): pl.pallas_call(functools.partial(expert_kernel, size, steps, count, hop a...  195 us
    pallas_call x7, Pallas kernels, joint_back(): pl.pallas_call(functools.partial(joint_kernel, len(lefts), len(base), pla...  142 us
    pallas_call x1, Pallas kernels, hop_now(): pl.pallas_call(functools.partial(hop_kernel, hop[0]), in_specs=[anywhere]...  64.7 us
    pallas_call x1, Pallas kernels, gather_now(): pl.pallas_call(functools.partial(gather_kernel, count), in_specs=[anywher...  57.7 us
    pallas_call x1, Pallas kernels, attend_backward(): pl.pallas_call(attend_backward_kernel, grid_spec=pltpu.PrefetchScalarGrid...  28.3 us
  transfers between devices with their start and end apart: 30, of which 2 were waited for; matrix products, arithmetic and copies ran while one was open for 18% of the time, Pallas kernels for 67%

profile of v15, /device:TPU:0, one launch (start us, length us, event | category | flops | bytes accessed | tf_op | source)
XLA Modules:
  0.0 1131.7 jit_solution(13017318022933431147)
XLA Ops:
  14.4 57.7 %gather_rows.1 = bf16[4,512,768]{2,1,0:T(8,128)(2,1)} custom-call(bf16[512,768]{1,0:T(8,128)(2,1)} %copy.135.refs_0_), custom_call_target="tpu_custom_call" | custom-call | flops 42467328000 | bytes 4718592 | tf_op jit(solution)/shard_map/gather_rows/pallas_call | solution.py:786
  108.2 6.3 collective-permute-done.6
  117.1 5.8 collective-permute-done.8
  132.9 10.5 fusion.12.raw_ref
  143.4 12.7 %attend_forward.1 = (bf16[2048,768]{1,0:T(8,128)(2,1)}, bf16[2048,256]{1,0:T(8,128)(2,1)}, f32[2048,256]{1,0:T(8,128)}) custom-call(s32[2]{0:T(128)} %dynamic_slice.101.length_ref, f32[2048,768]{1,0:T(8,128)} %fusion.12.raw_ref, f32[1024,128]{1,0:T(8,128)} %get-tuple-element.319.cos_ref, f32[1024,128]{1,0:T(8,128)} %get-tuple-element.320.sin_ref), custom_call_target="tpu_custom_call" | custom-call | flops 1610612736 | bytes 12582912 | tf_op jit(solution)/shard_map/attend_forward/pallas_call | solution.py:81
  156.1 8.7 joint_back.7.refs_0_
  164.8 112.2 %plane_step.3 = (f32[2048,256]{1,0:T(8,128)}, bf16[2048,2048]{1,0:T(8,128)(2,1)}, bf16[4,512,1536]{2,1,0:T(8,128)(2,1)}) custom-call(bf16[2,2,2,2048,256]{4,3,2,1,0:T(8,128)(2,1)} %joint_back.7.refs_0_, bf16[2048,256]{1,0:T(8,128)(2,1)} %refs_1_.1, f32[1,256]{1,0:T(1,128)} %reshape_convert_fusion.refs_2_.refs_5_, ...), custom_call_target="tpu_custom_call" | custom-call | flops 60000002048 | bytes 16777216 | tf_op jit(solution)/shard_map/plane_step/pallas_call | solution.py:751
  277.0 5.8 multiply_reduce_fusion
  289.1 37.4 %expert_chunk.5 = (bf16[2048,512]{1,0:T(8,128)(2,1)}, bf16[2048,256]{1,0:T(8,128)(2,1)}, f32[2048,2]{1,0:T(8,128)}, bf16[2048,768]{1,0:T(8,128)(2,1)}, bf16[2048...) custom-call(bf16[512,768]{1,0:T(8,128)(2,1)} %fusion.16.refs_0_, ...), custom_call_target="tpu_custom_call" | custom-call | flops 12884901888 | bytes 46137344 | tf_op jit(solution)/shard_map/expert_chunk/pallas_call | solution.py:1007
  334.4 40.4 %expert_chunk.6 = (bf16[2048,1024]{1,0:T(8,128)(2,1)}, bf16[2048,512]{1,0:T(8,128)(2,1)}, f32[2048,2]{1,0:T(8,128)}, bf16[2048,1536]{1,0:T(8,128)(2,1)}, bf16[20...) custom-call(bf16[512,1536]{1,0:T(8,128)(2,1)} %get-tuple-element.317.refs_3_.refs_0_, ...), custom_call_target="tpu_custom_call" | custom-call | flops 25769803776 | bytes 58720256 | tf_op jit(solution)/shard_map/expert_chunk/pallas_call | solution.py:1007
  389.9 36.8 %joint_back.8 = (f32[2048,2048]{1,0:T(8,128)}, bf16[512,1536]{1,0:T(8,128)(2,1)}) custom-call(bf16[2048,512]{1,0:T(8,128)(2,1)} %get-tuple-element.127.refs_0_, bf16[2048,1024]{1,0:T(8,128)(2,1)} %get-tuple-element.128.refs_1_, bf16[2048,768]{1,0:T(8,128)(2,1)} %get-tuple-element.129.refs_2_.refs_4_, bf16[2048,1536]{1,0:T(8,128)(2,1)} %get-tuple-element.130.refs_3_.refs_5_, ...), custom_call_target="tpu_custom_call" | custom-call | flops 12884901888 | bytes 29360128 | tf_op jit(solution)/shard_map/joint_back/pallas_call | solution.py:1093
  428.0 40.4 %expert_chunk.7 = (bf16[2048,1024]{1,0:T(8,128)(2,1)}, bf16[2048,512]{1,0:T(8,128)(2,1)}, f32[2048,2]{1,0:T(8,128)}, bf16[2048,1536]{1,0:T(8,128)(2,1)}, bf16[20...) custom-call(bf16[512,1536]{1,0:T(8,128)(2,1)} %get-tuple-element.318.refs_11_.refs_0_, ...), custom_call_target="tpu_custom_call" | custom-call | flops 25769803776 | bytes 58720256 | tf_op jit(solution)/shard_map/expert_chunk/pallas_call | solution.py:1007
  472.3 5.4 collective-permute-start.13
  477.7 64.7 %gather_hops.1 = (bf16[512,1536]{1,0:T(8,128)(2,1)}, bf16[512,1536]{1,0:T(8,128)(2,1)}, bf16[512,1536]{1,0:T(8,128)(2,1)}) custom-call(bf16[512,1536]{1,0:T(8,128)(2,1)} %get-tuple-element.138.refs_0_.refs_1_, bf16[512,1536]{1,0:T(8,128)(2,1)} %get-tuple-element.135.refs_1_.refs_2_), custom_call_target="tpu_custom_call" | custom-call | tf_op jit(solution)/shard_map/gather_hops/pallas_call | solution.py:515
  543.8 40.5 %expert_chunk.8 = (bf16[2048,1024]{1,0:T(8,128)(2,1)}, bf16[2048,512]{1,0:T(8,128)(2,1)}, f32[2048,2]{1,0:T(8,128)}, bf16[2048,1536]{1,0:T(8,128)(2,1)}, bf16[20...) custom-call(bf16[512,1536]{1,0:T(8,128)(2,1)} %pad_maximum_fusion.2.refs_11_.refs_0_, ...), custom_call_target="tpu_custom_call" | custom-call | flops 25769803776 | bytes 58720256 | tf_op jit(solution)/shard_map/expert_chunk/pallas_call | solution.py:1007
  595.9 29.7 %joint_back.9 = (bf16[2048,2048]{1,0:T(8,128)(2,1)}, bf16[512,1152]{1,0:T(8,128)(2,1)}, bf16[512,1152]{1,0:T(8,128)(2,1)}) custom-call(bf16[2048,1024]{1,0:T(8,128)(2,1)} %get-tuple-element.149.refs_0_, bf16[2048,1024]{1,0:T(8,128)(2,1)} %get-tuple-element.150.refs_1_, bf16[2048,1536]{1,0:T(8,128)(2,1)} %get-tuple-element.151.refs_2_.refs_6_, ...), custom_call_target="tpu_custom_call" | custom-call | flops 17179869184 | bytes 33554432 | tf_op jit(solution)/shard_map/joint_back/pallas_call | solution.py:1093
  642.3 28.5 %joint_back.10 = (bf16[2048,2048]{1,0:T(8,128)(2,1)}, bf16[512,1152]{1,0:T(8,128)(2,1)}) custom-call(bf16[2048,256]{1,0:T(8,128)(2,1)} %get-tuple-element.159.refs_0_, bf16[2048,512]{1,0:T(8,128)(2,1)} %get-tuple-element.160.refs_1_, bf16[2048,512]{1,0:T(8,128)(2,1)} %get-tuple-element.161.refs_2_, bf16[2048,512]{1,0:T(8,128)(2,1)} %get-tuple-element.162.refs_3_, ...), custom_call_target="tpu_custom_call" | custom-call | flops 15032385536 | bytes 31457280 | tf_op jit(solution)/shard_map/joint_back/pallas_call | solution.py:1093
  672.1 36.3 %expert_chunk.9 = (bf16[2048,768]{1,0:T(8,128)(2,1)}, bf16[2048,384]{1,0:T(8,128)(2,1)}, f32[2048,2]{1,0:T(8,128)}, bf16[2048,1152]{1,0:T(8,128)(2,1)}, bf16[2048,1152]{1,0:T(8,128)(2,1)}) custom-call(bf16[512,1152]{1,0:T(8,128)(2,1)} %pad_maximum_fusion.7.refs_11_.refs_0_, bf16[512,1152]{1,0:T(8,128)(2,1)} %get-tuple-element.143.refs_5_.refs_1_, ...), custom_call_target="tpu_custom_call" | custom-call | flops 19327352832 | bytes 52428800 | tf_op jit(solution)/shard_map/expert_chunk/pallas_call | solution.py:1007
  708.5 6.5 add_reduce_fusion.2
  715.0 12.9 %all-gather.1 = f32[8,3,2048]{2,1,0:T(4,128)S(1)} all-gather(f32[1,3,2048]{2,1,0:T(4,128)S(1)} %maximum_bitcast_fusion.3), channel_id=2, replica_groups=mesh['row'=4,'col'=8] {'col'}, dimensions={0}, use_global_device_ids=true | all-gather | bytes 221184 | tf_op jit(solution)/shard_map/all_gather | solution.py:1342
  735.1 14.0 %joint_back.11.refs_0_ = bf16[2,2,2,2048,256]{4,3,2,1,0:T(8,128)(2,1)} custom-call(bf16[2048,768]{1,0:T(8,128)(2,1)} %get-tuple-element.170.refs_0_, bf16[2048,1152]{1,0:T(8,128)(2,1)} %get-tuple-element.171.refs_1_, bf16[2048,2048]{1,0:T(8,128)(2,1)} %get-tuple-element.156.refs_2_), custom_call_target="tpu_custom_call" | custom-call | flops 6442450944 | bytes 23068672 | tf_op jit(solution)/shard_map/joint_back/pallas_call | solution.py:1093
  749.0 100.2 %plane_step.4 = (f32[2048,256]{1,0:T(8,128)}, f32[2048,256]{1,0:T(8,128)}, f32[512,1152]{1,0:T(8,128)}, bf16[2048,2048]{1,0:T(8,128)(2,1)}) custom-call(bf16[2,2,2,2048,256]{4,3,2,1,0:T(8,128)(2,1)} %joint_back.11.refs_0_, f32[2048,256]{1,0:T(8,128)} %fusion.30.refs_1_, bf16[2048,256]{1,0:T(8,128)(2,1)} %refs_2_.1, f32[2048,256]{1,0:T(8,128)} %get-tuple-element.114.refs_3_, ...), custom_call_target="tpu_custom_call" | custom-call | flops 60000002048 | bytes 16777216 | tf_op jit(solution)/shard_map/plane_step/pallas_call | solution.py:751
  849.2 5.9 convolution_convert_fusion.1
  866.9 5.6 fusion.46
  874.5 12.0 %joint_back.12 = bf16[2048,2048]{1,0:T(8,128)(2,1)} custom-call(bf16[2048,384]{1,0:T(8,128)(2,1)} %get-tuple-element.175.refs_0_, bf16[2048,1152]{1,0:T(8,128)(2,1)} %get-tuple-element.171.refs_1_, bf16[2048,2048]{1,0:T(8,128)(2,1)} %get-tuple-element.164.refs_2_), custom_call_target="tpu_custom_call" | custom-call | flops 3221225472 | bytes 19922944 | tf_op jit(solution)/shard_map/joint_back/pallas_call | solution.py:1093
  889.7 6.7 convolution_convert_fusion.2.dcontext_ref
  908.6 28.3 %attend_backward.1 = (bf16[2048,768]{1,0:T(8,128)(2,1)}, f32[2048,1]{1,0:T(8,128)}) custom-call(s32[2]{0:T(128)} %dynamic_slice.101.length_ref, bf16[2048,768]{1,0:T(8,128)(2,1)} %get-tuple-element.177.qkv_ref, bf16[2048,256]{1,0:T(8,128)(2,1)} %convolution_convert_fusion.2.dcontext_ref, f32[2048,256]{1,0:T(8,128)} %get-tuple-element.182.lse_ref, ...), custom_call_target="tpu_custom_call" | custom-call | flops 4294967296 | bytes 12582912 | tf_op jit(solution)/shard_map/attend_backward/pallas_call | solution.py:151
  946.6 11.2 convolution_convert_fusion
  959.3 12.1 %psum.21 = f32[2048]{0:T(1024)S(1)} all-reduce(f32[2048]{0:T(1024)S(1)} %reduce.5), channel_id=1, replica_groups=mesh['row'=4,'col'=8] {'col'}, use_global_device_ids=true, to_apply=%region_10.11 | all-reduce | flops 2048 | bytes 16384 | tf_op jit(solution)/shard_map/psum | solution.py:1386
  973.5 12.1 %joint_back.13.refs_0_ = bf16[2,2,2,2048,256]{4,3,2,1,0:T(8,128)(2,1)} custom-call(bf16[2048,768]{1,0:T(8,128)(2,1)} %get-tuple-element.189.refs_0_, bf16[2048,768]{1,0:T(8,128)(2,1)} %constant_dynamic-update-slice_fusion.4.refs_1_), custom_call_target="tpu_custom_call" | custom-call | flops 6442450944 | bytes 23068672 | tf_op jit(solution)/shard_map/joint_back/pallas_call | solution.py:1093
  985.6 80.4 %plane_step.5 = (f32[2048,256]{1,0:T(8,128)}, f32[512,768]{1,0:T(8,128)}) custom-call(bf16[2,2,2,2048,256]{4,3,2,1,0:T(8,128)(2,1)} %joint_back.13.refs_0_, bf16[4,512,768]{2,1,0:T(8,128)(2,1)} %bitcast.127), custom_call_target="tpu_custom_call" | custom-call | flops 60000002048 | bytes 16777216 | tf_op jit(solution)/shard_map/plane_step/pallas_call | solution.py:751
  1114.3 10.4 all-reduce.5
  (324 shorter events, 218.1 us)
Async XLA Ops:
  7.2 119.6 %all-gather.5.cloned.1.call-start = ((), (), s32[]{:S(2)}) async-start(), calls=%async_computation.2 | async-start | bytes 9510912 | tf_op jit(solution)/shard_map/all_gather | solution.py:1222
  11.0 153.8 %all-gather.7.cloned.1.call-start = ((), (), s32[]{:S(2)}) async-start(), calls=%async_computation.3 | async-start | bytes 9437184 | tf_op jit(solution)/shard_map/all_gather | solution.py:1226
  11.7 884.7 %reduce-scatter.5.cloned.1.call-start = ((), (), s32[]{:S(2)}) async-start(), calls=%async_computation.5 | async-start | bytes 163840 | tf_op jit(solution)/shard_map/reduce_scatter | solution.py:1382
  72.0 26.0 %collective-permute-start.4 = (bf16[512,384]{0,1:T(8,128)(2,1)}, bf16[512,384]{0,1:T(8,128)(2,1)}, u32[]{:S(2)}, u32[]{:S(2)}) collective-permute-start(bf16[512,384]{0,1:T(8,128)(2,1)} %get-tuple-element.112), channel_id=1, source_target_pairs={{0,8},{8,0},{16,24},{24,16},{1,9},{9,1},{17,25},{25,17},{2,10},{10... | collective-permute-start | bytes 1179656 | tf_op jit(solution)/shard_map/ppermute | solution.py:184
  72.1 29.4 %collective-permute-start.5 = (bf16[512,384]{0,1:T(8,128)(2,1)}, bf16[512,384]{0,1:T(8,128)(2,1)}, u32[]{:S(2)}, u32[]{:S(2)}) collective-permute-start(bf16[512,384]{0,1:T(8,128)(2,1)} %get-tuple-element.112), channel_id=1, source_target_pairs={{8,16},{16,8},{9,17},{17,9},{10,18},{18,10},{11,19},{19,11},{12,20... | collective-permute-start | bytes 1179656 | tf_op jit(solution)/shard_map/ppermute | solution.py:185
  75.0 31.6 %collective-permute-start = (bf16[512,768]{1,0:T(8,128)(2,1)}, bf16[512,768]{1,0:T(8,128)(2,1)}, u32[]{:S(2)}, u32[]{:S(2)}) collective-permute-start(bf16[512,768]{1,0:T(8,128)(2,1)} %fusion.16.refs_0_), channel_id=1, source_target_pairs={{0,8},{8,0},{16,24},{24,16},{1,9},{9,1},{17,25},{25,17},{2,10},{10... | collective-permute-start | bytes 2359304 | tf_op jit(solution)/shard_map/ppermute | solution.py:184
  79.0 36.7 %collective-permute-start.1 = (bf16[512,768]{1,0:T(8,128)(2,1)}, bf16[512,768]{1,0:T(8,128)(2,1)}, u32[]{:S(2)}, u32[]{:S(2)}) collective-permute-start(bf16[512,768]{1,0:T(8,128)(2,1)} %fusion.16.refs_0_), channel_id=1, source_target_pairs={{8,16},{16,8},{9,17},{17,9},{10,18},{18,10},{11,19},{19,11},{12,20... | collective-permute-start | bytes 2359304 | tf_op jit(solution)/shard_map/ppermute | solution.py:185
  98.0 7.2 collective-permute-start.7
  101.6 184.7 %copy-start.43 = (pred[2048]{0:T(1024)(128)(4,1)}, pred[2048]{0:T(1024)(128)(4,1)S(1)}, u32[]{:S(2)}) copy-start(pred[2048]{0:T(1024)(128)(4,1)S(1)} %compare_reduce_fusion) | copy-start | bytes 6148
  101.6 12.9 %collective-permute-start.6 = (bf16[512,384]{0,1:T(8,128)(2,1)}, bf16[512,384]{0,1:T(8,128)(2,1)S(1)}, u32[]{:S(2)}, u32[]{:S(2)}) collective-permute-start(bf16[512,384]{0,1:T(8,128)(2,1)} %collective-permute-done.5), channel_id=1, source_target_pairs={{8,0},{16,24},{9,1},{17,25},{10,2},{18,26},{11,3},{19,27},{12,4},{... | collective-permute-start | bytes 1179656 | tf_op jit(solution)/shard_map/ppermute | solution.py:190
  105.2 17.6 %collective-permute-start.8 = (bf16[512,384]{0,1:T(8,128)(2,1)}, bf16[512,384]{0,1:T(8,128)(2,1)S(1)}, u32[]{:S(2)}, u32[]{:S(2)}) collective-permute-start(bf16[512,384]{0,1:T(8,128)(2,1)} %collective-permute-done.7), channel_id=1, source_target_pairs={{8,0},{16,24},{9,1},{17,25},{10,2},{18,26},{11,3},{19,27},{12,4},{... | collective-permute-start | bytes 1179656 | tf_op jit(solution)/shard_map/ppermute | solution.py:197
  106.6 18.6 %collective-permute-start.2 = (bf16[512,768]{1,0:T(8,128)(2,1)}, bf16[512,768]{1,0:T(8,128)(2,1)}, u32[]{:S(2)}, u32[]{:S(2)}) collective-permute-start(bf16[512,768]{1,0:T(8,128)(2,1)} %collective-permute-done.refs_1_), channel_id=1, source_target_pairs={{8,16},{16,8},{9,17},{17,9},{10,18},{18,10},{11,19},{19,11},{12,20... | collective-permute-start | bytes 2359304 | tf_op jit(solution)/shard_map/ppermute | solution.py:191
  115.7 40.4 %collective-permute-start.3 = (bf16[512,768]{1,0:T(8,128)(2,1)}, bf16[512,768]{1,0:T(8,128)(2,1)S(1)}, u32[]{:S(2)}, u32[]{:S(2)}) collective-permute-start(bf16[512,768]{1,0:T(8,128)(2,1)} %collective-permute-done.1.refs_2_), channel_id=1, source_target_pairs={{8,0},{16,24},{9,1},{17,25},{10,2},{18,26},{11,3},{19,27},{12,4},{... | collective-permute-start | bytes 2359304 | tf_op jit(solution)/shard_map/ppermute | solution.py:190
  125.2 163.0 %collective-permute-start.9 = (bf16[512,768]{1,0:T(8,128)(2,1)}, bf16[512,768]{1,0:T(8,128)(2,1)S(1)}, u32[]{:S(2)}, u32[]{:S(2)}) collective-permute-start(bf16[512,768]{1,0:T(8,128)(2,1)} %collective-permute-done.2.refs_3_), channel_id=1, source_target_pairs={{8,0},{16,24},{9,1},{17,25},{10,2},{18,26},{11,3},{19,27},{12,4},{... | collective-permute-start | bytes 2359304 | tf_op jit(solution)/shard_map/ppermute | solution.py:197
  329.2 55.9 %collective-permute-start.10 = (bf16[1024,768]{1,0:T(8,128)(2,1)}, bf16[1024,768]{1,0:T(8,128)(2,1)}, u32[]{:S(2)}, u32[]{:S(2)}) collective-permute-start(bf16[1024,768]{1,0:T(8,128)(2,1)} %constant_dynamic-slice_fusion.7), channel_id=1, source_target_pairs={{0,8},{24,16},{1,9},{25,17},{2,10},{26,18},{3,11},{27,19},{4,12},{... | collective-permute-start | bytes 4718600 | tf_op jit(solution)/shard_map/ppermute | solution.py:833
  378.8 246.8 %collective-permute-start.11 = (bf16[512,1536]{1,0:T(8,128)(2,1)}, bf16[512,1536]{1,0:T(8,128)(2,1)}, u32[]{:S(2)}, u32[]{:S(2)}) collective-permute-start(bf16[512,1536]{1,0:T(8,128)(2,1)} %get-tuple-element.280), channel_id=1, source_target_pairs={{0,8},{24,16},{1,9},{25,17},{2,10},{26,18},{3,11},{27,19},{4,12},{... | collective-permute-start | bytes 4718600 | tf_op jit(solution)/shard_map/ppermute | solution.py:831
  388.1 341.7 %collective-permute-start.14 = (bf16[1024,768]{1,0:T(8,128)(2,1)}, bf16[1024,768]{1,0:T(8,128)(2,1)}, u32[]{:S(2)}, u32[]{:S(2)}) collective-permute-start(bf16[1024,768]{1,0:T(8,128)(2,1)} %add_convert_fusion.6), channel_id=1, source_target_pairs={{8,16},{16,8},{9,17},{17,9},{10,18},{18,10},{11,19},{19,11},{12,20... | collective-permute-start | bytes 4718600 | tf_op jit(solution)/shard_map/ppermute | solution.py:852
  472.3 162.7 %collective-permute-start.13 = (bf16[1024,1536]{1,0:T(8,128)(2,1)}, bf16[1024,1536]{1,0:T(8,128)(2,1)}, u32[]{:S(2)}, u32[]{:S(2)}) collective-permute-start(bf16[1024,1536]{1,0:T(8,128)(2,1)} %constant_dynamic-slice_fusion.5), channel_id=1, source_target_pairs={{0,8},{24,16},{1,9},{25,17},{2,10},{26,18},{3,11},{27,19},{4,12},{... | collective-permute-start | bytes 9437192 | tf_op jit(solution)/shard_map/ppermute | solution.py:833
  584.2 41.4 %collective-permute-start.12 = (bf16[512,1536]{1,0:T(8,128)(2,1)}, bf16[512,1536]{1,0:T(8,128)(2,1)}, u32[]{:S(2)}, u32[]{:S(2)}) collective-permute-start(bf16[512,1536]{1,0:T(8,128)(2,1)} %get-tuple-element.147), channel_id=1, source_target_pairs={{0,8},{24,16},{1,9},{25,17},{2,10},{26,18},{3,11},{27,19},{4,12},{... | collective-permute-start | bytes 4718600 | tf_op jit(solution)/shard_map/ppermute | solution.py:837
  593.0 262.2 %collective-permute-start.15 = (bf16[1024,1536]{1,0:T(8,128)(2,1)}, bf16[1024,1536]{1,0:T(8,128)(2,1)}, u32[]{:S(2)}, u32[]{:S(2)}) collective-permute-start(bf16[1024,1536]{1,0:T(8,128)(2,1)} %constant_dynamic-slice_fusion.4), channel_id=1, source_target_pairs={{0,8},{24,16},{1,9},{25,17},{2,10},{26,18},{3,11},{27,19},{4,12},{... | collective-permute-start | bytes 9437192 | tf_op jit(solution)/shard_map/ppermute | solution.py:833
  632.6 266.4 %collective-permute-start.16 = (bf16[1024,1536]{1,0:T(8,128)(2,1)}, bf16[1024,1536]{1,0:T(8,128)(2,1)}, u32[]{:S(2)}, u32[]{:S(2)}) collective-permute-start(bf16[1024,1536]{1,0:T(8,128)(2,1)} %add_convert_fusion.2), channel_id=1, source_target_pairs={{8,16},{16,8},{9,17},{17,9},{10,18},{18,10},{11,19},{19,11},{12,20... | collective-permute-start | bytes 9437192 | tf_op jit(solution)/shard_map/ppermute | solution.py:852
  639.6 263.8 %collective-permute-start.17 = (bf16[1024,1536]{1,0:T(8,128)(2,1)}, bf16[1024,1536]{1,0:T(8,128)(2,1)}, u32[]{:S(2)}, u32[]{:S(2)}) collective-permute-start(bf16[1024,1536]{1,0:T(8,128)(2,1)} %add_convert_fusion.1), channel_id=1, source_target_pairs={{8,16},{16,8},{9,17},{17,9},{10,18},{18,10},{11,19},{19,11},{12,20... | collective-permute-start | bytes 9437192 | tf_op jit(solution)/shard_map/ppermute | solution.py:852
  732.1 341.2 %collective-permute-start.23 = (bf16[512,768]{1,0:T(8,128)(2,1)}, bf16[512,768]{1,0:T(8,128)(2,1)}, u32[]{:S(2)}, u32[]{:S(2)}) collective-permute-start(bf16[512,768]{1,0:T(8,128)(2,1)} %add_convert_fusion.8), channel_id=1, source_target_pairs={{0,8},{8,0},{16,24},{24,16},{1,9},{9,1},{17,25},{25,17},{2,10},{10... | collective-permute-start | bytes 2359304 | tf_op jit(solution)/shard_map/ppermute | solution.py:860
  749.0 100.2 %copy-start.28 = (bf16[2048,256]{1,0:T(8,128)(2,1)S(1)}, bf16[2048,256]{1,0:T(8,128)(2,1)}, u32[]{:S(2)}) copy-start(bf16[2048,256]{1,0:T(8,128)(2,1)} %get-tuple-element.111.refs_0_) | copy-start | bytes 3145732
  856.9 80.0 %collective-permute-start.19 = (bf16[1024,256]{1,0:T(8,128)(2,1)}, bf16[1024,256]{1,0:T(8,128)(2,1)}, u32[]{:S(2)}, u32[]{:S(2)}) collective-permute-start(bf16[1024,256]{1,0:T(8,128)(2,1)} %constant_dynamic-slice_fusion.1), channel_id=1, source_target_pairs={{0,8},{24,16},{1,9},{25,17},{2,10},{26,18},{3,11},{27,19},{4,12},{... | collective-permute-start | bytes 1572872 | tf_op jit(solution)/shard_map/ppermute | solution.py:833
  866.0 73.3 %collective-permute-start.18 = (bf16[1024,1536]{1,0:T(8,128)(2,1)}, bf16[1024,1536]{1,0:T(8,128)(2,1)S(1)}, u32[]{:S(2)}, u32[]{:S(2)}) collective-permute-start(bf16[1024,1536]{1,0:T(8,128)(2,1)} %add_convert_fusion), channel_id=1, source_target_pairs={{8,16},{16,8},{9,17},{17,9},{10,18},{18,10},{11,19},{19,11},{12,20... | collective-permute-start | bytes 9437192 | tf_op jit(solution)/shard_map/ppermute | solution.py:852
  874.2 235.9 %reduce-scatter.3.cloned.1.call-start = ((), (), s32[]{:S(2)}) async-start(), calls=%async_computation.4 | async-start | bytes 9437184 | tf_op jit(solution)/shard_map/reduce_scatter | solution.py:1367
  902.6 163.4 %collective-permute-start.24 = (bf16[512,1536]{1,0:T(8,128)(2,1)}, bf16[512,1536]{1,0:T(8,128)(2,1)}, u32[]{:S(2)}, u32[]{:S(2)}) collective-permute-start(bf16[512,1536]{1,0:T(8,128)(2,1)} %add_convert_fusion.5), channel_id=1, source_target_pairs={{0,8},{8,0},{16,24},{24,16},{1,9},{9,1},{17,25},{25,17},{2,10},{10... | collective-permute-start | bytes 4718600 | tf_op jit(solution)/shard_map/ppermute | solution.py:860
  907.3 179.6 %collective-permute-start.25 = (bf16[512,1536]{1,0:T(8,128)(2,1)}, bf16[512,1536]{1,0:T(8,128)(2,1)}, u32[]{:S(2)}, u32[]{:S(2)}) collective-permute-start(bf16[512,1536]{1,0:T(8,128)(2,1)} %add_convert_fusion.4), channel_id=1, source_target_pairs={{0,8},{8,0},{16,24},{24,16},{1,9},{9,1},{17,25},{25,17},{2,10},{10... | collective-permute-start | bytes 4718600 | tf_op jit(solution)/shard_map/ppermute | solution.py:860
  939.3 32.2 %collective-permute-start.20 = (bf16[1024,256]{1,0:T(8,128)(2,1)}, bf16[1024,256]{1,0:T(8,128)(2,1)}, u32[]{:S(2)}, u32[]{:S(2)}) collective-permute-start(bf16[1024,256]{1,0:T(8,128)(2,1)} %add_convert_fusion.9), channel_id=1, source_target_pairs={{8,16},{16,8},{9,17},{17,9},{10,18},{18,10},{11,19},{19,11},{12,20... | collective-permute-start | bytes 1572872 | tf_op jit(solution)/shard_map/ppermute | solution.py:852
  944.5 149.3 %collective-permute-start.22 = (bf16[512,1536]{1,0:T(8,128)(2,1)}, bf16[512,1536]{1,0:T(8,128)(2,1)}, u32[]{:S(2)}, u32[]{:S(2)}) collective-permute-start(bf16[512,1536]{1,0:T(8,128)(2,1)} %add_convert_fusion.3), channel_id=1, source_target_pairs={{0,8},{8,0},{16,24},{24,16},{1,9},{9,1},{17,25},{25,17},{2,10},{10... | collective-permute-start | bytes 4718600 | tf_op jit(solution)/shard_map/ppermute | solution.py:860
  973.3 111.4 %collective-permute-start.21 = (bf16[512,256]{1,0:T(8,128)(2,1)}, bf16[512,256]{1,0:T(8,128)(2,1)}, u32[]{:S(2)}, u32[]{:S(2)}) collective-permute-start(bf16[512,256]{1,0:T(8,128)(2,1)} %add_convert_fusion.10), channel_id=1, source_target_pairs={{0,8},{8,0},{16,24},{24,16},{1,9},{9,1},{17,25},{25,17},{2,10},{10... | collective-permute-start | bytes 786440 | tf_op jit(solution)/shard_map/ppermute | solution.py:860
  (63 other events, 644.3 us)
Sparse Core Ops, SparseCore 0:
  11.1 58.9 all-gather.4
  71.9 55.9 all-gather.6
  874.3 17.6 reduce-scatter.4
  895.7 69.4 reduce-scatter.2

commit v16 on v15

--- a/solution.py
+++ b/solution.py
@@ -1323,10 +1323,10 @@
                 [first_hidden] + hiddens[1:], wholes, 2, bf16, hop=(3, next_pieces[:1]), number=12
             )
             gathered[4] = (packs[4], *carried, *next_pieces, last_piece)
-            waits = (dscaled_early, moe_early)
+            waits = (dscaled_early, moe_early) + reduced[0].third((moe_early,))
     now = (sums,)
     if planar:
-        waits = reduced[0].third(now)
+        waits = reduced[1].third(now)
     else:
         waits = ()
         for one in reduced:
@@ -1373,7 +1373,6 @@
         dcontext = after(
             dcontext,
             reduced[3].second((dattn,)),
-            reduced[1].third((dattn,)),
             reduced[2].third((dattn,)),
             (out_reduced.pair,),
         )

time: 1140 us -> 1140 us (level)
    unnamed x136 -> x144, local copies, waits for them, and re-layouts: 20.4 us -> 23.7 us
where the time goes in v16:
time: 1140 us; the launch traced here: 1130 us
  Pallas kernels  788 us (69%)
  other arithmetic  101 us (9%)
  local copies, waits for them, and re-layouts  72.1 us (6%)
  starting transfers between devices  55.9 us (5%)
  matrix products  45.1 us (4%)
  blocking collectives  36.7 us (3%)
  between operations  15.6 us (1%)
  waiting for transfers between devices  12.8 us (1%)
    pallas_call x3, Pallas kernels, plane_step(): pl.pallas_call(functools.partial(plane_kernel, pointwise, len(inputs), ma...  287 us
    pallas_call x5, Pallas kernels, expert_chunk(): pl.pallas_call(functools.partial(expert_kernel, size, steps, count, hop a...  196 us
    pallas_call x7, Pallas kernels, joint_back(): pl.pallas_call(functools.partial(joint_kernel, len(lefts), len(base), pla...  142 us
    pallas_call x1, Pallas kernels, hop_now(): pl.pallas_call(functools.partial(hop_kernel, hop[0]), in_specs=[anywhere]...  64.8 us
    pallas_call x1, Pallas kernels, gather_now(): pl.pallas_call(functools.partial(gather_kernel, count), in_specs=[anywher...  57.7 us
    pallas_call x1, Pallas kernels, attend_backward(): pl.pallas_call(attend_backward_kernel, grid_spec=pltpu.PrefetchScalarGrid...  28.8 us
    unnamed x144, local copies, waits for them, and re-layouts  23.7 us
    dot_general x3, matrix products, mm_tn(): lax.dot_general(left, right, (((0,), (0,)), ((), ())), preferred_element_...  22.8 us
  transfers between devices with their start and end apart: 30, of which 2 were waited for; matrix products, arithmetic and copies ran while one was open for 18% of the time, Pallas kernels for 67%

profile of v16, /device:TPU:0, one launch (start us, length us, event | category | flops | bytes accessed | tf_op | source)
XLA Modules:
  0.0 1127.2 jit_solution(9050170142374801426)
XLA Ops:
  14.4 57.7 %gather_rows.1 = bf16[4,512,768]{2,1,0:T(8,128)(2,1)} custom-call(bf16[512,768]{1,0:T(8,128)(2,1)} %copy.135.refs_0_), custom_call_target="tpu_custom_call" | custom-call | flops 42467328000 | bytes 4718592 | tf_op jit(solution)/shard_map/gather_rows/pallas_call | solution.py:786
  108.2 6.3 collective-permute-done.6
  117.1 5.8 collective-permute-done.8
  132.9 10.5 fusion.12.raw_ref
  143.4 12.7 %attend_forward.1 = (bf16[2048,768]{1,0:T(8,128)(2,1)}, bf16[2048,256]{1,0:T(8,128)(2,1)}, f32[2048,256]{1,0:T(8,128)}) custom-call(s32[2]{0:T(128)} %dynamic_slice.101.length_ref, f32[2048,768]{1,0:T(8,128)} %fusion.12.raw_ref, f32[1024,128]{1,0:T(8,128)} %get-tuple-element.319.cos_ref, f32[1024,128]{1,0:T(8,128)} %get-tuple-element.320.sin_ref), custom_call_target="tpu_custom_call" | custom-call | flops 1610612736 | bytes 12582912 | tf_op jit(solution)/shard_map/attend_forward/pallas_call | solution.py:81
  156.1 8.7 joint_back.7.refs_0_
  164.7 112.2 %plane_step.3 = (f32[2048,256]{1,0:T(8,128)}, bf16[2048,2048]{1,0:T(8,128)(2,1)}, bf16[4,512,1536]{2,1,0:T(8,128)(2,1)}) custom-call(bf16[2,2,2,2048,256]{4,3,2,1,0:T(8,128)(2,1)} %joint_back.7.refs_0_, bf16[2048,256]{1,0:T(8,128)(2,1)} %refs_1_.1, f32[1,256]{1,0:T(1,128)} %reshape_convert_fusion.refs_2_.refs_5_, ...), custom_call_target="tpu_custom_call" | custom-call | flops 60000002048 | bytes 16777216 | tf_op jit(solution)/shard_map/plane_step/pallas_call | solution.py:751
  276.9 5.8 multiply_reduce_fusion
  289.1 37.5 %expert_chunk.5 = (bf16[2048,512]{1,0:T(8,128)(2,1)}, bf16[2048,256]{1,0:T(8,128)(2,1)}, f32[2048,2]{1,0:T(8,128)}, bf16[2048,768]{1,0:T(8,128)(2,1)}, bf16[2048...) custom-call(bf16[512,768]{1,0:T(8,128)(2,1)} %fusion.16.refs_0_, ...), custom_call_target="tpu_custom_call" | custom-call | flops 12884901888 | bytes 46137344 | tf_op jit(solution)/shard_map/expert_chunk/pallas_call | solution.py:1007
  334.4 40.5 %expert_chunk.6 = (bf16[2048,1024]{1,0:T(8,128)(2,1)}, bf16[2048,512]{1,0:T(8,128)(2,1)}, f32[2048,2]{1,0:T(8,128)}, bf16[2048,1536]{1,0:T(8,128)(2,1)}, bf16[20...) custom-call(bf16[512,1536]{1,0:T(8,128)(2,1)} %get-tuple-element.317.refs_3_.refs_0_, ...), custom_call_target="tpu_custom_call" | custom-call | flops 25769803776 | bytes 58720256 | tf_op jit(solution)/shard_map/expert_chunk/pallas_call | solution.py:1007
  389.8 36.8 %joint_back.8 = (f32[2048,2048]{1,0:T(8,128)}, bf16[512,1536]{1,0:T(8,128)(2,1)}) custom-call(bf16[2048,512]{1,0:T(8,128)(2,1)} %get-tuple-element.127.refs_0_, bf16[2048,1024]{1,0:T(8,128)(2,1)} %get-tuple-element.128.refs_1_, bf16[2048,768]{1,0:T(8,128)(2,1)} %get-tuple-element.129.refs_2_.refs_4_, bf16[2048,1536]{1,0:T(8,128)(2,1)} %get-tuple-element.130.refs_3_.refs_5_, ...), custom_call_target="tpu_custom_call" | custom-call | flops 12884901888 | bytes 29360128 | tf_op jit(solution)/shard_map/joint_back/pallas_call | solution.py:1093
  428.0 40.5 %expert_chunk.7 = (bf16[2048,1024]{1,0:T(8,128)(2,1)}, bf16[2048,512]{1,0:T(8,128)(2,1)}, f32[2048,2]{1,0:T(8,128)}, bf16[2048,1536]{1,0:T(8,128)(2,1)}, bf16[20...) custom-call(bf16[512,1536]{1,0:T(8,128)(2,1)} %get-tuple-element.318.refs_11_.refs_0_, ...), custom_call_target="tpu_custom_call" | custom-call | flops 25769803776 | bytes 58720256 | tf_op jit(solution)/shard_map/expert_chunk/pallas_call | solution.py:1007
  472.2 5.4 collective-permute-start.13
  477.6 64.8 %gather_hops.1 = (bf16[512,1536]{1,0:T(8,128)(2,1)}, bf16[512,1536]{1,0:T(8,128)(2,1)}, bf16[512,1536]{1,0:T(8,128)(2,1)}) custom-call(bf16[512,1536]{1,0:T(8,128)(2,1)} %get-tuple-element.138.refs_0_.refs_1_, bf16[512,1536]{1,0:T(8,128)(2,1)} %get-tuple-element.135.refs_1_.refs_2_), custom_call_target="tpu_custom_call" | custom-call | tf_op jit(solution)/shard_map/gather_hops/pallas_call | solution.py:515
  543.7 40.4 %expert_chunk.8 = (bf16[2048,1024]{1,0:T(8,128)(2,1)}, bf16[2048,512]{1,0:T(8,128)(2,1)}, f32[2048,2]{1,0:T(8,128)}, bf16[2048,1536]{1,0:T(8,128)(2,1)}, bf16[20...) custom-call(bf16[512,1536]{1,0:T(8,128)(2,1)} %pad_maximum_fusion.2.refs_11_.refs_0_, ...), custom_call_target="tpu_custom_call" | custom-call | flops 25769803776 | bytes 58720256 | tf_op jit(solution)/shard_map/expert_chunk/pallas_call | solution.py:1007
  595.9 29.6 %joint_back.9 = (bf16[2048,2048]{1,0:T(8,128)(2,1)}, bf16[512,1152]{1,0:T(8,128)(2,1)}, bf16[512,1152]{1,0:T(8,128)(2,1)}) custom-call(bf16[2048,1024]{1,0:T(8,128)(2,1)} %get-tuple-element.149.refs_0_, bf16[2048,1024]{1,0:T(8,128)(2,1)} %get-tuple-element.150.refs_1_, bf16[2048,1536]{1,0:T(8,128)(2,1)} %get-tuple-element.151.refs_2_.refs_6_, ...), custom_call_target="tpu_custom_call" | custom-call | flops 17179869184 | bytes 33554432 | tf_op jit(solution)/shard_map/joint_back/pallas_call | solution.py:1093
  642.1 28.8 %joint_back.10 = (bf16[2048,2048]{1,0:T(8,128)(2,1)}, bf16[512,1152]{1,0:T(8,128)(2,1)}) custom-call(bf16[2048,256]{1,0:T(8,128)(2,1)} %get-tuple-element.159.refs_0_, bf16[2048,512]{1,0:T(8,128)(2,1)} %get-tuple-element.160.refs_1_, bf16[2048,512]{1,0:T(8,128)(2,1)} %get-tuple-element.161.refs_2_, bf16[2048,512]{1,0:T(8,128)(2,1)} %get-tuple-element.162.refs_3_, ...), custom_call_target="tpu_custom_call" | custom-call | flops 15032385536 | bytes 31457280 | tf_op jit(solution)/shard_map/joint_back/pallas_call | solution.py:1093
  674.4 37.0 %expert_chunk.9 = (bf16[2048,768]{1,0:T(8,128)(2,1)}, bf16[2048,384]{1,0:T(8,128)(2,1)}, f32[2048,2]{1,0:T(8,128)}, bf16[2048,1152]{1,0:T(8,128)(2,1)}, bf16[2048,1152]{1,0:T(8,128)(2,1)}) custom-call(bf16[512,1152]{1,0:T(8,128)(2,1)} %pad_maximum_fusion.7.refs_11_.refs_0_, bf16[512,1152]{1,0:T(8,128)(2,1)} %get-tuple-element.143.refs_5_.refs_1_, ...), custom_call_target="tpu_custom_call" | custom-call | flops 19327352832 | bytes 52428800 | tf_op jit(solution)/shard_map/expert_chunk/pallas_call | solution.py:1007
  716.3 13.5 %all-gather.1 = f32[8,3,2048]{2,1,0:T(4,128)S(1)} all-gather(f32[1,3,2048]{2,1,0:T(4,128)S(1)} %maximum_bitcast_fusion.3), channel_id=2, replica_groups=mesh['row'=4,'col'=8] {'col'}, dimensions={0}, use_global_device_ids=true | all-gather | bytes 221184 | tf_op jit(solution)/shard_map/all_gather | solution.py:1342
  739.0 13.9 %joint_back.11.refs_0_ = bf16[2,2,2,2048,256]{4,3,2,1,0:T(8,128)(2,1)} custom-call(bf16[2048,768]{1,0:T(8,128)(2,1)} %get-tuple-element.171.refs_0_, bf16[2048,1152]{1,0:T(8,128)(2,1)} %get-tuple-element.172.refs_1_, bf16[2048,2048]{1,0:T(8,128)(2,1)} %get-tuple-element.156.refs_2_), custom_call_target="tpu_custom_call" | custom-call | flops 6442450944 | bytes 23068672 | tf_op jit(solution)/shard_map/joint_back/pallas_call | solution.py:1093
  752.9 103.8 %plane_step.4 = (f32[2048,256]{1,0:T(8,128)}, f32[2048,256]{1,0:T(8,128)}, f32[512,1152]{1,0:T(8,128)}, bf16[2048,2048]{1,0:T(8,128)(2,1)}) custom-call(bf16[2,2,2,2048,256]{4,3,2,1,0:T(8,128)(2,1)} %joint_back.11.refs_0_, f32[2048,256]{1,0:T(8,128)} %fusion.30.refs_1_, bf16[2048,256]{1,0:T(8,128)(2,1)} %refs_2_.1, f32[2048,256]{1,0:T(8,128)} %get-tuple-element.114.refs_3_, ...), custom_call_target="tpu_custom_call" | custom-call | flops 60000002048 | bytes 16777216 | tf_op jit(solution)/shard_map/plane_step/pallas_call | solution.py:751
  856.8 5.9 convolution_convert_fusion.1
  867.5 5.3 add_convert_fusion
  873.7 5.6 fusion.46
  881.3 12.0 %joint_back.12 = bf16[2048,2048]{1,0:T(8,128)(2,1)} custom-call(bf16[2048,384]{1,0:T(8,128)(2,1)} %get-tuple-element.176.refs_0_, bf16[2048,1152]{1,0:T(8,128)(2,1)} %get-tuple-element.172.refs_1_, bf16[2048,2048]{1,0:T(8,128)(2,1)} %get-tuple-element.164.refs_2_), custom_call_target="tpu_custom_call" | custom-call | flops 3221225472 | bytes 19922944 | tf_op jit(solution)/shard_map/joint_back/pallas_call | solution.py:1093
  896.4 6.7 convolution_convert_fusion.2.dcontext_ref
  910.5 28.8 %attend_backward.1 = (bf16[2048,768]{1,0:T(8,128)(2,1)}, f32[2048,1]{1,0:T(8,128)}) custom-call(s32[2]{0:T(128)} %dynamic_slice.101.length_ref, bf16[2048,768]{1,0:T(8,128)(2,1)} %get-tuple-element.178.qkv_ref, bf16[2048,256]{1,0:T(8,128)(2,1)} %convolution_convert_fusion.2.dcontext_ref, f32[2048,256]{1,0:T(8,128)} %get-tuple-element.182.lse_ref, ...), custom_call_target="tpu_custom_call" | custom-call | flops 4294967296 | bytes 12582912 | tf_op jit(solution)/shard_map/attend_backward/pallas_call | solution.py:151
  944.6 12.6 %psum.21 = f32[2048]{0:T(1024)S(1)} all-reduce(f32[2048]{0:T(1024)S(1)} %reduce.5), channel_id=1, replica_groups=mesh['row'=4,'col'=8] {'col'}, use_global_device_ids=true, to_apply=%region_10.11 | all-reduce | flops 2048 | bytes 16384 | tf_op jit(solution)/shard_map/psum | solution.py:1385
  964.4 11.3 %convolution_convert_fusion = bf16[2048,768]{1,0:T(8,128)(2,1)} fusion(bf16[2048,768]{1,0:T(8,128)(2,1)S(1)} %copy-done.59, f32[2048]{0:T(1024)S(1)} %bitcast.122, f32[2048]{0:T(1024)S(1)} %copy-done.45, bf16[2064,2048]{1,0:T(8,128)(2,1)} %all-gather.5.cloned.1.call-done), kind=kOutput, calls=%fused_computation.10 | convolution fusion | flops 6460801024 | bytes 14696448 | tf_op jit(solution)/shard_map/dot_general | solution.py:30
  977.5 12.1 %joint_back.13.refs_0_ = bf16[2,2,2,2048,256]{4,3,2,1,0:T(8,128)(2,1)} custom-call(bf16[2048,768]{1,0:T(8,128)(2,1)} %get-tuple-element.189.refs_0_, bf16[2048,768]{1,0:T(8,128)(2,1)} %constant_dynamic-update-slice_fusion.4.refs_1_), custom_call_target="tpu_custom_call" | custom-call | flops 6442450944 | bytes 23068672 | tf_op jit(solution)/shard_map/joint_back/pallas_call | solution.py:1093
  989.6 70.8 %plane_step.5 = (f32[2048,256]{1,0:T(8,128)}, f32[512,768]{1,0:T(8,128)}) custom-call(bf16[2,2,2,2048,256]{4,3,2,1,0:T(8,128)(2,1)} %joint_back.13.refs_0_, bf16[4,512,768]{2,1,0:T(8,128)(2,1)} %bitcast.127), custom_call_target="tpu_custom_call" | custom-call | flops 60000002048 | bytes 16777216 | tf_op jit(solution)/shard_map/plane_step/pallas_call | solution.py:751
  1109.6 10.5 all-reduce.5
  (332 shorter events, 217.9 us)
Async XLA Ops:
  7.2 119.5 %all-gather.5.cloned.1.call-start = ((), (), s32[]{:S(2)}) async-start(), calls=%async_computation.2 | async-start | bytes 9510912 | tf_op jit(solution)/shard_map/all_gather | solution.py:1222
  11.0 153.8 %all-gather.7.cloned.1.call-start = ((), (), s32[]{:S(2)}) async-start(), calls=%async_computation.3 | async-start | bytes 9437184 | tf_op jit(solution)/shard_map/all_gather | solution.py:1226
  11.7 891.4 %reduce-scatter.5.cloned.1.call-start = ((), (), s32[]{:S(2)}) async-start(), calls=%async_computation.5 | async-start | bytes 163840 | tf_op jit(solution)/shard_map/reduce_scatter | solution.py:1381
  72.0 25.9 %collective-permute-start.4 = (bf16[512,384]{0,1:T(8,128)(2,1)}, bf16[512,384]{0,1:T(8,128)(2,1)}, u32[]{:S(2)}, u32[]{:S(2)}) collective-permute-start(bf16[512,384]{0,1:T(8,128)(2,1)} %get-tuple-element.112), channel_id=1, source_target_pairs={{0,8},{8,0},{16,24},{24,16},{1,9},{9,1},{17,25},{25,17},{2,10},{10... | collective-permute-start | bytes 1179656 | tf_op jit(solution)/shard_map/ppermute | solution.py:184
  72.1 29.5 %collective-permute-start.5 = (bf16[512,384]{0,1:T(8,128)(2,1)}, bf16[512,384]{0,1:T(8,128)(2,1)}, u32[]{:S(2)}, u32[]{:S(2)}) collective-permute-start(bf16[512,384]{0,1:T(8,128)(2,1)} %get-tuple-element.112), channel_id=1, source_target_pairs={{8,16},{16,8},{9,17},{17,9},{10,18},{18,10},{11,19},{19,11},{12,20... | collective-permute-start | bytes 1179656 | tf_op jit(solution)/shard_map/ppermute | solution.py:185
  75.0 31.7 %collective-permute-start = (bf16[512,768]{1,0:T(8,128)(2,1)}, bf16[512,768]{1,0:T(8,128)(2,1)}, u32[]{:S(2)}, u32[]{:S(2)}) collective-permute-start(bf16[512,768]{1,0:T(8,128)(2,1)} %fusion.16.refs_0_), channel_id=1, source_target_pairs={{0,8},{8,0},{16,24},{24,16},{1,9},{9,1},{17,25},{25,17},{2,10},{10... | collective-permute-start | bytes 2359304 | tf_op jit(solution)/shard_map/ppermute | solution.py:184
  79.0 36.8 %collective-permute-start.1 = (bf16[512,768]{1,0:T(8,128)(2,1)}, bf16[512,768]{1,0:T(8,128)(2,1)}, u32[]{:S(2)}, u32[]{:S(2)}) collective-permute-start(bf16[512,768]{1,0:T(8,128)(2,1)} %fusion.16.refs_0_), channel_id=1, source_target_pairs={{8,16},{16,8},{9,17},{17,9},{10,18},{18,10},{11,19},{19,11},{12,20... | collective-permute-start | bytes 2359304 | tf_op jit(solution)/shard_map/ppermute | solution.py:185
  98.0 7.3 collective-permute-start.7
  101.6 184.6 %copy-start.47 = (pred[2048]{0:T(1024)(128)(4,1)}, pred[2048]{0:T(1024)(128)(4,1)S(1)}, u32[]{:S(2)}) copy-start(pred[2048]{0:T(1024)(128)(4,1)S(1)} %compare_reduce_fusion) | copy-start | bytes 6148
  101.6 12.9 %collective-permute-start.6 = (bf16[512,384]{0,1:T(8,128)(2,1)}, bf16[512,384]{0,1:T(8,128)(2,1)S(1)}, u32[]{:S(2)}, u32[]{:S(2)}) collective-permute-start(bf16[512,384]{0,1:T(8,128)(2,1)} %collective-permute-done.5), channel_id=1, source_target_pairs={{8,0},{16,24},{9,1},{17,25},{10,2},{18,26},{11,3},{19,27},{12,4},{... | collective-permute-start | bytes 1179656 | tf_op jit(solution)/shard_map/ppermute | solution.py:190
  105.3 17.6 %collective-permute-start.8 = (bf16[512,384]{0,1:T(8,128)(2,1)}, bf16[512,384]{0,1:T(8,128)(2,1)S(1)}, u32[]{:S(2)}, u32[]{:S(2)}) collective-permute-start(bf16[512,384]{0,1:T(8,128)(2,1)} %collective-permute-done.7), channel_id=1, source_target_pairs={{8,0},{16,24},{9,1},{17,25},{10,2},{18,26},{11,3},{19,27},{12,4},{... | collective-permute-start | bytes 1179656 | tf_op jit(solution)/shard_map/ppermute | solution.py:197
  106.6 18.5 %collective-permute-start.2 = (bf16[512,768]{1,0:T(8,128)(2,1)}, bf16[512,768]{1,0:T(8,128)(2,1)}, u32[]{:S(2)}, u32[]{:S(2)}) collective-permute-start(bf16[512,768]{1,0:T(8,128)(2,1)} %collective-permute-done.refs_1_), channel_id=1, source_target_pairs={{8,16},{16,8},{9,17},{17,9},{10,18},{18,10},{11,19},{19,11},{12,20... | collective-permute-start | bytes 2359304 | tf_op jit(solution)/shard_map/ppermute | solution.py:191
  115.8 40.3 %collective-permute-start.3 = (bf16[512,768]{1,0:T(8,128)(2,1)}, bf16[512,768]{1,0:T(8,128)(2,1)S(1)}, u32[]{:S(2)}, u32[]{:S(2)}) collective-permute-start(bf16[512,768]{1,0:T(8,128)(2,1)} %collective-permute-done.1.refs_2_), channel_id=1, source_target_pairs={{8,0},{16,24},{9,1},{17,25},{10,2},{18,26},{11,3},{19,27},{12,4},{... | collective-permute-start | bytes 2359304 | tf_op jit(solution)/shard_map/ppermute | solution.py:190
  125.2 163.0 %collective-permute-start.9 = (bf16[512,768]{1,0:T(8,128)(2,1)}, bf16[512,768]{1,0:T(8,128)(2,1)S(1)}, u32[]{:S(2)}, u32[]{:S(2)}) collective-permute-start(bf16[512,768]{1,0:T(8,128)(2,1)} %collective-permute-done.2.refs_3_), channel_id=1, source_target_pairs={{8,0},{16,24},{9,1},{17,25},{10,2},{18,26},{11,3},{19,27},{12,4},{... | collective-permute-start | bytes 2359304 | tf_op jit(solution)/shard_map/ppermute | solution.py:197
  329.2 55.8 %collective-permute-start.10 = (bf16[1024,768]{1,0:T(8,128)(2,1)}, bf16[1024,768]{1,0:T(8,128)(2,1)}, u32[]{:S(2)}, u32[]{:S(2)}) collective-permute-start(bf16[1024,768]{1,0:T(8,128)(2,1)} %constant_dynamic-slice_fusion.7), channel_id=1, source_target_pairs={{0,8},{24,16},{1,9},{25,17},{2,10},{26,18},{3,11},{27,19},{4,12},{... | collective-permute-start | bytes 4718600 | tf_op jit(solution)/shard_map/ppermute | solution.py:833
  378.7 246.7 %collective-permute-start.11 = (bf16[512,1536]{1,0:T(8,128)(2,1)}, bf16[512,1536]{1,0:T(8,128)(2,1)}, u32[]{:S(2)}, u32[]{:S(2)}) collective-permute-start(bf16[512,1536]{1,0:T(8,128)(2,1)} %get-tuple-element.280), channel_id=1, source_target_pairs={{0,8},{24,16},{1,9},{25,17},{2,10},{26,18},{3,11},{27,19},{4,12},{... | collective-permute-start | bytes 4718600 | tf_op jit(solution)/shard_map/ppermute | solution.py:831
  388.0 282.9 %collective-permute-start.14 = (bf16[1024,768]{1,0:T(8,128)(2,1)}, bf16[1024,768]{1,0:T(8,128)(2,1)}, u32[]{:S(2)}, u32[]{:S(2)}) collective-permute-start(bf16[1024,768]{1,0:T(8,128)(2,1)} %add_convert_fusion.6), channel_id=1, source_target_pairs={{8,16},{16,8},{9,17},{17,9},{10,18},{18,10},{11,19},{19,11},{12,20... | collective-permute-start | bytes 4718600 | tf_op jit(solution)/shard_map/ppermute | solution.py:852
  472.2 162.7 %collective-permute-start.13 = (bf16[1024,1536]{1,0:T(8,128)(2,1)}, bf16[1024,1536]{1,0:T(8,128)(2,1)}, u32[]{:S(2)}, u32[]{:S(2)}) collective-permute-start(bf16[1024,1536]{1,0:T(8,128)(2,1)} %constant_dynamic-slice_fusion.5), channel_id=1, source_target_pairs={{0,8},{24,16},{1,9},{25,17},{2,10},{26,18},{3,11},{27,19},{4,12},{... | collective-permute-start | bytes 9437192 | tf_op jit(solution)/shard_map/ppermute | solution.py:833
  584.2 41.3 %collective-permute-start.12 = (bf16[512,1536]{1,0:T(8,128)(2,1)}, bf16[512,1536]{1,0:T(8,128)(2,1)}, u32[]{:S(2)}, u32[]{:S(2)}) collective-permute-start(bf16[512,1536]{1,0:T(8,128)(2,1)} %get-tuple-element.147), channel_id=1, source_target_pairs={{0,8},{24,16},{1,9},{25,17},{2,10},{26,18},{3,11},{27,19},{4,12},{... | collective-permute-start | bytes 4718600 | tf_op jit(solution)/shard_map/ppermute | solution.py:837
  592.9 269.8 %collective-permute-start.16 = (bf16[1024,1536]{1,0:T(8,128)(2,1)}, bf16[1024,1536]{1,0:T(8,128)(2,1)}, u32[]{:S(2)}, u32[]{:S(2)}) collective-permute-start(bf16[1024,1536]{1,0:T(8,128)(2,1)} %constant_dynamic-slice_fusion.4), channel_id=1, source_target_pairs={{0,8},{24,16},{1,9},{25,17},{2,10},{26,18},{3,11},{27,19},{4,12},{... | collective-permute-start | bytes 9437192 | tf_op jit(solution)/shard_map/ppermute | solution.py:833
  632.5 101.1 %collective-permute-start.15 = (bf16[1024,1536]{1,0:T(8,128)(2,1)}, bf16[1024,1536]{1,0:T(8,128)(2,1)}, u32[]{:S(2)}, u32[]{:S(2)}) collective-permute-start(bf16[1024,1536]{1,0:T(8,128)(2,1)} %add_convert_fusion.2), channel_id=1, source_target_pairs={{8,16},{16,8},{9,17},{17,9},{10,18},{18,10},{11,19},{19,11},{12,20... | collective-permute-start | bytes 9437192 | tf_op jit(solution)/shard_map/ppermute | solution.py:852
  639.4 266.4 %collective-permute-start.17 = (bf16[1024,1536]{1,0:T(8,128)(2,1)}, bf16[1024,1536]{1,0:T(8,128)(2,1)}, u32[]{:S(2)}, u32[]{:S(2)}) collective-permute-start(bf16[1024,1536]{1,0:T(8,128)(2,1)} %add_convert_fusion.1), channel_id=1, source_target_pairs={{8,16},{16,8},{9,17},{17,9},{10,18},{18,10},{11,19},{19,11},{12,20... | collective-permute-start | bytes 9437192 | tf_op jit(solution)/shard_map/ppermute | solution.py:852
  673.1 403.9 %collective-permute-start.23 = (bf16[512,768]{1,0:T(8,128)(2,1)}, bf16[512,768]{1,0:T(8,128)(2,1)}, u32[]{:S(2)}, u32[]{:S(2)}) collective-permute-start(bf16[512,768]{1,0:T(8,128)(2,1)} %add_convert_fusion.8), channel_id=1, source_target_pairs={{0,8},{8,0},{16,24},{24,16},{1,9},{9,1},{17,25},{25,17},{2,10},{10... | collective-permute-start | bytes 2359304 | tf_op jit(solution)/shard_map/ppermute | solution.py:860
  737.0 323.4 %collective-permute-start.24 = (bf16[512,1536]{1,0:T(8,128)(2,1)}, bf16[512,1536]{1,0:T(8,128)(2,1)}, u32[]{:S(2)}, u32[]{:S(2)}) collective-permute-start(bf16[512,1536]{1,0:T(8,128)(2,1)} %add_convert_fusion.5), channel_id=1, source_target_pairs={{0,8},{8,0},{16,24},{24,16},{1,9},{9,1},{17,25},{25,17},{2,10},{10... | collective-permute-start | bytes 4718600 | tf_op jit(solution)/shard_map/ppermute | solution.py:860
  752.9 103.8 %copy-start.32 = (bf16[2048,256]{1,0:T(8,128)(2,1)S(1)}, bf16[2048,256]{1,0:T(8,128)(2,1)}, u32[]{:S(2)}) copy-start(bf16[2048,256]{1,0:T(8,128)(2,1)} %get-tuple-element.111.refs_0_) | copy-start | bytes 3145732
  864.5 74.9 %collective-permute-start.19 = (bf16[1024,256]{1,0:T(8,128)(2,1)}, bf16[1024,256]{1,0:T(8,128)(2,1)}, u32[]{:S(2)}, u32[]{:S(2)}) collective-permute-start(bf16[1024,256]{1,0:T(8,128)(2,1)} %constant_dynamic-slice_fusion.1), channel_id=1, source_target_pairs={{0,8},{24,16},{1,9},{25,17},{2,10},{26,18},{3,11},{27,19},{4,12},{... | collective-permute-start | bytes 1572872 | tf_op jit(solution)/shard_map/ppermute | solution.py:833
  872.8 84.5 %collective-permute-start.18 = (bf16[1024,1536]{1,0:T(8,128)(2,1)}, bf16[1024,1536]{1,0:T(8,128)(2,1)S(1)}, u32[]{:S(2)}, u32[]{:S(2)}) collective-permute-start(bf16[1024,1536]{1,0:T(8,128)(2,1)} %add_convert_fusion), channel_id=1, source_target_pairs={{8,16},{16,8},{9,17},{17,9},{10,18},{18,10},{11,19},{19,11},{12,20... | collective-permute-start | bytes 9437192 | tf_op jit(solution)/shard_map/ppermute | solution.py:852
  881.0 224.8 %reduce-scatter.3.cloned.1.call-start = ((), (), s32[]{:S(2)}) async-start(), calls=%async_computation.4 | async-start | bytes 9437184 | tf_op jit(solution)/shard_map/reduce_scatter | solution.py:1367
  909.7 150.7 %collective-permute-start.25 = (bf16[512,1536]{1,0:T(8,128)(2,1)}, bf16[512,1536]{1,0:T(8,128)(2,1)}, u32[]{:S(2)}, u32[]{:S(2)}) collective-permute-start(bf16[512,1536]{1,0:T(8,128)(2,1)} %add_convert_fusion.4), channel_id=1, source_target_pairs={{0,8},{8,0},{16,24},{24,16},{1,9},{9,1},{17,25},{25,17},{2,10},{10... | collective-permute-start | bytes 4718600 | tf_op jit(solution)/shard_map/ppermute | solution.py:860
  941.5 34.2 %collective-permute-start.20 = (bf16[1024,256]{1,0:T(8,128)(2,1)}, bf16[1024,256]{1,0:T(8,128)(2,1)}, u32[]{:S(2)}, u32[]{:S(2)}) collective-permute-start(bf16[1024,256]{1,0:T(8,128)(2,1)} %add_convert_fusion.9), channel_id=1, source_target_pairs={{8,16},{16,8},{9,17},{17,9},{10,18},{18,10},{11,19},{19,11},{12,20... | collective-permute-start | bytes 1572872 | tf_op jit(solution)/shard_map/ppermute | solution.py:852
  961.6 133.7 %collective-permute-start.22 = (bf16[512,1536]{1,0:T(8,128)(2,1)}, bf16[512,1536]{1,0:T(8,128)(2,1)}, u32[]{:S(2)}, u32[]{:S(2)}) collective-permute-start(bf16[512,1536]{1,0:T(8,128)(2,1)} %add_convert_fusion.3), channel_id=1, source_target_pairs={{0,8},{8,0},{16,24},{24,16},{1,9},{9,1},{17,25},{25,17},{2,10},{10... | collective-permute-start | bytes 4718600 | tf_op jit(solution)/shard_map/ppermute | solution.py:860
  977.5 115.7 %collective-permute-start.21 = (bf16[512,256]{1,0:T(8,128)(2,1)}, bf16[512,256]{1,0:T(8,128)(2,1)}, u32[]{:S(2)}, u32[]{:S(2)}) collective-permute-start(bf16[512,256]{1,0:T(8,128)(2,1)} %add_convert_fusion.10), channel_id=1, source_target_pairs={{0,8},{8,0},{16,24},{24,16},{1,9},{9,1},{17,25},{25,17},{2,10},{10... | collective-permute-start | bytes 786440 | tf_op jit(solution)/shard_map/ppermute | solution.py:860
  (67 other events, 821.1 us)
Sparse Core Ops, SparseCore 0:
  11.1 58.9 all-gather.4
  71.9 55.9 all-gather.6
  881.1 18.7 reduce-scatter.4
  903.6 69.7 reduce-scatter.2
